TPU v7x, 32 devices: a whole 2x2x4 slice. The times are simulated.
32 devices in a mesh: ctx: 8 (over z, x), fsdp: 4 (over y, core).
Axes of the slice: x: 2, y: 2, z: 4, core: 2. Of those that a mesh axis runs over, the one named last changes fastest.
Arguments:
- inputs: bfloat16 [2, 4, 4096, 512], P(None, 'fsdp', 'ctx'), may hold values from -6 to 6
- out_grad: bfloat16 [2, 4, 4096, 512], P(None, 'fsdp', 'ctx'), may hold values from -6 to 6
- segment_ids: int32 [2, 4, 4096], P(None, 'fsdp', 'ctx'), may hold values from 0 to 15, never falling along the last dimension, each value on 1 to 2048 neighbouring positions
- block_order: int32 [16], replicated, may hold values from 0 to 15, each once
- w_qkv: bfloat16 [512, 1536], P('fsdp'), may hold values from -0.25 to 0.25
- w_out: bfloat16 [512, 512], P('fsdp'), may hold values from -1 to 1
- w_up: bfloat16 [512, 2048], P('fsdp'), may hold values from -0.25 to 0.25
- w_down: bfloat16 [2048, 512], P('fsdp'), may hold values from -0.125 to 0.125
- norm1_gain: bfloat16 [512], P('fsdp'), may hold values from 0.25 to 1.75
- norm1_bias: bfloat16 [512], P('fsdp'), may hold values from -2 to 2
- norm2_gain: bfloat16 [512], P('fsdp'), may hold values from 0.25 to 1.75
- norm2_bias: bfloat16 [512], P('fsdp'), may hold values from -2 to 2
- out_bias: bfloat16 [512], P('fsdp'), may hold values from -2 to 2
- up_bias: bfloat16 [2048], P('fsdp'), may hold values from -3 to 3
- down_bias: bfloat16 [512], P('fsdp'), may hold values from -2 to 2
Outputs:
- outputs: bfloat16 [2, 4, 4096, 512], P(None, 'fsdp', 'ctx')
- input_grad: float32 [2, 4, 4096, 512], P(None, 'fsdp', 'ctx')
- grad_w_qkv: float32 [512, 1536], P('fsdp')
- grad_w_out: float32 [512, 512], P('fsdp')
- grad_w_up: float32 [512, 2048], P('fsdp')
- grad_w_down: float32 [2048, 512], P('fsdp')
- grad_norm1_gain: float32 [512], P('fsdp')
- grad_norm1_bias: float32 [512], P('fsdp')
- grad_norm2_gain: float32 [512], P('fsdp')
- grad_norm2_bias: float32 [512], P('fsdp')
- grad_out_bias: float32 [512], P('fsdp')
- grad_up_bias: float32 [2048], P('fsdp')
- grad_down_bias: float32 [512], P('fsdp')
Inputs may be any that keep to these rules, and one draw needn't show every extreme that they name: `segment_ids`: along each sequence's true positions document numbers start at 0 and never fall; each document has 1 to 2048 tokens and one has exactly 2048. `block_order`: each value appears exactly once.
All inputs are finite; a program needn't handle non-finite values.
Results may differ from a plain program's by a relative error of at most 0.02.
Values may be sent and summed in bfloat16 or wider, within the bound.
A program may use at most 256 MiB of HBM per device.

v0:
```python
import math

import jax
import jax.numpy as jnp
from jax import lax
from jax.sharding import PartitionSpec as P

H = 8
HD = 64
BLK = 256


norm_eps = 1e-05
mask_fill = -1e30


def layer_norm(values, gain_vec, offset):
    center = values - jnp.mean(values, axis=-1, keepdims=True)
    spread = jnp.mean(center * center, axis=-1, keepdims=True)
    return center * lax.rsqrt(spread + norm_eps) * gain_vec + offset


def gelu_exact(values):
    return 0.5 * values * (1.0 + lax.erf(values * (1.0 / math.sqrt(2.0))))


def score_block(query_heads, key_heads, query_doc, query_pos, key_doc, key_pos):
    raw_scores = jnp.einsum(
        "qhd,khd->hqk", query_heads, key_heads, preferred_element_type=jnp.float32
    ) * (1.0 / math.sqrt(HD))
    allowed = (query_doc[:, None] == key_doc[None, :]) & (key_pos[None, :] <= query_pos[:, None])
    return (raw_scores, allowed[None])


def soft_block(raw_scores, allowed, log_norm):
    return jnp.exp(jnp.where(allowed, raw_scores, mask_fill) - log_norm[:, :, None])


def row_log_norm(query_heads, key_blocks, doc_blocks, pos_blocks, query_doc, query_pos):

    def row_visit(running, block_item):
        row_top, row_sum = running
        key_heads, key_doc, key_pos = block_item
        raw_scores, allowed = score_block(
            query_heads, key_heads, query_doc, query_pos, key_doc, key_pos
        )
        masked = jnp.where(allowed, raw_scores, mask_fill)
        new_top = jnp.maximum(row_top, jnp.max(masked, axis=-1))
        fresh = jnp.sum(jnp.where(allowed, jnp.exp(masked - new_top[:, :, None]), 0.0), axis=-1)
        return ((new_top, row_sum * jnp.exp(row_top - new_top) + fresh), None)

    query_count = query_doc.shape[0]
    start = (
        jnp.full((H, query_count), mask_fill, jnp.float32),
        jnp.zeros((H, query_count), jnp.float32),
    )
    (row_top, row_sum), unused = lax.scan(row_visit, start, (key_blocks, doc_blocks, pos_blocks))
    return row_top + jnp.log(row_sum)


def attend(
    query_heads, key_blocks, value_blocks, doc_blocks, pos_blocks, query_doc, query_pos, log_norm
):

    def attend_visit(accum_out, block_item):
        key_heads, value_heads, key_doc, key_pos = block_item
        raw_scores, allowed = score_block(
            query_heads, key_heads, query_doc, query_pos, key_doc, key_pos
        )
        soft_low = soft_block(raw_scores, allowed, log_norm).astype(jnp.bfloat16)
        return (
            accum_out
            + jnp.einsum("hqk,khd->qhd", soft_low, value_heads, preferred_element_type=jnp.float32),
            None,
        )

    start = jnp.zeros(query_heads.shape, jnp.float32)
    accum_out, unused = lax.scan(
        attend_visit, start, (key_blocks, value_blocks, doc_blocks, pos_blocks)
    )
    return accum_out


def grad_block(
    query_heads,
    grad_heads,
    log_norm,
    row_delta,
    query_doc,
    query_pos,
    key_heads,
    value_heads,
    key_doc,
    key_pos,
):
    raw_scores, allowed = score_block(
        query_heads, key_heads, query_doc, query_pos, key_doc, key_pos
    )
    soft = soft_block(raw_scores, allowed, log_norm)
    grad_soft = jnp.einsum(
        "qhd,khd->hqk", grad_heads, value_heads, preferred_element_type=jnp.float32
    )
    grad_scores = (soft * (grad_soft - row_delta[:, :, None])).astype(jnp.bfloat16)
    score_scale = 1.0 / math.sqrt(HD)
    part_q = (
        jnp.einsum("hqk,khd->qhd", grad_scores, key_heads, preferred_element_type=jnp.float32)
        * score_scale
    )
    part_k = (
        jnp.einsum("hqk,qhd->khd", grad_scores, query_heads, preferred_element_type=jnp.float32)
        * score_scale
    )
    part_v = jnp.einsum(
        "hqk,qhd->khd", soft.astype(jnp.bfloat16), grad_heads, preferred_element_type=jnp.float32
    )
    return (part_q, part_k, part_v)


def body(
    inputs,
    out_grad,
    segment_ids,
    block_order,
    w_qkv,
    w_out,
    w_up,
    w_down,
    norm1_gain,
    norm1_bias,
    norm2_gain,
    norm2_bias,
    out_bias,
    up_bias,
    down_bias,
):
    gathered = (
        lax.all_gather(w_qkv, "fsdp", axis=0, tiled=True),
        lax.all_gather(w_out, "fsdp", axis=0, tiled=True),
        lax.all_gather(w_up, "fsdp", axis=0, tiled=True),
        lax.all_gather(w_down, "fsdp", axis=0, tiled=True),
        lax.all_gather(norm1_gain, "fsdp", axis=0, tiled=True),
        lax.all_gather(norm1_bias, "fsdp", axis=0, tiled=True),
        lax.all_gather(norm2_gain, "fsdp", axis=0, tiled=True),
        lax.all_gather(norm2_bias, "fsdp", axis=0, tiled=True),
        lax.all_gather(out_bias, "fsdp", axis=0, tiled=True),
        lax.all_gather(up_bias, "fsdp", axis=0, tiled=True),
        lax.all_gather(down_bias, "fsdp", axis=0, tiled=True),
    )
    full_qkv, full_out, full_up, full_down = (gathered[0], gathered[1], gathered[2], gathered[3])
    gain_one, bias_one, gain_two, bias_two, full_obias, full_ubias, full_dbias = [
        member.astype(jnp.float32) for member in gathered[4:]
    ]
    model_width = full_qkv.shape[0]
    local_rows = inputs.shape[2]
    ctx_count = lax.axis_size("ctx")
    seq_len = local_rows * ctx_count
    key_block = min(512, seq_len)
    block_count = seq_len // key_block
    ctx_index = lax.axis_index("ctx")
    row_ids = jnp.arange(local_rows, dtype=jnp.int32)
    own_blocks = lax.dynamic_slice_in_dim(block_order, 2 * ctx_index, 2)
    own_pos = own_blocks[row_ids // BLK] * BLK + row_ids % BLK
    all_ids = jnp.arange(seq_len, dtype=jnp.int32)
    all_pos = block_order[all_ids // BLK] * BLK + all_ids % BLK
    pos_blocks = all_pos.reshape(block_count, key_block)
    grad_sums = [jnp.zeros(member.shape, jnp.float32) for member in gathered]
    outputs_list = []
    input_grads = []
    for micro_idx in range(inputs.shape[0]):
        seq_in = inputs[micro_idx, 0].astype(jnp.float32)
        normed, norm1_pull = jax.vjp(layer_norm, seq_in, gain_one, bias_one)
        normed_low = normed.astype(jnp.bfloat16)
        qkv_out = jnp.dot(normed_low, full_qkv, preferred_element_type=jnp.float32).astype(
            jnp.bfloat16
        )
        query_heads = qkv_out[:, :model_width].reshape(local_rows, H, HD)
        kv_all, doc_all = (
            lax.all_gather(qkv_out[:, model_width:], "ctx", axis=0, tiled=True),
            lax.all_gather(segment_ids[micro_idx, 0], "ctx", axis=0, tiled=True),
        )
        doc_rows = doc_all[all_pos]
        query_doc = doc_all[own_pos]
        kv_heads = kv_all.reshape(block_count, key_block, 2, H, HD)
        key_blocks = kv_heads[:, :, 0]
        value_blocks = kv_heads[:, :, 1]
        doc_blocks = doc_rows.reshape(block_count, key_block)
        log_norm = row_log_norm(query_heads, key_blocks, doc_blocks, pos_blocks, query_doc, own_pos)
        attn_acc = attend(
            query_heads,
            key_blocks,
            value_blocks,
            doc_blocks,
            pos_blocks,
            query_doc,
            own_pos,
            log_norm,
        )
        attn_low = attn_acc.reshape(local_rows, model_width).astype(jnp.bfloat16)
        branch = jnp.dot(attn_low, full_out, preferred_element_type=jnp.float32) + full_obias
        middle = seq_in + branch
        normed_two, norm2_pull = jax.vjp(layer_norm, middle, gain_two, bias_two)
        normed_two_low = normed_two.astype(jnp.bfloat16)
        hidden = jnp.dot(normed_two_low, full_up, preferred_element_type=jnp.float32) + full_ubias
        active, gelu_pull = jax.vjp(gelu_exact, hidden)
        active_low = active.astype(jnp.bfloat16)
        result = middle + (
            jnp.dot(active_low, full_down, preferred_element_type=jnp.float32) + full_dbias
        )
        outputs_list.append(result.astype(jnp.bfloat16))
        grad_y = out_grad[micro_idx, 0]
        grad_y32 = grad_y.astype(jnp.float32)
        grad_sums[3] = grad_sums[3] + jnp.einsum(
            "rf,rd->fd", active_low, grad_y, preferred_element_type=jnp.float32
        )
        grad_sums[10] = grad_sums[10] + jnp.sum(grad_y32, axis=0)
        grad_active = jnp.einsum("rd,fd->rf", grad_y, full_down, preferred_element_type=jnp.float32)
        (grad_hidden,) = gelu_pull(grad_active)
        grad_hidden_low = grad_hidden.astype(jnp.bfloat16)
        grad_sums[2] = grad_sums[2] + jnp.einsum(
            "rd,rf->df", normed_two_low, grad_hidden_low, preferred_element_type=jnp.float32
        )
        grad_sums[9] = grad_sums[9] + jnp.sum(grad_hidden_low.astype(jnp.float32), axis=0)
        grad_normed_two = jnp.einsum(
            "rf,df->rd", grad_hidden_low, full_up, preferred_element_type=jnp.float32
        )
        grad_mid_ln, grad_gain_two, grad_bias_two = norm2_pull(grad_normed_two)
        grad_sums[6] = grad_sums[6] + grad_gain_two
        grad_sums[7] = grad_sums[7] + grad_bias_two
        grad_mid = grad_y32 + grad_mid_ln
        grad_mid_low = grad_mid.astype(jnp.bfloat16)
        grad_sums[1] = grad_sums[1] + jnp.einsum(
            "rd,re->de", attn_low, grad_mid_low, preferred_element_type=jnp.float32
        )
        grad_sums[8] = grad_sums[8] + jnp.sum(grad_mid_low.astype(jnp.float32), axis=0)
        grad_attn_low = jnp.einsum(
            "re,de->rd", grad_mid_low, full_out, preferred_element_type=jnp.float32
        ).astype(jnp.bfloat16)
        grad_heads = grad_attn_low.reshape(local_rows, H, HD)
        row_delta = jnp.sum(grad_heads.astype(jnp.float32) * attn_acc, axis=-1).T

        def back_visit(grad_query, block_item):
            key_heads, value_heads, key_doc, key_pos = block_item
            part_q, part_k, part_v = grad_block(
                query_heads,
                grad_heads,
                log_norm,
                row_delta,
                query_doc,
                own_pos,
                key_heads,
                value_heads,
                key_doc,
                key_pos,
            )
            joined = jnp.concatenate(
                [part_k.reshape(key_block, model_width), part_v.reshape(key_block, model_width)],
                axis=1,
            )
            return (grad_query + part_q, joined)

        grad_query, kv_terms = lax.scan(
            back_visit,
            jnp.zeros((local_rows, H, HD), jnp.float32),
            (key_blocks, value_blocks, doc_blocks, pos_blocks),
        )
        kv_grad = lax.psum_scatter(
            kv_terms.reshape(seq_len, 2 * model_width).astype(jnp.bfloat16),
            "ctx",
            scatter_dimension=0,
            tiled=True,
        ).astype(jnp.float32)
        grad_qkv_low = jnp.concatenate(
            [grad_query.reshape(local_rows, model_width), kv_grad], axis=1
        ).astype(jnp.bfloat16)
        grad_sums[0] = grad_sums[0] + jnp.einsum(
            "rd,re->de", normed_low, grad_qkv_low, preferred_element_type=jnp.float32
        )
        grad_normed = jnp.einsum(
            "re,de->rd", grad_qkv_low, full_qkv, preferred_element_type=jnp.float32
        )
        grad_in_ln, grad_gain_one, grad_bias_one = norm1_pull(grad_normed)
        grad_sums[4] = grad_sums[4] + grad_gain_one
        grad_sums[5] = grad_sums[5] + grad_bias_one
        input_grads.append(grad_mid + grad_in_ln)
    owned = (
        lax.psum_scatter(
            grad_sums[0].astype(jnp.bfloat16), "fsdp", scatter_dimension=0, tiled=True
        ).astype(jnp.float32),
        lax.psum_scatter(
            grad_sums[1].astype(jnp.bfloat16), "fsdp", scatter_dimension=0, tiled=True
        ).astype(jnp.float32),
        lax.psum_scatter(
            grad_sums[2].astype(jnp.bfloat16), "fsdp", scatter_dimension=0, tiled=True
        ).astype(jnp.float32),
        lax.psum_scatter(
            grad_sums[3].astype(jnp.bfloat16), "fsdp", scatter_dimension=0, tiled=True
        ).astype(jnp.float32),
        lax.psum_scatter(
            grad_sums[4].astype(jnp.bfloat16), "fsdp", scatter_dimension=0, tiled=True
        ).astype(jnp.float32),
        lax.psum_scatter(
            grad_sums[5].astype(jnp.bfloat16), "fsdp", scatter_dimension=0, tiled=True
        ).astype(jnp.float32),
        lax.psum_scatter(
            grad_sums[6].astype(jnp.bfloat16), "fsdp", scatter_dimension=0, tiled=True
        ).astype(jnp.float32),
        lax.psum_scatter(
            grad_sums[7].astype(jnp.bfloat16), "fsdp", scatter_dimension=0, tiled=True
        ).astype(jnp.float32),
        lax.psum_scatter(
            grad_sums[8].astype(jnp.bfloat16), "fsdp", scatter_dimension=0, tiled=True
        ).astype(jnp.float32),
        lax.psum_scatter(
            grad_sums[9].astype(jnp.bfloat16), "fsdp", scatter_dimension=0, tiled=True
        ).astype(jnp.float32),
        lax.psum_scatter(
            grad_sums[10].astype(jnp.bfloat16), "fsdp", scatter_dimension=0, tiled=True
        ).astype(jnp.float32),
    )
    summed = (
        lax.psum(owned[0].astype(jnp.bfloat16), "ctx").astype(jnp.float32),
        lax.psum(owned[1].astype(jnp.bfloat16), "ctx").astype(jnp.float32),
        lax.psum(owned[2].astype(jnp.bfloat16), "ctx").astype(jnp.float32),
        lax.psum(owned[3].astype(jnp.bfloat16), "ctx").astype(jnp.float32),
        lax.psum(owned[4].astype(jnp.bfloat16), "ctx").astype(jnp.float32),
        lax.psum(owned[5].astype(jnp.bfloat16), "ctx").astype(jnp.float32),
        lax.psum(owned[6].astype(jnp.bfloat16), "ctx").astype(jnp.float32),
        lax.psum(owned[7].astype(jnp.bfloat16), "ctx").astype(jnp.float32),
        lax.psum(owned[8].astype(jnp.bfloat16), "ctx").astype(jnp.float32),
        lax.psum(owned[9].astype(jnp.bfloat16), "ctx").astype(jnp.float32),
        lax.psum(owned[10].astype(jnp.bfloat16), "ctx").astype(jnp.float32),
    )
    return (
        jnp.stack(outputs_list)[:, None],
        jnp.stack(input_grads)[:, None],
        summed[0],
        summed[1],
        summed[2],
        summed[3],
        summed[4],
        summed[5],
        summed[6],
        summed[7],
        summed[8],
        summed[9],
        summed[10],
    )


def solution(mesh):
    return jax.shard_map(
        body,
        mesh=mesh,
        in_specs=(
            P(None, "fsdp", "ctx", None),
            P(None, "fsdp", "ctx", None),
            P(None, "fsdp", "ctx"),
            P(),
            P("fsdp", None),
            P("fsdp", None),
            P("fsdp", None),
            P("fsdp", None),
            P("fsdp"),
            P("fsdp"),
            P("fsdp"),
            P("fsdp"),
            P("fsdp"),
            P("fsdp"),
            P("fsdp"),
        ),
        out_specs=(
            P(None, "fsdp", "ctx", None),
            P(None, "fsdp", "ctx", None),
            P("fsdp", None),
            P("fsdp", None),
            P("fsdp", None),
            P("fsdp", None),
            P("fsdp"),
            P("fsdp"),
            P("fsdp"),
            P("fsdp"),
            P("fsdp"),
            P("fsdp"),
            P("fsdp"),
        ),
        check_vma=False,
    )
```

profile of v0, /device:TPU:0, one launch (start us, length us, event | category | flops | bytes accessed | tf_op | source)
XLA Modules:
  0.0 1195.6 jit_solution(4293471570105327463)
XLA Ops:
  8.0 6.2 all-gather.2
  14.1 5.4 all-gather.3
  21.4 10.5 all-gather.15.cloned.1.call-done
  45.4 27.0 %all-gather = s32[1,1,4096]{2,1,0:T(1,128)S(1)} all-gather(s32[1,1,512]{2,1,0:T(1,128)S(1)} %get-tuple-element.1148), channel_id=2, replica_groups=mesh['ctx'=8,'fsdp'=4] {'ctx'}, dimensions={2}, use_global_device_ids=true | all-gather | bytes 18432 | tf_op jit(solution)/shard_map/all_gather | solution.py:179
  76.7 5.7 select_multiply_fusion.2
  85.7 23.0 %gather_fusion.1 = s32[4096]{0:T(1024)S(1)} fusion(s32[4096]{0:T(1024)S(1)} %bitcast.527, s32[4096]{0:T(1024)S(1)} %broadcast_clamp_fusion), kind=kCustom, calls=%fused_computation.1 | custom fusion | bytes 49152 | tf_op jit(solution)/shard_map/gather | solution.py:181
  108.7 26.6 %all-gather.1 = s32[1,1,4096]{2,1,0:T(1,128)S(1)} all-gather(s32[1,1,512]{2,1,0:T(1,128)S(1)} %get-tuple-element.1149), channel_id=3, replica_groups=mesh['ctx'=8,'fsdp'=4] {'ctx'}, dimensions={2}, use_global_device_ids=true | all-gather | bytes 18432 | tf_op jit(solution)/shard_map/all_gather | solution.py:179
  138.6 23.0 %gather_fusion.3 = s32[4096]{0:T(1024)S(1)} fusion(s32[4096]{0:T(1024)S(1)} %bitcast.529, s32[4096]{0:T(1024)S(1)} %broadcast_clamp_fusion), kind=kCustom, calls=%fused_computation.3 | custom fusion | bytes 49152 | tf_op jit(solution)/shard_map/gather | solution.py:181
  182.2 7.2 all_gather.50
  195.1 11.7 copy.162
  206.8 12.2 %copy.239 = bf16[128,8,8,512]{3,2,1,0:T(8,128)(2,1)} copy(bf16[128,8,8,512]{3,1,2,0:T(8,128)(2,1)} %bitcast.538) | data formatting | bytes 16777216
  219.0 5.3 slice_bitcast_fusion
  227.7 50.1 %while.76 = (s32[]{:T(128)}, f32[8,512]{1,0:T(8,128)S(1)}, f32[8,512]{1,0:T(8,128)S(1)}, s32[512]{0:T(512)S(1)}, s32[8,512]{1,0:T(8,128)S(1)}, /*index=5*/s32[8,...) while((s32[]{:T(128)}, f32[8,512]{1,0:T(8,128)S(1)}, ...), condition=%wide.region_15.16_spmd.clone, body=%wide.region_12.15_spmd.clone.sunk | while | flops 286030336 | bytes 18847896 | solution.py:57
  277.8 10.0 all-gather.17.cloned.1.call-done
  287.8 11.7 copy.155
  299.5 12.2 %copy.238 = bf16[128,8,8,512]{3,2,1,0:T(8,128)(2,1)} copy(bf16[128,8,8,512]{3,1,2,0:T(8,128)(2,1)} %bitcast.539) | data formatting | bytes 16777216
  320.4 50.3 %while.74 = (s32[]{:T(128)}, f32[8,512]{1,0:T(8,128)S(1)}, f32[8,512]{1,0:T(8,128)S(1)}, s32[512]{0:T(512)S(1)}, s32[8,512]{1,0:T(8,128)S(1)}, /*index=5*/s32[8,...) while((s32[]{:T(128)}, f32[8,512]{1,0:T(8,128)S(1)}, ...), condition=%wide.region_5.6_spmd.clone, body=%wide.region_2.5_spmd.clone.sunk | while | flops 286030336 | bytes 18847896 | solution.py:57
  370.8 5.7 copy.158
  377.0 46.4 %while.75 = (s32[]{:T(128)}, f32[512,8,64]{0,2,1:T(8,128)S(1)}, bf16[8,512,8,64]{1,3,2,0:T(8,128)(2,1)}, s32[512]{0:T(512)S(1)}, s32[8,512]{1,0:T(8,128)S(1)}, /...) while((s32[]{:T(128)}, f32[512,8,64]{0,2,1:T(8,128)S(1)}, ...), condition=%wide.region_7.8_spmd.clone, body=%wide.region_6.7_spmd.clone.sunk | while | flops 546580992 | bytes 4234906 | solution.py:78
  424.4 5.7 copy.165
  430.1 46.4 %while.77 = (s32[]{:T(128)}, f32[512,8,64]{0,2,1:T(8,128)S(1)}, bf16[8,512,8,64]{1,3,2,0:T(8,128)(2,1)}, s32[512]{0:T(512)S(1)}, s32[8,512]{1,0:T(8,128)S(1)}, /...) while((s32[]{:T(128)}, f32[512,8,64]{0,2,1:T(8,128)S(1)}, ...), condition=%wide.region_17.18_spmd.clone, body=%wide.region_16.17_spmd.clone.sunk | while | flops 546580992 | bytes 4234906 | solution.py:78
  486.1 6.2 convert_reduce_fusion
  497.7 6.1 multiply_convert_fusion.1
  525.5 138.8 %while.78 = (s32[]{:T(128)}, f32[512,8,64]{0,2,1:T(8,128)}, bf16[8,512,1024]{2,1,0:T(8,128)(2,1)}, bf16[8,512,8,64]{1,3,2,0:T(8,128)(2,1)}, s32[512]{0:T(512)S(1...) while((s32[]{:T(128)}, f32[512,8,64]{0,2,1:T(8,128)}, ...), condition=%wide.region_24.25_spmd.clone, body=%wide.region_23.24_spmd.clone.sunk | while | flops 1367353856 | bytes 51714240 | solution.py:261
  668.8 131.3 %while.79 = (s32[]{:T(128)}, f32[512,8,64]{0,2,1:T(8,128)}, bf16[8,512,1024]{2,1,0:T(8,128)(2,1)}, bf16[8,512,8,64]{1,3,2,0:T(8,128)(2,1)}, s32[512]{0:T(512)S(1...) while((s32[]{:T(128)}, f32[512,8,64]{0,2,1:T(8,128)}, ...), condition=%wide.region_32.33_spmd.clone, body=%wide.region_31.32_spmd.clone.sunk | while | flops 1367353856 | bytes 51714240 | solution.py:261
  834.7 129.0 %reduce-scatter.9.cloned.1.call-done = bf16[512,1024]{1,0:T(8,128)(2,1)} async-done(((bf16[4096,1024]{1,0:T(8,128)(2,1)}), bf16[512,1024]{1,0:T(8,128)(2,1)}) %reduce-scatter.9.cloned.1.call-update) | async-done | bytes 1048592 | tf_op jit(solution)/shard_map/reduce_scatter | solution.py:266
  986.9 34.2 %reduce-scatter.15.cloned.1.call-done = bf16[128,2048]{1,0:T(8,128)(2,1)} async-done(((bf16[512,2048]{1,0:T(8,128)(2,1)}), bf16[128,2048]{1,0:T(8,128)(2,1)}) %reduce-scatter.15.cloned.1.call-update) | async-done | bytes 524304 | tf_op jit(solution)/shard_map/reduce_scatter | solution.py:292
  1021.1 33.8 %reduce-scatter.17.cloned.1.call-done = bf16[512,512]{1,0:T(8,128)(2,1)} async-done(((bf16[2048,512]{1,0:T(8,128)(2,1)}), bf16[512,512]{1,0:T(8,128)(2,1)}) %reduce-scatter.17.cloned.1.call-update) | async-done | bytes 524304 | tf_op jit(solution)/shard_map/reduce_scatter | solution.py:295
  1054.9 31.5 %reduce-scatter.11.cloned.1.call-done = bf16[128,1536]{1,0:T(8,128)(2,1)} async-done(((bf16[512,1536]{1,0:T(8,128)(2,1)}), bf16[128,1536]{1,0:T(8,128)(2,1)}) %reduce-scatter.11.cloned.1.call-update) | async-done | bytes 393232 | tf_op jit(solution)/shard_map/reduce_scatter | solution.py:286
  1091.7 10.5 all-reduce.9
  1102.7 22.0 %all-reduce.7 = (bf16[128]{0:T(256)(128)(2,1)S(1)}, bf16[128]{0:T(256)(128)(2,1)S(1)}, bf16[128]{0:T(256)(128)(2,1)S(1)}, bf16[128]{0:T(256)(128)(2,1)S(1)}, bf1...) all-reduce(bf16[128]{0:T(256)(128)(2,1)S(1)} %dynamic-slice.1, ...), channel_id=1, replica_groups=mesh['ctx'=8,'fsdp'=4] {'ctx'}, use_global_device_ids=true, to_apply=%region_47.48 | all-reduce | flops 1280 | bytes 5120 | tf_op jit(solution)/shard_map/psum | solution.py:325
  1131.6 48.8 %all-reduce.12.cloned.1.call-done = (bf16[128,1536]{1,0:T(8,128)(2,1)}, bf16[128,512]{1,0:T(8,128)(2,1)}, bf16[128,2048]{1,0:T(8,128)(2,1)}, bf16[512,512]{1,0:T(8,128)(2,1)}) async-done(((bf16[128,1536]{1,0:T(8,128)(2,1)}, bf16[128,512]{1,0:T(8,128)(2,1)}, bf16[128,2048]{1,0:T(8,128)(2,1)}, bf16[512,512]{1,0:T(8,128)(2,1)}), (bf16[128,1536]{1,0:T(8,128)(2,1)}, bf16[128,512]{1,0:T(8,128)(2,1)}, ...) | async-done | bytes 1572880 | tf_op jit(solution)/shard_map/psum | solution.py:321
  (799 shorter events, 643.1 us)
Async XLA Ops:
  7.2 24.8 %all-gather.15.cloned.1.call-start = ((), (), s32[]{:S(2)}) async-start(), calls=%async_computation.6 | async-start | bytes 1966080 | tf_op jit(solution)/shard_map/all_gather | solution.py:137
  7.9 187.2 %all-gather.23.cloned.1.call-start = ((), (), s32[]{:S(2)}) async-start(), calls=%async_computation.10 | async-start | bytes 9437184 | tf_op jit(solution)/shard_map/all_gather | solution.py:178
  36.8 251.0 %all-gather.17.cloned.1.call-start = ((), (), s32[]{:S(2)}) async-start(), calls=%async_computation.7 | async-start | bytes 9437184 | tf_op jit(solution)/shard_map/all_gather | solution.py:178
  37.1 441.2 %copy-start.7 = (bf16[1,1,512,512]{2,3,1,0:T(8,128)(2,1)}, bf16[1,1,512,512]{2,3,1,0:T(8,128)(2,1)S(1)}, u32[]{:S(2)}) copy-start(bf16[1,1,512,512]{2,3,1,0:T(8,128)(2,1)S(1)} %copy.202) | copy-start | bytes 1572868
  40.9 440.1 %all-gather.19.cloned.1.call-start = ((), (), s32[]{:S(2)}) async-start(), calls=%async_computation.8 | async-start | bytes 2621440 | tf_op jit(solution)/shard_map/all_gather | solution.py:139
  41.5 444.6 %all-gather.21.cloned.1.call-start = ((), (), s32[]{:S(2)}) async-start(), calls=%async_computation.9 | async-start | bytes 2621440 | tf_op jit(solution)/shard_map/all_gather | solution.py:140
  42.1 788.4 %reduce-scatter.7.cloned.1.call-start = ((), (), s32[]{:S(2)}) async-start(), calls=%async_computation.11 | async-start | bytes 9437184 | tf_op jit(solution)/shard_map/reduce_scatter | solution.py:266
  138.5 38.4 %copy-start.91 = (bf16[512]{0:T(512)(128)(2,1)S(1)}, bf16[512]{0:T(512)(128)(2,1)}, u32[]{:S(2)}) copy-start(bf16[512]{0:T(512)(128)(2,1)} %param.40) | copy-start | bytes 3076
  138.5 43.7 %copy-start.51 = (bf16[128,512]{1,0:T(8,128)(2,1)S(1)}, bf16[128,512]{1,0:T(8,128)(2,1)}, u32[]{:S(2)}) copy-start(bf16[128,512]{1,0:T(8,128)(2,1)} %param.32) | copy-start | bytes 393220
  138.6 50.9 %copy-start.28 = (bf16[2,1,512,512]{3,2,1,0:T(8,128)(2,1)S(1)}, bf16[2,1,512,512]{3,2,1,0:T(8,128)(2,1)}, u32[]{:S(2)}) copy-start(bf16[2,1,512,512]{3,2,1,0:T(8,128)(2,1)} %param.28) | copy-start | bytes 3145732
  166.9 349.2 %copy-start.47 = (f32[4,1,128]{2,1,0:T(1,128)}, f32[4,1,128]{2,1,0:T(1,128)S(1)}, u32[]{:S(2)}) copy-start(f32[4,1,128]{2,1,0:T(1,128)S(1)} %convert_element_type.307) | copy-start | bytes 6148
  171.9 325.8 %copy-start.53 = (f32[4,1,128]{2,1,0:T(1,128)}, f32[4,1,128]{2,1,0:T(1,128)S(1)}, u32[]{:S(2)}) copy-start(f32[4,1,128]{2,1,0:T(1,128)S(1)} %convert_element_type.308) | copy-start | bytes 6148
  189.5 288.8 %copy-start.9 = (bf16[512,512]{1,0:T(8,128)(2,1)}, bf16[512,512]{1,0:T(8,128)(2,1)S(1)}, u32[]{:S(2)}) copy-start(bf16[512,512]{1,0:T(8,128)(2,1)S(1)} %all_gather.50) | copy-start | bytes 1572868
  478.8 37.2 %copy-start.2 = (f32[512,512]{0,1:T(8,128)}, f32[512,512]{0,1:T(8,128)S(1)}, u32[]{:S(2)}) copy-start(f32[512,512]{0,1:T(8,128)S(1)} %get-tuple-element.1175) | copy-start | bytes 3145732
  478.9 37.2 %copy-start.57 = (f32[512]{0:T(512)}, f32[512]{0:T(512)S(1)}, u32[]{:S(2)}) copy-start(f32[512]{0:T(512)S(1)} %broadcast_multiply_fusion.2) | copy-start | bytes 6148
  480.8 35.3 %copy-start = (f32[512,512]{0,1:T(8,128)}, f32[512,512]{0,1:T(8,128)S(1)}, u32[]{:S(2)}) copy-start(f32[512,512]{0,1:T(8,128)S(1)} %get-tuple-element.1177) | copy-start | bytes 3145732
  480.8 35.3 %copy-start.49 = (f32[512]{0:T(512)}, f32[512]{0:T(512)S(1)}, u32[]{:S(2)}) copy-start(f32[512]{0:T(512)S(1)} %broadcast_multiply_fusion) | copy-start | bytes 6148
  481.0 35.1 %copy-start.55 = (f32[512]{0:T(512)}, f32[512]{0:T(512)S(1)}, u32[]{:S(2)}) copy-start(f32[512]{0:T(512)S(1)} %get-tuple-element.1196) | copy-start | bytes 6148
  481.0 35.1 %copy-start.65 = (f32[512]{0:T(512)}, f32[512]{0:T(512)S(1)}, u32[]{:S(2)}) copy-start(f32[512]{0:T(512)S(1)} %get-tuple-element.1195) | copy-start | bytes 6148
  664.4 299.4 %reduce-scatter.9.cloned.1.call-start = ((), (), s32[]{:S(2)}) async-start(), calls=%async_computation.12 | async-start | bytes 9437184 | tf_op jit(solution)/shard_map/reduce_scatter | solution.py:266
  800.1 186.8 %reduce-scatter.13.cloned.1.call-start = ((), (), s32[]{:S(2)}) async-start(), calls=%async_computation.14 | async-start | bytes 655360 | tf_op jit(solution)/shard_map/reduce_scatter | solution.py:289
  803.1 218.0 %reduce-scatter.15.cloned.1.call-start = ((), (), s32[]{:S(2)}) async-start(), calls=%async_computation.15 | async-start | bytes 2621440 | tf_op jit(solution)/shard_map/reduce_scatter | solution.py:292
  809.0 245.9 %reduce-scatter.17.cloned.1.call-start = ((), (), s32[]{:S(2)}) async-start(), calls=%async_computation.16 | async-start | bytes 2621440 | tf_op jit(solution)/shard_map/reduce_scatter | solution.py:295
  815.0 271.5 %reduce-scatter.11.cloned.1.call-start = ((), (), s32[]{:S(2)}) async-start(), calls=%async_computation.13 | async-start | bytes 1966080 | tf_op jit(solution)/shard_map/reduce_scatter | solution.py:286
  830.5 133.3 %copy-start.6 = (bf16[1,1,512,512]{2,3,1,0:T(8,128)(2,1)S(1)}, bf16[1,1,512,512]{2,3,1,0:T(8,128)(2,1)}, u32[]{:S(2)}) copy-start(bf16[1,1,512,512]{2,3,1,0:T(8,128)(2,1)} %copy-done.4) | copy-start | bytes 1572868
  830.5 133.3 %copy-start.62 = (f32[512]{0:T(512)S(1)}, f32[512]{0:T(512)}, u32[]{:S(2)}) copy-start(f32[512]{0:T(512)} %copy-done.61) | copy-start | bytes 6148
  830.5 133.3 %copy-start.68 = (f32[512]{0:T(512)S(1)}, f32[512]{0:T(512)}, u32[]{:S(2)}) copy-start(f32[512]{0:T(512)} %copy-done.67) | copy-start | bytes 6148
  968.2 212.2 %all-reduce.12.cloned.1.call-start = ((), (), s32[]{:S(2)}) async-start(), calls=%async_computation.17 | async-start | bytes 3145728 | tf_op jit(solution)/shard_map/psum | solution.py:321
  981.3 105.1 %copy-start.27 = (bf16[1,1,512,512]{2,3,1,0:T(8,128)(2,1)S(1)}, bf16[1,1,512,512]{2,3,1,0:T(8,128)(2,1)}, u32[]{:S(2)}) copy-start(bf16[1,1,512,512]{2,3,1,0:T(8,128)(2,1)} %copy.204) | copy-start | bytes 1572868
  981.3 105.1 %copy-start.78 = (f32[512]{0:T(512)S(1)}, f32[512]{0:T(512)}, u32[]{:S(2)}) copy-start(f32[512]{0:T(512)} %copy-done.77) | copy-start | bytes 6148
  986.3 103.6 %copy-start.23 = (bf16[1,1,512,512]{2,3,1,0:T(8,128)(2,1)S(1)}, bf16[1,1,512,512]{2,3,1,0:T(8,128)(2,1)}, u32[]{:S(2)}) copy-start(bf16[1,1,512,512]{2,3,1,0:T(8,128)(2,1)} %copy.205) | copy-start | bytes 1572868
  986.3 103.6 %copy-start.76 = (f32[512]{0:T(512)S(1)}, f32[512]{0:T(512)}, u32[]{:S(2)}) copy-start(f32[512]{0:T(512)} %copy-done.75) | copy-start | bytes 6148
  (80 other events, 436.3 us)
Sparse Core Ops, SparseCore 0:
  9.6 22.3 all-gather.14
  36.9 125.5 all-gather.22
  164.7 123.0 all-gather.16
  289.2 20.7 all-gather.18
  311.4 22.5 all-gather.20
  664.5 147.1 reduce-scatter.6
  815.7 148.0 reduce-scatter.8
  966.3 20.6 reduce-scatter.12
  989.6 31.4 reduce-scatter.14
  1023.5 31.4 reduce-scatter.16
  1058.2 28.1 reduce-scatter.10
  1090.1 90.2 all-reduce.11
where the time goes:
time: 1210 us; the launch traced here: 1200 us
  matrix products  395 us (33%)
  waiting for transfers between devices  300 us (25%)
  local copies, waits for them, and re-layouts  193 us (16%)
  other arithmetic  155 us (13%)
  blocking collectives  131 us (11%)
  between operations  17.5 us (1%)
    reduce_scatter x2, waiting for transfers between devices, body(): lax.psum_scatter(kv_terms.reshape(seq_len, 2 * model_width).astype(jnp.bf...  129 us
    dot_general x32, matrix products, score_block(): jnp.einsum('qhd,khd->hqk', query_heads, key_heads, preferred_element_type...  77.9 us
    dot_general x16, matrix products, attend_visit(): jnp.einsum('hqk,khd->qhd', soft_low, value_heads, preferred_element_type=...  66.4 us
    dot_general x16, matrix products, grad_block(): jnp.einsum('qhd,khd->hqk', grad_heads, value_heads, preferred_element_typ...  64.5 us
    mul x48, other arithmetic, body(): own_pos = own_blocks[row_ids // BLK] * BLK + row_ids % BLK  62.6 us
    unnamed x219, local copies, waits for them, and re-layouts  55.3 us
    all_gather x2, blocking collectives, body(): lax.all_gather(segment_ids[micro_idx, 0], 'ctx', axis=0, tiled=True)  53.6 us
    dot_general x16, matrix products, grad_block(): jnp.einsum('hqk,khd->qhd', grad_scores, key_heads, preferred_element_type...  50 us
  transfers between devices with their start and end apart: 12, of which 8 were waited for; matrix products, arithmetic and copies ran while one was open for 46% of the time, Pallas kernels for 0%

commit v1 on v0

--- a/solution.py
+++ b/solution.py
@@ -1,17 +1,422 @@
+import functools
 import math
 
 import jax
 import jax.numpy as jnp
 from jax import lax
+from jax.experimental import pallas as pl
+from jax.experimental.pallas import tpu as pltpu
+from jax.sharding import Mesh
 from jax.sharding import PartitionSpec as P
 
 H = 8
 HD = 64
 BLK = 256
-
+PAIR = 2 * HD
 
 norm_eps = 1e-05
 mask_fill = -1e30
+LOG2E = math.log2(math.e)
+LN2 = math.log(2.0)
+SCORE_SCALE = 1.0 / math.sqrt(HD)
+
+f32 = jnp.float32
+bf16 = jnp.bfloat16
+
+
+def contract(a, b, da, db):
+    return lax.dot_general(a, b, (((da,), (db,)), ((), ())), preferred_element_type=f32)
+
+
+def norm_parts(values):
+    center = values - jnp.mean(values, axis=-1, keepdims=True)
+    spread = jnp.mean(center * center, axis=-1, keepdims=True)
+    inv = lax.rsqrt(spread + norm_eps)
+    return center * inv, inv
+
+
+def whole(shape):
+    zeros = (0,) * len(shape)
+    return pl.BlockSpec(shape, lambda *_: zeros)
+
+
+def project_kernel(true_ref, x_ref, gain_ref, bias_ref, w_ref, q_ref, k_ref, kt_ref, v_ref, vt_ref, h_ref):
+    unit, _ = norm_parts(x_ref[...].astype(f32))
+    low = (unit * gain_ref[...] + bias_ref[...]).astype(bf16)
+    h_ref[...] = low
+    qkv = jnp.dot(low, w_ref[...], preferred_element_type=f32)
+    q_ref[...] = (qkv[:, :PAIR] * (SCORE_SCALE * LOG2E)).astype(bf16)
+    k = qkv[:, PAIR : 2 * PAIR].astype(bf16)
+    v = qkv[:, 2 * PAIR :].astype(bf16)
+    k_ref[...] = k
+    v_ref[...] = v
+    kt_ref[...] = k.T
+    vt_ref[...] = v.T
+
+
+def project(true_of, rows, gain, bias, weight):
+    count, width = rows.shape
+    blocks = count // BLK
+    by_true = pl.BlockSpec((BLK, PAIR), lambda t, tab: (tab[t], 0))
+    by_true_t = pl.BlockSpec((PAIR, BLK), lambda t, tab: (0, tab[t]))
+    return pl.pallas_call(
+        project_kernel,
+        grid_spec=pltpu.PrefetchScalarGridSpec(
+            num_scalar_prefetch=1,
+            grid=(blocks,),
+            in_specs=[
+                pl.BlockSpec((BLK, width), lambda t, tab: (t, 0)),
+                whole(gain.shape),
+                whole(bias.shape),
+                whole(weight.shape),
+            ],
+            out_specs=[
+                by_true,
+                by_true,
+                by_true_t,
+                by_true,
+                by_true_t,
+                pl.BlockSpec((BLK, width), lambda t, tab: (tab[t], 0)),
+            ],
+        ),
+        out_shape=[
+            jax.ShapeDtypeStruct((count, PAIR), bf16),
+            jax.ShapeDtypeStruct((count, PAIR), bf16),
+            jax.ShapeDtypeStruct((PAIR, count), bf16),
+            jax.ShapeDtypeStruct((count, PAIR), bf16),
+            jax.ShapeDtypeStruct((PAIR, count), bf16),
+            jax.ShapeDtypeStruct((count, width), bf16),
+        ],
+        name="project",
+    )(true_of, rows, gain, bias, weight)
+
+
+def split_heads(block):
+    lane = lax.broadcasted_iota(jnp.int32, block.shape, 1)
+    zero = jnp.zeros_like(block)
+    first = lane < HD
+    return jnp.concatenate([jnp.where(first, block, zero), jnp.where(first, zero, block)], axis=0)
+
+
+def attend_kernel(slot_ref, low_ref, q_ref, start_ref, k_ref, vt_ref, o_ref, ot_ref, lse_ref, acc, top):
+    qb = pl.program_id(0)
+    both = split_heads(q_ref[...])
+    start = jnp.concatenate([start_ref[0], start_ref[0]], axis=1)
+    row = lax.broadcasted_iota(jnp.int32, (BLK, 2 * BLK), 0)
+    col = lax.broadcasted_iota(jnp.int32, (BLK, 2 * BLK), 1)
+    ones = jnp.ones((16, BLK), bf16)
+
+    def scores(kb):
+        base = pl.multiple_of(kb * BLK, BLK)
+        return contract(k_ref[pl.ds(base, BLK), :], both, 1, 1)
+
+    def values(kb):
+        base = pl.multiple_of(kb * BLK, BLK)
+        return jnp.concatenate([vt_ref[:, pl.ds(base, BLK)], ones], axis=0)
+
+    st = scores(qb)
+    allowed = (row >= start - qb * BLK) & (row <= jnp.bitwise_and(col, BLK - 1))
+    st = jnp.where(allowed, st, mask_fill)
+    peak = jnp.max(st, axis=0, keepdims=True)
+    probs = jnp.exp2(st - peak).astype(bf16)
+    top[...] = peak
+    acc[...] = jnp.dot(values(qb), probs, preferred_element_type=f32)
+
+    def visit(kb, carry):
+        st = jnp.where(row >= start - kb * BLK, scores(kb), mask_fill)
+        old = top[...]
+        peak = jnp.maximum(old, jnp.max(st, axis=0, keepdims=True))
+        probs = jnp.exp2(st - peak).astype(bf16)
+        top[...] = peak
+        acc[...] = acc[...] * jnp.exp2(old - peak) + jnp.dot(values(kb), probs, preferred_element_type=f32)
+        return carry
+
+    lax.fori_loop(low_ref[qb], qb, visit, 0)
+    total = acc[PAIR : PAIR + 1, :]
+    lse_ref[0] = top[...] + jnp.log2(total)
+    out = acc[:PAIR, :] / total
+    heads = jnp.concatenate([out[:HD, :BLK], out[HD:, BLK:]], axis=0)
+    ot_ref[0] = heads
+    o_ref[...] = heads.T.astype(bf16)
+
+
+def attend(slot_of, low_of, q, start, k, vt):
+    count = q.shape[0]
+    blocks = count // BLK
+    return pl.pallas_call(
+        attend_kernel,
+        grid_spec=pltpu.PrefetchScalarGridSpec(
+            num_scalar_prefetch=2,
+            grid=(blocks,),
+            in_specs=[
+                pl.BlockSpec((BLK, PAIR), lambda b, s, l: (b, 0)),
+                pl.BlockSpec((1, 1, BLK), lambda b, s, l: (b, 0, 0)),
+                whole(k.shape),
+                whole(vt.shape),
+            ],
+            out_specs=[
+                pl.BlockSpec((BLK, PAIR), lambda b, s, l: (s[b], 0)),
+                pl.BlockSpec((1, PAIR, BLK), lambda b, s, l: (b, 0, 0)),
+                pl.BlockSpec((1, 1, 2 * BLK), lambda b, s, l: (b, 0, 0)),
+            ],
+            scratch_shapes=[
+                pltpu.VMEM((PAIR + 16, 2 * BLK), f32),
+                pltpu.VMEM((1, 2 * BLK), f32),
+            ],
+        ),
+        out_shape=[
+            jax.ShapeDtypeStruct((count, PAIR), bf16),
+            jax.ShapeDtypeStruct((blocks, PAIR, BLK), f32),
+            jax.ShapeDtypeStruct((blocks, 1, 2 * BLK), f32),
+        ],
+        name="attend",
+    )(slot_of, low_of, q, start, k, vt)
+
+
+def attend_back_kernel(
+    slot_ref, high_ref, k_ref, kt_ref, v_ref, h_ref, w_ref, q_ref, start_ref, do_ref, ot_ref, lse_ref,
+    dh_ref, gw_ref, dqt, dk, dv, delta,
+):
+    kb = pl.program_id(0)
+    blocks = pl.num_programs(0)
+    row = lax.broadcasted_iota(jnp.int32, (BLK, 2 * BLK), 0)
+    col = lax.broadcasted_iota(jnp.int32, (BLK, 2 * BLK), 1)
+
+    def d_out(qb):
+        return do_ref[pl.ds(pl.multiple_of(slot_ref[qb] * BLK, BLK), BLK), :]
+
+    @pl.when(kb == 0)
+    def _():
+        gw_ref[...] = jnp.zeros_like(gw_ref)
+
+        def prepare(qb, carry):
+            dqt[qb] = jnp.zeros((PAIR, BLK), f32)
+            both = d_out(qb).astype(f32).T * ot_ref[qb]
+            delta[qb] = jnp.concatenate(
+                [
+                    jnp.sum(both[:HD], axis=0, keepdims=True),
+                    jnp.sum(both[HD:], axis=0, keepdims=True),
+                ],
+                axis=1,
+            )
+            return carry
+
+        lax.fori_loop(0, blocks, prepare, 0)
+
+    k = k_ref[...]
+    v = v_ref[...]
+    kt = kt_ref[...]
+
+    def tile(qb, diagonal):
+        both_q = split_heads(q_ref[pl.ds(pl.multiple_of(qb * BLK, BLK), BLK), :])
+        both_do = split_heads(d_out(qb))
+        start = jnp.concatenate([start_ref[qb], start_ref[qb]], axis=1)
+        st = contract(k, both_q, 1, 1)
+        dpt = contract(v, both_do, 1, 1)
+        allowed = row >= start - kb * BLK
+        if diagonal:
+            allowed = allowed & (row <= jnp.bitwise_and(col, BLK - 1))
+        pt = jnp.exp2(jnp.where(allowed, st - lse_ref[qb], mask_fill))
+        dst = (pt * (dpt - delta[qb])).astype(bf16)
+        part_v = jnp.dot(pt.astype(bf16), both_do, preferred_element_type=f32)
+        part_k = jnp.dot(dst, both_q, preferred_element_type=f32)
+        if diagonal:
+            dv[...] = part_v
+            dk[...] = part_k
+        else:
+            dv[...] += part_v
+            dk[...] += part_k
+        dqt[qb] += jnp.concatenate(
+            [
+                jnp.dot(kt[:HD], dst[:, :BLK], preferred_element_type=f32),
+                jnp.dot(kt[HD:], dst[:, BLK:], preferred_element_type=f32),
+            ],
+            axis=0,
+        )
+
+    tile(kb, True)
+
+    def visit(qb, carry):
+        tile(qb, False)
+        return carry
+
+    lax.fori_loop(kb + 1, high_ref[kb] + 1, visit, 0)
+    dq = (dqt[kb] * SCORE_SCALE).T.astype(bf16)
+    joined = jnp.concatenate([dq, (dk[...] * LN2).astype(bf16), dv[...].astype(bf16)], axis=1)
+    dh_ref[...] = contract(joined, w_ref[...], 1, 1).astype(bf16)
+    gw_ref[...] += contract(h_ref[...], joined, 0, 0)
+
+
+def attend_back(slot_of, high_of, k, kt, v, h, weight, q, start, d_out, ot, lse):
+    count = q.shape[0]
+    width = h.shape[1]
+    blocks = count // BLK
+    return pl.pallas_call(
+        attend_back_kernel,
+        grid_spec=pltpu.PrefetchScalarGridSpec(
+            num_scalar_prefetch=2,
+            grid=(blocks,),
+            in_specs=[
+                pl.BlockSpec((BLK, PAIR), lambda b, s, l: (b, 0)),
+                pl.BlockSpec((PAIR, BLK), lambda b, s, l: (0, b)),
+                pl.BlockSpec((BLK, PAIR), lambda b, s, l: (b, 0)),
+                pl.BlockSpec((BLK, width), lambda b, s, l: (b, 0)),
+                whole(weight.shape),
+                whole(q.shape),
+                whole(start.shape),
+                whole(d_out.shape),
+                whole(ot.shape),
+                whole(lse.shape),
+            ],
+            out_specs=[
+                pl.BlockSpec((BLK, width), lambda b, s, l: (s[b], 0)),
+                whole(weight.shape),
+            ],
+            scratch_shapes=[
+                pltpu.VMEM((blocks, PAIR, BLK), f32),
+                pltpu.VMEM((BLK, PAIR), f32),
+                pltpu.VMEM((BLK, PAIR), f32),
+                pltpu.VMEM((blocks, 1, 2 * BLK), f32),
+            ],
+        ),
+        out_shape=[
+            jax.ShapeDtypeStruct((count, width), bf16),
+            jax.ShapeDtypeStruct(weight.shape, f32),
+        ],
+        name="attend_back",
+    )(slot_of, high_of, k, kt, v, h, weight, q, start, d_out, ot, lse)
+
+
+FF_TILE = 512
+
+
+def feed_kernel(
+    pair_ref, attn_ref, x_ref, dy_ref, wo_ref, wu_ref, wd_ref, vec_ref, ub_ref,
+    y_ref, do_ref, dmid_ref, gd_ref, gu_ref, go_ref, gvec_ref, gub_ref, attn_all,
+):
+    step = pl.program_id(0)
+    groups = attn_ref.shape[0]
+
+    @pl.when(step == 0)
+    def _():
+        for ref in (gd_ref, gu_ref, go_ref, gvec_ref, gub_ref):
+            ref[...] = jnp.zeros_like(ref)
+
+    for g in range(groups):
+        attn_all[:, pl.ds(pl.multiple_of(pair_ref[g] * PAIR, PAIR), PAIR)] = attn_ref[g]
+    attn = attn_all[...]
+    out_bias, gain, bias, down_bias = (vec_ref[i : i + 1, :] for i in range(4))
+    middle = (
+        x_ref[...].astype(f32) + jnp.dot(attn, wo_ref[...], preferred_element_type=f32) + out_bias
+    )
+    unit, inv = norm_parts(middle)
+    low = (unit * gain + bias).astype(bf16)
+    dy = dy_ref[...]
+    dy32 = dy.astype(f32)
+    total = middle + down_bias
+    d_low = jnp.zeros_like(middle)
+    width = wu_ref.shape[1]
+    for j in range(0, width, FF_TILE):
+        part = pl.ds(j, FF_TILE)
+        up = wu_ref[:, part]
+        down = wd_ref[part, :]
+        hidden = jnp.dot(low, up, preferred_element_type=f32) + ub_ref[:, part]
+        cdf = 0.5 * (1.0 + lax.erf(hidden * (1.0 / math.sqrt(2.0))))
+        active = (hidden * cdf).astype(bf16)
+        slope = cdf + hidden * (jnp.exp2(hidden * hidden * (-0.5 * LOG2E)) * (1.0 / math.sqrt(2.0 * math.pi)))
+        total = total + jnp.dot(active, down, preferred_element_type=f32)
+        d_hidden = contract(dy, down, 1, 1) * slope
+        d_hidden_low = d_hidden.astype(bf16)
+        gub_ref[:, part] += jnp.sum(d_hidden, axis=0, keepdims=True)
+        d_low = d_low + contract(d_hidden_low, up, 1, 1)
+        gd_ref[part, :] += contract(active, dy, 0, 0)
+        gu_ref[:, part] += contract(low, d_hidden_low, 0, 0)
+    y_ref[...] = total.astype(bf16)
+    scaled = d_low * gain
+    d_middle = dy32 + inv * (
+        scaled
+        - jnp.mean(scaled, axis=-1, keepdims=True)
+        - unit * jnp.mean(scaled * unit, axis=-1, keepdims=True)
+    )
+    dmid_ref[...] = d_middle
+    branch = d_middle.astype(bf16)
+    go_ref[...] += contract(attn, branch, 0, 0)
+    gvec_ref[0:1, :] += jnp.sum(d_middle, axis=0, keepdims=True)
+    gvec_ref[1:2, :] += jnp.sum(d_low * unit, axis=0, keepdims=True)
+    gvec_ref[2:3, :] += jnp.sum(d_low, axis=0, keepdims=True)
+    gvec_ref[3:4, :] += jnp.sum(dy32, axis=0, keepdims=True)
+    attn_all[...] = contract(branch, wo_ref[...], 1, 1).astype(bf16)
+    for g in range(groups):
+        do_ref[g] = attn_all[:, pl.ds(pl.multiple_of(pair_ref[g] * PAIR, PAIR), PAIR)]
+
+
+def feed(pair_of, attn, x, dy, w_out, w_up, w_down, vecs, up_bias, tile=BLK):
+    groups, count, _ = attn.shape
+    width = x.shape[1]
+    rows = pl.BlockSpec((tile, width), lambda i, p: (i, 0))
+    heads = pl.BlockSpec((groups, tile, PAIR), lambda i, p: (0, i, 0))
+    return pl.pallas_call(
+        feed_kernel,
+        grid_spec=pltpu.PrefetchScalarGridSpec(
+            num_scalar_prefetch=1,
+            grid=(count // tile,),
+            in_specs=[
+                heads, rows, rows, whole(w_out.shape), whole(w_up.shape), whole(w_down.shape),
+                whole(vecs.shape), whole(up_bias.shape),
+            ],
+            out_specs=[
+                rows, heads, rows, whole(w_down.shape), whole(w_up.shape), whole(w_out.shape),
+                whole(vecs.shape), whole(up_bias.shape),
+            ],
+            scratch_shapes=[pltpu.VMEM((tile, width), bf16)],
+        ),
+        out_shape=[
+            jax.ShapeDtypeStruct((count, width), bf16),
+            jax.ShapeDtypeStruct((groups, count, PAIR), bf16),
+            jax.ShapeDtypeStruct((count, width), f32),
+            jax.ShapeDtypeStruct(w_down.shape, f32),
+            jax.ShapeDtypeStruct(w_up.shape, f32),
+            jax.ShapeDtypeStruct(w_out.shape, f32),
+            jax.ShapeDtypeStruct(vecs.shape, f32),
+            jax.ShapeDtypeStruct(up_bias.shape, f32),
+        ],
+        compiler_params=pltpu.CompilerParams(vmem_limit_bytes=60 * 1024 * 1024),
+        name="feed",
+    )(pair_of, attn, x, dy, w_out, w_up, w_down, vecs, up_bias)
+
+
+def norm_back_kernel(dh_a_ref, dh_b_ref, x_ref, dmid_ref, gain_ref, dx_ref, gvec_ref):
+    @pl.when(pl.program_id(0) == 0)
+    def _():
+        gvec_ref[...] = jnp.zeros_like(gvec_ref)
+
+    d_low = dh_a_ref[...].astype(f32) + dh_b_ref[...].astype(f32)
+    unit, inv = norm_parts(x_ref[...].astype(f32))
+    scaled = d_low * gain_ref[...]
+    dx = dmid_ref[...] + inv * (
+        scaled
+        - jnp.mean(scaled, axis=-1, keepdims=True)
+        - unit * jnp.mean(scaled * unit, axis=-1, keepdims=True)
+    )
+    dx_ref[...] = dx.astype(bf16)
+    gvec_ref[0:1, :] += jnp.sum(d_low * unit, axis=0, keepdims=True)
+    gvec_ref[1:2, :] += jnp.sum(d_low, axis=0, keepdims=True)
+
+
+def norm_back(dh_a, dh_b, x, dmid, gain):
+    count, width = x.shape
+    rows = pl.BlockSpec((BLK, width), lambda i: (i, 0))
+    return pl.pallas_call(
+        norm_back_kernel,
+        grid=(count // BLK,),
+        in_specs=[rows, rows, rows, rows, whole(gain.shape)],
+        out_specs=[rows, whole((8, width))],
+        out_shape=[
+            jax.ShapeDtypeStruct((count, width), bf16),
+            jax.ShapeDtypeStruct((8, width), f32),
+        ],
+        name="norm_back",
+    )(dh_a, dh_b, x, dmid, gain)
 
 
 def layer_norm(values, gain_vec, offset):
@@ -58,7 +463,7 @@
     return row_top + jnp.log(row_sum)
 
 
-def attend(
+def attend_all(
     query_heads, key_blocks, value_blocks, doc_blocks, pos_blocks, query_doc, query_pos, log_norm
 ):
 
@@ -116,7 +521,7 @@
     return (part_q, part_k, part_v)
 
 
-def body(
+def general_body(
     inputs,
     out_grad,
     segment_ids,
@@ -185,7 +590,7 @@
         value_blocks = kv_heads[:, :, 1]
         doc_blocks = doc_rows.reshape(block_count, key_block)
         log_norm = row_log_norm(query_heads, key_blocks, doc_blocks, pos_blocks, query_doc, own_pos)
-        attn_acc = attend(
+        attn_acc = attend_all(
             query_heads,
             key_blocks,
             value_blocks,
@@ -347,41 +752,183 @@
     )
 
 
+AXES = ("z", "x", "y", "c")
+SIZES = (4, 2, 2, 2)
+
+
+def place(z, x, y, c):
+    return ((z * SIZES[1] + x) * SIZES[2] + y) * SIZES[3] + c
+
+
+def everyone():
+    return [
+        (z, x, y, c)
+        for z in range(SIZES[0])
+        for x in range(SIZES[1])
+        for y in range(SIZES[2])
+        for c in range(SIZES[3])
+    ]
+
+
+def gather_pairs(turn):
+    return [
+        (place(z, x, y, c), place(2 * ((z % 2) ^ turn) + c, x, y, z // 2))
+        for z, x, y, c in everyone()
+    ]
+
+
+def swap_pairs(dx, dy, dc):
+    return [(place(z, x, y, c), place(z, x ^ dx, y ^ dy, c ^ dc)) for z, x, y, c in everyone()]
+
+
+def move(value, pairs):
+    return lax.ppermute(value, AXES, pairs)
+
+
+def swap(value, dx=0, dy=0, dc=0):
+    return move(value, swap_pairs(dx, dy, dc))
+
+
+def to_pair(value, odd):
+    return [
+        move(lax.dynamic_index_in_dim(value, odd ^ turn, 0, keepdims=False)[0], gather_pairs(turn))
+        for turn in range(2)
+    ]
+
+
+def from_pair(value, odd):
+    back = [move(value[turn], [(b, a) for a, b in gather_pairs(turn)]) for turn in range(2)]
+    first = jnp.where(odd == 0, back[0], back[1])
+    second = jnp.where(odd == 0, back[1], back[0])
+    return jnp.stack([first, second])[:, None]
+
+
+def paired_body(
+    inputs, out_grad, segment_ids, block_order, w_qkv, w_out, w_up, w_down,
+    norm1_gain, norm1_bias, norm2_gain, norm2_bias, out_bias, up_bias, down_bias,
+):
+    z, x, y, c = (lax.axis_index(name) for name in AXES)
+    odd, upper = z % 2, z // 2
+    rows, width = inputs.shape[2], inputs.shape[3]
+    blocks = block_order.shape[0]
+    seq_len = blocks * BLK
+    shard = norm1_gain.shape[0]
+
+    x_piece = to_pair(inputs, odd)
+    def head_columns(pair):
+        parts = [
+            lax.dynamic_slice_in_dim(w_qkv, part * width + pair * PAIR, PAIR, axis=1) for part in range(3)
+        ]
+        return jnp.concatenate(parts, axis=1)
+
+    head_mine, head_other = head_columns(2 * x + c), head_columns(2 * x + 1 - c)
+    from_core = swap(head_other, dc=1)
+    from_y = swap(head_mine, dy=1)
+    from_both = swap(head_other, dy=1, dc=1)
+    low_half = jnp.where(c == 0, jnp.stack([head_mine, from_core]), jnp.stack([from_core, head_mine]))
+    high_half = jnp.where(c == 0, jnp.stack([from_y, from_both]), jnp.stack([from_both, from_y]))
+    w_heads = jnp.where(
+        y == 0, jnp.stack([low_half, high_half]), jnp.stack([high_half, low_half])
+    ).reshape(width, 3 * PAIR)
+
+    vectors = jnp.concatenate(
+        [norm1_gain, norm1_bias, norm2_gain, norm2_bias, out_bias, down_bias, up_bias]
+    ).reshape(-1, shard)
+    vectors = lax.all_gather(vectors, ("y", "c")).astype(f32)
+    gain_one, bias_one, gain_two, bias_two, full_obias, full_dbias = (
+        vectors[:, i].reshape(1, width) for i in range(6)
+    )
+    full_ubias = vectors[:, 6:].reshape(1, -1)
+
+    docs = lax.all_gather(segment_ids[:, 0], ("z", "x", "c"))
+    docs = lax.dynamic_index_in_dim(docs.reshape(-1, 2, 2, rows), odd, 1, keepdims=False)
+    docs = lax.dynamic_index_in_dim(docs, upper, 1, keepdims=False).reshape(seq_len)
+    ids = jnp.arange(blocks, dtype=jnp.int32)
+    before = jnp.sum((docs[None, :] < ids[:, None]).astype(jnp.int32), axis=1)
+    start = jnp.sum(jnp.where(docs[None, :] == ids[:, None], before[:, None], 0), axis=0)
+    low_of = start[::BLK] // BLK
+    high_of = jnp.sum((low_of[None, :] <= ids[:, None]).astype(jnp.int32), axis=1) - 1
+    start = start.reshape(blocks, 1, BLK)
+
+    slot = jnp.arange(blocks, dtype=jnp.int32)
+    group, turn, half = slot // 4, slot // 2 % 2, slot % 2
+    stored = 2 * (2 * (2 * (c ^ (group % 2)) + (upper ^ turn)) + (x ^ (group // 2))) + half
+    true_of = jnp.sum(jnp.where(stored[:, None] == ids[None, :], block_order[None, :], 0), axis=1)
+    slot_of = jnp.sum(jnp.where(true_of[None, :] == ids[:, None], slot[None, :], 0), axis=1)
+    groups = jnp.arange(4, dtype=jnp.int32)
+    pair_of = 2 * (x ^ (groups // 2)) + (c ^ (groups % 2))
+
+    across = [swap(piece, dx=1) for piece in x_piece]
+    beside = [swap(jnp.stack([own, far]), dc=1) for own, far in zip(x_piece, across)]
+    x_rows = jnp.stack([
+        *x_piece, beside[0][0], beside[1][0], *across, beside[0][1], beside[1][1]
+    ]).reshape(seq_len, width)
+
+    q, k, kt, v, vt, h = project(true_of, x_rows, gain_one, bias_one, w_heads)
+    dy_piece = to_pair(out_grad, odd)
+    o, ot, lse = attend(slot_of, low_of, q, start, k, vt)
+    o = o.reshape(4, -1, PAIR)
+    attn = jnp.stack([o[0], swap(o[1], dc=1), swap(o[2], dx=1), swap(o[3], dx=1, dc=1)])
+
+    full_out, full_up, full_down = (
+        lax.all_gather(member, ("y", "c"), axis=0, tiled=True) for member in (w_out, w_up, w_down)
+    )
+    vecs = jnp.concatenate([full_obias, gain_two, bias_two, full_dbias], axis=0)
+    own_x = jnp.concatenate(x_piece, axis=0)
+    own_dy = jnp.concatenate(dy_piece, axis=0)
+    result, d_o, d_middle, g_down, g_up, g_out, g_vecs, g_ubias = feed(
+        pair_of, attn, own_x, own_dy, full_out, full_up, full_down, vecs, full_ubias
+    )
+    outputs = from_pair(result.reshape(2, rows, width), odd)
+
+    def reduce_rows(value):
+        part = lax.psum_scatter(value.astype(bf16), ("y", "c"), scatter_dimension=0, tiled=True)
+        return lax.psum(part, ("z", "x")).astype(f32)
+
+    d_o = jnp.concatenate([d_o[0], swap(d_o[1], dc=1), swap(d_o[2], dx=1), swap(d_o[3], dx=1, dc=1)])
+    grad_out, grad_up, grad_down = reduce_rows(g_out), reduce_rows(g_up), reduce_rows(g_down)
+    dh, g_heads = attend_back(slot_of, high_of, k, kt, v, h, w_heads, q, start, d_o, ot, lse)
+    dh = dh.reshape(4, -1, width)
+    other = swap(jnp.stack([dh[1], dh[3]]), dc=1)
+    far = swap((dh[2].astype(f32) + other[1].astype(f32)).astype(bf16), dx=1)
+    near = (dh[0].astype(f32) + other[0].astype(f32)).astype(bf16)
+    dx, g_norm = norm_back(near, far, own_x, d_middle, gain_one)
+    input_grad = from_pair(dx.reshape(2, rows, width), odd).astype(f32)
+
+    g_heads = lax.psum_scatter(g_heads.astype(bf16), "y", scatter_dimension=0, tiled=True)
+    g_heads = lax.psum(g_heads, "z")
+    g_heads = lax.all_gather(g_heads, ("x", "c"))
+    g_heads = lax.dynamic_slice_in_dim(g_heads, c * shard, shard, axis=1)
+    grad_qkv = g_heads.reshape(4, shard, 3, PAIR).transpose(1, 2, 0, 3).reshape(shard, -1).astype(f32)
+
+    small = jnp.concatenate([
+        g_norm[0], g_norm[1], g_vecs[1], g_vecs[2], g_vecs[0], g_vecs[3], g_ubias[0]
+    ])
+    small = lax.psum(small, AXES)
+    index = 2 * y + c
+    owned = [
+        lax.dynamic_slice_in_dim(small, i * width + index * shard, shard) for i in range(6)
+    ]
+    owned_up = lax.dynamic_slice_in_dim(small, 6 * width + index * 4 * shard, 4 * shard)
+    return (
+        outputs, input_grad, grad_qkv, grad_out, grad_up, grad_down,
+        owned[0], owned[1], owned[2], owned[3], owned[4], owned_up, owned[5],
+    )
+
+
 def solution(mesh):
+    paired = mesh.shape["ctx"] == SIZES[0] * SIZES[1] and mesh.shape["fsdp"] == SIZES[2] * SIZES[3]
+    if paired:
+        mesh = Mesh(mesh.devices.reshape(SIZES), AXES)
+        ctx, fsdp, program = ("z", "x"), ("y", "c"), paired_body
+    else:
+        ctx, fsdp, program = "ctx", "fsdp", general_body
+    tokens = P(None, fsdp, ctx, None)
+    matrix, vector = P(fsdp, None), P(fsdp)
     return jax.shard_map(
-        body,
+        program,
         mesh=mesh,
-        in_specs=(
-            P(None, "fsdp", "ctx", None),
-            P(None, "fsdp", "ctx", None),
-            P(None, "fsdp", "ctx"),
-            P(),
-            P("fsdp", None),
-            P("fsdp", None),
-            P("fsdp", None),
-            P("fsdp", None),
-            P("fsdp"),
-            P("fsdp"),
-            P("fsdp"),
-            P("fsdp"),
-            P("fsdp"),
-            P("fsdp"),
-            P("fsdp"),
-        ),
-        out_specs=(
-            P(None, "fsdp", "ctx", None),
-            P(None, "fsdp", "ctx", None),
-            P("fsdp", None),
-            P("fsdp", None),
-            P("fsdp", None),
-            P("fsdp", None),
-            P("fsdp"),
-            P("fsdp"),
-            P("fsdp"),
-            P("fsdp"),
-            P("fsdp"),
-            P("fsdp"),
-            P("fsdp"),
-        ),
+        in_specs=(tokens, tokens, P(None, fsdp, ctx), P()) + (matrix,) * 4 + (vector,) * 7,
+        out_specs=(tokens, tokens) + (matrix,) * 4 + (vector,) * 7,
         check_vma=False,
     )

time: 1210 us -> 491 us (0.41)
  matrix products: 395 us -> 0 us
  local copies, waits for them, and re-layouts: 193 us -> 25.6 us
  waiting for transfers between devices: 300 us -> 166 us
  Pallas kernels: 0 us -> 127 us
  other arithmetic: 155 us -> 36.8 us
  blocking collectives: 131 us -> 85.6 us
  starting transfers between devices: 0.49 us -> 33.3 us
    dot_general x136 -> x0, matrix products: 395 us -> none  [the longest x32 77.9 us: score_block(): jnp.einsum('qhd,khd->hqk', query_heads, key_heads, preferred_element_type...]
    reduce_scatter x6 -> x4, waiting for transfers between devices: 229 us -> 77.8 us  [the longest x3 63.1 us: reduce_rows(): lax.psum_scatter(value.astype(bf16), ('y', 'c'), scatter_dimension=0, til...]
    pallas_call x0 -> x5, Pallas kernels: none -> 127 us  [the longest x1 42.7 us: attend_back(): pl.pallas_call(attend_back_kernel, grid_spec=pltpu.PrefetchScalarGridSpec...]
    mul x49 -> x0, other arithmetic: 68.3 us -> none  [the longest x48 62.6 us: body(): own_pos = own_blocks[row_ids // BLK] * BLK + row_ids % BLK]
    gather x6 -> x0, local copies, waits for them, and re-layouts: 53.6 us -> none  [the longest x2 46.1 us: body(): doc_rows = doc_all[all_pos]]
    all_gather x10 -> x4, blocking collectives: 98.1 us -> 44.7 us  [the longest x1 20.9 us: paired_body(): docs = lax.all_gather(segment_ids[:, 0], ('z', 'x', 'c'))]
    reduce_sum x30 -> x5, other arithmetic: 47 us -> 1.19 us  [the longest x1 0.63 us: paired_body(): jnp.sum(jnp.where(true_of[None, :] == ids[:, None], slot[None, :], 0), ax...]
    ppermute x0 -> x23, waiting for transfers between devices: none -> 44.9 us  [move(): return lax.ppermute(value, AXES, pairs)]
  transfers between devices with their start and end apart: 12 -> 31, of which waited for: 8 -> 10; matrix products, arithmetic and copies ran while one was open for 46% -> 10% of each run, Pallas kernels for 0% -> 11%
where the time goes in v1:
time: 491 us; the launch traced here: 488 us
  waiting for transfers between devices  166 us (34%)
  Pallas kernels  127 us (26%)
  blocking collectives  85.6 us (17%)
  other arithmetic  36.8 us (7%)
  starting transfers between devices  33.3 us (7%)
  local copies, waits for them, and re-layouts  25.6 us (5%)
  between operations  14.6 us (3%)
    reduce_scatter x3, waiting for transfers between devices, reduce_rows(): lax.psum_scatter(value.astype(bf16), ('y', 'c'), scatter_dimension=0, til...  63.1 us
    ppermute x23, waiting for transfers between devices, move(): return lax.ppermute(value, AXES, pairs)  44.9 us
    pallas_call x1, Pallas kernels, attend_back(): pl.pallas_call(attend_back_kernel, grid_spec=pltpu.PrefetchScalarGridSpec...  42.7 us
    psum x1, waiting for transfers between devices, reduce_rows(): return lax.psum(part, ('z', 'x')).astype(f32)  42.1 us
    psum x1, blocking collectives, paired_body(): small = lax.psum(small, AXES)  40.9 us
    pallas_call x1, Pallas kernels, attend(): pl.pallas_call(attend_kernel, grid_spec=pltpu.PrefetchScalarGridSpec(num_...  34.3 us
    ppermute x23, starting transfers between devices, move(): return lax.ppermute(value, AXES, pairs)  33 us
    pallas_call x1, Pallas kernels, feed(): pl.pallas_call(feed_kernel, grid_spec=pltpu.PrefetchScalarGridSpec(num_sc...  29 us
  transfers between devices with their start and end apart: 31, of which 10 were waited for; matrix products, arithmetic and copies ran while one was open for 10% of the time, Pallas kernels for 11%

profile of v1, /device:TPU:0, one launch (start us, length us, event | category | flops | bytes accessed | tf_op | source)
XLA Modules:
  0.0 488.2 jit_solution(9188342733830432653)
XLA Ops:
  9.6 2.4 collective-permute-start.8
  14.7 3.9 collective-permute-start.1
  22.6 5.6 %all_gather.22 = bf16[4,10,128]{2,1,0:T(8,128)(2,1)S(1)} all-gather(bf16[1,10,128]{2,1,0:T(8,128)(2,1)S(1)} %bitcast.115), channel_id=1, replica_groups=mesh['z'=4,'x'=2,'y'=2,'c'=2] {'y','c'}, dimensions={0}, use_global_device_ids=true | all-gather | bytes 12800 | tf_op jit(solution)/shard_map/all_gather | solution.py:837
  28.8 20.9 %all-gather = s32[32,1,512]{2,1,0:T(1,128)S(1)} all-gather(s32[2,1,512]{2,1,0:T(1,128)S(1)} %copy-done.8), channel_id=2, replica_groups=mesh['z'=4,'x'=2,'y'=2,'c'=2] {'z','x','c'}, dimensions={0}, use_global_device_ids=true | all-gather | bytes 69632 | tf_op jit(solution)/shard_map/all_gather | solution.py:843
  54.5 9.4 %all_gather.23.wo_ref = bf16[512,512]{1,0:T(8,128)(2,1)} all-gather(bf16[128,512]{1,0:T(8,128)(2,1)S(1)} %copy-done.5), channel_id=1, replica_groups=mesh['z'=4,'x'=2,'y'=2,'c'=2] {'y','c'}, dimensions={0}, use_global_device_ids=true | all-gather | bytes 655360 | tf_op jit(solution)/shard_map/all_gather | solution.py:874
  67.1 5.4 %collective-permute-start.12 = (bf16[512,512]{1,0:T(8,128)(2,1)}, bf16[512,512]{1,0:T(8,128)(2,1)}, u32[]{:S(2)}, u32[]{:S(2)}) collective-permute-start(bf16[512,512]{1,0:T(8,128)(2,1)} %get-tuple-element.139), channel_id=1, source_target_pairs={{0,0},{1,8},{2,2},{3,10},{4,4},{5,12},{6,6},{7,14},{8,16},{9,24},{... | collective-permute-start | bytes 1572872 | tf_op jit(solution)/shard_map/ppermute | solution.py:785
  75.5 2.7 collective-permute-done.4
  87.1 15.7 %project.1 = (bf16[4096,128]{1,0:T(8,128)(2,1)}, bf16[4096,128]{1,0:T(8,128)(2,1)}, bf16[128,4096]{1,0:T(8,128)(2,1)}, bf16[4096,128]{1,0:T(8,128)(2,1)}, bf16[1...) custom-call(s32[16]{0:T(128)} %copy-done.11, bf16[4096,512]{1,0:T(8,128)(2,1)} %bitcast.7.x_ref, ...), custom_call_target="tpu_custom_call" | custom-call | tf_op jit(solution)/shard_map/project/pallas_call | solution.py:62
  102.7 34.3 %attend.1 = (bf16[4096,128]{1,0:T(8,128)(2,1)}, f32[16,128,256]{2,1,0:T(8,128)}, f32[16,1,512]{2,1,0:T(1,128)}) custom-call(s32[16]{0:T(128)} %select_reduce_fusion.1.slot_ref, s32[16]{0:T(128)} %and_select_fusion.low_ref, bf16[4096,128]{1,0:T(8,128)(2,1)} %get-tuple-element.34.q_ref, s32[16,1,256]{2,1,0:T(1,128)} %bitcast.103, ...), custom_call_target="tpu_custom_call" | custom-call | tf_op jit(solution)/shard_map/attend/pallas_call | solution.py:146
  140.6 2.6 pad_maximum_fusion.4.dy_ref
  143.2 4.8 collective-permute-done.10
  148.0 4.0 collective-permute-done.11
  153.1 29.0 %feed.1 = (bf16[1024,512]{1,0:T(8,128)(2,1)}, bf16[4,1024,128]{2,1,0:T(8,128)(2,1)}, f32[1024,512]{1,0:T(8,128)}, f32[2048,512]{1,0:T(8,128)}, f32[512,2048]{1,0...) custom-call(s32[4]{0:T(128)} %fusion.4.pair_ref, ...), custom_call_target="tpu_custom_call" | custom-call | tf_op jit(solution)/shard_map/feed/pallas_call | solution.py:358
  186.4 6.8 %collective-permute-done.17 = bf16[1024,128]{1,0:T(8,128)(2,1)S(1)} collective-permute-done((bf16[1024,128]{1,0:T(8,128)(2,1)S(1)}, bf16[1024,128]{1,0:T(8,128)(2,1)S(1)}, u32[]{:S(2)}, u32[]{:S(2)}) %collective-permute-start.17) | collective-permute-done | bytes 262176 | tf_op jit(solution)/shard_map/ppermute | solution.py:785
  193.2 4.0 collective-permute-done.18
  198.2 42.7 %attend_back.1 = (bf16[4096,512]{1,0:T(8,128)(2,1)}, f32[512,384]{1,0:T(8,128)}) custom-call(s32[16]{0:T(128)} %select_reduce_fusion.1.slot_ref, s32[16]{0:T(128)} %broadcast_add_fusion.high_ref, bf16[4096,128]{1,0:T(8,128)(2,1)} %get-tuple-element.35.k_ref, bf16[128,4096]{1,0:T(8,128)(2,1)} %get-tuple-element.39.kt_ref, ...), custom_call_target="tpu_custom_call" | custom-call | tf_op jit(solution)/shard_map/attend_back/pallas_call | solution.py:254
  240.9 1.9 convert_element_type.89
  242.9 14.7 %reduce-scatter.5.cloned.1.call-done = bf16[256,384]{1,0:T(8,128)(2,1)} async-done(((bf16[512,384]{1,0:T(8,128)(2,1)}), bf16[256,384]{1,0:T(8,128)(2,1)}) %reduce-scatter.5.cloned.1.call-update) | async-done | bytes 196624 | tf_op jit(solution)/shard_map/reduce_scatter | solution.py:898
  258.6 3.8 convert_element_type.98
  262.5 3.8 convert_element_type.96
  271.6 3.6 collective-permute-start.15
  275.3 3.5 fusion
  280.2 22.7 %collective-permute-done.15 = bf16[512,512]{1,0:T(8,128)(2,1)S(1)} collective-permute-done((bf16[512,512]{1,0:T(8,128)(2,1)S(1)}, bf16[512,512]{1,0:T(8,128)(2,1)S(1)}, u32[]{:S(2)}, u32[]{:S(2)}) %collective-permute-start.15) | collective-permute-done | bytes 524320 | tf_op jit(solution)/shard_map/ppermute | solution.py:785
  304.0 8.8 %all_gather.27 = bf16[4,256,384]{2,1,0:T(8,128)(2,1)S(1)} all-gather(bf16[1,256,384]{2,1,0:T(8,128)(2,1)} %all-reduce.4.cloned.1.call-done), channel_id=1, replica_groups=mesh['z'=4,'x'=2,'y'=2,'c'=2] {'x','c'}, dimensions={0}, use_global_device_ids=true | all-gather | bytes 983040 | tf_op jit(solution)/shard_map/all_gather | solution.py:900
  315.4 4.9 %norm_back.1 = (bf16[1024,512]{1,0:T(8,128)(2,1)}, f32[8,512]{1,0:T(8,128)}) custom-call(bf16[1024,512]{1,0:T(8,128)(2,1)} %get-tuple-element.124.dh_a_ref, bf16[1024,512]{1,0:T(8,128)(2,1)} %copy-done.1, bf16[1024,512]{1,0:T(8,128)(2,1)} %copy-done, f32[1024,512]{1,0:T(8,128)} %get-tuple-element.46.dmid_ref, f32[1,512]{1,0:T(1,128)} %get-tuple-element.160.gain_ref), custom_call_target="tpu_custom_call" | custom-call | tf_op jit(solution)/shard_map/norm_back/pallas_call | solution.py:409
  322.3 3.3 collective-permute-start.22
  326.4 29.2 %reduce-scatter.11.cloned.1.call-done = bf16[512,512]{1,0:T(8,128)(2,1)} async-done(((bf16[2048,512]{1,0:T(8,128)(2,1)}), bf16[512,512]{1,0:T(8,128)(2,1)}) %reduce-scatter.11.cloned.1.call-update) | async-done | bytes 524304 | tf_op jit(solution)/shard_map/reduce_scatter | solution.py:885
  355.5 34.0 %reduce-scatter.9.cloned.1.call-done = bf16[128,2048]{1,0:T(8,128)(2,1)} async-done(((bf16[512,2048]{1,0:T(8,128)(2,1)}), bf16[128,2048]{1,0:T(8,128)(2,1)}) %reduce-scatter.9.cloned.1.call-update) | async-done | bytes 524304 | tf_op jit(solution)/shard_map/reduce_scatter | solution.py:885
  389.6 40.9 %psum.39 = f32[5120]{0:T(1024)S(1)} all-reduce(f32[5120]{0:T(1024)S(1)} %constant_dynamic-update-slice_fusion.7), channel_id=1, replica_groups=mesh['z'=4,'x'=2,'y'=2,'c'=2] {'z','x','y','c'}, use_global_device_ids=true, to_apply=%region_13.14 | all-reduce | flops 5120 | bytes 40960 | tf_op jit(solution)/shard_map/psum | solution.py:907
  433.3 42.1 %all-reduce.6.cloned.1.call-done = (bf16[128,512]{1,0:T(8,128)(2,1)}, bf16[128,2048]{1,0:T(8,128)(2,1)}, bf16[512,512]{1,0:T(8,128)(2,1)}) async-done(((bf16[128,512]{1,0:T(8,128)(2,1)}, bf16[128,2048]{1,0:T(8,128)(2,1)}, bf16[512,512]{1,0:T(8,128)(2,1)}), (bf16[128,512]{1,0:T(8,128)(2,1)}, bf16[128,2048]{1,0:T(8,128)(2,1)}, bf16[512,512]{1,0:T(8,128)(2,1)})) %all-reduce.6.cloned.1.call-update) | async-done | bytes 1179664 | tf_op jit(solution)/shard_map/psum | solution.py:886
  475.4 2.1 convert_element_type.97
  477.6 2.1 convert_element_type.99
  (165 shorter events, 58.1 us)
Async XLA Ops:
  7.3 145.8 %all-gather.4.cloned.1.call-start = ((), (), s32[]{:S(2)}) async-start(), calls=%async_computation.4 | async-start | bytes 2621440 | tf_op jit(solution)/shard_map/all_gather | solution.py:874
  8.0 145.1 %all-gather.6.cloned.1.call-start = ((), (), s32[]{:S(2)}) async-start(), calls=%async_computation.5 | async-start | bytes 2621440 | tf_op jit(solution)/shard_map/all_gather | solution.py:874
  9.6 64.0 %collective-permute-start.8 = (bf16[128,384]{1,0:T(8,128)(2,1)}, bf16[128,384]{1,0:T(8,128)(2,1)}, u32[]{:S(2)}, u32[]{:S(2)}) collective-permute-start(bf16[128,384]{1,0:T(8,128)(2,1)} %pad_maximum_fusion.7), channel_id=1, source_target_pairs={{0,3},{1,2},{2,1},{3,0},{4,7},{5,6},{6,5},{7,4},{8,11},{9,10},{10,... | collective-permute-start | bytes 294920 | tf_op jit(solution)/shard_map/ppermute | solution.py:785
  12.0 66.3 %collective-permute-start.6 = (bf16[128,384]{1,0:T(8,128)(2,1)}, bf16[128,384]{1,0:T(8,128)(2,1)}, u32[]{:S(2)}, u32[]{:S(2)}) collective-permute-start(bf16[128,384]{1,0:T(8,128)(2,1)} %pad_maximum_fusion.7), channel_id=1, source_target_pairs={{0,1},{1,0},{2,3},{3,2},{4,5},{5,4},{6,7},{7,6},{8,9},{9,8},{10,11... | collective-permute-start | bytes 294920 | tf_op jit(solution)/shard_map/ppermute | solution.py:785
  14.0 38.8 %collective-permute-start = (bf16[512,512]{1,0:T(8,128)(2,1)S(1)}, bf16[512,512]{1,0:T(8,128)(2,1)S(1)}, u32[]{:S(2)}, u32[]{:S(2)}) collective-permute-start(bf16[512,512]{1,0:T(8,128)(2,1)S(1)} %get-tuple-element.146), channel_id=1, source_target_pairs={{0,0},{1,8},{2,2},{3,10},{4,4},{5,12},{6,6},{7,14},{8,16},{9,24},{... | collective-permute-start | bytes 1572872 | tf_op jit(solution)/shard_map/ppermute | solution.py:785
  14.7 49.3 %collective-permute-start.1 = (bf16[512,512]{1,0:T(8,128)(2,1)S(1)}, bf16[512,512]{1,0:T(8,128)(2,1)S(1)}, u32[]{:S(2)}, u32[]{:S(2)}) collective-permute-start(bf16[512,512]{1,0:T(8,128)(2,1)S(1)} %get-tuple-element.145), channel_id=1, source_target_pairs={{0,16},{1,24},{2,18},{3,26},{4,20},{5,28},{6,22},{7,30},{8,0},{9,8... | collective-permute-start | bytes 1572872 | tf_op jit(solution)/shard_map/ppermute | solution.py:785
  19.2 53.4 %collective-permute-start.7 = (bf16[128,384]{1,0:T(8,128)(2,1)}, bf16[128,384]{1,0:T(8,128)(2,1)}, u32[]{:S(2)}, u32[]{:S(2)}) collective-permute-start(bf16[128,384]{1,0:T(8,128)(2,1)} %get-tuple-element.154), channel_id=1, source_target_pairs={{0,2},{1,3},{2,0},{3,1},{4,6},{5,7},{6,4},{7,5},{8,10},{9,11},{10,... | collective-permute-start | bytes 294920 | tf_op jit(solution)/shard_map/ppermute | solution.py:785
  19.7 237.9 %reduce-scatter.5.cloned.1.call-start = ((), (), s32[]{:S(2)}) async-start(), calls=%async_computation.6 | async-start | bytes 589824 | tf_op jit(solution)/shard_map/reduce_scatter | solution.py:898
  52.8 14.4 %collective-permute-start.2 = (bf16[512,512]{1,0:T(8,128)(2,1)S(1)}, bf16[512,512]{1,0:T(8,128)(2,1)S(1)}, u32[]{:S(2)}, u32[]{:S(2)}) collective-permute-start(bf16[512,512]{1,0:T(8,128)(2,1)S(1)} %collective-permute-done), channel_id=1, source_target_pairs={{0,4},{1,5},{2,6},{3,7},{4,0},{5,1},{6,2},{7,3},{8,12},{9,13},{10,... | collective-permute-start | bytes 1572872 | tf_op jit(solution)/shard_map/ppermute | solution.py:785
  63.9 14.3 %collective-permute-start.4 = (bf16[512,512]{1,0:T(8,128)(2,1)S(1)}, bf16[512,512]{1,0:T(8,128)(2,1)S(1)}, u32[]{:S(2)}, u32[]{:S(2)}) collective-permute-start(bf16[512,512]{1,0:T(8,128)(2,1)S(1)} %collective-permute-done.1), channel_id=1, source_target_pairs={{0,4},{1,5},{2,6},{3,7},{4,0},{5,1},{6,2},{7,3},{8,12},{9,13},{10,... | collective-permute-start | bytes 1572872 | tf_op jit(solution)/shard_map/ppermute | solution.py:785
  67.1 73.5 %collective-permute-start.12 = (bf16[512,512]{1,0:T(8,128)(2,1)}, bf16[512,512]{1,0:T(8,128)(2,1)}, u32[]{:S(2)}, u32[]{:S(2)}) collective-permute-start(bf16[512,512]{1,0:T(8,128)(2,1)} %get-tuple-element.139), channel_id=1, source_target_pairs={{0,0},{1,8},{2,2},{3,10},{4,4},{5,12},{6,6},{7,14},{8,16},{9,24},{... | collective-permute-start | bytes 1572872 | tf_op jit(solution)/shard_map/ppermute | solution.py:785
  72.6 68.0 %collective-permute-start.13 = (bf16[512,512]{1,0:T(8,128)(2,1)}, bf16[512,512]{1,0:T(8,128)(2,1)}, u32[]{:S(2)}, u32[]{:S(2)}) collective-permute-start(bf16[512,512]{1,0:T(8,128)(2,1)} %get-tuple-element.140), channel_id=1, source_target_pairs={{0,16},{1,24},{2,18},{3,26},{4,20},{5,28},{6,22},{7,30},{8,0},{9,8... | collective-permute-start | bytes 1572872 | tf_op jit(solution)/shard_map/ppermute | solution.py:785
  73.6 8.3 %collective-permute-start.3 = (bf16[2,512,512]{2,1,0:T(8,128)(2,1)S(1)}, bf16[2,512,512]{2,1,0:T(8,128)(2,1)S(1)}, u32[]{:S(2)}, u32[]{:S(2)}) collective-permute-start(bf16[2,512,512]{2,1,0:T(8,128)(2,1)S(1)} %pad_maximum_fusion.1), channel_id=1, source_target_pairs={{0,1},{1,0},{2,3},{3,2},{4,5},{5,4},{6,7},{7,6},{8,9},{9,8},{10,11... | collective-permute-start | bytes 3145736 | tf_op jit(solution)/shard_map/ppermute | solution.py:785
  78.3 4.5 collective-permute-start.5
  138.2 5.0 %collective-permute-start.9 = (bf16[1024,128]{1,0:T(8,128)(2,1)S(1)}, bf16[1024,128]{1,0:T(8,128)(2,1)S(1)}, u32[]{:S(2)}, u32[]{:S(2)}) collective-permute-start(bf16[1024,128]{1,0:T(8,128)(2,1)S(1)} %get-tuple-element.144), channel_id=1, source_target_pairs={{0,1},{1,0},{2,3},{3,2},{4,5},{5,4},{6,7},{7,6},{8,9},{9,8},{10,11... | collective-permute-start | bytes 786440 | tf_op jit(solution)/shard_map/ppermute | solution.py:785
  138.8 9.2 %collective-permute-start.10 = (bf16[1024,128]{1,0:T(8,128)(2,1)S(1)}, bf16[1024,128]{1,0:T(8,128)(2,1)S(1)}, u32[]{:S(2)}, u32[]{:S(2)}) collective-permute-start(bf16[1024,128]{1,0:T(8,128)(2,1)S(1)} %get-tuple-element.143), channel_id=1, source_target_pairs={{0,4},{1,5},{2,6},{3,7},{4,0},{5,1},{6,2},{7,3},{8,12},{9,13},{10,... | collective-permute-start | bytes 786440 | tf_op jit(solution)/shard_map/ppermute | solution.py:785
  140.5 11.4 %collective-permute-start.11 = (bf16[1024,128]{1,0:T(8,128)(2,1)S(1)}, bf16[1024,128]{1,0:T(8,128)(2,1)S(1)}, u32[]{:S(2)}, u32[]{:S(2)}) collective-permute-start(bf16[1024,128]{1,0:T(8,128)(2,1)S(1)} %get-tuple-element.142), channel_id=1, source_target_pairs={{0,5},{1,4},{2,7},{3,6},{4,1},{5,0},{6,3},{7,2},{8,13},{9,12},{10,... | collective-permute-start | bytes 786440 | tf_op jit(solution)/shard_map/ppermute | solution.py:785
  183.4 3.0 collective-permute-start.16
  184.1 9.2 %collective-permute-start.17 = (bf16[1024,128]{1,0:T(8,128)(2,1)S(1)}, bf16[1024,128]{1,0:T(8,128)(2,1)S(1)}, u32[]{:S(2)}, u32[]{:S(2)}) collective-permute-start(bf16[1024,128]{1,0:T(8,128)(2,1)S(1)} %get-tuple-element.133), channel_id=1, source_target_pairs={{0,4},{1,5},{2,6},{3,7},{4,0},{5,1},{6,2},{7,3},{8,12},{9,13},{10,... | collective-permute-start | bytes 786440 | tf_op jit(solution)/shard_map/ppermute | solution.py:785
  185.8 11.4 %collective-permute-start.18 = (bf16[1024,128]{1,0:T(8,128)(2,1)S(1)}, bf16[1024,128]{1,0:T(8,128)(2,1)S(1)}, u32[]{:S(2)}, u32[]{:S(2)}) collective-permute-start(bf16[1024,128]{1,0:T(8,128)(2,1)S(1)} %get-tuple-element.132), channel_id=1, source_target_pairs={{0,5},{1,4},{2,7},{3,6},{4,1},{5,0},{6,3},{7,2},{8,13},{9,12},{10,... | collective-permute-start | bytes 786440 | tf_op jit(solution)/shard_map/ppermute | solution.py:785
  242.9 61.2 %all-reduce.4.cloned.1.call-start = ((), (), s32[]{:S(2)}) async-start(), calls=%async_computation.7 | async-start | bytes 393216 | tf_op jit(solution)/shard_map/psum | solution.py:899
  257.6 68.7 %reduce-scatter.7.cloned.1.call-start = ((), (), s32[]{:S(2)}) async-start(), calls=%async_computation.8 | async-start | bytes 655360 | tf_op jit(solution)/shard_map/reduce_scatter | solution.py:885
  258.6 96.9 %reduce-scatter.11.cloned.1.call-start = ((), (), s32[]{:S(2)}) async-start(), calls=%async_computation.10 | async-start | bytes 2621440 | tf_op jit(solution)/shard_map/reduce_scatter | solution.py:885
  262.5 127.0 %reduce-scatter.9.cloned.1.call-start = ((), (), s32[]{:S(2)}) async-start(), calls=%async_computation.9 | async-start | bytes 2621440 | tf_op jit(solution)/shard_map/reduce_scatter | solution.py:885
  266.4 209.1 %all-reduce.6.cloned.1.call-start = ((), (), s32[]{:S(2)}) async-start(), calls=%async_computation.11 | async-start | bytes 2359296 | tf_op jit(solution)/shard_map/psum | solution.py:886
  269.6 5.6 %collective-permute-start.19 = (bf16[2,1024,512]{2,1,0:T(8,128)(2,1)}, bf16[2,1024,512]{2,1,0:T(8,128)(2,1)S(1)}, u32[]{:S(2)}, u32[]{:S(2)}) collective-permute-start(bf16[2,1024,512]{2,1,0:T(8,128)(2,1)} %pad_maximum_fusion), channel_id=1, source_target_pairs={{0,1},{1,0},{2,3},{3,2},{4,5},{5,4},{6,7},{7,6},{8,9},{9,8},{10,11... | collective-permute-start | bytes 6291464 | tf_op jit(solution)/shard_map/ppermute | solution.py:785
  270.9 9.3 %collective-permute-start.14 = (bf16[512,512]{1,0:T(8,128)(2,1)S(1)}, bf16[512,512]{1,0:T(8,128)(2,1)S(1)}, u32[]{:S(2)}, u32[]{:S(2)}) collective-permute-start(bf16[512,512]{1,0:T(8,128)(2,1)S(1)} %get-tuple-element.137), channel_id=1, source_target_pairs={{0,0},{8,1},{2,2},{10,3},{4,4},{12,5},{6,6},{14,7},{16,8},{24,9},{... | collective-permute-start | bytes 1572872 | tf_op jit(solution)/shard_map/ppermute | solution.py:785
  271.6 31.3 %collective-permute-start.15 = (bf16[512,512]{1,0:T(8,128)(2,1)S(1)}, bf16[512,512]{1,0:T(8,128)(2,1)S(1)}, u32[]{:S(2)}, u32[]{:S(2)}) collective-permute-start(bf16[512,512]{1,0:T(8,128)(2,1)S(1)} %get-tuple-element.138), channel_id=1, source_target_pairs={{16,0},{24,1},{18,2},{26,3},{20,4},{28,5},{22,6},{30,7},{0,8},{8,9... | collective-permute-start | bytes 1572872 | tf_op jit(solution)/shard_map/ppermute | solution.py:785
  278.7 35.7 %collective-permute-start.20 = (bf16[1024,512]{1,0:T(8,128)(2,1)}, bf16[1024,512]{1,0:T(8,128)(2,1)S(1)}, u32[]{:S(2)}, u32[]{:S(2)}) collective-permute-start(bf16[1024,512]{1,0:T(8,128)(2,1)} %get-tuple-element.123), channel_id=1, source_target_pairs={{0,4},{1,5},{2,6},{3,7},{4,0},{5,1},{6,2},{7,3},{8,12},{9,13},{10,... | collective-permute-start | bytes 3145736 | tf_op jit(solution)/shard_map/ppermute | solution.py:785
  315.4 74.2 %copy-start.6 = (f32[1,2048]{1,0:T(1,128)S(1)}, f32[1,2048]{1,0:T(1,128)}, u32[]{:S(2)}) copy-start(f32[1,2048]{1,0:T(1,128)} %get-tuple-element.54) | copy-start | bytes 24580
  321.6 110.2 %collective-permute-start.21 = (bf16[512,512]{1,0:T(8,128)(2,1)S(1)}, bf16[512,512]{1,0:T(8,128)(2,1)S(1)}, u32[]{:S(2)}, u32[]{:S(2)}) collective-permute-start(bf16[512,512]{1,0:T(8,128)(2,1)S(1)} %get-tuple-element.129), channel_id=1, source_target_pairs={{0,0},{8,1},{2,2},{10,3},{4,4},{12,5},{6,6},{14,7},{16,8},{24,9},{... | collective-permute-start | bytes 1572872 | tf_op jit(solution)/shard_map/ppermute | solution.py:785
  322.3 109.5 %collective-permute-start.22 = (bf16[512,512]{1,0:T(8,128)(2,1)S(1)}, bf16[512,512]{1,0:T(8,128)(2,1)S(1)}, u32[]{:S(2)}, u32[]{:S(2)}) collective-permute-start(bf16[512,512]{1,0:T(8,128)(2,1)S(1)} %get-tuple-element.130), channel_id=1, source_target_pairs={{16,0},{24,1},{18,2},{26,3},{20,4},{28,5},{22,6},{30,7},{0,8},{8,9... | collective-permute-start | bytes 1572872 | tf_op jit(solution)/shard_map/ppermute | solution.py:785
  (16 other events, 401.1 us)
Sparse Core Ops, SparseCore 0:
  9.7 27.4 all-gather.3
  38.7 24.4 all-gather.5
  243.0 14.5 reduce-scatter.4
  259.9 38.8 all-reduce.3
  301.1 20.3 reduce-scatter.6
  324.1 31.4 reduce-scatter.10
  358.1 31.3 reduce-scatter.8
  393.8 81.5 all-reduce.5

commit v2 on v1

--- a/solution.py
+++ b/solution.py
@@ -40,57 +40,6 @@
     return pl.BlockSpec(shape, lambda *_: zeros)
 
 
-def project_kernel(true_ref, x_ref, gain_ref, bias_ref, w_ref, q_ref, k_ref, kt_ref, v_ref, vt_ref, h_ref):
-    unit, _ = norm_parts(x_ref[...].astype(f32))
-    low = (unit * gain_ref[...] + bias_ref[...]).astype(bf16)
-    h_ref[...] = low
-    qkv = jnp.dot(low, w_ref[...], preferred_element_type=f32)
-    q_ref[...] = (qkv[:, :PAIR] * (SCORE_SCALE * LOG2E)).astype(bf16)
-    k = qkv[:, PAIR : 2 * PAIR].astype(bf16)
-    v = qkv[:, 2 * PAIR :].astype(bf16)
-    k_ref[...] = k
-    v_ref[...] = v
-    kt_ref[...] = k.T
-    vt_ref[...] = v.T
-
-
-def project(true_of, rows, gain, bias, weight):
-    count, width = rows.shape
-    blocks = count // BLK
-    by_true = pl.BlockSpec((BLK, PAIR), lambda t, tab: (tab[t], 0))
-    by_true_t = pl.BlockSpec((PAIR, BLK), lambda t, tab: (0, tab[t]))
-    return pl.pallas_call(
-        project_kernel,
-        grid_spec=pltpu.PrefetchScalarGridSpec(
-            num_scalar_prefetch=1,
-            grid=(blocks,),
-            in_specs=[
-                pl.BlockSpec((BLK, width), lambda t, tab: (t, 0)),
-                whole(gain.shape),
-                whole(bias.shape),
-                whole(weight.shape),
-            ],
-            out_specs=[
-                by_true,
-                by_true,
-                by_true_t,
-                by_true,
-                by_true_t,
-                pl.BlockSpec((BLK, width), lambda t, tab: (tab[t], 0)),
-            ],
-        ),
-        out_shape=[
-            jax.ShapeDtypeStruct((count, PAIR), bf16),
-            jax.ShapeDtypeStruct((count, PAIR), bf16),
-            jax.ShapeDtypeStruct((PAIR, count), bf16),
-            jax.ShapeDtypeStruct((count, PAIR), bf16),
-            jax.ShapeDtypeStruct((PAIR, count), bf16),
-            jax.ShapeDtypeStruct((count, width), bf16),
-        ],
-        name="project",
-    )(true_of, rows, gain, bias, weight)
-
-
 def split_heads(block):
     lane = lax.broadcasted_iota(jnp.int32, block.shape, 1)
     zero = jnp.zeros_like(block)
@@ -98,7 +47,7 @@
     return jnp.concatenate([jnp.where(first, block, zero), jnp.where(first, zero, block)], axis=0)
 
 
-def attend_kernel(slot_ref, low_ref, q_ref, start_ref, k_ref, vt_ref, o_ref, ot_ref, lse_ref, acc, top):
+def attend_kernel(tab_ref, q_ref, start_ref, k_ref, vt_ref, o_ref, ot_ref, lse_ref, acc, top):
     qb = pl.program_id(0)
     both = split_heads(q_ref[...])
     start = jnp.concatenate([start_ref[0], start_ref[0]], axis=1)
@@ -107,11 +56,11 @@
     ones = jnp.ones((16, BLK), bf16)
 
     def scores(kb):
-        base = pl.multiple_of(kb * BLK, BLK)
+        base = pl.multiple_of(tab_ref[2, kb] * BLK, BLK)
         return contract(k_ref[pl.ds(base, BLK), :], both, 1, 1)
 
     def values(kb):
-        base = pl.multiple_of(kb * BLK, BLK)
+        base = pl.multiple_of(tab_ref[2, kb] * BLK, BLK)
         return jnp.concatenate([vt_ref[:, pl.ds(base, BLK)], ones], axis=0)
 
     st = scores(qb)
@@ -131,7 +80,7 @@
         acc[...] = acc[...] * jnp.exp2(old - peak) + jnp.dot(values(kb), probs, preferred_element_type=f32)
         return carry
 
-    lax.fori_loop(low_ref[qb], qb, visit, 0)
+    lax.fori_loop(tab_ref[0, qb], qb, visit, 0)
     total = acc[PAIR : PAIR + 1, :]
     lse_ref[0] = top[...] + jnp.log2(total)
     out = acc[:PAIR, :] / total
@@ -140,24 +89,24 @@
     o_ref[...] = heads.T.astype(bf16)
 
 
-def attend(slot_of, low_of, q, start, k, vt):
+def attend(tab, q, start, k, vt):
     count = q.shape[0]
     blocks = count // BLK
     return pl.pallas_call(
         attend_kernel,
         grid_spec=pltpu.PrefetchScalarGridSpec(
-            num_scalar_prefetch=2,
+            num_scalar_prefetch=1,
             grid=(blocks,),
             in_specs=[
-                pl.BlockSpec((BLK, PAIR), lambda b, s, l: (b, 0)),
-                pl.BlockSpec((1, 1, BLK), lambda b, s, l: (b, 0, 0)),
+                pl.BlockSpec((BLK, PAIR), lambda b, t: (t[2, b], 0)),
+                pl.BlockSpec((1, 1, BLK), lambda b, t: (b, 0, 0)),
                 whole(k.shape),
                 whole(vt.shape),
             ],
             out_specs=[
-                pl.BlockSpec((BLK, PAIR), lambda b, s, l: (s[b], 0)),
-                pl.BlockSpec((1, PAIR, BLK), lambda b, s, l: (b, 0, 0)),
-                pl.BlockSpec((1, 1, 2 * BLK), lambda b, s, l: (b, 0, 0)),
+                pl.BlockSpec((BLK, PAIR), lambda b, t: (t[2, b], 0)),
+                pl.BlockSpec((1, PAIR, BLK), lambda b, t: (b, 0, 0)),
+                pl.BlockSpec((1, 1, 2 * BLK), lambda b, t: (b, 0, 0)),
             ],
             scratch_shapes=[
                 pltpu.VMEM((PAIR + 16, 2 * BLK), f32),
@@ -170,28 +119,29 @@
             jax.ShapeDtypeStruct((blocks, 1, 2 * BLK), f32),
         ],
         name="attend",
-    )(slot_of, low_of, q, start, k, vt)
+    )(tab, q, start, k, vt)
 
 
 def attend_back_kernel(
-    slot_ref, high_ref, k_ref, kt_ref, v_ref, h_ref, w_ref, q_ref, start_ref, do_ref, ot_ref, lse_ref,
-    dh_ref, gw_ref, dqt, dk, dv, delta,
+    tab_ref, k_ref, kt_ref, v_ref, h_ref, w_ref, q_ref, start_ref, do_ref, ot_ref, lse_ref,
+    gain_ref, bias_ref, dh_ref, gw_ref, gn_ref, dqt, dk, dv, delta, total, sums,
 ):
     kb = pl.program_id(0)
     blocks = pl.num_programs(0)
     row = lax.broadcasted_iota(jnp.int32, (BLK, 2 * BLK), 0)
     col = lax.broadcasted_iota(jnp.int32, (BLK, 2 * BLK), 1)
 
-    def d_out(qb):
-        return do_ref[pl.ds(pl.multiple_of(slot_ref[qb] * BLK, BLK), BLK), :]
+    def at(qb):
+        return pl.ds(pl.multiple_of(tab_ref[2, qb] * BLK, BLK), BLK)
 
     @pl.when(kb == 0)
     def _():
-        gw_ref[...] = jnp.zeros_like(gw_ref)
+        total[...] = jnp.zeros_like(total)
+        sums[...] = jnp.zeros_like(sums)
 
         def prepare(qb, carry):
             dqt[qb] = jnp.zeros((PAIR, BLK), f32)
-            both = d_out(qb).astype(f32).T * ot_ref[qb]
+            both = do_ref[at(qb), :].astype(f32).T * ot_ref[qb]
             delta[qb] = jnp.concatenate(
                 [
                     jnp.sum(both[:HD], axis=0, keepdims=True),
@@ -208,8 +158,8 @@
     kt = kt_ref[...]
 
     def tile(qb, diagonal):
-        both_q = split_heads(q_ref[pl.ds(pl.multiple_of(qb * BLK, BLK), BLK), :])
-        both_do = split_heads(d_out(qb))
+        both_q = split_heads(q_ref[at(qb), :])
+        both_do = split_heads(do_ref[at(qb), :])
         start = jnp.concatenate([start_ref[qb], start_ref[qb]], axis=1)
         st = contract(k, both_q, 1, 1)
         dpt = contract(v, both_do, 1, 1)
@@ -240,51 +190,71 @@
         tile(qb, False)
         return carry
 
-    lax.fori_loop(kb + 1, high_ref[kb] + 1, visit, 0)
+    lax.fori_loop(kb + 1, tab_ref[1, kb] + 1, visit, 0)
     dq = (dqt[kb] * SCORE_SCALE).T.astype(bf16)
     joined = jnp.concatenate([dq, (dk[...] * LN2).astype(bf16), dv[...].astype(bf16)], axis=1)
     dh_ref[...] = contract(joined, w_ref[...], 1, 1).astype(bf16)
-    gw_ref[...] += contract(h_ref[...], joined, 0, 0)
-
-
-def attend_back(slot_of, high_of, k, kt, v, h, weight, q, start, d_out, ot, lse):
+    total[...] += contract(h_ref[...], joined, 0, 0)
+    sums[...] += jnp.sum(joined.astype(f32), axis=0, keepdims=True)
+
+    @pl.when(kb == blocks - 1)
+    def _():
+        shard = gw_ref.shape[1]
+        for j in range(gw_ref.shape[0]):
+            part = pl.ds(j * shard, shard)
+            gw_ref[j] = (total[part] * gain_ref[part] + bias_ref[part] * sums[...]).astype(bf16)
+            w = w_ref[part].astype(f32)
+            for i, term in enumerate((w * total[part], w * sums[...])):
+                column = jnp.sum(term, axis=1, keepdims=True)
+                gn_ref[i : i + 1, part] = jnp.broadcast_to(column, (shard, shard)).T[:1]
+
+
+def attend_back(tab, k, kt, v, h, weight, q, start, d_out, ot, lse, gain, bias, shards):
     count = q.shape[0]
     width = h.shape[1]
+    shard = width // shards
+    gain, bias = gain.reshape(width, 1), bias.reshape(width, 1)
     blocks = count // BLK
     return pl.pallas_call(
         attend_back_kernel,
         grid_spec=pltpu.PrefetchScalarGridSpec(
-            num_scalar_prefetch=2,
+            num_scalar_prefetch=1,
             grid=(blocks,),
             in_specs=[
-                pl.BlockSpec((BLK, PAIR), lambda b, s, l: (b, 0)),
-                pl.BlockSpec((PAIR, BLK), lambda b, s, l: (0, b)),
-                pl.BlockSpec((BLK, PAIR), lambda b, s, l: (b, 0)),
-                pl.BlockSpec((BLK, width), lambda b, s, l: (b, 0)),
+                pl.BlockSpec((BLK, PAIR), lambda b, t: (t[2, b], 0)),
+                pl.BlockSpec((PAIR, BLK), lambda b, t: (0, t[2, b])),
+                pl.BlockSpec((BLK, PAIR), lambda b, t: (t[2, b], 0)),
+                pl.BlockSpec((BLK, width), lambda b, t: (t[2, b], 0)),
                 whole(weight.shape),
                 whole(q.shape),
                 whole(start.shape),
                 whole(d_out.shape),
                 whole(ot.shape),
                 whole(lse.shape),
+                whole(gain.shape),
+                whole(bias.shape),
             ],
             out_specs=[
-                pl.BlockSpec((BLK, width), lambda b, s, l: (s[b], 0)),
-                whole(weight.shape),
+                pl.BlockSpec((BLK, width), lambda b, t: (t[2, b], 0)),
+                whole((shards, shard, 3 * PAIR)),
+                whole((2, width)),
             ],
             scratch_shapes=[
                 pltpu.VMEM((blocks, PAIR, BLK), f32),
                 pltpu.VMEM((BLK, PAIR), f32),
                 pltpu.VMEM((BLK, PAIR), f32),
                 pltpu.VMEM((blocks, 1, 2 * BLK), f32),
+                pltpu.VMEM(weight.shape, f32),
+                pltpu.VMEM((1, 3 * PAIR), f32),
             ],
         ),
         out_shape=[
             jax.ShapeDtypeStruct((count, width), bf16),
-            jax.ShapeDtypeStruct(weight.shape, f32),
+            jax.ShapeDtypeStruct((shards, shard, 3 * PAIR), bf16),
+            jax.ShapeDtypeStruct((2, width), f32),
         ],
         name="attend_back",
-    )(slot_of, high_of, k, kt, v, h, weight, q, start, d_out, ot, lse)
+    )(tab, k, kt, v, h, weight, q, start, d_out, ot, lse, gain, bias)
 
 
 FF_TILE = 512
@@ -292,7 +262,7 @@
 
 def feed_kernel(
     pair_ref, attn_ref, x_ref, dy_ref, wo_ref, wu_ref, wd_ref, vec_ref, ub_ref,
-    y_ref, do_ref, dmid_ref, gd_ref, gu_ref, go_ref, gvec_ref, gub_ref, attn_all,
+    y_ref, do_ref, dmid_ref, grad_ref, gvec_ref, gub_ref, attn_all, gd_ref, gu_ref, go_ref,
 ):
     step = pl.program_id(0)
     groups = attn_ref.shape[0]
@@ -305,7 +275,7 @@
     for g in range(groups):
         attn_all[:, pl.ds(pl.multiple_of(pair_ref[g] * PAIR, PAIR), PAIR)] = attn_ref[g]
     attn = attn_all[...]
-    out_bias, gain, bias, down_bias = (vec_ref[i : i + 1, :] for i in range(4))
+    gain, bias, out_bias, down_bias = (vec_ref[i : i + 1, :] for i in range(2, 6))
     middle = (
         x_ref[...].astype(f32) + jnp.dot(attn, wo_ref[...], preferred_element_type=f32) + out_bias
     )
@@ -349,10 +319,25 @@
     for g in range(groups):
         do_ref[g] = attn_all[:, pl.ds(pl.multiple_of(pair_ref[g] * PAIR, PAIR), PAIR)]
 
-
-def feed(pair_of, attn, x, dy, w_out, w_up, w_down, vecs, up_bias, tile=BLK):
+    @pl.when(step == pl.num_programs(0) - 1)
+    def _():
+        shards = grad_ref.shape[0]
+        d_model = x_ref.shape[1]
+        down_rows, up_rows = gd_ref.shape[0] // shards, d_model // shards
+        for j in range(shards):
+            grad_ref[j, :down_rows] = gd_ref[j * down_rows : (j + 1) * down_rows].astype(bf16)
+            rows = slice(j * up_rows, (j + 1) * up_rows)
+            at = down_rows
+            for t in range(0, width, d_model):
+                grad_ref[j, at : at + up_rows] = gu_ref[rows, t : t + d_model].astype(bf16)
+                at += up_rows
+            grad_ref[j, at : at + up_rows] = go_ref[rows].astype(bf16)
+
+
+def feed(pair_of, attn, x, dy, w_out, w_up, w_down, vecs, up_bias, shards, tile=BLK):
     groups, count, _ = attn.shape
     width = x.shape[1]
+    flat = (w_out.size + w_up.size + w_down.size) // shards // width
     rows = pl.BlockSpec((tile, width), lambda i, p: (i, 0))
     heads = pl.BlockSpec((groups, tile, PAIR), lambda i, p: (0, i, 0))
     return pl.pallas_call(
@@ -365,58 +350,26 @@
                 whole(vecs.shape), whole(up_bias.shape),
             ],
             out_specs=[
-                rows, heads, rows, whole(w_down.shape), whole(w_up.shape), whole(w_out.shape),
-                whole(vecs.shape), whole(up_bias.shape),
+                rows, heads, rows, whole((shards, flat, width)), whole(vecs.shape), whole(up_bias.shape),
             ],
-            scratch_shapes=[pltpu.VMEM((tile, width), bf16)],
+            scratch_shapes=[
+                pltpu.VMEM((tile, width), bf16),
+                pltpu.VMEM(w_down.shape, f32),
+                pltpu.VMEM(w_up.shape, f32),
+                pltpu.VMEM(w_out.shape, f32),
+            ],
         ),
         out_shape=[
             jax.ShapeDtypeStruct((count, width), bf16),
             jax.ShapeDtypeStruct((groups, count, PAIR), bf16),
             jax.ShapeDtypeStruct((count, width), f32),
-            jax.ShapeDtypeStruct(w_down.shape, f32),
-            jax.ShapeDtypeStruct(w_up.shape, f32),
-            jax.ShapeDtypeStruct(w_out.shape, f32),
+            jax.ShapeDtypeStruct((shards, flat, width), bf16),
             jax.ShapeDtypeStruct(vecs.shape, f32),
             jax.ShapeDtypeStruct(up_bias.shape, f32),
         ],
         compiler_params=pltpu.CompilerParams(vmem_limit_bytes=60 * 1024 * 1024),
         name="feed",
     )(pair_of, attn, x, dy, w_out, w_up, w_down, vecs, up_bias)
-
-
-def norm_back_kernel(dh_a_ref, dh_b_ref, x_ref, dmid_ref, gain_ref, dx_ref, gvec_ref):
-    @pl.when(pl.program_id(0) == 0)
-    def _():
-        gvec_ref[...] = jnp.zeros_like(gvec_ref)
-
-    d_low = dh_a_ref[...].astype(f32) + dh_b_ref[...].astype(f32)
-    unit, inv = norm_parts(x_ref[...].astype(f32))
-    scaled = d_low * gain_ref[...]
-    dx = dmid_ref[...] + inv * (
-        scaled
-        - jnp.mean(scaled, axis=-1, keepdims=True)
-        - unit * jnp.mean(scaled * unit, axis=-1, keepdims=True)
-    )
-    dx_ref[...] = dx.astype(bf16)
-    gvec_ref[0:1, :] += jnp.sum(d_low * unit, axis=0, keepdims=True)
-    gvec_ref[1:2, :] += jnp.sum(d_low, axis=0, keepdims=True)
-
-
-def norm_back(dh_a, dh_b, x, dmid, gain):
-    count, width = x.shape
-    rows = pl.BlockSpec((BLK, width), lambda i: (i, 0))
-    return pl.pallas_call(
-        norm_back_kernel,
-        grid=(count // BLK,),
-        in_specs=[rows, rows, rows, rows, whole(gain.shape)],
-        out_specs=[rows, whole((8, width))],
-        out_shape=[
-            jax.ShapeDtypeStruct((count, width), bf16),
-            jax.ShapeDtypeStruct((8, width), f32),
-        ],
-        name="norm_back",
-    )(dh_a, dh_b, x, dmid, gain)
 
 
 def layer_norm(values, gain_vec, offset):
@@ -756,6 +709,639 @@
 SIZES = (4, 2, 2, 2)
 
 
+MESH = pl.DeviceIdType.MESH
+
+
+def send(src, dst, sems, recv_sems, index, peer):
+    copy = pltpu.make_async_remote_copy(
+        src_ref=src,
+        dst_ref=dst,
+        send_sem=sems.at[index],
+        recv_sem=recv_sems.at[index],
+        device_id=peer,
+        device_id_type=MESH,
+    )
+    copy.start()
+    return copy
+
+
+def greet(peers, extra, extra_on):
+    barrier = pltpu.get_barrier_semaphore()
+    for peer in peers:
+        pl.semaphore_signal(barrier, inc=1, device_id=peer, device_id_type=MESH)
+
+    @pl.when(extra_on)
+    def _():
+        for peer in extra:
+            pl.semaphore_signal(barrier, inc=1, device_id=peer, device_id_type=MESH)
+
+    pl.semaphore_wait(barrier, len(peers) + jnp.where(extra_on, len(extra), 0))
+
+
+HEAD_CHUNK = 128
+
+
+def head_kernel(
+    x_in_ref, docs_in_ref, order_ref, vec_in_ref, wq_ref, wo_ref, wu_ref, wd_ref,
+    q_ref, k_ref, kt_ref, v_ref, vt_ref, u_ref, own_ref, wh_ref, vec_ref, ub_ref, start_ref, tab_ref,
+    wo_all, wu_all, wd_all,
+    rows, docs, docs_true, vec_all, wo_tmp, wu_tmp, wd_tmp,
+    z_s, z_r, x_s, x_r, c_s, c_r, f_s, f_r, docs_s, docs_r, vec_s, vec_r, wh_s, wh_r, wh_l,
+    y_s, y_r, n_s, n_r, o_s, o_r, load_sem, put_sem, self_sem,
+):
+    z, x, y, c = (lax.axis_index(name) for name in AXES)
+    odd, upper = lax.rem(z, 2), lax.div(z, 2)
+    width = x_in_ref.shape[-1]
+    chunks = rows.shape[1] // HEAD_CHUNK
+    per_turn = chunks // 2
+    by_core, by_x, by_y, by_yc = {"c": 1 - c}, {"x": 1 - x}, {"y": 1 - y}, {"y": 1 - y, "c": 1 - c}
+    home = [{"z": 2 * c + upper, "c": odd}, {"z": 2 * c + 1 - upper, "c": odd}]
+    target = [{"z": 2 * odd + c, "c": upper}, {"z": 2 * (1 - odd) + c, "c": upper}]
+    block = [odd, 1 - odd]
+    stay = (c == upper) & (odd == c)
+    leave = jnp.logical_not(stay)
+    greet([by_core, by_x, by_y, by_yc, home[1], target[1]], [home[0], target[0]], leave)
+
+    def piece(i):
+        turn, row = i // per_turn, (i % per_turn) * HEAD_CHUNK
+        return (
+            x_in_ref.at[block[turn], 0, pl.ds(row, HEAD_CHUNK)],
+            rows.at[0, pl.ds(i * HEAD_CHUNK, HEAD_CHUNK)],
+        )
+
+    for turn in range(2):
+        src, dst = docs_in_ref.at[block[turn]], docs.at[0, turn]
+
+        def start_docs():
+            send(src, dst, docs_s, docs_r, turn, target[turn])
+
+        if turn == 0:
+            pl.when(stay)(lambda: pltpu.make_async_copy(src, dst, self_sem.at[per_turn]).start())
+            pl.when(leave)(start_docs)
+        else:
+            start_docs()
+    for i in range(chunks):
+        src, dst = piece(i)
+        if i < per_turn:
+            pl.when(stay)(lambda: pltpu.make_async_copy(src, dst, self_sem.at[i]).start())
+            pl.when(leave)(lambda: send(src, dst, z_s, z_r, i, target[0]) and None)
+        else:
+            send(src, dst, z_s, z_r, i, target[1])
+
+    def landed(src, dst, sems, recv_sems, index, turn, self_index):
+        def remote():
+            pltpu.make_async_remote_copy(
+                src_ref=src, dst_ref=dst, send_sem=sems.at[index], recv_sem=recv_sems.at[index],
+                device_id=target[turn], device_id_type=MESH,
+            ).wait()
+
+        if turn == 0:
+            pl.when(stay)(lambda: pltpu.make_async_copy(src, dst, self_sem.at[self_index]).wait())
+            pl.when(leave)(remote)
+        else:
+            remote()
+
+    mine = 2 * y + c
+    vec_copy = [
+        send(vec_in_ref, vec_all.at[mine], vec_s, vec_r, i, peer)
+        for i, peer in enumerate((by_core, by_y, by_yc))
+    ]
+    vec_all[mine] = vec_in_ref[...]
+    wh_copy = []
+    shard = wq_ref.shape[0]
+    own_rows = pl.ds(pl.multiple_of(mine * shard, shard), shard)
+    for part in range(3):
+        to = wh_ref.at[own_rows, pl.ds(part * PAIR, PAIR)]
+
+        def columns(core):
+            return wq_ref.at[:, pl.ds(pl.multiple_of(part * width + (2 * x + core) * PAIR, PAIR), PAIR)]
+
+        for i, (peer, core) in enumerate(((by_core, 1 - c), (by_y, c), (by_yc, 1 - c))):
+            wh_copy.append(send(columns(core), to, wh_s, wh_r, 3 * part + i, peer))
+        copy = pltpu.make_async_copy(columns(c), to, wh_l.at[part])
+        copy.start()
+        wh_copy.append(copy)
+
+    up_rows, down_rows = wu_ref.shape[0] // 4, wd_ref.shape[0] // 4
+    parts = [(wo_ref, wo_all, wo_ref.shape[0], 0)]
+    parts += [(wu_ref, wu_all, up_rows, i * up_rows) for i in range(4)]
+    parts += [(wd_ref, wd_all, down_rows, i * down_rows) for i in range(4)]
+
+    def at_owner(full, src, size, offset, owner):
+        return full.at[pl.ds(pl.multiple_of(owner * src.shape[0] + offset, 32), size)]
+
+    other = 2 * (1 - y) + c
+    y_copy = []
+    for i, (src, full, size, offset) in enumerate(parts):
+        y_copy.append(
+            send(src.at[pl.ds(offset, size)], at_owner(full, src, size, offset, mine), y_s, y_r, i, by_y)
+        )
+    n_copy, load_copy, put_copy = [], [], []
+    for i, (src, full, tmp) in enumerate(((wo_ref, wo_all, wo_tmp), (wu_ref, wu_all, wu_tmp), (wd_ref, wd_all, wd_tmp))):
+        n_copy.append(send(src, at_owner(full, src, src.shape[0], 0, mine), n_s, n_r, i, by_core))
+        load_copy.append(pltpu.make_async_copy(src, tmp, load_sem.at[i]))
+        load_copy[-1].start()
+
+    def put(i):
+        src, full, tmp = ((wo_ref, wo_all, wo_tmp), (wu_ref, wu_all, wu_tmp), (wd_ref, wd_all, wd_tmp))[i]
+        load_copy[i].wait()
+        put_copy.append(pltpu.make_async_copy(tmp, at_owner(full, src, src.shape[0], 0, mine), put_sem.at[i]))
+        put_copy[-1].start()
+
+    o_copy = []
+
+    def forward(i):
+        src, full, size, offset = parts[i]
+        y_copy[i].wait()
+        held = at_owner(full, src, size, offset, other)
+        o_copy.append(send(held, held, o_s, o_r, i, by_core))
+
+    blocks = order_ref.shape[0]
+    lane = lax.broadcasted_iota(jnp.int32, (1, 128), 1)
+    slots = jnp.zeros((1, 128), jnp.int32)
+    for t in range(blocks):
+        dc, dx, turn, half = t // 8, t // 4 % 2, t // 2 % 2, t % 2
+        core, side = (1 - c if dc else c), (1 - x if dx else x)
+        stored = 2 * (2 * (2 * core + (1 - upper if turn else upper)) + side) + half
+        slots = jnp.where(lane == order_ref[stored], t, slots)
+
+    docs_copy = {}
+    for turn in range(2):
+        landed(docs_in_ref.at[block[turn]], docs.at[0, turn], docs_s, docs_r, turn, turn, per_turn)
+    docs_copy["x"] = send(docs.at[0], docs.at[1], docs_s, docs_r, 2, by_x)
+    docs_copy["c"] = send(docs.at[0], docs.at[2], docs_s, docs_r, 3, by_core)
+
+    for copy in vec_copy:
+        copy.wait()
+    vec_width = vec_in_ref.shape[1]
+    for j in range(4):
+        for i in range(6):
+            vec_ref[i : i + 1, j * vec_width : (j + 1) * vec_width] = vec_all[j, i : i + 1].astype(f32)
+        for i in range(4):
+            at = (4 * j + i) * vec_width
+            ub_ref[:, at : at + vec_width] = vec_all[j, 6 + i : 7 + i].astype(f32)
+    vec_ref[6:8] = jnp.zeros((2, width), f32)
+    for copy in wh_copy:
+        copy.wait()
+
+    docs_copy["x"].wait()
+    docs_copy["f"] = send(docs.at[1], docs.at[3], docs_s, docs_r, 4, by_core)
+
+    def finish_docs():
+        docs_copy["c"].wait()
+        docs_copy["f"].wait()
+        for g in range(4):
+            core, side = (1 - c if g // 2 else c), (1 - x if g % 2 else x)
+            for turn in range(2):
+                docs_true[2 * (2 * core + (1 - upper if turn else upper)) + side] = docs[g, turn]
+        numbers = docs_true[...]
+        first = jnp.zeros_like(numbers)
+        for d in range(1, blocks):
+            before = jnp.sum((numbers < d).astype(jnp.int32), axis=(0, 1, 2), keepdims=True)
+            first = jnp.where(numbers == d, before, first)
+        docs_true[...] = first
+        low = jnp.zeros((1, 128), jnp.int32)
+        for b in range(blocks):
+            line = docs_true[b // 2]
+            at = 2 * (b % 2)
+            line = jnp.concatenate([line[at : at + 1], line[at + 1 : at + 2]], axis=1)
+            start_ref[b] = line
+            low = jnp.where(lane == b, line[:, :1] // BLK, low)
+        high = jnp.zeros((1, 128), jnp.int32) - 1
+        for b in range(blocks):
+            high = high + (low[:, b : b + 1] <= lane).astype(jnp.int32)
+        tab_ref[...] = jnp.concatenate([low, high, slots, jnp.zeros((5, 128), jnp.int32)], axis=0)
+
+    x_copy, c_copy, f_copy = [], [], []
+
+    def relay(i):
+        src, dst = piece(i)
+        landed(src, dst, z_s, z_r, i, i // per_turn, i)
+        part = pl.ds(i * HEAD_CHUNK, HEAD_CHUNK)
+        x_copy.append(send(rows.at[0, part], rows.at[1, part], x_s, x_r, i, by_x))
+        c_copy.append(send(rows.at[0, part], rows.at[2, part], c_s, c_r, i, by_core))
+
+    def relay_far(i):
+        x_copy[i].wait()
+        part = pl.ds(i * HEAD_CHUNK, HEAD_CHUNK)
+        f_copy.append(send(rows.at[1, part], rows.at[3, part], f_s, f_r, i, by_core))
+
+    def compute(g, i):
+        count = rows.shape[1]
+        unit, _ = norm_parts(rows[g, i * HEAD_CHUNK : (i + 1) * HEAD_CHUNK].astype(f32))
+        at = slice(g * count + i * HEAD_CHUNK, g * count + (i + 1) * HEAD_CHUNK)
+        u_ref[at] = unit.astype(bf16)
+        low = (unit * vec_ref[0:1] + vec_ref[1:2]).astype(bf16)
+        qkv = jnp.dot(low, wh_ref[...], preferred_element_type=f32)
+        q_ref[at] = (qkv[:, :PAIR] * (SCORE_SCALE * LOG2E)).astype(bf16)
+        k = qkv[:, PAIR : 2 * PAIR].astype(bf16)
+        v = qkv[:, 2 * PAIR :].astype(bf16)
+        k_ref[at] = k
+        v_ref[at] = v
+        kt_ref[:, at] = k.T
+        vt_ref[:, at] = v.T
+
+    for i in range(chunks + 2):
+        if i < chunks:
+            relay(i)
+            compute(0, i)
+        if 1 <= i <= chunks:
+            relay_far(i - 1)
+            compute(1, i - 1)
+            c_copy[i - 1].wait()
+            compute(2, i - 1)
+        if i >= 2:
+            f_copy[i - 2].wait()
+            compute(3, i - 2)
+        if i == 1:
+            finish_docs()
+        if 2 <= i < 5:
+            put(i - 2)
+        if i >= 3 and i - 3 < len(parts):
+            forward(i - 3)
+    own_ref[...] = rows[0]
+    for i in range(chunks - 1, len(parts)):
+        forward(i)
+    for copy in n_copy + put_copy + o_copy:
+        copy.wait()
+
+
+def head(x_in, docs_in, order, vec_in, w_qkv, w_out, w_up, w_down):
+    width = x_in.shape[-1]
+    count = 2 * x_in.shape[2]
+    total = 4 * count
+    shard = w_qkv.shape[0]
+    chunks = count // HEAD_CHUNK
+    blocks = order.shape[0]
+    vmem, any_ = pl.BlockSpec(memory_space=pltpu.VMEM), pl.BlockSpec(memory_space=pl.ANY)
+    smem = pl.BlockSpec(memory_space=pltpu.SMEM)
+    dma, buf, shape = pltpu.SemaphoreType.DMA, pltpu.VMEM, jax.ShapeDtypeStruct
+    return pl.pallas_call(
+        head_kernel,
+        in_specs=[any_, vmem, smem, vmem, any_, any_, any_, any_],
+        out_specs=[vmem] * 12 + [any_] * 3,
+        out_shape=[
+            shape((total, PAIR), bf16),
+            shape((total, PAIR), bf16),
+            shape((PAIR, total), bf16),
+            shape((total, PAIR), bf16),
+            shape((PAIR, total), bf16),
+            shape((total, width), bf16),
+            shape((count, width), bf16),
+            shape((width, 3 * PAIR), bf16),
+            shape((8, width), f32),
+            shape((1, 4 * w_down.shape[0]), f32),
+            shape((blocks, 1, BLK), jnp.int32),
+            shape((8, 128), jnp.int32),
+            shape((4 * w_out.shape[0], w_out.shape[1]), bf16),
+            shape((4 * w_up.shape[0], w_up.shape[1]), bf16),
+            shape((4 * w_down.shape[0], w_down.shape[1]), bf16),
+        ],
+        scratch_shapes=[
+            buf((4, count, width), bf16),
+            buf((4, 2) + docs_in.shape[1:], jnp.int32),
+            buf((blocks // 2,) + docs_in.shape[1:], jnp.int32),
+            buf((4,) + vec_in.shape, bf16),
+            buf(w_out.shape, bf16),
+            buf(w_up.shape, bf16),
+            buf(w_down.shape, bf16),
+        ]
+        + [dma((chunks,))] * 8
+        + [dma((5,)), dma((5,)), dma((3,)), dma((3,)), dma((9,)), dma((9,)), dma((3,))]
+        + [dma((9,)), dma((9,)), dma((3,)), dma((3,)), dma((9,)), dma((9,)), dma((3,)), dma((3,))]
+        + [dma((chunks // 2 + 1,))],
+        compiler_params=pltpu.CompilerParams(
+            collective_id=1, has_side_effects=True, vmem_limit_bytes=56 * 1024 * 1024
+        ),
+        name="head",
+    )(x_in, docs_in, order, vec_in, w_qkv, w_out, w_up, w_down)
+TAIL_CHUNK = 128
+PIECES = 3
+
+
+def tail_kernel(
+    dh_ref, x_ref, dmid_ref, gain_ref, keep_ref, from_y_ref, from_x_ref, from_xy_ref, gw_ref, small_ref,
+    dx_ref, gd_ref, gu_ref, go_ref, gq_ref, gvec_ref, gub_ref,
+    core_buf, own_dh, x_out, x_buf, dx_out, home_buf,
+    gsum, gz1s, gz1r, gz2s, gz2r, gfull,
+    wy, ws, wz1s, wz1r, wz2s, wz2r, wfull, wall,
+    small_out, small_in,
+    local_sem, self_sem, core_s, core_r, x_s, x_r, home_s, home_r, g_s, g_r, w_s, w_r, s_s, s_r,
+):
+    z, x, y, c = (lax.axis_index(name) for name in AXES)
+    odd, upper = lax.rem(z, 2), lax.div(z, 2)
+    width = x_ref.shape[1]
+    chunks = x_ref.shape[0] // TAIL_CHUNK
+    per_turn = chunks // 2
+    by_core, by_x, by_y, by_xc = {"c": 1 - c}, {"x": 1 - x}, {"y": 1 - y}, {"x": 1 - x, "c": 1 - c}
+    by_z1, by_z2 = {"z": z + 1 - 2 * odd}, {"z": z + 2 - 4 * upper}
+    home = [{"z": 2 * c + upper, "c": odd}, {"z": 2 * c + 1 - upper, "c": odd}]
+    origin = [{"z": 2 * odd + c, "c": upper}, {"z": 2 * (1 - odd) + c, "c": upper}]
+    stay = (c == upper) & (odd == c)
+    greet(
+        [by_core, by_x, by_y, by_xc, by_z1, by_z2, home[1], origin[1]],
+        [home[0], origin[0]],
+        jnp.logical_not(stay),
+    )
+    small_peers = [by_x, by_core, by_y, by_z1, by_z2]
+    s_copy = [send(small_ref, small_in.at[0], s_s, s_r, 0, small_peers[0])]
+    to_core, locals_ = [], []
+    for i in range(chunks):
+        part = pl.ds(i * TAIL_CHUNK, TAIL_CHUNK)
+        to_core.append(
+            send(dh_ref.at[pl.ds(2, 2), part], core_buf.at[:, part], core_s, core_r, i, by_core)
+        )
+        copy = pltpu.make_async_copy(dh_ref.at[pl.ds(0, 2), part], own_dh.at[:, part], local_sem.at[i])
+        copy.start()
+        locals_.append(copy)
+    w_copy = {}
+    w_copy["y"] = send(gw_ref.at[pl.ds(2 * (1 - y), 2)], wy, w_s, w_r, 0, by_y)
+    g_copy = {}
+
+    def g_start(p):
+        for half in range(2):
+            part = pl.ds(96 * half, 96)
+            gsum[p, part] = (
+                keep_ref[p, part].astype(f32)
+                + from_y_ref[p, part].astype(f32)
+                + from_x_ref[p, part].astype(f32)
+                + from_xy_ref[p, part].astype(f32)
+            )
+        gz1s[p] = gsum[p, pl.ds(pl.multiple_of(96 * (1 - odd), 16), 96)].astype(bf16)
+        g_copy["z1", p] = send(gz1s.at[p], gz1r.at[p], g_s, g_r, 5 * p, by_z1)
+
+    mine_half = pl.multiple_of(96 * odd, 16)
+    mine_quarter = pl.multiple_of(96 * odd + 48 * upper, 16)
+    give_quarter = pl.multiple_of(96 * odd + 48 * (1 - upper), 16)
+
+    def g_second(p):
+        g_copy["z1", p].wait()
+        gsum[p, pl.ds(mine_half, 96)] += gz1r[p].astype(f32)
+        gz2s[p] = gsum[p, pl.ds(give_quarter, 48)].astype(bf16)
+        g_copy["z2", p] = send(gz2s.at[p], gz2r.at[p], g_s, g_r, 5 * p + 1, by_z2)
+
+    def g_third(p):
+        g_copy["z2", p].wait()
+        part = pl.ds(mine_quarter, 48)
+        gfull[p, x, part] = (gsum[p, part] + gz2r[p].astype(f32)).astype(bf16)
+        place_ = gfull.at[p, x, part]
+        g_copy["z2b", p] = send(place_, place_, g_s, g_r, 5 * p + 2, by_z2)
+
+    def g_fourth(p):
+        g_copy["z2b", p].wait()
+        place_ = gfull.at[p, x, pl.ds(mine_half, 96)]
+        g_copy["z1b", p] = send(place_, place_, g_s, g_r, 5 * p + 3, by_z1)
+
+    def g_fifth(p):
+        g_copy["z1b", p].wait()
+        g_copy["x", p] = send(gfull.at[p, x], gfull.at[p, x], g_s, g_r, 5 * p + 4, by_x)
+
+    def w_second():
+        w_copy["y"].wait()
+        for i in range(2):
+            ws[i] = gw_ref[2 * y + i].astype(f32) + wy[i].astype(f32)
+        wz1s[...] = ws[1 - odd].astype(bf16)
+        w_copy["z1"] = send(wz1s, wz1r, w_s, w_r, 1, by_z1)
+
+    def w_third():
+        w_copy["z1"].wait()
+        ws[odd] += wz1r[...].astype(f32)
+        wz2s[...] = ws[odd, pl.ds(pl.multiple_of(64 * (1 - upper), 64), 64)].astype(bf16)
+        w_copy["z2"] = send(wz2s, wz2r, w_s, w_r, 2, by_z2)
+
+    def w_fourth():
+        w_copy["z2"].wait()
+        part = pl.ds(pl.multiple_of(64 * upper, 64), 64)
+        wfull[odd, part] = (ws[odd, part] + wz2r[...].astype(f32)).astype(bf16)
+        place_ = wfull.at[odd, part]
+        w_copy["z2b"] = send(place_, place_, w_s, w_r, 3, by_z2)
+
+    def w_fifth():
+        w_copy["z2b"].wait()
+        w_copy["z1b"] = send(wfull.at[odd], wfull.at[odd], w_s, w_r, 4, by_z1)
+
+    def w_sixth():
+        w_copy["z1b"].wait()
+        mine = 2 * x + c
+        w_copy["core"] = send(wfull.at[1 - c], wall.at[mine], w_s, w_r, 5, by_core)
+        w_copy["x"] = send(wfull.at[c], wall.at[mine], w_s, w_r, 6, by_x)
+        w_copy["xc"] = send(wfull.at[1 - c], wall.at[mine], w_s, w_r, 7, by_xc)
+
+    def s_next(step):
+        s_copy[step].wait()
+        before = small_ref[...] if step == 0 else small_out[step - 1]
+        small_out[step] = before + small_in[step]
+        if step + 1 < len(small_peers):
+            s_copy.append(
+                send(small_out.at[step], small_in.at[step + 1], s_s, s_r, step + 1, small_peers[step + 1])
+            )
+
+    x_copy, home_copy = [], []
+
+    def add_core(i):
+        part = pl.ds(i * TAIL_CHUNK, TAIL_CHUNK)
+        to_core[i].wait()
+        locals_[i].wait()
+        x_out[part] = (own_dh[1, part].astype(f32) + core_buf[1, part].astype(f32)).astype(bf16)
+        x_copy.append(send(x_out.at[part], x_buf.at[part], x_s, x_r, i, by_x))
+
+    def finish(i):
+        part = pl.ds(i * TAIL_CHUNK, TAIL_CHUNK)
+        x_copy[i].wait()
+        d_low = own_dh[0, part].astype(f32) + core_buf[0, part].astype(f32) + x_buf[part].astype(f32)
+        unit, inv = norm_parts(x_ref[part].astype(f32))
+        scaled = d_low * gain_ref[...]
+        dx = dmid_ref[part] + inv * (
+            scaled
+            - jnp.mean(scaled, axis=-1, keepdims=True)
+            - unit * jnp.mean(scaled * unit, axis=-1, keepdims=True)
+        )
+        dx_out[part] = dx.astype(bf16)
+        turn, row = i // per_turn, (i % per_turn) * TAIL_CHUNK
+        target = home_buf.at[upper, pl.ds(row, TAIL_CHUNK)]
+        if turn == 0:
+            @pl.when(stay)
+            def _():
+                pltpu.make_async_copy(dx_out.at[part], target, self_sem.at[i]).start()
+
+            @pl.when(jnp.logical_not(stay))
+            def _():
+                send(dx_out.at[part], target, home_s, home_r, i, home[0])
+        else:
+            send(dx_out.at[part], target, home_s, home_r, i, home[1])
+
+    def arrive(i):
+        part = pl.ds(i * TAIL_CHUNK, TAIL_CHUNK)
+        turn, row = i // per_turn, (i % per_turn) * TAIL_CHUNK
+        block = odd if turn == 0 else 1 - odd
+        landed = home_buf.at[block, pl.ds(row, TAIL_CHUNK)]
+
+        def remote():
+            copy = pltpu.make_async_remote_copy(
+                src_ref=dx_out.at[part], dst_ref=landed, send_sem=home_s.at[i], recv_sem=home_r.at[i],
+                device_id=home[turn], device_id_type=MESH,
+            )
+            copy.wait_send()
+            copy.wait_recv()
+
+        if turn == 0:
+            @pl.when(stay)
+            def _():
+                pltpu.make_async_copy(dx_out.at[part], landed, self_sem.at[i]).wait()
+
+            pl.when(jnp.logical_not(stay))(remote)
+        else:
+            remote()
+        dx_ref[block, pl.ds(row, TAIL_CHUNK)] = home_buf[block, pl.ds(row, TAIL_CHUNK)].astype(f32)
+
+    g_start(0)
+    add_core(0)
+    g_start(1)
+    add_core(1)
+    g_start(2)
+    add_core(2)
+    s_next(0)
+    s_next(1)
+    g_second(0)
+    w_second()
+    g_second(1)
+    g_second(2)
+    finish(0)
+    add_core(3)
+    s_next(2)
+    g_third(0)
+    finish(1)
+    add_core(4)
+    w_third()
+    g_third(1)
+    g_third(2)
+    s_next(3)
+    finish(2)
+    add_core(5)
+    g_fourth(0)
+    w_fourth()
+    finish(3)
+    add_core(6)
+    s_next(4)
+    g_fourth(1)
+    g_fourth(2)
+    w_fifth()
+    finish(4)
+    add_core(7)
+    g_fifth(0)
+    finish(5)
+    w_sixth()
+    g_fifth(1)
+    finish(6)
+    g_fifth(2)
+    finish(7)
+    w_copy["core"].wait()
+    w_copy["x"].wait()
+    w_copy["xc"].wait()
+    wall[2 * x + c] = wfull[c]
+    for pair in range(4):
+        for part in range(3):
+            gq_ref[:, part * width + pair * PAIR : part * width + (pair + 1) * PAIR] = wall[
+                pair, :, part * PAIR : (part + 1) * PAIR
+            ].astype(f32)
+    shard = go_ref.shape[0]
+    lanes = pl.ds(pl.multiple_of(shard * (2 * y + c), shard), shard)
+    for i in range(6):
+        gvec_ref[i : i + 1, :] = small_out[4, i : i + 1, lanes]
+    gub_ref[...] = small_out[4, pl.ds(6 + 2 * y + c, 1), :]
+    for i in range(chunks):
+        arrive(i)
+    for p in range(PIECES):
+        g_copy["x", p].wait()
+    flat = gd_ref.shape[0] + (gu_ref.shape[1] // width + 1) * shard
+    for row in range(0, flat, 64):
+        p, rest = divmod(row, flat // PIECES)
+        side, inner = divmod(rest, flat // PIECES // 2)
+        value = gfull[p, side, inner : inner + 64].astype(f32)
+        if row < gd_ref.shape[0]:
+            gd_ref[row : row + 64] = value
+        elif row < flat - shard:
+            t, r = divmod(row - gd_ref.shape[0], shard)
+            gu_ref[r : r + 64, t * width : (t + 1) * width] = value
+        else:
+            r = row - (flat - shard)
+            go_ref[r : r + 64] = value
+
+
+def tail(dh, x, dmid, gain, keep, from_y, from_x, from_xy, gw, small, ff_shard):
+    count, width = x.shape
+    shard = gw.shape[1]
+    half = count // 2
+    chunks = count // TAIL_CHUNK
+    sixth = keep.shape[1]
+    vmem = pl.BlockSpec(memory_space=pltpu.VMEM)
+    dma = pltpu.SemaphoreType.DMA
+    buf = pltpu.VMEM
+    return pl.pallas_call(
+        tail_kernel,
+        in_specs=[pl.BlockSpec(memory_space=pl.ANY)] + [vmem] * 9,
+        out_specs=[vmem] * 7,
+        out_shape=[
+            jax.ShapeDtypeStruct((2, half, width), f32),
+            jax.ShapeDtypeStruct((ff_shard, width), f32),
+            jax.ShapeDtypeStruct((shard, 4 * ff_shard), f32),
+            jax.ShapeDtypeStruct((shard, width), f32),
+            jax.ShapeDtypeStruct((shard, 3 * width), f32),
+            jax.ShapeDtypeStruct((8, shard), f32),
+            jax.ShapeDtypeStruct((1, ff_shard), f32),
+        ],
+        scratch_shapes=[
+            buf((2, count, width), bf16),
+            buf((2, count, width), bf16),
+            buf((count, width), bf16),
+            buf((count, width), bf16),
+            buf((count, width), bf16),
+            buf((2, half, width), bf16),
+            buf((PIECES, sixth, width), f32),
+            buf((PIECES, sixth // 2, width), bf16),
+            buf((PIECES, sixth // 2, width), bf16),
+            buf((PIECES, sixth // 4, width), bf16),
+            buf((PIECES, sixth // 4, width), bf16),
+            buf((PIECES, 2, sixth, width), bf16),
+            buf((2, shard, 3 * PAIR), bf16),
+            buf((2, shard, 3 * PAIR), f32),
+            buf((shard, 3 * PAIR), bf16),
+            buf((shard, 3 * PAIR), bf16),
+            buf((shard // 2, 3 * PAIR), bf16),
+            buf((shard // 2, 3 * PAIR), bf16),
+            buf((2, shard, 3 * PAIR), bf16),
+            buf((4, shard, 3 * PAIR), bf16),
+            buf((5,) + small.shape, f32),
+            buf((5,) + small.shape, f32),
+            dma((chunks,)),
+            dma((chunks // 2,)),
+            dma((chunks,)),
+            dma((chunks,)),
+            dma((chunks,)),
+            dma((chunks,)),
+            dma((chunks,)),
+            dma((chunks,)),
+            dma((5 * PIECES,)),
+            dma((5 * PIECES,)),
+            dma((8,)),
+            dma((8,)),
+            dma((5,)),
+            dma((5,)),
+        ],
+        compiler_params=pltpu.CompilerParams(
+            collective_id=5, has_side_effects=True, vmem_limit_bytes=56 * 1024 * 1024
+        ),
+        name="tail",
+    )(dh, x, dmid, gain, keep, from_y, from_x, from_xy, gw, small)
+def stack_rows(members, width, count):
+    at, total = 0, 0
+    for member in members:
+        rows = member.reshape(-1, width)
+        total = total + jnp.pad(rows, ((at, count - at - rows.shape[0]), (0, 0)))
+        at += rows.shape[0]
+    return total
+
+
 def place(z, x, y, c):
     return ((z * SIZES[1] + x) * SIZES[2] + y) * SIZES[3] + c
 
@@ -808,111 +1394,57 @@
     norm1_gain, norm1_bias, norm2_gain, norm2_bias, out_bias, up_bias, down_bias,
 ):
     z, x, y, c = (lax.axis_index(name) for name in AXES)
-    odd, upper = z % 2, z // 2
+    odd = z % 2
     rows, width = inputs.shape[2], inputs.shape[3]
-    blocks = block_order.shape[0]
-    seq_len = blocks * BLK
     shard = norm1_gain.shape[0]
-
-    x_piece = to_pair(inputs, odd)
-    def head_columns(pair):
-        parts = [
-            lax.dynamic_slice_in_dim(w_qkv, part * width + pair * PAIR, PAIR, axis=1) for part in range(3)
-        ]
-        return jnp.concatenate(parts, axis=1)
-
-    head_mine, head_other = head_columns(2 * x + c), head_columns(2 * x + 1 - c)
-    from_core = swap(head_other, dc=1)
-    from_y = swap(head_mine, dy=1)
-    from_both = swap(head_other, dy=1, dc=1)
-    low_half = jnp.where(c == 0, jnp.stack([head_mine, from_core]), jnp.stack([from_core, head_mine]))
-    high_half = jnp.where(c == 0, jnp.stack([from_y, from_both]), jnp.stack([from_both, from_y]))
-    w_heads = jnp.where(
-        y == 0, jnp.stack([low_half, high_half]), jnp.stack([high_half, low_half])
-    ).reshape(width, 3 * PAIR)
-
-    vectors = jnp.concatenate(
-        [norm1_gain, norm1_bias, norm2_gain, norm2_bias, out_bias, down_bias, up_bias]
-    ).reshape(-1, shard)
-    vectors = lax.all_gather(vectors, ("y", "c")).astype(f32)
-    gain_one, bias_one, gain_two, bias_two, full_obias, full_dbias = (
-        vectors[:, i].reshape(1, width) for i in range(6)
-    )
-    full_ubias = vectors[:, 6:].reshape(1, -1)
-
-    docs = lax.all_gather(segment_ids[:, 0], ("z", "x", "c"))
-    docs = lax.dynamic_index_in_dim(docs.reshape(-1, 2, 2, rows), odd, 1, keepdims=False)
-    docs = lax.dynamic_index_in_dim(docs, upper, 1, keepdims=False).reshape(seq_len)
-    ids = jnp.arange(blocks, dtype=jnp.int32)
-    before = jnp.sum((docs[None, :] < ids[:, None]).astype(jnp.int32), axis=1)
-    start = jnp.sum(jnp.where(docs[None, :] == ids[:, None], before[:, None], 0), axis=0)
-    low_of = start[::BLK] // BLK
-    high_of = jnp.sum((low_of[None, :] <= ids[:, None]).astype(jnp.int32), axis=1) - 1
-    start = start.reshape(blocks, 1, BLK)
-
-    slot = jnp.arange(blocks, dtype=jnp.int32)
-    group, turn, half = slot // 4, slot // 2 % 2, slot % 2
-    stored = 2 * (2 * (2 * (c ^ (group % 2)) + (upper ^ turn)) + (x ^ (group // 2))) + half
-    true_of = jnp.sum(jnp.where(stored[:, None] == ids[None, :], block_order[None, :], 0), axis=1)
-    slot_of = jnp.sum(jnp.where(true_of[None, :] == ids[:, None], slot[None, :], 0), axis=1)
+    vectors = stack_rows(
+        [norm1_gain, norm1_bias, norm2_gain, norm2_bias, out_bias, down_bias, up_bias], shard, 16
+    )
+    (
+        q, k, kt, v, vt, unit, own_x, w_heads, vecs, full_ubias, start, tab, full_out, full_up, full_down
+    ) = head(
+        inputs, segment_ids.reshape(2, -1, 128), block_order, vectors, w_qkv, w_out, w_up, w_down
+    )
+    gain_one, bias_one = vecs[0:1], vecs[1:2]
     groups = jnp.arange(4, dtype=jnp.int32)
-    pair_of = 2 * (x ^ (groups // 2)) + (c ^ (groups % 2))
-
-    across = [swap(piece, dx=1) for piece in x_piece]
-    beside = [swap(jnp.stack([own, far]), dc=1) for own, far in zip(x_piece, across)]
-    x_rows = jnp.stack([
-        *x_piece, beside[0][0], beside[1][0], *across, beside[0][1], beside[1][1]
-    ]).reshape(seq_len, width)
-
-    q, k, kt, v, vt, h = project(true_of, x_rows, gain_one, bias_one, w_heads)
+    pair_of = 2 * (x ^ (groups % 2)) + (c ^ (groups // 2))
+
     dy_piece = to_pair(out_grad, odd)
-    o, ot, lse = attend(slot_of, low_of, q, start, k, vt)
+    o, ot, lse = attend(tab, q, start, k, vt)
     o = o.reshape(4, -1, PAIR)
-    attn = jnp.stack([o[0], swap(o[1], dc=1), swap(o[2], dx=1), swap(o[3], dx=1, dc=1)])
-
-    full_out, full_up, full_down = (
-        lax.all_gather(member, ("y", "c"), axis=0, tiled=True) for member in (w_out, w_up, w_down)
-    )
-    vecs = jnp.concatenate([full_obias, gain_two, bias_two, full_dbias], axis=0)
-    own_x = jnp.concatenate(x_piece, axis=0)
+    attn = jnp.stack([o[0], swap(o[1], dx=1), swap(o[2], dc=1), swap(o[3], dx=1, dc=1)])
+
     own_dy = jnp.concatenate(dy_piece, axis=0)
-    result, d_o, d_middle, g_down, g_up, g_out, g_vecs, g_ubias = feed(
-        pair_of, attn, own_x, own_dy, full_out, full_up, full_down, vecs, full_ubias
+    result, d_o, d_middle, g_flat, g_vecs, g_ubias = feed(
+        pair_of, attn, own_x, own_dy, full_out, full_up, full_down, vecs, full_ubias, 4
     )
     outputs = from_pair(result.reshape(2, rows, width), odd)
 
-    def reduce_rows(value):
-        part = lax.psum_scatter(value.astype(bf16), ("y", "c"), scatter_dimension=0, tiled=True)
-        return lax.psum(part, ("z", "x")).astype(f32)
-
-    d_o = jnp.concatenate([d_o[0], swap(d_o[1], dc=1), swap(d_o[2], dx=1), swap(d_o[3], dx=1, dc=1)])
-    grad_out, grad_up, grad_down = reduce_rows(g_out), reduce_rows(g_up), reduce_rows(g_down)
-    dh, g_heads = attend_back(slot_of, high_of, k, kt, v, h, w_heads, q, start, d_o, ot, lse)
-    dh = dh.reshape(4, -1, width)
-    other = swap(jnp.stack([dh[1], dh[3]]), dc=1)
-    far = swap((dh[2].astype(f32) + other[1].astype(f32)).astype(bf16), dx=1)
-    near = (dh[0].astype(f32) + other[0].astype(f32)).astype(bf16)
-    dx, g_norm = norm_back(near, far, own_x, d_middle, gain_one)
-    input_grad = from_pair(dx.reshape(2, rows, width), odd).astype(f32)
-
-    g_heads = lax.psum_scatter(g_heads.astype(bf16), "y", scatter_dimension=0, tiled=True)
-    g_heads = lax.psum(g_heads, "z")
-    g_heads = lax.all_gather(g_heads, ("x", "c"))
-    g_heads = lax.dynamic_slice_in_dim(g_heads, c * shard, shard, axis=1)
-    grad_qkv = g_heads.reshape(4, shard, 3, PAIR).transpose(1, 2, 0, 3).reshape(shard, -1).astype(f32)
-
-    small = jnp.concatenate([
-        g_norm[0], g_norm[1], g_vecs[1], g_vecs[2], g_vecs[0], g_vecs[3], g_ubias[0]
-    ])
-    small = lax.psum(small, AXES)
-    index = 2 * y + c
-    owned = [
-        lax.dynamic_slice_in_dim(small, i * width + index * shard, shard) for i in range(6)
-    ]
-    owned_up = lax.dynamic_slice_in_dim(small, 6 * width + index * 4 * shard, 4 * shard)
+    d_o = jnp.concatenate([d_o[0], swap(d_o[1], dx=1), swap(d_o[2], dc=1), swap(d_o[3], dx=1, dc=1)])
+    g_flat = g_flat.reshape((2, 2) + g_flat.shape[1:])
+    given = lax.dynamic_index_in_dim(g_flat, 1 - c, 1, keepdims=False)
+    kept = lax.dynamic_index_in_dim(g_flat, c, 1, keepdims=False)
+    flat = (kept.astype(f32) + swap(given, dc=1).astype(f32)).astype(bf16)
+    flat = flat.reshape(2, PIECES, 2, -1, width)
+
+    def quarter(dy, dx):
+        part = lax.dynamic_index_in_dim(flat, y ^ dy, 0, keepdims=False)
+        return lax.dynamic_index_in_dim(part, x ^ dx, 1, keepdims=False)
+
+    from_y, from_x, from_xy = (
+        swap(quarter(1, 0), dy=1), swap(quarter(0, 1), dx=1), swap(quarter(1, 1), dy=1, dx=1)
+    )
+    dh, g_heads, g_norm = attend_back(
+        tab, k, kt, v, unit, w_heads, q, start, d_o, ot, lse, gain_one, bias_one, 4
+    )
+    small = stack_rows([g_norm, g_vecs[1:3], g_vecs[0:1], g_vecs[3:4], g_ubias], width, 16)
+    dx, grad_down, grad_up, grad_out, grad_qkv, g_vec, g_ub = tail(
+        dh.reshape(4, -1, width), own_x, d_middle, gain_one, quarter(0, 0), from_y, from_x, from_xy,
+        g_heads, small, w_down.shape[0],
+    )
     return (
-        outputs, input_grad, grad_qkv, grad_out, grad_up, grad_down,
-        owned[0], owned[1], owned[2], owned[3], owned[4], owned_up, owned[5],
+        outputs, dx[:, None], grad_qkv, grad_out, grad_up, grad_down,
+        g_vec[0], g_vec[1], g_vec[2], g_vec[3], g_vec[4], g_ub[0], g_vec[5],
     )
 
 

time: 491 us -> 315 us (0.64)
  waiting for transfers between devices: 166 us -> 11.9 us
  Pallas kernels: 127 us -> 239 us
  blocking collectives: 85.6 us -> 0 us
  other arithmetic: 36.8 us -> 13.8 us
  between operations: 14.6 us -> 0.85 us
  starting transfers between devices: 33.3 us -> 19.7 us
    pallas_call x2, Pallas kernels: 20.6 us -> 132 us  [the longest x1 68.2 us: head(): pl.pallas_call(head_kernel, in_specs=[any_, vmem, smem, vmem, any_, any_,...]
    reduce_scatter x4 -> x0, waiting for transfers between devices: 77.8 us -> none  [the longest x3 63.1 us: reduce_rows(): lax.psum_scatter(value.astype(bf16), ('y', 'c'), scatter_dimension=0, til...]
    all_gather x4 -> x0, blocking collectives: 44.7 us -> none  [the longest x1 20.9 us: paired_body(): docs = lax.all_gather(segment_ids[:, 0], ('z', 'x', 'c'))]
    psum x2 -> x0, waiting for transfers between devices: 42.1 us -> none  [the longest x1 42.1 us: reduce_rows(): return lax.psum(part, ('z', 'x')).astype(f32)]
    psum x1 -> x0, blocking collectives: 40.9 us -> none  [paired_body(): small = lax.psum(small, AXES)]
    ppermute x23 -> x14, waiting for transfers between devices: 44.9 us -> 11.9 us  [move(): return lax.ppermute(value, AXES, pairs)]
    convert_element_type x11 -> x1, other arithmetic: 21.3 us -> 2.33 us  [paired_body(): flat = (kept.astype(f32) + swap(given, dc=1).astype(f32)).astype(bf16)]
    ppermute x23 -> x14, starting transfers between devices: 33 us -> 19.7 us  [move(): return lax.ppermute(value, AXES, pairs)]
  transfers between devices with their start and end apart: 31 -> 14, of which waited for: 10 -> 2; matrix products, arithmetic and copies ran while one was open for 10% -> 7% of each run, Pallas kernels for 11% -> 47%
where the time goes in v2:
time: 315 us; the launch traced here: 310 us
  Pallas kernels  239 us (76%)
  local copies, waits for them, and re-layouts  24.9 us (8%)
  starting transfers between devices  19.7 us (6%)
  other arithmetic  13.8 us (4%)
  waiting for transfers between devices  11.9 us (4%)
    pallas_call x1, Pallas kernels, head(): pl.pallas_call(head_kernel, in_specs=[any_, vmem, smem, vmem, any_, any_,...  68.2 us
    pallas_call x1, Pallas kernels, tail(): pl.pallas_call(tail_kernel, in_specs=[pl.BlockSpec(memory_space=pl.ANY)]...  63.7 us
    pallas_call x1, Pallas kernels, attend_back(): pl.pallas_call(attend_back_kernel, grid_spec=pltpu.PrefetchScalarGridSpec...  44.4 us
    pallas_call x1, Pallas kernels, attend(): pl.pallas_call(attend_kernel, grid_spec=pltpu.PrefetchScalarGridSpec(num_...  34.3 us
    pallas_call x1, Pallas kernels, feed(): pl.pallas_call(feed_kernel, grid_spec=pltpu.PrefetchScalarGridSpec(num_sc...  28.1 us
    ppermute x14, starting transfers between devices, move(): return lax.ppermute(value, AXES, pairs)  19.7 us
    ppermute x14, waiting for transfers between devices, move(): return lax.ppermute(value, AXES, pairs)  11.9 us
    unnamed x30, local copies, waits for them, and re-layouts  8.49 us
  transfers between devices with their start and end apart: 14, of which 2 were waited for; matrix products, arithmetic and copies ran while one was open for 7% of the time, Pallas kernels for 47%

profile of v2, /device:TPU:0, one launch (start us, length us, event | category | flops | bytes accessed | tf_op | source)
XLA Modules:
  0.0 309.7 jit_solution(12218270106572101635)
XLA Ops:
  0.7 1.3 dynamic-slice_bitcast_fusion.6
  2.6 5.3 %collective-permute-start.4 = (bf16[512,512]{1,0:T(8,128)(2,1)S(1)}, bf16[512,512]{1,0:T(8,128)(2,1)S(1)}, u32[]{:S(2)}, u32[]{:S(2)}) collective-permute-start(bf16[512,512]{1,0:T(8,128)(2,1)S(1)} %get-tuple-element.120), channel_id=1, source_target_pairs={{0,16},{1,24},{2,18},{3,26},{4,20},{5,28},{6,22},{7,30},{8,0},{9,8... | collective-permute-start | bytes 1572872 | tf_op jit(solution)/shard_map/ppermute | solution.py:1371
  8.0 1.4 pad_add_fusion.1.vec_in_ref
  9.3 68.2 %head.1 = (bf16[4096,128]{1,0:T(8,128)(2,1)}, bf16[4096,128]{1,0:T(8,128)(2,1)}, bf16[128,4096]{1,0:T(8,128)(2,1)}, bf16[4096,128]{1,0:T(8,128)(2,1)}, bf16[128,...) custom-call(bf16[2,1,512,512]{3,2,1,0:T(8,128)(2,1)} %x_in_ref.1, ...), custom_call_target="tpu_custom_call" | custom-call | tf_op jit(solution)/shard_map/head/pallas_call | solution.py:979
  77.6 34.3 %attend.1 = (bf16[4096,128]{1,0:T(8,128)(2,1)}, f32[16,128,256]{2,1,0:T(8,128)}, f32[16,1,512]{2,1,0:T(1,128)}) custom-call(s32[8,128]{1,0:T(8,128)} %get-tuple-element.47.tab_ref, bf16[4096,128]{1,0:T(8,128)(2,1)} %get-tuple-element.48.q_ref, s32[16,1,256]{2,1,0:T(1,128)} %get-tuple-element.49.start_ref, bf16[4096,128]{1,0:T(8,128)(2,1)} %get-tuple-element.50.k_ref, ...), custom_call_target="tpu_custom_call" | custom-call | tf_op jit(solution)/shard_map/attend/pallas_call | solution.py:95
  111.8 2.0 slice_bitcast_fusion.4
  114.9 1.0 collective-permute-start
  116.5 5.6 %collective-permute-done.2 = bf16[1024,128]{1,0:T(8,128)(2,1)S(1)} collective-permute-done((bf16[1024,128]{1,0:T(8,128)(2,1)S(1)}, bf16[1024,128]{1,0:T(8,128)(2,1)S(1)}, u32[]{:S(2)}, u32[]{:S(2)}) %collective-permute-start.2) | collective-permute-done | bytes 262176 | tf_op jit(solution)/shard_map/ppermute | solution.py:1371
  122.1 6.2 %collective-permute-done = bf16[1024,128]{1,0:T(8,128)(2,1)} collective-permute-done((bf16[1024,128]{1,0:T(8,128)(2,1)S(1)}, bf16[1024,128]{1,0:T(8,128)(2,1)}, u32[]{:S(2)}, u32[]{:S(2)}) %collective-permute-start) | collective-permute-done | bytes 262176 | tf_op jit(solution)/shard_map/ppermute | solution.py:1371
  128.3 2.1 pad_maximum_fusion.attn_ref
  130.3 1.0 pad_maximum_fusion.1.dy_ref
  131.4 28.1 %feed.1 = (bf16[1024,512]{1,0:T(8,128)(2,1)}, bf16[4,1024,128]{2,1,0:T(8,128)(2,1)}, f32[1024,512]{1,0:T(8,128)}, bf16[4,1152,512]{2,1,0:T(8,128)(2,1)}, f32[8,512]{1,0:T(8,128)}, /*index=5*/f32[1,2048]{1,0:T(1,128)}) custom-call(s32[4]{0:T(128)} %fusion.3.pair_ref, bf16[4,1024,128]{2,1,0:T(8,128)(2,1)} %pad_maximum_fusion.attn_ref, ...), custom_call_target="tpu_custom_call" | custom-call | tf_op jit(solution)/shard_map/feed/pallas_call | solution.py:343
  159.5 3.2 %dynamic-slice_bitcast_fusion = bf16[2,1152,512]{2,1,0:T(8,128)(2,1)} fusion(bf16[2,2,1152,512]{3,2,1,0:T(8,128)(2,1)} %bitcast.72, s32[]{:T(128)S(6)} %select_n.79), kind=kLoop, calls=%fused_computation.2 | loop fusion | bytes 4718596 | tf_op jit(solution)/shard_map/jit(dynamic_index_in_dim)/squeeze | solution.py:1425
  162.7 1.4 fusion.7
  165.9 2.2 slice_bitcast_fusion.3
  168.0 1.0 collective-permute-start.7
  169.2 1.0 collective-permute-start.9
  171.4 1.0 fusion.5
  172.4 5.3 %collective-permute-start.5 = (bf16[512,512]{1,0:T(8,128)(2,1)}, bf16[512,512]{1,0:T(8,128)(2,1)}, u32[]{:S(2)}, u32[]{:S(2)}) collective-permute-start(bf16[512,512]{1,0:T(8,128)(2,1)} %get-tuple-element.117), channel_id=1, source_target_pairs={{0,0},{8,1},{2,2},{10,3},{4,4},{12,5},{6,6},{14,7},{16,8},{24,9},{... | collective-permute-start | bytes 1572872 | tf_op jit(solution)/shard_map/ppermute | solution.py:1371
  178.9 2.3 fusion
  181.2 1.1 dynamic-slice_bitcast_fusion.1
  182.3 1.0 collective-permute-start.11
  184.3 1.5 collective-permute-start.13
  185.8 2.1 pad_maximum_fusion.2.do_ref
  188.0 44.4 %attend_back.1 = (bf16[4096,512]{1,0:T(8,128)(2,1)}, bf16[4,128,384]{2,1,0:T(8,128)(2,1)}, f32[2,512]{1,0:T(2,128)}) custom-call(s32[8,128]{1,0:T(8,128)} %get-tuple-element.47.tab_ref, bf16[4096,128]{1,0:T(8,128)(2,1)} %get-tuple-element.50.k_ref, bf16[128,4096]{1,0:T(8,128)(2,1)} %get-tuple-element.60.kt_ref, bf16[4096,128]{1,0:T(8,128)(2,1)} %get-tuple-element.61.v_ref, ...), custom_call_target="tpu_custom_call" | custom-call | tf_op jit(solution)/shard_map/attend_back/pallas_call | solution.py:218
  232.3 1.3 pad_add_fusion.small_ref
  233.7 1.3 select_bitcast_fusion.1
  234.9 1.1 maximum_bitcast_fusion
  237.2 63.7 %tail.1 = (f32[2,512,512]{2,1,0:T(8,128)}, f32[512,512]{1,0:T(8,128)}, f32[128,2048]{1,0:T(8,128)}, f32[128,512]{1,0:T(8,128)}, f32[128,1536]{1,0:T(8,128)}, /*index=5*/f32[8,128]{1,0:T(8,128)}, f32[1,512]{1,0:T(1,128)}) custom-call(bf16[4,1024,512]{2,1,0:T(8,128)(2,1)} %bitcast.74, bf16[1024,512]{1,0:T(8,128)(2,1)} %get-tuple-element.53.x_ref, ...), custom_call_target="tpu_custom_call" | custom-call | tf_op jit(solution)/shard_map/tail/pallas_call | solution.py:1280
  300.9 1.4 slice_bitcast_fusion.6
  302.4 3.2 %copy.42 = f32[2,1,512,512]{3,2,1,0:T(8,128)} copy(f32[2,1,512,512]{3,2,1,0:T(8,128)} %bitcast.75) | data formatting | bytes 4194304
  307.1 1.0 copy.45
  (55 shorter events, 11.8 us)
Async XLA Ops:
  1.9 128.4 %collective-permute-start.3 = (bf16[512,512]{1,0:T(8,128)(2,1)S(1)}, bf16[512,512]{1,0:T(8,128)(2,1)S(1)}, u32[]{:S(2)}, u32[]{:S(2)}) collective-permute-start(bf16[512,512]{1,0:T(8,128)(2,1)S(1)} %get-tuple-element.119), channel_id=1, source_target_pairs={{0,0},{1,8},{2,2},{3,10},{4,4},{5,12},{6,6},{7,14},{8,16},{9,24},{... | collective-permute-start | bytes 1572872 | tf_op jit(solution)/shard_map/ppermute | solution.py:1371
  2.6 127.7 %collective-permute-start.4 = (bf16[512,512]{1,0:T(8,128)(2,1)S(1)}, bf16[512,512]{1,0:T(8,128)(2,1)S(1)}, u32[]{:S(2)}, u32[]{:S(2)}) collective-permute-start(bf16[512,512]{1,0:T(8,128)(2,1)S(1)} %get-tuple-element.120), channel_id=1, source_target_pairs={{0,16},{1,24},{2,18},{3,26},{4,20},{5,28},{6,22},{7,30},{8,0},{9,8... | collective-permute-start | bytes 1572872 | tf_op jit(solution)/shard_map/ppermute | solution.py:1371
  113.8 2.7 collective-permute-start.1
  113.9 8.1 %collective-permute-start.2 = (bf16[1024,128]{1,0:T(8,128)(2,1)S(1)}, bf16[1024,128]{1,0:T(8,128)(2,1)S(1)}, u32[]{:S(2)}, u32[]{:S(2)}) collective-permute-start(bf16[1024,128]{1,0:T(8,128)(2,1)S(1)} %get-tuple-element.122), channel_id=1, source_target_pairs={{0,5},{1,4},{2,7},{3,6},{4,1},{5,0},{6,3},{7,2},{8,13},{9,12},{10,... | collective-permute-start | bytes 786440 | tf_op jit(solution)/shard_map/ppermute | solution.py:1371
  114.9 13.4 %collective-permute-start = (bf16[1024,128]{1,0:T(8,128)(2,1)S(1)}, bf16[1024,128]{1,0:T(8,128)(2,1)}, u32[]{:S(2)}, u32[]{:S(2)}) collective-permute-start(bf16[1024,128]{1,0:T(8,128)(2,1)S(1)} %get-tuple-element.124), channel_id=1, source_target_pairs={{0,4},{1,5},{2,6},{3,7},{4,0},{5,1},{6,2},{7,3},{8,12},{9,13},{10,... | collective-permute-start | bytes 786440 | tf_op jit(solution)/shard_map/ppermute | solution.py:1371
  162.7 8.0 %copy-start.9 = (f32[1,2048]{1,0:T(1,128)S(1)}, f32[1,2048]{1,0:T(1,128)}, u32[]{:S(2)}) copy-start(f32[1,2048]{1,0:T(1,128)} %get-tuple-element.73) | copy-start | bytes 24580
  162.7 8.7 %copy-start.10 = (f32[8,512]{1,0:T(8,128)S(1)}, f32[8,512]{1,0:T(8,128)}, u32[]{:S(2)}) copy-start(f32[8,512]{1,0:T(8,128)} %get-tuple-element.72) | copy-start | bytes 49156
  162.7 8.7 %copy-start = (bf16[1024,512]{1,0:T(8,128)(2,1)S(1)}, bf16[1024,512]{1,0:T(8,128)(2,1)}, u32[]{:S(2)}) copy-start(bf16[1024,512]{1,0:T(8,128)(2,1)} %get-tuple-element.59) | copy-start | bytes 3145732
  162.7 15.6 %collective-permute-start.10 = (bf16[2,1152,512]{2,1,0:T(8,128)(2,1)}, bf16[2,1152,512]{2,1,0:T(8,128)(2,1)S(1)}, u32[]{:S(2)}, u32[]{:S(2)}) collective-permute-start(bf16[2,1152,512]{2,1,0:T(8,128)(2,1)} %dynamic-slice_bitcast_fusion), channel_id=1, source_target_pairs={{0,1},{1,0},{2,3},{3,2},{4,5},{5,4},{6,7},{7,6},{8,9},{9,8},{10,11... | collective-permute-start | bytes 7077896 | tf_op jit(solution)/shard_map/ppermute | solution.py:1371
  168.0 14.3 %collective-permute-start.7 = (bf16[1024,128]{1,0:T(8,128)(2,1)}, bf16[1024,128]{1,0:T(8,128)(2,1)}, u32[]{:S(2)}, u32[]{:S(2)}) collective-permute-start(bf16[1024,128]{1,0:T(8,128)(2,1)} %get-tuple-element.114), channel_id=1, source_target_pairs={{0,4},{1,5},{2,6},{3,7},{4,0},{5,1},{6,2},{7,3},{8,12},{9,13},{10,... | collective-permute-start | bytes 786440 | tf_op jit(solution)/shard_map/ppermute | solution.py:1371
  169.0 14.3 %collective-permute-start.8 = (bf16[1024,128]{1,0:T(8,128)(2,1)}, bf16[1024,128]{1,0:T(8,128)(2,1)}, u32[]{:S(2)}, u32[]{:S(2)}) collective-permute-start(bf16[1024,128]{1,0:T(8,128)(2,1)} %get-tuple-element.113), channel_id=1, source_target_pairs={{0,1},{1,0},{2,3},{3,2},{4,5},{5,4},{6,7},{7,6},{8,9},{9,8},{10,11... | collective-permute-start | bytes 786440 | tf_op jit(solution)/shard_map/ppermute | solution.py:1371
  169.2 15.1 %collective-permute-start.9 = (bf16[1024,128]{1,0:T(8,128)(2,1)}, bf16[1024,128]{1,0:T(8,128)(2,1)}, u32[]{:S(2)}, u32[]{:S(2)}) collective-permute-start(bf16[1024,128]{1,0:T(8,128)(2,1)} %get-tuple-element.112), channel_id=1, source_target_pairs={{0,5},{1,4},{2,7},{3,6},{4,1},{5,0},{6,3},{7,2},{8,13},{9,12},{10,... | collective-permute-start | bytes 786440 | tf_op jit(solution)/shard_map/ppermute | solution.py:1371
  172.4 61.2 %collective-permute-start.5 = (bf16[512,512]{1,0:T(8,128)(2,1)}, bf16[512,512]{1,0:T(8,128)(2,1)}, u32[]{:S(2)}, u32[]{:S(2)}) collective-permute-start(bf16[512,512]{1,0:T(8,128)(2,1)} %get-tuple-element.117), channel_id=1, source_target_pairs={{0,0},{8,1},{2,2},{10,3},{4,4},{12,5},{6,6},{14,7},{16,8},{24,9},{... | collective-permute-start | bytes 1572872 | tf_op jit(solution)/shard_map/ppermute | solution.py:1371
  178.3 55.3 %collective-permute-start.6 = (bf16[512,512]{1,0:T(8,128)(2,1)}, bf16[512,512]{1,0:T(8,128)(2,1)}, u32[]{:S(2)}, u32[]{:S(2)}) collective-permute-start(bf16[512,512]{1,0:T(8,128)(2,1)} %get-tuple-element.118), channel_id=1, source_target_pairs={{16,0},{24,1},{18,2},{26,3},{20,4},{28,5},{22,6},{30,7},{0,8},{8,9... | collective-permute-start | bytes 1572872 | tf_op jit(solution)/shard_map/ppermute | solution.py:1371
  181.2 4.6 %copy-start.3 = (bf16[1024,128]{1,0:T(8,128)(2,1)S(1)}, bf16[1024,128]{1,0:T(8,128)(2,1)}, u32[]{:S(2)}) copy-start(bf16[1024,128]{1,0:T(8,128)(2,1)} %get-tuple-element.111) | copy-start | bytes 786436
  182.3 53.7 %collective-permute-start.11 = (bf16[3,192,512]{2,1,0:T(8,128)(2,1)S(1)}, bf16[3,192,512]{2,1,0:T(8,128)(2,1)S(1)}, u32[]{:S(2)}, u32[]{:S(2)}) collective-permute-start(bf16[3,192,512]{2,1,0:T(8,128)(2,1)S(1)} %get-tuple-element.109), channel_id=1, source_target_pairs={{0,2},{1,3},{2,0},{3,1},{4,6},{5,7},{6,4},{7,5},{8,10},{9,11},{10,... | collective-permute-start | bytes 1769480 | tf_op jit(solution)/shard_map/ppermute | solution.py:1371
  183.3 52.7 %collective-permute-start.12 = (bf16[3,192,512]{2,1,0:T(8,128)(2,1)S(1)}, bf16[3,192,512]{2,1,0:T(8,128)(2,1)S(1)}, u32[]{:S(2)}, u32[]{:S(2)}) collective-permute-start(bf16[3,192,512]{2,1,0:T(8,128)(2,1)S(1)} %get-tuple-element.108), channel_id=1, source_target_pairs={{0,4},{1,5},{2,6},{3,7},{4,0},{5,1},{6,2},{7,3},{8,12},{9,13},{10,... | collective-permute-start | bytes 1769480 | tf_op jit(solution)/shard_map/ppermute | solution.py:1371
  184.3 51.7 %collective-permute-start.13 = (bf16[3,192,512]{2,1,0:T(8,128)(2,1)S(1)}, bf16[3,192,512]{2,1,0:T(8,128)(2,1)S(1)}, u32[]{:S(2)}, u32[]{:S(2)}) collective-permute-start(bf16[3,192,512]{2,1,0:T(8,128)(2,1)S(1)} %get-tuple-element.107), channel_id=1, source_target_pairs={{0,6},{1,7},{2,4},{3,5},{4,2},{5,3},{6,0},{7,1},{8,14},{9,15},{10,... | collective-permute-start | bytes 1769480 | tf_op jit(solution)/shard_map/ppermute | solution.py:1371
  236.0 0.8 copy-start.5
  236.0 1.0 copy-start.6
  236.0 1.2 copy-start.7
  300.9 4.6 %copy-start.4 = (f32[128,1536]{1,0:T(8,128)S(1)}, f32[128,1536]{1,0:T(8,128)}, u32[]{:S(2)}) copy-start(f32[128,1536]{1,0:T(8,128)} %get-tuple-element.151) | copy-start | bytes 2359300
  302.4 4.1 %copy-start.8 = (f32[128,512]{1,0:T(8,128)S(1)}, f32[128,512]{1,0:T(8,128)}, u32[]{:S(2)}) copy-start(f32[128,512]{1,0:T(8,128)} %get-tuple-element.152) | copy-start | bytes 786436
  302.4 4.8 %copy-start.2 = (f32[128,2048]{1,0:T(8,128)S(1)}, f32[128,2048]{1,0:T(8,128)}, u32[]{:S(2)}) copy-start(f32[128,2048]{1,0:T(8,128)} %get-tuple-element.153) | copy-start | bytes 3145732
  305.5 2.6 copy-start.1
  306.4 2.7 copy-start.11

commit v3 on v2

--- a/solution.py
+++ b/solution.py
@@ -40,57 +40,68 @@
     return pl.BlockSpec(shape, lambda *_: zeros)
 
 
-def split_heads(block):
-    lane = lax.broadcasted_iota(jnp.int32, block.shape, 1)
-    zero = jnp.zeros_like(block)
-    first = lane < HD
-    return jnp.concatenate([jnp.where(first, block, zero), jnp.where(first, zero, block)], axis=0)
-
-
-def attend_kernel(tab_ref, q_ref, start_ref, k_ref, vt_ref, o_ref, ot_ref, lse_ref, acc, top):
+def two_heads(block):
+    zero = jnp.zeros((HD, block.shape[1]), block.dtype)
+    return jnp.concatenate(
+        [jnp.concatenate([block[:HD], zero], axis=0), jnp.concatenate([zero, block[HD:]], axis=0)], axis=1
+    )
+
+
+EXTRA = 16
+
+
+def attend_kernel(tab_ref, qt_ref, start_ref, k_ref, vt_ref, o_ref, ot_ref, lse_ref, acc, top):
     qb = pl.program_id(0)
-    both = split_heads(q_ref[...])
+    both = two_heads(qt_ref[...])
     start = jnp.concatenate([start_ref[0], start_ref[0]], axis=1)
     row = lax.broadcasted_iota(jnp.int32, (BLK, 2 * BLK), 0)
-    col = lax.broadcasted_iota(jnp.int32, (BLK, 2 * BLK), 1)
-    ones = jnp.ones((16, BLK), bf16)
-
-    def scores(kb):
-        base = pl.multiple_of(tab_ref[2, kb] * BLK, BLK)
-        return contract(k_ref[pl.ds(base, BLK), :], both, 1, 1)
-
-    def values(kb):
-        base = pl.multiple_of(tab_ref[2, kb] * BLK, BLK)
-        return jnp.concatenate([vt_ref[:, pl.ds(base, BLK)], ones], axis=0)
-
-    st = scores(qb)
-    allowed = (row >= start - qb * BLK) & (row <= jnp.bitwise_and(col, BLK - 1))
-    st = jnp.where(allowed, st, mask_fill)
-    peak = jnp.max(st, axis=0, keepdims=True)
-    probs = jnp.exp2(st - peak).astype(bf16)
-    top[...] = peak
-    acc[...] = jnp.dot(values(qb), probs, preferred_element_type=f32)
-
-    def visit(kb, carry):
-        st = jnp.where(row >= start - kb * BLK, scores(kb), mask_fill)
-        old = top[...]
-        peak = jnp.maximum(old, jnp.max(st, axis=0, keepdims=True))
-        probs = jnp.exp2(st - peak).astype(bf16)
+    ones = jnp.ones((EXTRA, 2 * BLK), bf16)
+
+    def place_of(kb):
+        return pl.ds(pl.multiple_of(tab_ref[2, jnp.maximum(kb, 0)] * BLK, BLK), BLK)
+
+    def visit(kb, first):
+        places = [place_of(kb), place_of(kb - 1)]
+        terms = []
+        for i in range(2):
+            allowed = row >= start - (kb - i) * BLK
+            if first and i == 0:
+                col = lax.broadcasted_iota(jnp.int32, (BLK, 2 * BLK), 1)
+                allowed = allowed & (row <= jnp.bitwise_and(col, BLK - 1))
+            st = jnp.dot(k_ref[places[i], :], both, preferred_element_type=f32)
+            terms.append(jnp.where(allowed, st, mask_fill))
+        peak = jnp.maximum(
+            jnp.max(terms[0], axis=0, keepdims=True), jnp.max(terms[1], axis=0, keepdims=True)
+        )
+        if not first:
+            old = top[...]
+            peak = jnp.maximum(old, peak)
+            shrink = jnp.exp2(old - peak)
         top[...] = peak
-        acc[...] = acc[...] * jnp.exp2(old - peak) + jnp.dot(values(kb), probs, preferred_element_type=f32)
+        probs = jnp.concatenate([jnp.exp2(term - peak).astype(bf16) for term in terms], axis=0)
+        vt = jnp.concatenate([vt_ref[:, places[0]], vt_ref[:, places[1]]], axis=1)
+        for head in range(2):
+            cols = slice(head * BLK, (head + 1) * BLK)
+            left = jnp.concatenate([vt[head * HD : (head + 1) * HD], ones], axis=0)
+            part = jnp.dot(left, probs[:, cols], preferred_element_type=f32)
+            acc[head] = part if first else acc[head] * shrink[:, cols] + part
+
+    visit(qb, True)
+
+    def more(i, carry):
+        visit(qb - 2 * i, False)
         return carry
 
-    lax.fori_loop(tab_ref[0, qb], qb, visit, 0)
-    total = acc[PAIR : PAIR + 1, :]
+    lax.fori_loop(1, (qb - tab_ref[0, qb]) // 2 + 1, more, 0)
+    total = jnp.concatenate([acc[0, HD : HD + 1], acc[1, HD : HD + 1]], axis=1)
     lse_ref[0] = top[...] + jnp.log2(total)
-    out = acc[:PAIR, :] / total
-    heads = jnp.concatenate([out[:HD, :BLK], out[HD:, BLK:]], axis=0)
+    heads = jnp.concatenate([acc[h, :HD] / acc[h, HD : HD + 1] for h in range(2)], axis=0)
     ot_ref[0] = heads
     o_ref[...] = heads.T.astype(bf16)
 
 
-def attend(tab, q, start, k, vt):
-    count = q.shape[0]
+def attend(tab, qt, start, k, vt):
+    count = k.shape[0]
     blocks = count // BLK
     return pl.pallas_call(
         attend_kernel,
@@ -98,7 +109,7 @@
             num_scalar_prefetch=1,
             grid=(blocks,),
             in_specs=[
-                pl.BlockSpec((BLK, PAIR), lambda b, t: (t[2, b], 0)),
+                pl.BlockSpec((PAIR, BLK), lambda b, t: (0, t[2, b])),
                 pl.BlockSpec((1, 1, BLK), lambda b, t: (b, 0, 0)),
                 whole(k.shape),
                 whole(vt.shape),
@@ -109,7 +120,7 @@
                 pl.BlockSpec((1, 1, 2 * BLK), lambda b, t: (b, 0, 0)),
             ],
             scratch_shapes=[
-                pltpu.VMEM((PAIR + 16, 2 * BLK), f32),
+                pltpu.VMEM((2, HD + EXTRA, BLK), f32),
                 pltpu.VMEM((1, 2 * BLK), f32),
             ],
         ),
@@ -119,17 +130,16 @@
             jax.ShapeDtypeStruct((blocks, 1, 2 * BLK), f32),
         ],
         name="attend",
-    )(tab, q, start, k, vt)
+    )(tab, qt, start, k, vt)
 
 
 def attend_back_kernel(
-    tab_ref, k_ref, kt_ref, v_ref, h_ref, w_ref, q_ref, start_ref, do_ref, ot_ref, lse_ref,
-    gain_ref, bias_ref, dh_ref, gw_ref, gn_ref, dqt, dk, dv, delta, total, sums,
+    tab_ref, k_ref, kt_ref, v_ref, u_ref, w_ref, qt_ref, start_ref, do_ref, ot_ref, lse_ref,
+    gain_ref, bias_ref, dh_ref, gw_ref, gn_ref, dqt, dkt, dvt, dot, delta, total, sums,
 ):
     kb = pl.program_id(0)
     blocks = pl.num_programs(0)
     row = lax.broadcasted_iota(jnp.int32, (BLK, 2 * BLK), 0)
-    col = lax.broadcasted_iota(jnp.int32, (BLK, 2 * BLK), 1)
 
     def at(qb):
         return pl.ds(pl.multiple_of(tab_ref[2, qb] * BLK, BLK), BLK)
@@ -141,7 +151,9 @@
 
         def prepare(qb, carry):
             dqt[qb] = jnp.zeros((PAIR, BLK), f32)
-            both = do_ref[at(qb), :].astype(f32).T * ot_ref[qb]
+            turned = do_ref[at(qb), :].astype(f32).T
+            dot[qb] = turned.astype(bf16)
+            both = turned * ot_ref[qb]
             delta[qb] = jnp.concatenate(
                 [
                     jnp.sum(both[:HD], axis=0, keepdims=True),
@@ -158,31 +170,30 @@
     kt = kt_ref[...]
 
     def tile(qb, diagonal):
-        both_q = split_heads(q_ref[at(qb), :])
-        both_do = split_heads(do_ref[at(qb), :])
+        qt = qt_ref[:, at(qb)]
+        d_out = dot[qb]
         start = jnp.concatenate([start_ref[qb], start_ref[qb]], axis=1)
-        st = contract(k, both_q, 1, 1)
-        dpt = contract(v, both_do, 1, 1)
+        st = jnp.dot(k, two_heads(qt), preferred_element_type=f32)
+        dpt = jnp.dot(v, two_heads(d_out), preferred_element_type=f32)
         allowed = row >= start - kb * BLK
         if diagonal:
+            col = lax.broadcasted_iota(jnp.int32, (BLK, 2 * BLK), 1)
             allowed = allowed & (row <= jnp.bitwise_and(col, BLK - 1))
         pt = jnp.exp2(jnp.where(allowed, st - lse_ref[qb], mask_fill))
         dst = (pt * (dpt - delta[qb])).astype(bf16)
-        part_v = jnp.dot(pt.astype(bf16), both_do, preferred_element_type=f32)
-        part_k = jnp.dot(dst, both_q, preferred_element_type=f32)
-        if diagonal:
-            dv[...] = part_v
-            dk[...] = part_k
-        else:
-            dv[...] += part_v
-            dk[...] += part_k
-        dqt[qb] += jnp.concatenate(
-            [
-                jnp.dot(kt[:HD], dst[:, :BLK], preferred_element_type=f32),
-                jnp.dot(kt[HD:], dst[:, BLK:], preferred_element_type=f32),
-            ],
-            axis=0,
-        )
+        pt = pt.astype(bf16)
+        for head in range(2):
+            mine = slice(head * HD, (head + 1) * HD)
+            cols = slice(head * BLK, (head + 1) * BLK)
+            part_v = contract(d_out[mine], pt[:, cols], 1, 1)
+            part_k = contract(qt[mine], dst[:, cols], 1, 1)
+            if diagonal:
+                dvt[mine] = part_v
+                dkt[mine] = part_k
+            else:
+                dvt[mine] += part_v
+                dkt[mine] += part_k
+            dqt[qb, mine] += jnp.dot(kt[mine], dst[:, cols], preferred_element_type=f32)
 
     tile(kb, True)
 
@@ -192,9 +203,10 @@
 
     lax.fori_loop(kb + 1, tab_ref[1, kb] + 1, visit, 0)
     dq = (dqt[kb] * SCORE_SCALE).T.astype(bf16)
-    joined = jnp.concatenate([dq, (dk[...] * LN2).astype(bf16), dv[...].astype(bf16)], axis=1)
+    dk = (dkt[...] * LN2).T.astype(bf16)
+    joined = jnp.concatenate([dq, dk, dvt[...].T.astype(bf16)], axis=1)
     dh_ref[...] = contract(joined, w_ref[...], 1, 1).astype(bf16)
-    total[...] += contract(h_ref[...], joined, 0, 0)
+    total[...] += contract(u_ref[...], joined, 0, 0)
     sums[...] += jnp.sum(joined.astype(f32), axis=0, keepdims=True)
 
     @pl.when(kb == blocks - 1)
@@ -209,9 +221,9 @@
                 gn_ref[i : i + 1, part] = jnp.broadcast_to(column, (shard, shard)).T[:1]
 
 
-def attend_back(tab, k, kt, v, h, weight, q, start, d_out, ot, lse, gain, bias, shards):
-    count = q.shape[0]
-    width = h.shape[1]
+def attend_back(tab, k, kt, v, unit, weight, qt, start, d_out, ot, lse, gain, bias, shards):
+    count = k.shape[0]
+    width = unit.shape[1]
     shard = width // shards
     gain, bias = gain.reshape(width, 1), bias.reshape(width, 1)
     blocks = count // BLK
@@ -226,7 +238,7 @@
                 pl.BlockSpec((BLK, PAIR), lambda b, t: (t[2, b], 0)),
                 pl.BlockSpec((BLK, width), lambda b, t: (t[2, b], 0)),
                 whole(weight.shape),
-                whole(q.shape),
+                whole(qt.shape),
                 whole(start.shape),
                 whole(d_out.shape),
                 whole(ot.shape),
@@ -241,8 +253,9 @@
             ],
             scratch_shapes=[
                 pltpu.VMEM((blocks, PAIR, BLK), f32),
-                pltpu.VMEM((BLK, PAIR), f32),
-                pltpu.VMEM((BLK, PAIR), f32),
+                pltpu.VMEM((PAIR, BLK), f32),
+                pltpu.VMEM((PAIR, BLK), f32),
+                pltpu.VMEM((blocks, PAIR, BLK), bf16),
                 pltpu.VMEM((blocks, 1, 2 * BLK), f32),
                 pltpu.VMEM(weight.shape, f32),
                 pltpu.VMEM((1, 3 * PAIR), f32),
@@ -254,122 +267,7 @@
             jax.ShapeDtypeStruct((2, width), f32),
         ],
         name="attend_back",
-    )(tab, k, kt, v, h, weight, q, start, d_out, ot, lse, gain, bias)
-
-
-FF_TILE = 512
-
-
-def feed_kernel(
-    pair_ref, attn_ref, x_ref, dy_ref, wo_ref, wu_ref, wd_ref, vec_ref, ub_ref,
-    y_ref, do_ref, dmid_ref, grad_ref, gvec_ref, gub_ref, attn_all, gd_ref, gu_ref, go_ref,
-):
-    step = pl.program_id(0)
-    groups = attn_ref.shape[0]
-
-    @pl.when(step == 0)
-    def _():
-        for ref in (gd_ref, gu_ref, go_ref, gvec_ref, gub_ref):
-            ref[...] = jnp.zeros_like(ref)
-
-    for g in range(groups):
-        attn_all[:, pl.ds(pl.multiple_of(pair_ref[g] * PAIR, PAIR), PAIR)] = attn_ref[g]
-    attn = attn_all[...]
-    gain, bias, out_bias, down_bias = (vec_ref[i : i + 1, :] for i in range(2, 6))
-    middle = (
-        x_ref[...].astype(f32) + jnp.dot(attn, wo_ref[...], preferred_element_type=f32) + out_bias
-    )
-    unit, inv = norm_parts(middle)
-    low = (unit * gain + bias).astype(bf16)
-    dy = dy_ref[...]
-    dy32 = dy.astype(f32)
-    total = middle + down_bias
-    d_low = jnp.zeros_like(middle)
-    width = wu_ref.shape[1]
-    for j in range(0, width, FF_TILE):
-        part = pl.ds(j, FF_TILE)
-        up = wu_ref[:, part]
-        down = wd_ref[part, :]
-        hidden = jnp.dot(low, up, preferred_element_type=f32) + ub_ref[:, part]
-        cdf = 0.5 * (1.0 + lax.erf(hidden * (1.0 / math.sqrt(2.0))))
-        active = (hidden * cdf).astype(bf16)
-        slope = cdf + hidden * (jnp.exp2(hidden * hidden * (-0.5 * LOG2E)) * (1.0 / math.sqrt(2.0 * math.pi)))
-        total = total + jnp.dot(active, down, preferred_element_type=f32)
-        d_hidden = contract(dy, down, 1, 1) * slope
-        d_hidden_low = d_hidden.astype(bf16)
-        gub_ref[:, part] += jnp.sum(d_hidden, axis=0, keepdims=True)
-        d_low = d_low + contract(d_hidden_low, up, 1, 1)
-        gd_ref[part, :] += contract(active, dy, 0, 0)
-        gu_ref[:, part] += contract(low, d_hidden_low, 0, 0)
-    y_ref[...] = total.astype(bf16)
-    scaled = d_low * gain
-    d_middle = dy32 + inv * (
-        scaled
-        - jnp.mean(scaled, axis=-1, keepdims=True)
-        - unit * jnp.mean(scaled * unit, axis=-1, keepdims=True)
-    )
-    dmid_ref[...] = d_middle
-    branch = d_middle.astype(bf16)
-    go_ref[...] += contract(attn, branch, 0, 0)
-    gvec_ref[0:1, :] += jnp.sum(d_middle, axis=0, keepdims=True)
-    gvec_ref[1:2, :] += jnp.sum(d_low * unit, axis=0, keepdims=True)
-    gvec_ref[2:3, :] += jnp.sum(d_low, axis=0, keepdims=True)
-    gvec_ref[3:4, :] += jnp.sum(dy32, axis=0, keepdims=True)
-    attn_all[...] = contract(branch, wo_ref[...], 1, 1).astype(bf16)
-    for g in range(groups):
-        do_ref[g] = attn_all[:, pl.ds(pl.multiple_of(pair_ref[g] * PAIR, PAIR), PAIR)]
-
-    @pl.when(step == pl.num_programs(0) - 1)
-    def _():
-        shards = grad_ref.shape[0]
-        d_model = x_ref.shape[1]
-        down_rows, up_rows = gd_ref.shape[0] // shards, d_model // shards
-        for j in range(shards):
-            grad_ref[j, :down_rows] = gd_ref[j * down_rows : (j + 1) * down_rows].astype(bf16)
-            rows = slice(j * up_rows, (j + 1) * up_rows)
-            at = down_rows
-            for t in range(0, width, d_model):
-                grad_ref[j, at : at + up_rows] = gu_ref[rows, t : t + d_model].astype(bf16)
-                at += up_rows
-            grad_ref[j, at : at + up_rows] = go_ref[rows].astype(bf16)
-
-
-def feed(pair_of, attn, x, dy, w_out, w_up, w_down, vecs, up_bias, shards, tile=BLK):
-    groups, count, _ = attn.shape
-    width = x.shape[1]
-    flat = (w_out.size + w_up.size + w_down.size) // shards // width
-    rows = pl.BlockSpec((tile, width), lambda i, p: (i, 0))
-    heads = pl.BlockSpec((groups, tile, PAIR), lambda i, p: (0, i, 0))
-    return pl.pallas_call(
-        feed_kernel,
-        grid_spec=pltpu.PrefetchScalarGridSpec(
-            num_scalar_prefetch=1,
-            grid=(count // tile,),
-            in_specs=[
-                heads, rows, rows, whole(w_out.shape), whole(w_up.shape), whole(w_down.shape),
-                whole(vecs.shape), whole(up_bias.shape),
-            ],
-            out_specs=[
-                rows, heads, rows, whole((shards, flat, width)), whole(vecs.shape), whole(up_bias.shape),
-            ],
-            scratch_shapes=[
-                pltpu.VMEM((tile, width), bf16),
-                pltpu.VMEM(w_down.shape, f32),
-                pltpu.VMEM(w_up.shape, f32),
-                pltpu.VMEM(w_out.shape, f32),
-            ],
-        ),
-        out_shape=[
-            jax.ShapeDtypeStruct((count, width), bf16),
-            jax.ShapeDtypeStruct((groups, count, PAIR), bf16),
-            jax.ShapeDtypeStruct((count, width), f32),
-            jax.ShapeDtypeStruct((shards, flat, width), bf16),
-            jax.ShapeDtypeStruct(vecs.shape, f32),
-            jax.ShapeDtypeStruct(up_bias.shape, f32),
-        ],
-        compiler_params=pltpu.CompilerParams(vmem_limit_bytes=60 * 1024 * 1024),
-        name="feed",
-    )(pair_of, attn, x, dy, w_out, w_up, w_down, vecs, up_bias)
+    )(tab, k, kt, v, unit, weight, qt, start, d_out, ot, lse, gain, bias)
 
 
 def layer_norm(values, gain_vec, offset):
@@ -742,12 +640,12 @@
 
 
 def head_kernel(
-    x_in_ref, docs_in_ref, order_ref, vec_in_ref, wq_ref, wo_ref, wu_ref, wd_ref,
-    q_ref, k_ref, kt_ref, v_ref, vt_ref, u_ref, own_ref, wh_ref, vec_ref, ub_ref, start_ref, tab_ref,
-    wo_all, wu_all, wd_all,
+    x_in_ref, dy_in_ref, docs_in_ref, order_ref, vec_in_ref, wq_ref, wo_ref, wu_ref, wd_ref,
+    qt_ref, k_ref, kt_ref, v_ref, vt_ref, u_ref, own_ref, wh_ref, vec_ref, ub_ref, start_ref, tab_ref,
+    wo_all, wu_all, wd_all, dy_ref,
     rows, docs, docs_true, vec_all, wo_tmp, wu_tmp, wd_tmp,
     z_s, z_r, x_s, x_r, c_s, c_r, f_s, f_r, docs_s, docs_r, vec_s, vec_r, wh_s, wh_r, wh_l,
-    y_s, y_r, n_s, n_r, o_s, o_r, load_sem, put_sem, self_sem,
+    y_s, y_r, n_s, n_r, o_s, o_r, load_sem, put_sem, self_sem, d_s, d_r, d_self,
 ):
     z, x, y, c = (lax.axis_index(name) for name in AXES)
     odd, upper = lax.rem(z, 2), lax.div(z, 2)
@@ -787,6 +685,36 @@
             pl.when(leave)(lambda: send(src, dst, z_s, z_r, i, target[0]) and None)
         else:
             send(src, dst, z_s, z_r, i, target[1])
+
+    def piece_dy(i):
+        turn, row = i // per_turn, (i % per_turn) * HEAD_CHUNK
+        return (
+            dy_in_ref.at[block[turn], 0, pl.ds(row, HEAD_CHUNK)],
+            dy_ref.at[pl.ds(i * HEAD_CHUNK, HEAD_CHUNK)],
+        )
+
+    def send_dy(i):
+        src, dst = piece_dy(i)
+        if i < per_turn:
+            pl.when(stay)(lambda: pltpu.make_async_copy(src, dst, d_self.at[i]).start())
+            pl.when(leave)(lambda: send(src, dst, d_s, d_r, i, target[0]) and None)
+        else:
+            send(src, dst, d_s, d_r, i, target[1])
+
+    def land_dy(i):
+        src, dst = piece_dy(i)
+
+        def remote():
+            pltpu.make_async_remote_copy(
+                src_ref=src, dst_ref=dst, send_sem=d_s.at[i], recv_sem=d_r.at[i],
+                device_id=target[i // per_turn], device_id_type=MESH,
+            ).wait()
+
+        if i < per_turn:
+            pl.when(stay)(lambda: pltpu.make_async_copy(src, dst, d_self.at[i]).wait())
+            pl.when(leave)(remote)
+        else:
+            remote()
 
     def landed(src, dst, sems, recv_sems, index, turn, self_index):
         def remote():
@@ -933,7 +861,7 @@
         u_ref[at] = unit.astype(bf16)
         low = (unit * vec_ref[0:1] + vec_ref[1:2]).astype(bf16)
         qkv = jnp.dot(low, wh_ref[...], preferred_element_type=f32)
-        q_ref[at] = (qkv[:, :PAIR] * (SCORE_SCALE * LOG2E)).astype(bf16)
+        qt_ref[:, at] = (qkv[:, :PAIR] * (SCORE_SCALE * LOG2E)).astype(bf16).T
         k = qkv[:, PAIR : 2 * PAIR].astype(bf16)
         v = qkv[:, 2 * PAIR :].astype(bf16)
         k_ref[at] = k
@@ -943,6 +871,7 @@
 
     for i in range(chunks + 2):
         if i < chunks:
+            send_dy(i)
             relay(i)
             compute(0, i)
         if 1 <= i <= chunks:
@@ -964,9 +893,11 @@
         forward(i)
     for copy in n_copy + put_copy + o_copy:
         copy.wait()
-
-
-def head(x_in, docs_in, order, vec_in, w_qkv, w_out, w_up, w_down):
+    for i in range(chunks):
+        land_dy(i)
+
+
+def head(x_in, dy_in, docs_in, order, vec_in, w_qkv, w_out, w_up, w_down):
     width = x_in.shape[-1]
     count = 2 * x_in.shape[2]
     total = 4 * count
@@ -978,10 +909,10 @@
     dma, buf, shape = pltpu.SemaphoreType.DMA, pltpu.VMEM, jax.ShapeDtypeStruct
     return pl.pallas_call(
         head_kernel,
-        in_specs=[any_, vmem, smem, vmem, any_, any_, any_, any_],
-        out_specs=[vmem] * 12 + [any_] * 3,
+        in_specs=[any_, any_, vmem, smem, vmem, any_, any_, any_, any_],
+        out_specs=[vmem] * 12 + [any_] * 4,
         out_shape=[
-            shape((total, PAIR), bf16),
+            shape((PAIR, total), bf16),
             shape((total, PAIR), bf16),
             shape((PAIR, total), bf16),
             shape((total, PAIR), bf16),
@@ -996,6 +927,7 @@
             shape((4 * w_out.shape[0], w_out.shape[1]), bf16),
             shape((4 * w_up.shape[0], w_up.shape[1]), bf16),
             shape((4 * w_down.shape[0], w_down.shape[1]), bf16),
+            shape((count, width), bf16),
         ],
         scratch_shapes=[
             buf((4, count, width), bf16),
@@ -1009,14 +941,257 @@
         + [dma((chunks,))] * 8
         + [dma((5,)), dma((5,)), dma((3,)), dma((3,)), dma((9,)), dma((9,)), dma((3,))]
         + [dma((9,)), dma((9,)), dma((3,)), dma((3,)), dma((9,)), dma((9,)), dma((3,)), dma((3,))]
-        + [dma((chunks // 2 + 1,))],
+        + [dma((chunks // 2 + 1,)), dma((chunks,)), dma((chunks,)), dma((chunks // 2,))],
         compiler_params=pltpu.CompilerParams(
             collective_id=1, has_side_effects=True, vmem_limit_bytes=56 * 1024 * 1024
         ),
         name="head",
-    )(x_in, docs_in, order, vec_in, w_qkv, w_out, w_up, w_down)
+    )(x_in, dy_in, docs_in, order, vec_in, w_qkv, w_out, w_up, w_down)
+FF_TILE = 512
+PIECES = 3
+feed_steps = 4
+
+
+def feed_kernel(
+    o_ref, x_ref, dy_ref, wo_ref, wu_ref, wd_ref, vec_ref, ub_ref,
+    do_ref, y_home, dmid_ref, keep_ref, to_y_ref, to_x_ref, to_xy_ref, gvec_ref, gub_ref,
+    attn_all, gd_ref, gu_ref, go_ref, attn_in, do_out, y_out, grad_ref, grad_in,
+    a_s, a_r, a_l, d_s, d_r, d_l, y_s, y_r, y_l, g_s, g_r,
+):
+    step = pl.program_id(0)
+    steps = pl.num_programs(0)
+    groups = attn_in.shape[0]
+    tile = x_ref.shape[0]
+    z, x, y, c = (lax.axis_index(name) for name in AXES)
+    odd, upper = lax.rem(z, 2), lax.div(z, 2)
+    mates = [None, {"x": 1 - x}, {"c": 1 - c}, {"x": 1 - x, "c": 1 - c}]
+    pair_of = [2 * x + c, 2 * (1 - x) + c, 2 * x + 1 - c, 2 * (1 - x) + 1 - c]
+    home = [{"z": 2 * c + upper, "c": odd}, {"z": 2 * c + 1 - upper, "c": odd}]
+    origin = [{"z": 2 * odd + c, "c": upper}, {"z": 2 * (1 - odd) + c, "c": upper}]
+    stay = (c == upper) & (odd == c)
+    leave = jnp.logical_not(stay)
+    half = feed_steps // 2
+
+    def attn_copy(g, i):
+        part = pl.ds(i * tile, tile)
+        return pltpu.make_async_remote_copy(
+            src_ref=o_ref.at[g, part], dst_ref=attn_in.at[g, part],
+            send_sem=a_s.at[g - 1, i], recv_sem=a_r.at[g - 1, i], device_id=mates[g], device_id_type=MESH,
+        )
+
+    def attn_own(i):
+        part = pl.ds(i * tile, tile)
+        return pltpu.make_async_copy(o_ref.at[0, part], attn_in.at[0, part], a_l.at[i])
+
+    def do_copy(g, i):
+        return pltpu.make_async_remote_copy(
+            src_ref=do_out.at[i, g], dst_ref=do_ref.at[g, pl.ds(i * tile, tile)],
+            send_sem=d_s.at[g - 1, i], recv_sem=d_r.at[g - 1, i], device_id=mates[g], device_id_type=MESH,
+        )
+
+    def do_own(i):
+        return pltpu.make_async_copy(do_out.at[i, 0], do_ref.at[0, pl.ds(i * tile, tile)], d_l.at[i])
+
+    def y_rows(i, block):
+        return y_home.at[block, pl.ds(lax.rem(i, half) * tile, tile)]
+
+    def y_copy(i, turn, block):
+        return pltpu.make_async_remote_copy(
+            src_ref=y_out.at[i], dst_ref=y_rows(i, block),
+            send_sem=y_s.at[i], recv_sem=y_r.at[i], device_id=home[turn], device_id_type=MESH,
+        )
+
+    def y_own(i, block):
+        return pltpu.make_async_copy(y_out.at[i], y_rows(i, block), y_l.at[i])
+
+    def grad_copy(i):
+        return pltpu.make_async_remote_copy(
+            src_ref=grad_ref.at[2 * i + 1 - c], dst_ref=grad_in.at[i],
+            send_sem=g_s.at[i], recv_sem=g_r.at[i], device_id=mates[2], device_id_type=MESH,
+        )
+
+    @pl.when(step == 0)
+    def _():
+        greet(mates[1:] + [home[1], origin[1]], [home[0], origin[0]], leave)
+        for i in range(feed_steps):
+            for g in (1, 3, 2):
+                attn_copy(g, i).start()
+            attn_own(i).start()
+
+    @pl.when(step == 0)
+    def _():
+        for ref in (gd_ref, gu_ref, go_ref, gvec_ref, gub_ref):
+            ref[...] = jnp.zeros_like(ref)
+
+    attn_own(step).wait()
+    for g in range(1, groups):
+        attn_copy(g, step).wait()
+    for g in range(groups):
+        attn_all[:, pl.ds(pl.multiple_of(pair_of[g] * PAIR, PAIR), PAIR)] = attn_in[
+            g, pl.ds(pl.multiple_of(step * tile, tile), tile)
+        ]
+    attn = attn_all[...]
+    gain, bias, out_bias, down_bias = (vec_ref[i : i + 1, :] for i in range(2, 6))
+    middle = (
+        x_ref[...].astype(f32) + jnp.dot(attn, wo_ref[...], preferred_element_type=f32) + out_bias
+    )
+    unit, inv = norm_parts(middle)
+    low = (unit * gain + bias).astype(bf16)
+    dy = dy_ref[...]
+    dy32 = dy.astype(f32)
+    total = middle + down_bias
+    d_low = jnp.zeros_like(middle)
+    width = wu_ref.shape[1]
+    for j in range(0, width, FF_TILE):
+        part = pl.ds(j, FF_TILE)
+        up = wu_ref[:, part]
+        down = wd_ref[part, :]
+        hidden = jnp.dot(low, up, preferred_element_type=f32) + ub_ref[:, part]
+        cdf = 0.5 * (1.0 + lax.erf(hidden * (1.0 / math.sqrt(2.0))))
+        active = (hidden * cdf).astype(bf16)
+        slope = cdf + hidden * (jnp.exp2(hidden * hidden * (-0.5 * LOG2E)) * (1.0 / math.sqrt(2.0 * math.pi)))
+        total = total + jnp.dot(active, down, preferred_element_type=f32)
+        d_hidden = contract(dy, down, 1, 1) * slope
+        d_hidden_low = d_hidden.astype(bf16)
+        gub_ref[:, part] += jnp.sum(d_hidden, axis=0, keepdims=True)
+        d_low = d_low + contract(d_hidden_low, up, 1, 1)
+        gd_ref[part, :] += contract(active, dy, 0, 0)
+        gu_ref[:, part] += contract(low, d_hidden_low, 0, 0)
+    y_out[step] = total.astype(bf16)
+
+    @pl.when((step < half) & stay)
+    def _():
+        y_own(step, upper).start()
+
+    @pl.when((step < half) & leave)
+    def _():
+        y_copy(step, 0, upper).start()
+
+    @pl.when(step >= half)
+    def _():
+        y_copy(step, 1, upper).start()
+
+    scaled = d_low * gain
+    d_middle = dy32 + inv * (
+        scaled
+        - jnp.mean(scaled, axis=-1, keepdims=True)
+        - unit * jnp.mean(scaled * unit, axis=-1, keepdims=True)
+    )
+    dmid_ref[...] = d_middle
+    branch = d_middle.astype(bf16)
+    go_ref[...] += contract(attn, branch, 0, 0)
+    gvec_ref[0:1, :] += jnp.sum(d_middle, axis=0, keepdims=True)
+    gvec_ref[1:2, :] += jnp.sum(d_low * unit, axis=0, keepdims=True)
+    gvec_ref[2:3, :] += jnp.sum(d_low, axis=0, keepdims=True)
+    gvec_ref[3:4, :] += jnp.sum(dy32, axis=0, keepdims=True)
+    attn_all[...] = contract(branch, wo_ref[...], 1, 1).astype(bf16)
+    for g in (1, 3, 2, 0):
+        do_out[step, g] = attn_all[:, pl.ds(pl.multiple_of(pair_of[g] * PAIR, PAIR), PAIR)]
+        if g:
+            do_copy(g, step).start()
+        else:
+            do_own(step).start()
+
+    @pl.when(step == steps - 1)
+    def _():
+        shards = grad_ref.shape[0]
+        d_model = x_ref.shape[1]
+        down_rows, up_rows = gd_ref.shape[0] // shards, d_model // shards
+        for j in range(shards):
+            grad_ref[j, :down_rows] = gd_ref[j * down_rows : (j + 1) * down_rows].astype(bf16)
+            rows = slice(j * up_rows, (j + 1) * up_rows)
+            at = down_rows
+            for t in range(0, width, d_model):
+                grad_ref[j, at : at + up_rows] = gu_ref[rows, t : t + d_model].astype(bf16)
+                at += up_rows
+            grad_ref[j, at : at + up_rows] = go_ref[rows].astype(bf16)
+        for j in range(2):
+            grad_copy(j).start()
+        for j in range(feed_steps):
+            do_own(j).wait()
+            for g in range(1, groups):
+                do_copy(g, j).wait()
+            if j < half:
+                @pl.when(stay)
+                def _():
+                    y_own(j, odd).wait()
+
+                @pl.when(leave)
+                def _():
+                    y_copy(j, 0, odd).wait()
+            else:
+                y_copy(j, 1, 1 - odd).wait()
+        sixth = keep_ref.shape[1]
+        for j in range(2):
+            grad_copy(j).wait()
+        for dy_, dx_, ref in ((0, 0, keep_ref), (1, 0, to_y_ref), (0, 1, to_x_ref), (1, 1, to_xy_ref)):
+            row = 1 - y if dy_ else y
+            side = 1 - x if dx_ else x
+            for p in range(PIECES):
+                part = pl.ds(pl.multiple_of((2 * p + side) * sixth, 16), sixth)
+                ref[p] = (
+                    grad_ref[2 * row + c, part].astype(f32) + grad_in[row, part].astype(f32)
+                ).astype(bf16)
+
+
+def feed(o, x, dy, w_out, w_up, w_down, vecs, up_bias, shards):
+    groups, count, _ = o.shape
+    width = x.shape[1]
+    flat = (w_out.size + w_up.size + w_down.size) // shards // width
+    tile = count // feed_steps
+    piece = (PIECES, flat // PIECES // 2, width)
+    rows = pl.BlockSpec((tile, width), lambda i: (i, 0))
+    any_ = pl.BlockSpec(memory_space=pl.ANY)
+    dma, buf, shape = pltpu.SemaphoreType.DMA, pltpu.VMEM, jax.ShapeDtypeStruct
+    return pl.pallas_call(
+        feed_kernel,
+        grid=(feed_steps,),
+        in_specs=[
+            any_, rows, rows, whole(w_out.shape), whole(w_up.shape), whole(w_down.shape),
+            whole(vecs.shape), whole(up_bias.shape),
+        ],
+        out_specs=[any_, any_, rows] + [whole(piece)] * 4 + [whole(vecs.shape), whole(up_bias.shape)],
+        out_shape=[
+            shape((groups, count, PAIR), bf16),
+            shape((2, count // 2, width), bf16),
+            shape((count, width), f32),
+            shape(piece, bf16),
+            shape(piece, bf16),
+            shape(piece, bf16),
+            shape(piece, bf16),
+            shape(vecs.shape, f32),
+            shape(up_bias.shape, f32),
+        ],
+        scratch_shapes=[
+            buf((tile, width), bf16),
+            buf(w_down.shape, f32),
+            buf(w_up.shape, f32),
+            buf(w_out.shape, f32),
+            buf((groups, count, PAIR), bf16),
+            buf((feed_steps, groups, tile, PAIR), bf16),
+            buf((feed_steps, tile, width), bf16),
+            buf((shards, flat, width), bf16),
+            buf((2, flat, width), bf16),
+            dma((3, feed_steps)),
+            dma((3, feed_steps)),
+            dma((feed_steps,)),
+            dma((3, feed_steps)),
+            dma((3, feed_steps)),
+            dma((feed_steps,)),
+            dma((feed_steps,)),
+            dma((feed_steps,)),
+            dma((feed_steps,)),
+            dma((2,)),
+            dma((2,)),
+        ],
+        compiler_params=pltpu.CompilerParams(
+            collective_id=3, has_side_effects=True, vmem_limit_bytes=60 * 1024 * 1024
+        ),
+        name="feed",
+    )(o, x, dy, w_out, w_up, w_down, vecs, up_bias)
+
+
 TAIL_CHUNK = 128
-PIECES = 3
 
 
 def tail_kernel(
@@ -1356,13 +1531,6 @@
     ]
 
 
-def gather_pairs(turn):
-    return [
-        (place(z, x, y, c), place(2 * ((z % 2) ^ turn) + c, x, y, z // 2))
-        for z, x, y, c in everyone()
-    ]
-
-
 def swap_pairs(dx, dy, dc):
     return [(place(z, x, y, c), place(z, x ^ dx, y ^ dy, c ^ dc)) for z, x, y, c in everyone()]
 
@@ -1373,77 +1541,38 @@
 
 def swap(value, dx=0, dy=0, dc=0):
     return move(value, swap_pairs(dx, dy, dc))
-
-
-def to_pair(value, odd):
-    return [
-        move(lax.dynamic_index_in_dim(value, odd ^ turn, 0, keepdims=False)[0], gather_pairs(turn))
-        for turn in range(2)
-    ]
-
-
-def from_pair(value, odd):
-    back = [move(value[turn], [(b, a) for a, b in gather_pairs(turn)]) for turn in range(2)]
-    first = jnp.where(odd == 0, back[0], back[1])
-    second = jnp.where(odd == 0, back[1], back[0])
-    return jnp.stack([first, second])[:, None]
 
 
 def paired_body(
     inputs, out_grad, segment_ids, block_order, w_qkv, w_out, w_up, w_down,
     norm1_gain, norm1_bias, norm2_gain, norm2_bias, out_bias, up_bias, down_bias,
 ):
-    z, x, y, c = (lax.axis_index(name) for name in AXES)
-    odd = z % 2
-    rows, width = inputs.shape[2], inputs.shape[3]
+    width = inputs.shape[3]
     shard = norm1_gain.shape[0]
     vectors = stack_rows(
         [norm1_gain, norm1_bias, norm2_gain, norm2_bias, out_bias, down_bias, up_bias], shard, 16
     )
     (
-        q, k, kt, v, vt, unit, own_x, w_heads, vecs, full_ubias, start, tab, full_out, full_up, full_down
+        qt, k, kt, v, vt, unit, own_x, w_heads, vecs, full_ubias, start, tab, full_out, full_up, full_down, own_dy
     ) = head(
-        inputs, segment_ids.reshape(2, -1, 128), block_order, vectors, w_qkv, w_out, w_up, w_down
+        inputs, out_grad, segment_ids.reshape(2, -1, 128), block_order, vectors, w_qkv, w_out, w_up, w_down
     )
     gain_one, bias_one = vecs[0:1], vecs[1:2]
-    groups = jnp.arange(4, dtype=jnp.int32)
-    pair_of = 2 * (x ^ (groups % 2)) + (c ^ (groups // 2))
-
-    dy_piece = to_pair(out_grad, odd)
-    o, ot, lse = attend(tab, q, start, k, vt)
-    o = o.reshape(4, -1, PAIR)
-    attn = jnp.stack([o[0], swap(o[1], dx=1), swap(o[2], dc=1), swap(o[3], dx=1, dc=1)])
-
-    own_dy = jnp.concatenate(dy_piece, axis=0)
-    result, d_o, d_middle, g_flat, g_vecs, g_ubias = feed(
-        pair_of, attn, own_x, own_dy, full_out, full_up, full_down, vecs, full_ubias, 4
-    )
-    outputs = from_pair(result.reshape(2, rows, width), odd)
-
-    d_o = jnp.concatenate([d_o[0], swap(d_o[1], dx=1), swap(d_o[2], dc=1), swap(d_o[3], dx=1, dc=1)])
-    g_flat = g_flat.reshape((2, 2) + g_flat.shape[1:])
-    given = lax.dynamic_index_in_dim(g_flat, 1 - c, 1, keepdims=False)
-    kept = lax.dynamic_index_in_dim(g_flat, c, 1, keepdims=False)
-    flat = (kept.astype(f32) + swap(given, dc=1).astype(f32)).astype(bf16)
-    flat = flat.reshape(2, PIECES, 2, -1, width)
-
-    def quarter(dy, dx):
-        part = lax.dynamic_index_in_dim(flat, y ^ dy, 0, keepdims=False)
-        return lax.dynamic_index_in_dim(part, x ^ dx, 1, keepdims=False)
-
-    from_y, from_x, from_xy = (
-        swap(quarter(1, 0), dy=1), swap(quarter(0, 1), dx=1), swap(quarter(1, 1), dy=1, dx=1)
-    )
+    o, ot, lse = attend(tab, qt, start, k, vt)
+    d_o, outputs, d_middle, keep, to_y, to_x, to_xy, g_vecs, g_ubias = feed(
+        o.reshape(4, -1, PAIR), own_x, own_dy, full_out, full_up, full_down, vecs, full_ubias, 4
+    )
+    from_y, from_x, from_xy = swap(to_y, dy=1), swap(to_x, dx=1), swap(to_xy, dy=1, dx=1)
     dh, g_heads, g_norm = attend_back(
-        tab, k, kt, v, unit, w_heads, q, start, d_o, ot, lse, gain_one, bias_one, 4
+        tab, k, kt, v, unit, w_heads, qt, start, d_o.reshape(-1, PAIR), ot, lse, gain_one, bias_one, 4
     )
     small = stack_rows([g_norm, g_vecs[1:3], g_vecs[0:1], g_vecs[3:4], g_ubias], width, 16)
     dx, grad_down, grad_up, grad_out, grad_qkv, g_vec, g_ub = tail(
-        dh.reshape(4, -1, width), own_x, d_middle, gain_one, quarter(0, 0), from_y, from_x, from_xy,
+        dh.reshape(4, -1, width), own_x, d_middle, gain_one, keep, from_y, from_x, from_xy,
         g_heads, small, w_down.shape[0],
     )
     return (
-        outputs, dx[:, None], grad_qkv, grad_out, grad_up, grad_down,
+        outputs[:, None], dx[:, None], grad_qkv, grad_out, grad_up, grad_down,
         g_vec[0], g_vec[1], g_vec[2], g_vec[3], g_vec[4], g_ub[0], g_vec[5],
     )
 

time: 315 us -> 268 us (0.85); the launches traced: 310 us -> 266 us
  starting transfers between devices: 19.7 us -> 3.55 us
  waiting for transfers between devices: 11.9 us -> 0.01 us
  local copies, waits for them, and re-layouts: 24.9 us -> 14.5 us
  other arithmetic: 13.8 us -> 4.05 us
  Pallas kernels: 239 us -> 244 us
    ppermute x14 -> x3, starting transfers between devices: 19.7 us -> 3.55 us  [move(): return lax.ppermute(value, AXES, pairs)]
    ppermute x14 -> x3, waiting for transfers between devices: 11.9 us -> 0.01 us  [move(): return lax.ppermute(value, AXES, pairs)]
    pallas_call x1, Pallas kernels: 34.3 us -> 26.4 us  [attend(): pl.pallas_call(attend_kernel, grid_spec=pltpu.PrefetchScalarGridSpec(num_...]
    squeeze x4 -> x0, local copies, waits for them, and re-layouts: 7.73 us -> none  [the longest x1 3.21 us: paired_body(): given = lax.dynamic_index_in_dim(g_flat, 1 - c, 1, keepdims=False)]
    pallas_call x1, Pallas kernels: 44.4 us -> 49.7 us  [attend_back(): pl.pallas_call(attend_back_kernel, grid_spec=pltpu.PrefetchScalarGridSpec...]
    pallas_call x2, Pallas kernels: 96.3 us -> 100 us  [the longest x1 55 us: head(): pl.pallas_call(head_kernel, in_specs=[any_, any_, vmem, smem, vmem, any_,...]
    pallas_call x1, Pallas kernels: 63.7 us -> 67 us  [tail(): pl.pallas_call(tail_kernel, in_specs=[pl.BlockSpec(memory_space=pl.ANY)]...]
    another operation x2 -> x0, other arithmetic: 3.32 us -> none  [the longest x1 2.05 us: paired_body(): jnp.stack([o[0], swap(o[1], dx=1), swap(o[2], dc=1), swap(o[3], dx=1, dc=...]
  transfers between devices with their start and end apart: 14 -> 3, of which waited for: 2 -> 0; matrix products, arithmetic and copies ran while one was open for 7% -> 3% of each run, Pallas kernels for 47% -> 19%
where the time goes in v3:
time: 268 us; the launch traced here: 266 us
  Pallas kernels  244 us (91%)
  local copies, waits for them, and re-layouts  14.5 us (5%)
  other arithmetic  4.05 us (2%)
  starting transfers between devices  3.55 us (1%)
    pallas_call x1, Pallas kernels, tail(): pl.pallas_call(tail_kernel, in_specs=[pl.BlockSpec(memory_space=pl.ANY)]...  67 us
    pallas_call x1, Pallas kernels, head(): pl.pallas_call(head_kernel, in_specs=[any_, any_, vmem, smem, vmem, any_,...  55 us
    pallas_call x1, Pallas kernels, attend_back(): pl.pallas_call(attend_back_kernel, grid_spec=pltpu.PrefetchScalarGridSpec...  49.7 us
    pallas_call x1, Pallas kernels, feed(): pl.pallas_call(feed_kernel, grid=(feed_steps,), in_specs=[any_, rows, row...  45.3 us
    pallas_call x1, Pallas kernels, attend(): pl.pallas_call(attend_kernel, grid_spec=pltpu.PrefetchScalarGridSpec(num_...  26.4 us
    unnamed x27, local copies, waits for them, and re-layouts  7.94 us
  transfers between devices with their start and end apart: 3, of which 0 were waited for; matrix products, arithmetic and copies ran while one was open for 3% of the time, Pallas kernels for 19%

profile of v3, /device:TPU:0, one launch (start us, length us, event | category | flops | bytes accessed | tf_op | source)
XLA Modules:
  0.0 266.4 jit_solution(4614835887351709149)
XLA Ops:
  0.6 1.4 pad_add_fusion.1.vec_in_ref
  2.0 55.0 %head.1 = (bf16[128,4096]{1,0:T(8,128)(2,1)}, bf16[4096,128]{1,0:T(8,128)(2,1)}, bf16[128,4096]{1,0:T(8,128)(2,1)}, bf16[4096,128]{1,0:T(8,128)(2,1)}, bf16[128,...) custom-call(bf16[2,1,512,512]{3,2,1,0:T(8,128)(2,1)} %x_in_ref.1, ...), custom_call_target="tpu_custom_call" | custom-call | tf_op jit(solution)/shard_map/head/pallas_call | solution.py:910
  57.1 26.4 %attend.1 = (bf16[4096,128]{1,0:T(8,128)(2,1)}, f32[16,128,256]{2,1,0:T(8,128)}, f32[16,1,512]{2,1,0:T(1,128)}) custom-call(s32[8,128]{1,0:T(8,128)} %get-tuple-element.51.tab_ref, bf16[128,4096]{1,0:T(8,128)(2,1)} %get-tuple-element.52.qt_ref, s32[16,1,256]{2,1,0:T(1,128)} %get-tuple-element.53.start_ref, bf16[4096,128]{1,0:T(8,128)(2,1)} %get-tuple-element.54.k_ref, ...), custom_call_target="tpu_custom_call" | custom-call | tf_op jit(solution)/shard_map/attend/pallas_call | solution.py:106
  83.5 45.3 %feed.1 = (bf16[4,1024,128]{2,1,0:T(8,128)(2,1)}, bf16[2,512,512]{2,1,0:T(8,128)(2,1)}, f32[1024,512]{1,0:T(8,128)}, bf16[3,192,512]{2,1,0:T(8,128)(2,1)}, bf16[...) custom-call(bf16[4,1024,128]{2,1,0:T(8,128)(2,1)} %bitcast.37, ...), custom_call_target="tpu_custom_call" | custom-call | tf_op jit(solution)/shard_map/feed/pallas_call | solution.py:1146
  128.8 0.1 collective-permute-start
  128.9 1.1 collective-permute-start.1
  130.0 2.4 collective-permute-start.2
  132.4 1.4 fusion.1
  133.8 0.9 copy.30.gain_ref
  134.6 0.9 copy.31.bias_ref
  135.5 0.5 broadcast.27
  136.0 1.4 reduce.3
  137.4 0.7 slice.35
  138.1 49.7 %attend_back.1 = (bf16[4096,512]{1,0:T(8,128)(2,1)}, bf16[4,128,384]{2,1,0:T(8,128)(2,1)}, f32[2,512]{1,0:T(2,128)}) custom-call(s32[8,128]{1,0:T(8,128)} %get-tuple-element.51.tab_ref, bf16[4096,128]{1,0:T(8,128)(2,1)} %get-tuple-element.54.k_ref, bf16[128,4096]{1,0:T(8,128)(2,1)} %get-tuple-element.65.kt_ref, bf16[4096,128]{1,0:T(8,128)(2,1)} %get-tuple-element.66.v_ref, ...), custom_call_target="tpu_custom_call" | custom-call | tf_op jit(solution)/shard_map/attend_back/pallas_call | solution.py:230
  187.8 0.8 fusion
  188.6 1.3 pad_add_fusion.small_ref
  189.9 0.0 copy-start.6
  189.9 0.0 collective-permute-done.2.from_xy_ref
  190.0 0.0 copy-start.7
  190.0 0.8 copy-done.5
  190.7 0.2 copy-done.6
  190.9 0.2 copy-done.7
  191.1 67.0 %tail.1 = (f32[2,512,512]{2,1,0:T(8,128)}, f32[512,512]{1,0:T(8,128)}, f32[128,2048]{1,0:T(8,128)}, f32[128,512]{1,0:T(8,128)}, f32[128,1536]{1,0:T(8,128)}, /*index=5*/f32[8,128]{1,0:T(8,128)}, f32[1,512]{1,0:T(1,128)}) custom-call(bf16[4,1024,512]{2,1,0:T(8,128)(2,1)} %bitcast.34, bf16[1024,512]{1,0:T(8,128)(2,1)} %get-tuple-element.57.x_ref, ...), custom_call_target="tpu_custom_call" | custom-call | tf_op jit(solution)/shard_map/tail/pallas_call | solution.py:1455
  258.2 1.4 slice_bitcast_fusion.1
  259.6 1.0 copy.41
  260.6 1.3 copy.42
  261.9 0.4 copy-done.4
  262.3 0.9 copy.43
  263.1 0.7 copy.44
  263.9 1.0 copy.45
  264.8 1.0 copy.46
  265.8 0.6 copy.47
  (17 shorter events, 0.0 us)
Async XLA Ops:
  128.8 61.1 %collective-permute-start = (bf16[3,192,512]{2,1,0:T(8,128)(2,1)}, bf16[3,192,512]{2,1,0:T(8,128)(2,1)S(1)}, u32[]{:S(2)}, u32[]{:S(2)}) collective-permute-start(bf16[3,192,512]{2,1,0:T(8,128)(2,1)} %get-tuple-element.75), channel_id=1, source_target_pairs={{0,2},{1,3},{2,0},{3,1},{4,6},{5,7},{6,4},{7,5},{8,10},{9,11},{10,... | collective-permute-start | bytes 1769480 | tf_op jit(solution)/shard_map/ppermute | solution.py:1539
  128.9 61.0 %collective-permute-start.1 = (bf16[3,192,512]{2,1,0:T(8,128)(2,1)}, bf16[3,192,512]{2,1,0:T(8,128)(2,1)S(1)}, u32[]{:S(2)}, u32[]{:S(2)}) collective-permute-start(bf16[3,192,512]{2,1,0:T(8,128)(2,1)} %get-tuple-element.76), channel_id=1, source_target_pairs={{0,4},{1,5},{2,6},{3,7},{4,0},{5,1},{6,2},{7,3},{8,12},{9,13},{10,... | collective-permute-start | bytes 1769480 | tf_op jit(solution)/shard_map/ppermute | solution.py:1539
  130.0 59.9 %collective-permute-start.2 = (bf16[3,192,512]{2,1,0:T(8,128)(2,1)}, bf16[3,192,512]{2,1,0:T(8,128)(2,1)S(1)}, u32[]{:S(2)}, u32[]{:S(2)}) collective-permute-start(bf16[3,192,512]{2,1,0:T(8,128)(2,1)} %get-tuple-element.77), channel_id=1, source_target_pairs={{0,6},{1,7},{2,4},{3,5},{4,2},{5,3},{6,0},{7,1},{8,14},{9,15},{10,... | collective-permute-start | bytes 1769480 | tf_op jit(solution)/shard_map/ppermute | solution.py:1539
  189.9 0.8 copy-start.5
  189.9 1.0 copy-start.6
  190.0 1.2 copy-start.7
  191.1 68.5 %copy-start.1 = (bf16[2,512,512]{2,1,0:T(8,128)(2,1)S(1)}, bf16[2,512,512]{2,1,0:T(8,128)(2,1)}, u32[]{:S(2)}) copy-start(bf16[2,512,512]{2,1,0:T(8,128)(2,1)} %get-tuple-element.64) | copy-start | bytes 3145732
  258.2 2.4 copy-start
  260.6 1.7 copy-start.4
  260.6 2.6 copy-start.8
  262.3 1.6 copy-start.3
  262.3 2.6 copy-start.2
  263.8 1.9 copy-start.9

commit v4 on v3

--- a/solution.py
+++ b/solution.py
@@ -60,39 +60,59 @@
     def place_of(kb):
         return pl.ds(pl.multiple_of(tab_ref[2, jnp.maximum(kb, 0)] * BLK, BLK), BLK)
 
-    def visit(kb, first):
+    def masked_scores(kb, at, diagonal):
+        allowed = row >= start - kb * BLK
+        if diagonal:
+            col = lax.broadcasted_iota(jnp.int32, (BLK, 2 * BLK), 1)
+            allowed = allowed & (row <= jnp.bitwise_and(col, BLK - 1))
+        st = jnp.dot(k_ref[at, :], both, preferred_element_type=f32)
+        return jnp.where(allowed, st, mask_fill)
+
+    def visit(kb, first, bounded):
         places = [place_of(kb), place_of(kb - 1)]
-        terms = []
-        for i in range(2):
-            allowed = row >= start - (kb - i) * BLK
-            if first and i == 0:
-                col = lax.broadcasted_iota(jnp.int32, (BLK, 2 * BLK), 1)
-                allowed = allowed & (row <= jnp.bitwise_and(col, BLK - 1))
-            st = jnp.dot(k_ref[places[i], :], both, preferred_element_type=f32)
-            terms.append(jnp.where(allowed, st, mask_fill))
-        peak = jnp.maximum(
-            jnp.max(terms[0], axis=0, keepdims=True), jnp.max(terms[1], axis=0, keepdims=True)
-        )
-        if not first:
-            old = top[...]
-            peak = jnp.maximum(old, peak)
-            shrink = jnp.exp2(old - peak)
-        top[...] = peak
-        probs = jnp.concatenate([jnp.exp2(term - peak).astype(bf16) for term in terms], axis=0)
+        terms = [masked_scores(kb - i, places[i], first and i == 0) for i in range(2)]
+        if bounded:
+            probs = [jnp.exp2(term).astype(bf16) for term in terms]
+        else:
+            peak = jnp.maximum(
+                jnp.max(terms[0], axis=0, keepdims=True), jnp.max(terms[1], axis=0, keepdims=True)
+            )
+            if not first:
+                old = top[...]
+                peak = jnp.maximum(old, peak)
+                shrink = jnp.exp2(old - peak)
+            top[...] = peak
+            probs = [jnp.exp2(term - peak).astype(bf16) for term in terms]
+        probs = jnp.concatenate(probs, axis=0)
         vt = jnp.concatenate([vt_ref[:, places[0]], vt_ref[:, places[1]]], axis=1)
         for head in range(2):
             cols = slice(head * BLK, (head + 1) * BLK)
             left = jnp.concatenate([vt[head * HD : (head + 1) * HD], ones], axis=0)
             part = jnp.dot(left, probs[:, cols], preferred_element_type=f32)
-            acc[head] = part if first else acc[head] * shrink[:, cols] + part
-
-    visit(qb, True)
-
-    def more(i, carry):
-        visit(qb - 2 * i, False)
-        return carry
-
-    lax.fori_loop(1, (qb - tab_ref[0, qb]) // 2 + 1, more, 0)
+            if first:
+                acc[head] = part
+            elif bounded:
+                acc[head] += part
+            else:
+                acc[head] = acc[head] * shrink[:, cols] + part
+
+    def all_visits(bounded):
+        visit(qb, True, bounded)
+
+        def more(i, carry):
+            visit(qb - 2 * i, False, bounded)
+            return carry
+
+        lax.fori_loop(1, (qb - tab_ref[0, qb]) // 2 + 1, more, 0)
+
+    small = tab_ref[3, 0] > 0
+
+    @pl.when(small)
+    def _():
+        top[...] = jnp.zeros_like(top)
+        all_visits(True)
+
+    pl.when(jnp.logical_not(small))(lambda: all_visits(False))
     total = jnp.concatenate([acc[0, HD : HD + 1], acc[1, HD : HD + 1]], axis=1)
     lse_ref[0] = top[...] + jnp.log2(total)
     heads = jnp.concatenate([acc[h, :HD] / acc[h, HD : HD + 1] for h in range(2)], axis=0)
@@ -133,12 +153,20 @@
     )(tab, qt, start, k, vt)
 
 
+def split_heads(block):
+    lane = lax.broadcasted_iota(jnp.int32, block.shape, 1)
+    zero = jnp.zeros_like(block)
+    first = lane < HD
+    return jnp.concatenate([jnp.where(first, block, zero), jnp.where(first, zero, block)], axis=0)
+
+
 def attend_back_kernel(
-    tab_ref, k_ref, kt_ref, v_ref, u_ref, w_ref, qt_ref, start_ref, do_ref, ot_ref, lse_ref,
-    gain_ref, bias_ref, dh_ref, gw_ref, gn_ref, dqt, dkt, dvt, dot, delta, total, sums,
+    tab_ref, k_ref, kt_ref, v_ref, ut_ref, w_ref, qt_ref, start_ref, do_ref, ot_ref, lse_ref,
+    gain_ref, bias_ref, dh_ref, gw_ref, gn_ref, dqt, dk_acc, dv_acc, dot, dom, qm, delta, total, sums,
 ):
     kb = pl.program_id(0)
-    blocks = pl.num_programs(0)
+    blocks = pl.num_programs(0) - 1
+    now, before = kb % 2, (kb + 1) % 2
     row = lax.broadcasted_iota(jnp.int32, (BLK, 2 * BLK), 0)
 
     def at(qb):
@@ -148,10 +176,15 @@
     def _():
         total[...] = jnp.zeros_like(total)
         sums[...] = jnp.zeros_like(sums)
+        dk_acc[1] = jnp.zeros(dk_acc.shape[1:], f32)
+        dv_acc[1] = jnp.zeros(dv_acc.shape[1:], f32)
 
         def prepare(qb, carry):
             dqt[qb] = jnp.zeros((PAIR, BLK), f32)
-            turned = do_ref[at(qb), :].astype(f32).T
+            d_out = do_ref[at(qb), :]
+            dom[qb] = split_heads(d_out)
+            qm[qb] = split_heads(qt_ref[:, at(qb)].T)
+            turned = d_out.astype(f32).T
             dot[qb] = turned.astype(bf16)
             both = turned * ot_ref[qb]
             delta[qb] = jnp.concatenate(
@@ -181,62 +214,77 @@
             allowed = allowed & (row <= jnp.bitwise_and(col, BLK - 1))
         pt = jnp.exp2(jnp.where(allowed, st - lse_ref[qb], mask_fill))
         dst = (pt * (dpt - delta[qb])).astype(bf16)
-        pt = pt.astype(bf16)
+        part_v = jnp.dot(pt.astype(bf16), dom[qb], preferred_element_type=f32)
+        part_k = jnp.dot(dst, qm[qb], preferred_element_type=f32)
+        if diagonal:
+            dv_acc[now] = part_v
+            dk_acc[now] = part_k
+        else:
+            dv_acc[now] += part_v
+            dk_acc[now] += part_k
         for head in range(2):
             mine = slice(head * HD, (head + 1) * HD)
             cols = slice(head * BLK, (head + 1) * BLK)
-            part_v = contract(d_out[mine], pt[:, cols], 1, 1)
-            part_k = contract(qt[mine], dst[:, cols], 1, 1)
-            if diagonal:
-                dvt[mine] = part_v
-                dkt[mine] = part_k
-            else:
-                dvt[mine] += part_v
-                dkt[mine] += part_k
             dqt[qb, mine] += jnp.dot(kt[mine], dst[:, cols], preferred_element_type=f32)
 
-    tile(kb, True)
-
-    def visit(qb, carry):
-        tile(qb, False)
-        return carry
-
-    lax.fori_loop(kb + 1, tab_ref[1, kb] + 1, visit, 0)
-    dq = (dqt[kb] * SCORE_SCALE).T.astype(bf16)
-    dk = (dkt[...] * LN2).T.astype(bf16)
-    joined = jnp.concatenate([dq, dk, dvt[...].T.astype(bf16)], axis=1)
-    dh_ref[...] = contract(joined, w_ref[...], 1, 1).astype(bf16)
-    total[...] += contract(u_ref[...], joined, 0, 0)
-    sums[...] += jnp.sum(joined.astype(f32), axis=0, keepdims=True)
-
-    @pl.when(kb == blocks - 1)
+    def close():
+        block = jnp.maximum(kb - 1, 0)
+        dq = (dqt[block] * SCORE_SCALE).T
+        joined = jnp.concatenate([dq, dk_acc[before] * LN2, dv_acc[before]], axis=1)
+        if_any = jnp.where(kb == 0, 0.0, 1.0)
+        joined = (joined * if_any).astype(bf16)
+        dh_ref[...] = contract(joined, w_ref[...], 1, 1).astype(bf16)
+        total[...] += jnp.dot(ut_ref[...], joined, preferred_element_type=f32)
+        sums[...] += jnp.sum(joined.astype(f32), axis=0, keepdims=True)
+
+    @pl.when(kb < blocks)
     def _():
+        close()
+        tile(kb, True)
+        last = tab_ref[1, kb]
+
+        def visit(i, carry):
+            tile(kb + 1 + 2 * i, False)
+            tile(kb + 2 + 2 * i, False)
+            return carry
+
+        lax.fori_loop(0, (last - kb) // 2, visit, 0)
+
+        @pl.when((last - kb) % 2 == 1)
+        def _():
+            tile(last, False)
+
+    @pl.when(kb == blocks)
+    def _():
+        close()
         shard = gw_ref.shape[1]
         for j in range(gw_ref.shape[0]):
             part = pl.ds(j * shard, shard)
-            gw_ref[j] = (total[part] * gain_ref[part] + bias_ref[part] * sums[...]).astype(bf16)
+            gain, bias = (
+                jnp.broadcast_to(ref[:, part], (shard, shard)).T[:, :1] for ref in (gain_ref, bias_ref)
+            )
+            gw_ref[j] = (total[part] * gain + bias * sums[...]).astype(bf16)
             w = w_ref[part].astype(f32)
             for i, term in enumerate((w * total[part], w * sums[...])):
                 column = jnp.sum(term, axis=1, keepdims=True)
                 gn_ref[i : i + 1, part] = jnp.broadcast_to(column, (shard, shard)).T[:1]
 
 
-def attend_back(tab, k, kt, v, unit, weight, qt, start, d_out, ot, lse, gain, bias, shards):
+def attend_back(tab, k, kt, v, unit_t, weight, qt, start, d_out, ot, lse, gain, bias, shards):
     count = k.shape[0]
-    width = unit.shape[1]
+    width = unit_t.shape[0]
     shard = width // shards
-    gain, bias = gain.reshape(width, 1), bias.reshape(width, 1)
     blocks = count // BLK
     return pl.pallas_call(
         attend_back_kernel,
         grid_spec=pltpu.PrefetchScalarGridSpec(
             num_scalar_prefetch=1,
-            grid=(blocks,),
+            grid=(blocks + 1,),
             in_specs=[
-                pl.BlockSpec((BLK, PAIR), lambda b, t: (t[2, b], 0)),
-                pl.BlockSpec((PAIR, BLK), lambda b, t: (0, t[2, b])),
-                pl.BlockSpec((BLK, PAIR), lambda b, t: (t[2, b], 0)),
-                pl.BlockSpec((BLK, width), lambda b, t: (t[2, b], 0)),
+                pl.BlockSpec((BLK, PAIR), lambda b, t: (t[2, jnp.minimum(b, blocks - 1)], 0)),
+                pl.BlockSpec((PAIR, BLK), lambda b, t: (0, t[2, jnp.minimum(b, blocks - 1)])),
+                pl.BlockSpec((BLK, PAIR), lambda b, t: (t[2, jnp.minimum(b, blocks - 1)], 0)),
+                pl.BlockSpec((width, BLK), lambda b, t: (0, t[2, jnp.maximum(b - 1, 0)])),
                 whole(weight.shape),
                 whole(qt.shape),
                 whole(start.shape),
@@ -247,15 +295,17 @@
                 whole(bias.shape),
             ],
             out_specs=[
-                pl.BlockSpec((BLK, width), lambda b, t: (t[2, b], 0)),
+                pl.BlockSpec((BLK, width), lambda b, t: (t[2, jnp.maximum(b - 1, 0)], 0)),
                 whole((shards, shard, 3 * PAIR)),
                 whole((2, width)),
             ],
             scratch_shapes=[
                 pltpu.VMEM((blocks, PAIR, BLK), f32),
-                pltpu.VMEM((PAIR, BLK), f32),
-                pltpu.VMEM((PAIR, BLK), f32),
+                pltpu.VMEM((2, BLK, PAIR), f32),
+                pltpu.VMEM((2, BLK, PAIR), f32),
                 pltpu.VMEM((blocks, PAIR, BLK), bf16),
+                pltpu.VMEM((blocks, 2 * BLK, PAIR), bf16),
+                pltpu.VMEM((blocks, 2 * BLK, PAIR), bf16),
                 pltpu.VMEM((blocks, 1, 2 * BLK), f32),
                 pltpu.VMEM(weight.shape, f32),
                 pltpu.VMEM((1, 3 * PAIR), f32),
@@ -267,7 +317,7 @@
             jax.ShapeDtypeStruct((2, width), f32),
         ],
         name="attend_back",
-    )(tab, k, kt, v, unit, weight, qt, start, d_out, ot, lse, gain, bias)
+    )(tab, k, kt, v, unit_t, weight, qt, start, d_out, ot, lse, gain, bias)
 
 
 def layer_norm(values, gain_vec, offset):
@@ -637,15 +687,16 @@
 
 
 HEAD_CHUNK = 128
+SAFE_SCORE = 80.0
 
 
 def head_kernel(
-    x_in_ref, dy_in_ref, docs_in_ref, order_ref, vec_in_ref, wq_ref, wo_ref, wu_ref, wd_ref,
-    qt_ref, k_ref, kt_ref, v_ref, vt_ref, u_ref, own_ref, wh_ref, vec_ref, ub_ref, start_ref, tab_ref,
-    wo_all, wu_all, wd_all, dy_ref,
-    rows, docs, docs_true, vec_all, wo_tmp, wu_tmp, wd_tmp,
+    x_in_ref, dy_in_ref, docs_in_ref, order_ref, g1_ref, b1_ref, g2_ref, b2_ref, ob_ref, db_ref, ub_in_ref, wq_ref, wo_ref, wu_ref, wd_ref,
+    qt_ref, k_ref, kt_ref, v_ref, vt_ref, ut_ref, own_ref, wo_all, wu_all, wd_all, dy_ref,
+    wh_ref, vec_ref, ub_ref, start_ref, tab_ref,
+    qt_buf, k_buf, kt_buf, v_buf, vt_buf, ut_buf, rows, docs, docs_true, norms, vec_in_ref, vec_all, wo_tmp, wu_tmp, wd_tmp,
     z_s, z_r, x_s, x_r, c_s, c_r, f_s, f_r, docs_s, docs_r, vec_s, vec_r, wh_s, wh_r, wh_l,
-    y_s, y_r, n_s, n_r, o_s, o_r, load_sem, put_sem, self_sem, d_s, d_r, d_self,
+    y_s, y_r, n_s, n_r, o_s, o_r, load_sem, put_sem, self_sem, d_s, d_r, d_self, out_sem,
 ):
     z, x, y, c = (lax.axis_index(name) for name in AXES)
     odd, upper = lax.rem(z, 2), lax.div(z, 2)
@@ -658,13 +709,18 @@
     block = [odd, 1 - odd]
     stay = (c == upper) & (odd == c)
     leave = jnp.logical_not(stay)
+    for i, ref in enumerate((g1_ref, b1_ref, g2_ref, b2_ref, ob_ref, db_ref, ub_in_ref)):
+        vec_in_ref[i : i + ref.shape[0]] = ref[...]
     greet([by_core, by_x, by_y, by_yc, home[1], target[1]], [home[0], target[0]], leave)
 
+    def order_of(i):
+        return i % 2 * per_turn + i // 2
+
     def piece(i):
-        turn, row = i // per_turn, (i % per_turn) * HEAD_CHUNK
+        turn, row = order_of(i) // per_turn, (order_of(i) % per_turn) * HEAD_CHUNK
         return (
             x_in_ref.at[block[turn], 0, pl.ds(row, HEAD_CHUNK)],
-            rows.at[0, pl.ds(i * HEAD_CHUNK, HEAD_CHUNK)],
+            rows.at[0, pl.ds(order_of(i) * HEAD_CHUNK, HEAD_CHUNK)],
         )
 
     for turn in range(2):
@@ -680,41 +736,30 @@
             start_docs()
     for i in range(chunks):
         src, dst = piece(i)
-        if i < per_turn:
-            pl.when(stay)(lambda: pltpu.make_async_copy(src, dst, self_sem.at[i]).start())
+        if i % 2 == 0:
+            pl.when(stay)(lambda: pltpu.make_async_copy(src, dst, self_sem.at[i // 2]).start())
             pl.when(leave)(lambda: send(src, dst, z_s, z_r, i, target[0]) and None)
         else:
             send(src, dst, z_s, z_r, i, target[1])
 
     def piece_dy(i):
-        turn, row = i // per_turn, (i % per_turn) * HEAD_CHUNK
-        return (
-            dy_in_ref.at[block[turn], 0, pl.ds(row, HEAD_CHUNK)],
-            dy_ref.at[pl.ds(i * HEAD_CHUNK, HEAD_CHUNK)],
-        )
+        part = pl.ds(i * HEAD_CHUNK, HEAD_CHUNK)
+        return dy_in_ref.at[odd, 0, part], dy_ref.at[part]
 
     def send_dy(i):
         src, dst = piece_dy(i)
-        if i < per_turn:
-            pl.when(stay)(lambda: pltpu.make_async_copy(src, dst, d_self.at[i]).start())
-            pl.when(leave)(lambda: send(src, dst, d_s, d_r, i, target[0]) and None)
-        else:
-            send(src, dst, d_s, d_r, i, target[1])
+        pl.when(stay)(lambda: pltpu.make_async_copy(src, dst, d_self.at[i]).start())
+        pl.when(leave)(lambda: send(src, dst, d_s, d_r, i, target[0]) and None)
 
     def land_dy(i):
         src, dst = piece_dy(i)
-
-        def remote():
-            pltpu.make_async_remote_copy(
+        pl.when(stay)(lambda: pltpu.make_async_copy(src, dst, d_self.at[i]).wait())
+        pl.when(leave)(
+            lambda: pltpu.make_async_remote_copy(
                 src_ref=src, dst_ref=dst, send_sem=d_s.at[i], recv_sem=d_r.at[i],
-                device_id=target[i // per_turn], device_id_type=MESH,
+                device_id=target[0], device_id_type=MESH,
             ).wait()
-
-        if i < per_turn:
-            pl.when(stay)(lambda: pltpu.make_async_copy(src, dst, d_self.at[i]).wait())
-            pl.when(leave)(remote)
-        else:
-            remote()
+        )
 
     def landed(src, dst, sems, recv_sems, index, turn, self_index):
         def remote():
@@ -794,26 +839,6 @@
         slots = jnp.where(lane == order_ref[stored], t, slots)
 
     docs_copy = {}
-    for turn in range(2):
-        landed(docs_in_ref.at[block[turn]], docs.at[0, turn], docs_s, docs_r, turn, turn, per_turn)
-    docs_copy["x"] = send(docs.at[0], docs.at[1], docs_s, docs_r, 2, by_x)
-    docs_copy["c"] = send(docs.at[0], docs.at[2], docs_s, docs_r, 3, by_core)
-
-    for copy in vec_copy:
-        copy.wait()
-    vec_width = vec_in_ref.shape[1]
-    for j in range(4):
-        for i in range(6):
-            vec_ref[i : i + 1, j * vec_width : (j + 1) * vec_width] = vec_all[j, i : i + 1].astype(f32)
-        for i in range(4):
-            at = (4 * j + i) * vec_width
-            ub_ref[:, at : at + vec_width] = vec_all[j, 6 + i : 7 + i].astype(f32)
-    vec_ref[6:8] = jnp.zeros((2, width), f32)
-    for copy in wh_copy:
-        copy.wait()
-
-    docs_copy["x"].wait()
-    docs_copy["f"] = send(docs.at[1], docs.at[3], docs_s, docs_r, 4, by_core)
 
     def finish_docs():
         docs_copy["c"].wait()
@@ -840,42 +865,94 @@
             high = high + (low[:, b : b + 1] <= lane).astype(jnp.int32)
         tab_ref[...] = jnp.concatenate([low, high, slots, jnp.zeros((5, 128), jnp.int32)], axis=0)
 
+    def docs_first():
+        for turn in range(2):
+            landed(docs_in_ref.at[block[turn]], docs.at[0, turn], docs_s, docs_r, turn, turn, per_turn)
+        docs_copy["x"] = send(docs.at[0], docs.at[1], docs_s, docs_r, 2, by_x)
+        docs_copy["c"] = send(docs.at[0], docs.at[2], docs_s, docs_r, 3, by_core)
+
+
+    def vectors_and_weight():
+        for copy in vec_copy:
+            copy.wait()
+        vec_width = vec_in_ref.shape[1]
+        for j in range(4):
+            for i in range(6):
+                vec_ref[i : i + 1, j * vec_width : (j + 1) * vec_width] = vec_all[j, i : i + 1].astype(f32)
+            for i in range(4):
+                at = (4 * j + i) * vec_width
+                ub_ref[:, at : at + vec_width] = vec_all[j, 6 + i : 7 + i].astype(f32)
+        vec_ref[6:8] = jnp.zeros((2, width), f32)
+        for copy in wh_copy:
+            copy.wait()
+
+
+    def docs_second():
+        docs_copy["x"].wait()
+        docs_copy["f"] = send(docs.at[1], docs.at[3], docs_s, docs_r, 4, by_core)
+
+
     x_copy, c_copy, f_copy = [], [], []
 
     def relay(i):
         src, dst = piece(i)
-        landed(src, dst, z_s, z_r, i, i // per_turn, i)
-        part = pl.ds(i * HEAD_CHUNK, HEAD_CHUNK)
+        landed(src, dst, z_s, z_r, i, i % 2, i // 2)
+        part = pl.ds(order_of(i) * HEAD_CHUNK, HEAD_CHUNK)
         x_copy.append(send(rows.at[0, part], rows.at[1, part], x_s, x_r, i, by_x))
         c_copy.append(send(rows.at[0, part], rows.at[2, part], c_s, c_r, i, by_core))
 
     def relay_far(i):
         x_copy[i].wait()
-        part = pl.ds(i * HEAD_CHUNK, HEAD_CHUNK)
+        part = pl.ds(order_of(i) * HEAD_CHUNK, HEAD_CHUNK)
         f_copy.append(send(rows.at[1, part], rows.at[3, part], f_s, f_r, i, by_core))
+
+    streams = (
+        (qt_buf, qt_ref, 1), (k_buf, k_ref, 0), (kt_buf, kt_ref, 1), (v_buf, v_ref, 0), (vt_buf, vt_ref, 1),
+        (ut_buf, ut_ref, 1),
+    )
 
     def compute(g, i):
         count = rows.shape[1]
-        unit, _ = norm_parts(rows[g, i * HEAD_CHUNK : (i + 1) * HEAD_CHUNK].astype(f32))
-        at = slice(g * count + i * HEAD_CHUNK, g * count + (i + 1) * HEAD_CHUNK)
-        u_ref[at] = unit.astype(bf16)
+        chunk = order_of(i)
+        unit, _ = norm_parts(rows[g, chunk * HEAD_CHUNK : (chunk + 1) * HEAD_CHUNK].astype(f32))
+        at = pl.ds(g * count + chunk * HEAD_CHUNK, HEAD_CHUNK)
+        ut_buf[:, at] = unit.astype(bf16).T
         low = (unit * vec_ref[0:1] + vec_ref[1:2]).astype(bf16)
         qkv = jnp.dot(low, wh_ref[...], preferred_element_type=f32)
-        qt_ref[:, at] = (qkv[:, :PAIR] * (SCORE_SCALE * LOG2E)).astype(bf16).T
+        qt = (qkv[:, :PAIR] * (SCORE_SCALE * LOG2E)).astype(bf16).T
+        qt_buf[:, at] = qt
         k = qkv[:, PAIR : 2 * PAIR].astype(bf16)
         v = qkv[:, 2 * PAIR :].astype(bf16)
-        k_ref[at] = k
-        v_ref[at] = v
-        kt_ref[:, at] = k.T
-        vt_ref[:, at] = v.T
-
+        k_buf[at] = k
+        v_buf[at] = v
+        kt = k.T
+        kt_buf[:, at] = kt
+        vt_buf[:, at] = v.T
+        found = []
+        for block_ in (qt, kt):
+            squares = block_.astype(f32) * block_.astype(f32)
+            found += [jnp.sum(squares[head * HD : (head + 1) * HD], axis=0, keepdims=True) for head in range(2)]
+        found = jnp.concatenate(found, axis=0)
+        norms[...] = found if g == 0 and i == 0 else jnp.maximum(norms[...], found)
+        for index, (source, out, columns) in enumerate(streams):
+            if columns:
+                source, out = source.at[:, at], out.at[:, at]
+            else:
+                source, out = source.at[at], out.at[at]
+            pltpu.make_async_copy(source, out, out_sem.at[index]).start()
+
+    docs_first()
     for i in range(chunks + 2):
         if i < chunks:
-            send_dy(i)
+            if i < per_turn:
+                send_dy(i)
             relay(i)
-            compute(0, i)
+        if i == 0:
+            vectors_and_weight()
+            docs_second()
         if 1 <= i <= chunks:
             relay_far(i - 1)
+            compute(0, i - 1)
             compute(1, i - 1)
             c_copy[i - 1].wait()
             compute(2, i - 1)
@@ -888,16 +965,24 @@
             put(i - 2)
         if i >= 3 and i - 3 < len(parts):
             forward(i - 3)
-    own_ref[...] = rows[0]
+        if i == chunks - 1:
+            own_copy = pltpu.make_async_copy(rows.at[0], own_ref, out_sem.at[len(streams)])
+            own_copy.start()
+    largest = jnp.max(norms[...], axis=1, keepdims=True)
+    bound = jnp.maximum(largest[0:1] * largest[2:3], largest[1:2] * largest[3:4])
+    tab_ref[3:4] = jnp.broadcast_to((bound <= SAFE_SCORE * SAFE_SCORE).astype(jnp.int32), (1, 128))
     for i in range(chunks - 1, len(parts)):
         forward(i)
+    for index, (source, out, _) in enumerate(streams):
+        pltpu.make_async_copy(source, out, out_sem.at[index]).wait()
+    own_copy.wait()
     for copy in n_copy + put_copy + o_copy:
         copy.wait()
-    for i in range(chunks):
+    for i in range(per_turn):
         land_dy(i)
 
 
-def head(x_in, dy_in, docs_in, order, vec_in, w_qkv, w_out, w_up, w_down):
+def head(x_in, dy_in, docs_in, order, vectors, w_qkv, w_out, w_up, w_down):
     width = x_in.shape[-1]
     count = 2 * x_in.shape[2]
     total = 4 * count
@@ -909,31 +994,39 @@
     dma, buf, shape = pltpu.SemaphoreType.DMA, pltpu.VMEM, jax.ShapeDtypeStruct
     return pl.pallas_call(
         head_kernel,
-        in_specs=[any_, any_, vmem, smem, vmem, any_, any_, any_, any_],
-        out_specs=[vmem] * 12 + [any_] * 4,
+        in_specs=[any_, any_, vmem, smem] + [vmem] * 7 + [any_] * 4,
+        out_specs=[any_] * 11 + [vmem] * 5,
         out_shape=[
             shape((PAIR, total), bf16),
             shape((total, PAIR), bf16),
             shape((PAIR, total), bf16),
             shape((total, PAIR), bf16),
             shape((PAIR, total), bf16),
-            shape((total, width), bf16),
+            shape((width, total), bf16),
             shape((count, width), bf16),
+            shape((4 * w_out.shape[0], w_out.shape[1]), bf16),
+            shape((4 * w_up.shape[0], w_up.shape[1]), bf16),
+            shape((4 * w_down.shape[0], w_down.shape[1]), bf16),
+            shape((count // 2, width), bf16),
             shape((width, 3 * PAIR), bf16),
             shape((8, width), f32),
             shape((1, 4 * w_down.shape[0]), f32),
             shape((blocks, 1, BLK), jnp.int32),
             shape((8, 128), jnp.int32),
-            shape((4 * w_out.shape[0], w_out.shape[1]), bf16),
-            shape((4 * w_up.shape[0], w_up.shape[1]), bf16),
-            shape((4 * w_down.shape[0], w_down.shape[1]), bf16),
-            shape((count, width), bf16),
         ],
         scratch_shapes=[
+            buf((PAIR, total), bf16),
+            buf((total, PAIR), bf16),
+            buf((PAIR, total), bf16),
+            buf((total, PAIR), bf16),
+            buf((PAIR, total), bf16),
+            buf((width, total), bf16),
             buf((4, count, width), bf16),
             buf((4, 2) + docs_in.shape[1:], jnp.int32),
             buf((blocks // 2,) + docs_in.shape[1:], jnp.int32),
-            buf((4,) + vec_in.shape, bf16),
+            buf((4, HEAD_CHUNK), f32),
+            buf((16, shard), bf16),
+            buf((4, 16, shard), bf16),
             buf(w_out.shape, bf16),
             buf(w_up.shape, bf16),
             buf(w_down.shape, bf16),
@@ -941,22 +1034,22 @@
         + [dma((chunks,))] * 8
         + [dma((5,)), dma((5,)), dma((3,)), dma((3,)), dma((9,)), dma((9,)), dma((3,))]
         + [dma((9,)), dma((9,)), dma((3,)), dma((3,)), dma((9,)), dma((9,)), dma((3,)), dma((3,))]
-        + [dma((chunks // 2 + 1,)), dma((chunks,)), dma((chunks,)), dma((chunks // 2,))],
+        + [dma((chunks // 2 + 1,)), dma((chunks // 2,))] + [dma((chunks // 2,))] * 2 + [dma((7,))],
         compiler_params=pltpu.CompilerParams(
             collective_id=1, has_side_effects=True, vmem_limit_bytes=56 * 1024 * 1024
         ),
         name="head",
-    )(x_in, dy_in, docs_in, order, vec_in, w_qkv, w_out, w_up, w_down)
+    )(x_in, dy_in, docs_in, order, *[v.reshape(-1, shard) for v in vectors], w_qkv, w_out, w_up, w_down)
 FF_TILE = 512
 PIECES = 3
 feed_steps = 4
 
 
 def feed_kernel(
-    o_ref, x_ref, dy_ref, wo_ref, wu_ref, wd_ref, vec_ref, ub_ref,
+    o_ref, x_ref, dy_near_ref, dy_in_ref, wo_ref, wu_ref, wd_ref, vec_ref, ub_ref,
     do_ref, y_home, dmid_ref, keep_ref, to_y_ref, to_x_ref, to_xy_ref, gvec_ref, gub_ref,
     attn_all, gd_ref, gu_ref, go_ref, attn_in, do_out, y_out, grad_ref, grad_in,
-    a_s, a_r, a_l, d_s, d_r, d_l, y_s, y_r, y_l, g_s, g_r,
+    dy_ref, dy_far, a_s, a_r, a_l, d_s, d_r, d_l, y_s, y_r, y_l, g_s, g_r, c_s, c_r,
 ):
     step = pl.program_id(0)
     steps = pl.num_programs(0)
@@ -1010,6 +1103,13 @@
             send_sem=g_s.at[i], recv_sem=g_r.at[i], device_id=mates[2], device_id_type=MESH,
         )
 
+    def dy_copy(i):
+        part = pl.ds(i * tile, tile)
+        return pltpu.make_async_remote_copy(
+            src_ref=dy_in_ref.at[1 - odd, 0, part], dst_ref=dy_far.at[part],
+            send_sem=c_s.at[i], recv_sem=c_r.at[i], device_id=origin[1], device_id_type=MESH,
+        )
+
     @pl.when(step == 0)
     def _():
         greet(mates[1:] + [home[1], origin[1]], [home[0], origin[0]], leave)
@@ -1017,11 +1117,22 @@
             for g in (1, 3, 2):
                 attn_copy(g, i).start()
             attn_own(i).start()
+        for i in range(half):
+            dy_copy(i).start()
 
     @pl.when(step == 0)
     def _():
         for ref in (gd_ref, gu_ref, go_ref, gvec_ref, gub_ref):
             ref[...] = jnp.zeros_like(ref)
+
+    @pl.when(step < half)
+    def _():
+        dy_ref[...] = dy_near_ref[...]
+
+    @pl.when(step >= half)
+    def _():
+        dy_copy(step - half).wait()
+        dy_ref[...] = dy_far[pl.ds(pl.multiple_of((step - half) * tile, tile), tile)]
 
     attn_own(step).wait()
     for g in range(1, groups):
@@ -1134,7 +1245,7 @@
                 ).astype(bf16)
 
 
-def feed(o, x, dy, w_out, w_up, w_down, vecs, up_bias, shards):
+def feed(o, x, dy_near, dy_in, w_out, w_up, w_down, vecs, up_bias, shards):
     groups, count, _ = o.shape
     width = x.shape[1]
     flat = (w_out.size + w_up.size + w_down.size) // shards // width
@@ -1147,7 +1258,7 @@
         feed_kernel,
         grid=(feed_steps,),
         in_specs=[
-            any_, rows, rows, whole(w_out.shape), whole(w_up.shape), whole(w_down.shape),
+            any_, rows, pl.BlockSpec((tile, width), lambda i: (jnp.minimum(i, feed_steps // 2 - 1), 0)), any_, whole(w_out.shape), whole(w_up.shape), whole(w_down.shape),
             whole(vecs.shape), whole(up_bias.shape),
         ],
         out_specs=[any_, any_, rows] + [whole(piece)] * 4 + [whole(vecs.shape), whole(up_bias.shape)],
@@ -1172,6 +1283,8 @@
             buf((feed_steps, tile, width), bf16),
             buf((shards, flat, width), bf16),
             buf((2, flat, width), bf16),
+            buf((tile, width), bf16),
+            buf((count // 2, width), bf16),
             dma((3, feed_steps)),
             dma((3, feed_steps)),
             dma((feed_steps,)),
@@ -1183,25 +1296,27 @@
             dma((feed_steps,)),
             dma((2,)),
             dma((2,)),
+            dma((feed_steps // 2,)),
+            dma((feed_steps // 2,)),
         ],
         compiler_params=pltpu.CompilerParams(
             collective_id=3, has_side_effects=True, vmem_limit_bytes=60 * 1024 * 1024
         ),
         name="feed",
-    )(o, x, dy, w_out, w_up, w_down, vecs, up_bias)
+    )(o, x, dy_near, dy_in, w_out, w_up, w_down, vecs, up_bias)
 
 
 TAIL_CHUNK = 128
 
 
 def tail_kernel(
-    dh_ref, x_ref, dmid_ref, gain_ref, keep_ref, from_y_ref, from_x_ref, from_xy_ref, gw_ref, small_ref,
-    dx_ref, gd_ref, gu_ref, go_ref, gq_ref, gvec_ref, gub_ref,
-    core_buf, own_dh, x_out, x_buf, dx_out, home_buf,
-    gsum, gz1s, gz1r, gz2s, gz2r, gfull,
-    wy, ws, wz1s, wz1r, wz2s, wz2r, wfull, wall,
-    small_out, small_in,
-    local_sem, self_sem, core_s, core_r, x_s, x_r, home_s, home_r, g_s, g_r, w_s, w_r, s_s, s_r,
+    dh_ref, x_hbm, dmid_hbm, gain_ref, keep_ref, from_y_ref, from_x_ref, from_xy_ref, gw_ref, gn_ref, gvecs_ref, gub_ref,
+    home_buf, gfull, wall, sum_ref,
+    x_ref, dmid_ref, core_buf, own_dh, x_out, x_buf, dx_out,
+    gsum, gz1s, gz1r, gz2s, gz2r,
+    wy, ws, wz1s, wz1r, wz2s, wz2r, wfull,
+    small_ref, small_out, small_in,
+    local_sem, self_sem, core_s, core_r, x_s, x_r, home_s, home_r, g_s, g_r, w_s, w_r, s_s, s_r, in_sem,
 ):
     z, x, y, c = (lax.axis_index(name) for name in AXES)
     odd, upper = lax.rem(z, 2), lax.div(z, 2)
@@ -1213,6 +1328,18 @@
     home = [{"z": 2 * c + upper, "c": odd}, {"z": 2 * c + 1 - upper, "c": odd}]
     origin = [{"z": 2 * odd + c, "c": upper}, {"z": 2 * (1 - odd) + c, "c": upper}]
     stay = (c == upper) & (odd == c)
+    inputs = [
+        pltpu.make_async_copy(x_hbm, x_ref, in_sem.at[0]), pltpu.make_async_copy(dmid_hbm, dmid_ref, in_sem.at[1])
+    ]
+    for copy in inputs:
+        copy.start()
+    small_ref[...] = jnp.zeros_like(small_ref)
+    small_ref[0:2] = gn_ref[...]
+    small_ref[2:4] = gvecs_ref[1:3]
+    small_ref[4:5] = gvecs_ref[0:1]
+    small_ref[5:6] = gvecs_ref[3:4]
+    for i in range(4):
+        small_ref[6 + i : 7 + i] = gub_ref[:, i * width : (i + 1) * width]
     greet(
         [by_core, by_x, by_y, by_xc, by_z1, by_z2, home[1], origin[1]],
         [home[0], origin[0]],
@@ -1322,6 +1449,9 @@
 
     def finish(i):
         part = pl.ds(i * TAIL_CHUNK, TAIL_CHUNK)
+        if i == 0:
+            for copy in inputs:
+                copy.wait()
         x_copy[i].wait()
         d_low = own_dh[0, part].astype(f32) + core_buf[0, part].astype(f32) + x_buf[part].astype(f32)
         unit, inv = norm_parts(x_ref[part].astype(f32))
@@ -1367,7 +1497,6 @@
             pl.when(jnp.logical_not(stay))(remote)
         else:
             remote()
-        dx_ref[block, pl.ds(row, TAIL_CHUNK)] = home_buf[block, pl.ds(row, TAIL_CHUNK)].astype(f32)
 
     g_start(0)
     add_core(0)
@@ -1414,36 +1543,14 @@
     w_copy["x"].wait()
     w_copy["xc"].wait()
     wall[2 * x + c] = wfull[c]
-    for pair in range(4):
-        for part in range(3):
-            gq_ref[:, part * width + pair * PAIR : part * width + (pair + 1) * PAIR] = wall[
-                pair, :, part * PAIR : (part + 1) * PAIR
-            ].astype(f32)
-    shard = go_ref.shape[0]
-    lanes = pl.ds(pl.multiple_of(shard * (2 * y + c), shard), shard)
-    for i in range(6):
-        gvec_ref[i : i + 1, :] = small_out[4, i : i + 1, lanes]
-    gub_ref[...] = small_out[4, pl.ds(6 + 2 * y + c, 1), :]
+    sum_ref[...] = small_out[4]
     for i in range(chunks):
         arrive(i)
     for p in range(PIECES):
         g_copy["x", p].wait()
-    flat = gd_ref.shape[0] + (gu_ref.shape[1] // width + 1) * shard
-    for row in range(0, flat, 64):
-        p, rest = divmod(row, flat // PIECES)
-        side, inner = divmod(rest, flat // PIECES // 2)
-        value = gfull[p, side, inner : inner + 64].astype(f32)
-        if row < gd_ref.shape[0]:
-            gd_ref[row : row + 64] = value
-        elif row < flat - shard:
-            t, r = divmod(row - gd_ref.shape[0], shard)
-            gu_ref[r : r + 64, t * width : (t + 1) * width] = value
-        else:
-            r = row - (flat - shard)
-            go_ref[r : r + 64] = value
-
-
-def tail(dh, x, dmid, gain, keep, from_y, from_x, from_xy, gw, small, ff_shard):
+
+
+def tail(dh, x, dmid, gain, keep, from_y, from_x, from_xy, gw, gn, gvecs, gub):
     count, width = x.shape
     shard = gw.shape[1]
     half = count // 2
@@ -1454,30 +1561,27 @@
     buf = pltpu.VMEM
     return pl.pallas_call(
         tail_kernel,
-        in_specs=[pl.BlockSpec(memory_space=pl.ANY)] + [vmem] * 9,
-        out_specs=[vmem] * 7,
+        in_specs=[pl.BlockSpec(memory_space=pl.ANY)] * 3 + [vmem] * 9,
+        out_specs=[vmem] * 4,
         out_shape=[
-            jax.ShapeDtypeStruct((2, half, width), f32),
-            jax.ShapeDtypeStruct((ff_shard, width), f32),
-            jax.ShapeDtypeStruct((shard, 4 * ff_shard), f32),
-            jax.ShapeDtypeStruct((shard, width), f32),
-            jax.ShapeDtypeStruct((shard, 3 * width), f32),
-            jax.ShapeDtypeStruct((8, shard), f32),
-            jax.ShapeDtypeStruct((1, ff_shard), f32),
+            jax.ShapeDtypeStruct((2, half, width), bf16),
+            jax.ShapeDtypeStruct((PIECES, 2, sixth, width), bf16),
+            jax.ShapeDtypeStruct((4, shard, 3 * PAIR), bf16),
+            jax.ShapeDtypeStruct((16, width), f32),
         ],
         scratch_shapes=[
+            buf((count, width), bf16),
+            buf((count, width), f32),
             buf((2, count, width), bf16),
             buf((2, count, width), bf16),
             buf((count, width), bf16),
             buf((count, width), bf16),
             buf((count, width), bf16),
-            buf((2, half, width), bf16),
             buf((PIECES, sixth, width), f32),
             buf((PIECES, sixth // 2, width), bf16),
             buf((PIECES, sixth // 2, width), bf16),
             buf((PIECES, sixth // 4, width), bf16),
             buf((PIECES, sixth // 4, width), bf16),
-            buf((PIECES, 2, sixth, width), bf16),
             buf((2, shard, 3 * PAIR), bf16),
             buf((2, shard, 3 * PAIR), f32),
             buf((shard, 3 * PAIR), bf16),
@@ -1485,9 +1589,9 @@
             buf((shard // 2, 3 * PAIR), bf16),
             buf((shard // 2, 3 * PAIR), bf16),
             buf((2, shard, 3 * PAIR), bf16),
-            buf((4, shard, 3 * PAIR), bf16),
-            buf((5,) + small.shape, f32),
-            buf((5,) + small.shape, f32),
+            buf((16, width), f32),
+            buf((5, 16, width), f32),
+            buf((5, 16, width), f32),
             dma((chunks,)),
             dma((chunks // 2,)),
             dma((chunks,)),
@@ -1502,19 +1606,77 @@
             dma((8,)),
             dma((5,)),
             dma((5,)),
+            dma((2,)),
         ],
         compiler_params=pltpu.CompilerParams(
             collective_id=5, has_side_effects=True, vmem_limit_bytes=56 * 1024 * 1024
         ),
         name="tail",
-    )(dh, x, dmid, gain, keep, from_y, from_x, from_xy, gw, small)
-def stack_rows(members, width, count):
-    at, total = 0, 0
-    for member in members:
-        rows = member.reshape(-1, width)
-        total = total + jnp.pad(rows, ((at, count - at - rows.shape[0]), (0, 0)))
-        at += rows.shape[0]
-    return total
+    )(dh, x, dmid, gain, keep, from_y, from_x, from_xy, gw, gn, gvecs, gub)
+
+def results_kernel(
+    y_ref, dx_ref, down_ref, up_ref, out_ref, wall_ref, sum_ref,
+    y_out, dx_out, gd_ref, gu_ref, go_ref, gq_ref, *vectors,
+):
+    step = pl.program_id(0)
+    width = dx_ref.shape[-1]
+    y_out[:, 0] = y_ref[...]
+    dx_out[:, 0] = dx_ref[...].astype(f32)
+    gd_ref[...] = down_ref[...].astype(f32)
+    gu_ref[...] = up_ref[...].astype(f32)
+    go_ref[...] = out_ref[...].astype(f32)
+    for part in range(3):
+        at = pl.multiple_of(part * width + step * PAIR, PAIR)
+        gq_ref[:, pl.ds(at, PAIR)] = wall_ref[0, :, part * PAIR : (part + 1) * PAIR].astype(f32)
+    shard = go_ref.shape[0]
+    mine = 2 * lax.axis_index("y") + lax.axis_index("c")
+    for i in range(6):
+        vectors[i][...] = sum_ref[i : i + 1, pl.ds(pl.multiple_of(mine * shard, shard), shard)]
+    vectors[6][...] = sum_ref[pl.ds(6 + mine, 1), :]
+
+
+def results(y, dx, flat, wall, sums):
+    half, width = dx.shape[1:]
+    shard = wall.shape[1]
+    steps = 4
+    flat = flat.reshape(-1, width)
+    tokens = pl.BlockSpec((2, half // steps, width), lambda i: (0, i, 0))
+    tokens_out = pl.BlockSpec((2, 1, half // steps, width), lambda i: (0, 0, i, 0))
+    shape = jax.ShapeDtypeStruct
+    return pl.pallas_call(
+        results_kernel,
+        grid=(steps,),
+        in_specs=[
+            tokens,
+            tokens,
+            pl.BlockSpec((shard, width), lambda i: (i, 0)),
+            pl.BlockSpec((shard, width), lambda i: (steps + i, 0)),
+            pl.BlockSpec((shard, width), lambda i: (2 * steps, 0)),
+            pl.BlockSpec((1, shard, 3 * PAIR), lambda i: (i, 0, 0)),
+            whole(sums.shape),
+        ],
+        out_specs=[
+            tokens_out,
+            tokens_out,
+            pl.BlockSpec((shard, width), lambda i: (i, 0)),
+            pl.BlockSpec((shard, width), lambda i: (0, i)),
+            whole((shard, width)),
+            whole((shard, 3 * width)),
+        ]
+        + [whole((1, shard))] * 6
+        + [whole((1, width))],
+        out_shape=[
+            shape((2, 1, half, width), bf16),
+            shape((2, 1, half, width), f32),
+            shape((width, width), f32),
+            shape((shard, 4 * width), f32),
+            shape((shard, width), f32),
+            shape((shard, 3 * width), f32),
+        ]
+        + [shape((1, shard), f32)] * 6
+        + [shape((1, width), f32)],
+        name="results",
+    )(y, dx, flat, flat, flat, wall, sums)
 
 
 def place(z, x, y, c):
@@ -1547,33 +1709,30 @@
     inputs, out_grad, segment_ids, block_order, w_qkv, w_out, w_up, w_down,
     norm1_gain, norm1_bias, norm2_gain, norm2_bias, out_bias, up_bias, down_bias,
 ):
-    width = inputs.shape[3]
-    shard = norm1_gain.shape[0]
-    vectors = stack_rows(
-        [norm1_gain, norm1_bias, norm2_gain, norm2_bias, out_bias, down_bias, up_bias], shard, 16
-    )
+    vectors = (norm1_gain, norm1_bias, norm2_gain, norm2_bias, out_bias, down_bias, up_bias)
     (
-        qt, k, kt, v, vt, unit, own_x, w_heads, vecs, full_ubias, start, tab, full_out, full_up, full_down, own_dy
+        qt, k, kt, v, vt, unit, own_x, full_out, full_up, full_down, near_dy, w_heads, vecs, full_ubias, start, tab
     ) = head(
         inputs, out_grad, segment_ids.reshape(2, -1, 128), block_order, vectors, w_qkv, w_out, w_up, w_down
     )
     gain_one, bias_one = vecs[0:1], vecs[1:2]
     o, ot, lse = attend(tab, qt, start, k, vt)
     d_o, outputs, d_middle, keep, to_y, to_x, to_xy, g_vecs, g_ubias = feed(
-        o.reshape(4, -1, PAIR), own_x, own_dy, full_out, full_up, full_down, vecs, full_ubias, 4
+        o.reshape(4, -1, PAIR), own_x, near_dy, out_grad, full_out, full_up, full_down, vecs, full_ubias, 4
     )
     from_y, from_x, from_xy = swap(to_y, dy=1), swap(to_x, dx=1), swap(to_xy, dy=1, dx=1)
     dh, g_heads, g_norm = attend_back(
         tab, k, kt, v, unit, w_heads, qt, start, d_o.reshape(-1, PAIR), ot, lse, gain_one, bias_one, 4
     )
-    small = stack_rows([g_norm, g_vecs[1:3], g_vecs[0:1], g_vecs[3:4], g_ubias], width, 16)
-    dx, grad_down, grad_up, grad_out, grad_qkv, g_vec, g_ub = tail(
-        dh.reshape(4, -1, width), own_x, d_middle, gain_one, keep, from_y, from_x, from_xy,
-        g_heads, small, w_down.shape[0],
-    )
+    dx, flat, heads, sums = tail(
+        dh.reshape(4, -1, dh.shape[1]), own_x, d_middle, gain_one, keep, from_y, from_x, from_xy,
+        g_heads, g_norm, g_vecs, g_ubias,
+    )
+    outputs, input_grad, grad_down, grad_up, grad_out, grad_qkv, *vec = results(outputs, dx, flat, heads, sums)
+    vec = [member.reshape(-1) for member in vec]
     return (
-        outputs[:, None], dx[:, None], grad_qkv, grad_out, grad_up, grad_down,
-        g_vec[0], g_vec[1], g_vec[2], g_vec[3], g_vec[4], g_ub[0], g_vec[5],
+        outputs, input_grad, grad_qkv, grad_out, grad_up, grad_down,
+        vec[0], vec[1], vec[2], vec[3], vec[4], vec[6], vec[5],
     )
 
 

time: 268 us -> 233 us (0.87)
  Pallas kernels: 244 us -> 225 us
  local copies, waits for them, and re-layouts: 14.5 us -> 2.54 us
  other arithmetic: 4.05 us -> 0 us
    pallas_call x1, Pallas kernels: 49.7 us -> 36.2 us  [attend_back(): pl.pallas_call(attend_back_kernel, grid_spec=pltpu.PrefetchScalarGridSpec...]
    pallas_call x1, Pallas kernels: 26.4 us -> 19.4 us  [attend(): pl.pallas_call(attend_kernel, grid_spec=pltpu.PrefetchScalarGridSpec(num_...]
    unnamed x27 -> x6, local copies, waits for them, and re-layouts: 7.94 us -> 1.16 us
    add x2 -> x0, other arithmetic: 2.68 us -> none  [stack_rows(): total = total + jnp.pad(rows, ((at, count - at - rows.shape[0]), (0, 0)))]
    pallas_call x2 -> x3, Pallas kernels: 100 us -> 99.7 us  [the longest x1 47.2 us: feed(): pl.pallas_call(feed_kernel, grid=(feed_steps,), in_specs=[any_, rows, pl....]
  transfers between devices with their start and end apart: 3 -> 3, of which waited for: 0 -> 0; matrix products, arithmetic and copies ran while one was open for 3% -> 1% of each run, Pallas kernels for 19% -> 16%
where the time goes in v4:
time: 233 us; the launch traced here: 232 us
  Pallas kernels  225 us (97%)
  starting transfers between devices  3.55 us (2%)
  local copies, waits for them, and re-layouts  2.54 us (1%)
    pallas_call x1, Pallas kernels, tail(): pl.pallas_call(tail_kernel, in_specs=[pl.BlockSpec(memory_space=pl.ANY)]...  69.6 us
    pallas_call x1, Pallas kernels, feed(): pl.pallas_call(feed_kernel, grid=(feed_steps,), in_specs=[any_, rows, pl....  47.2 us
    pallas_call x1, Pallas kernels, head(): pl.pallas_call(head_kernel, in_specs=[any_, any_, vmem, smem] + [vmem] *...  47.1 us
    pallas_call x1, Pallas kernels, attend_back(): pl.pallas_call(attend_back_kernel, grid_spec=pltpu.PrefetchScalarGridSpec...  36.2 us
    pallas_call x1, Pallas kernels, attend(): pl.pallas_call(attend_kernel, grid_spec=pltpu.PrefetchScalarGridSpec(num_...  19.4 us
    pallas_call x1, Pallas kernels, results(): pl.pallas_call(results_kernel, grid=(steps,), in_specs=[tokens, tokens, p...  5.37 us
  transfers between devices with their start and end apart: 3, of which 0 were waited for; matrix products, arithmetic and copies ran while one was open for 1% of the time, Pallas kernels for 16%

profile of v4, /device:TPU:0, one launch (start us, length us, event | category | flops | bytes accessed | tf_op | source)
XLA Modules:
  0.0 231.8 jit_solution(8919757663538750490)
XLA Ops:
  0.7 47.1 %head.1 = (bf16[128,4096]{1,0:T(8,128)(2,1)}, bf16[4096,128]{1,0:T(8,128)(2,1)}, bf16[128,4096]{1,0:T(8,128)(2,1)}, bf16[4096,128]{1,0:T(8,128)(2,1)}, bf16[128,...) custom-call(bf16[2,1,512,512]{3,2,1,0:T(8,128)(2,1)} %x_in_ref.1, ...), custom_call_target="tpu_custom_call" | custom-call | tf_op jit(solution)/shard_map/head/pallas_call | solution.py:995
  47.8 19.4 %attend.1 = (bf16[4096,128]{1,0:T(8,128)(2,1)}, f32[16,128,256]{2,1,0:T(8,128)}, f32[16,1,512]{2,1,0:T(1,128)}) custom-call(s32[8,128]{1,0:T(8,128)} %get-tuple-element.61.tab_ref, bf16[128,4096]{1,0:T(8,128)(2,1)} %get-tuple-element.62.qt_ref, s32[16,1,256]{2,1,0:T(1,128)} %get-tuple-element.63.start_ref, bf16[4096,128]{1,0:T(8,128)(2,1)} %get-tuple-element.64.k_ref, ...), custom_call_target="tpu_custom_call" | custom-call | tf_op jit(solution)/shard_map/attend/pallas_call | solution.py:126
  67.1 47.2 %feed.1 = (bf16[4,1024,128]{2,1,0:T(8,128)(2,1)}, bf16[2,512,512]{2,1,0:T(8,128)(2,1)}, f32[1024,512]{1,0:T(8,128)}, bf16[3,192,512]{2,1,0:T(8,128)(2,1)}, bf16[...) custom-call(bf16[4,1024,128]{2,1,0:T(8,128)(2,1)} %bitcast.24, ...), custom_call_target="tpu_custom_call" | custom-call | tf_op jit(solution)/shard_map/feed/pallas_call | solution.py:1257
  114.4 1.4 collective-permute-start
  115.7 1.5 collective-permute-start.1
  117.2 0.7 collective-permute-start.2
  117.9 1.4 fusion
  119.3 36.2 %attend_back.1 = (bf16[4096,512]{1,0:T(8,128)(2,1)}, bf16[4,128,384]{2,1,0:T(8,128)(2,1)}, f32[2,512]{1,0:T(2,128)}) custom-call(s32[8,128]{1,0:T(8,128)} %get-tuple-element.61.tab_ref, bf16[4096,128]{1,0:T(8,128)(2,1)} %get-tuple-element.64.k_ref, bf16[128,4096]{1,0:T(8,128)(2,1)} %get-tuple-element.75.kt_ref, bf16[4096,128]{1,0:T(8,128)(2,1)} %get-tuple-element.76.v_ref, ...), custom_call_target="tpu_custom_call" | custom-call | tf_op jit(solution)/shard_map/attend_back/pallas_call | solution.py:278
  155.5 0.0 collective-permute-done.from_y_ref
  155.5 0.0 copy-start
  155.5 0.0 collective-permute-done.1.from_x_ref
  155.5 0.0 copy-start.1
  155.5 0.0 collective-permute-done.2.from_xy_ref
  155.5 0.0 copy-start.2
  155.6 0.8 copy-done
  156.3 0.2 copy-done.1
  156.5 0.2 copy-done.2
  156.7 69.6 %tail.1 = (bf16[2,512,512]{2,1,0:T(8,128)(2,1)}, bf16[3,2,192,512]{3,2,1,0:T(8,128)(2,1)}, bf16[4,128,384]{2,1,0:T(8,128)(2,1)}, f32[16,512]{1,0:T(8,128)}) custom-call(bf16[4,1024,512]{2,1,0:T(8,128)(2,1)} %bitcast.22, bf16[1024,512]{1,0:T(8,128)(2,1)} %get-tuple-element.67.x_ref.x_hbm, f32[1024,512]{1,0:T(8,128)} %get-tuple-element.83.dmid_hbm, ...), custom_call_target="tpu_custom_call" | custom-call | tf_op jit(solution)/shard_map/tail/pallas_call | solution.py:1562
  226.3 5.4 %results.1 = (bf16[2,1,512,512]{3,2,1,0:T(8,128)(2,1)}, f32[2,1,512,512]{3,2,1,0:T(8,128)}, f32[512,512]{1,0:T(8,128)}, f32[128,2048]{1,0:T(8,128)}, f32[128,512...) custom-call(bf16[2,512,512]{2,1,0:T(8,128)(2,1)} %get-tuple-element., ...), custom_call_target="tpu_custom_call" | custom-call | tf_op jit(solution)/shard_map/results/pallas_call | solution.py:1646
Async XLA Ops:
  114.4 41.1 %collective-permute-start = (bf16[3,192,512]{2,1,0:T(8,128)(2,1)}, bf16[3,192,512]{2,1,0:T(8,128)(2,1)S(1)}, u32[]{:S(2)}, u32[]{:S(2)}) collective-permute-start(bf16[3,192,512]{2,1,0:T(8,128)(2,1)} %get-tuple-element.85), channel_id=1, source_target_pairs={{0,2},{1,3},{2,0},{3,1},{4,6},{5,7},{6,4},{7,5},{8,10},{9,11},{10,... | collective-permute-start | bytes 1769480 | tf_op jit(solution)/shard_map/ppermute | solution.py:1701
  115.7 39.8 %collective-permute-start.1 = (bf16[3,192,512]{2,1,0:T(8,128)(2,1)}, bf16[3,192,512]{2,1,0:T(8,128)(2,1)S(1)}, u32[]{:S(2)}, u32[]{:S(2)}) collective-permute-start(bf16[3,192,512]{2,1,0:T(8,128)(2,1)} %get-tuple-element.86), channel_id=1, source_target_pairs={{0,4},{1,5},{2,6},{3,7},{4,0},{5,1},{6,2},{7,3},{8,12},{9,13},{10,... | collective-permute-start | bytes 1769480 | tf_op jit(solution)/shard_map/ppermute | solution.py:1701
  117.2 38.3 %collective-permute-start.2 = (bf16[3,192,512]{2,1,0:T(8,128)(2,1)}, bf16[3,192,512]{2,1,0:T(8,128)(2,1)S(1)}, u32[]{:S(2)}, u32[]{:S(2)}) collective-permute-start(bf16[3,192,512]{2,1,0:T(8,128)(2,1)} %get-tuple-element.87), channel_id=1, source_target_pairs={{0,6},{1,7},{2,4},{3,5},{4,2},{5,3},{6,0},{7,1},{8,14},{9,15},{10,... | collective-permute-start | bytes 1769480 | tf_op jit(solution)/shard_map/ppermute | solution.py:1701
  155.5 0.8 copy-start
  155.5 1.0 copy-start.1
  155.5 1.2 copy-start.2

commit v5 on v4

--- a/solution.py
+++ b/solution.py
@@ -50,38 +50,42 @@
 EXTRA = 16
 
 
-def attend_kernel(tab_ref, qt_ref, start_ref, k_ref, vt_ref, o_ref, ot_ref, lse_ref, acc, top):
-    qb = pl.program_id(0)
-    both = two_heads(qt_ref[...])
-    start = jnp.concatenate([start_ref[0], start_ref[0]], axis=1)
+def attend_kernel(
+    tab_ref, qt_ref, start_ref, k_ref, vt_ref, o_hbm, ot_hbm, lse_ref, acc, top, o_buf, ot_buf, out_sem
+):
+    blocks = start_ref.shape[0]
     row = lax.broadcasted_iota(jnp.int32, (BLK, 2 * BLK), 0)
+    reach = row - jnp.bitwise_and(lax.broadcasted_iota(jnp.int32, (BLK, 2 * BLK), 1), BLK - 1)
     ones = jnp.ones((EXTRA, 2 * BLK), bf16)
 
-    def place_of(kb):
-        return pl.ds(pl.multiple_of(tab_ref[2, jnp.maximum(kb, 0)] * BLK, BLK), BLK)
-
-    def masked_scores(kb, at, diagonal):
-        allowed = row >= start - kb * BLK
-        if diagonal:
-            col = lax.broadcasted_iota(jnp.int32, (BLK, 2 * BLK), 1)
-            allowed = allowed & (row <= jnp.bitwise_and(col, BLK - 1))
-        st = jnp.dot(k_ref[at, :], both, preferred_element_type=f32)
-        return jnp.where(allowed, st, mask_fill)
-
-    def visit(kb, first, bounded):
+    def place_of(b):
+        return pl.ds(pl.multiple_of(tab_ref[2, jnp.maximum(b, 0)] * BLK, BLK), BLK)
+
+    def visits_of(qb):
+        return (qb - tab_ref[0, qb]) // 2 + 1
+
+    def visit(qb, i, bounded):
+        kb = qb - 2 * i
+        both = two_heads(qt_ref[:, place_of(qb)])
+        start = jnp.concatenate([start_ref[qb], start_ref[qb]], axis=1)
         places = [place_of(kb), place_of(kb - 1)]
-        terms = [masked_scores(kb - i, places[i], first and i == 0) for i in range(2)]
+        terms = []
+        for n in range(2):
+            allowed = row >= start - (kb - n) * BLK
+            if n == 0:
+                allowed = allowed & (reach <= (qb - kb) * BLK)
+            st = jnp.dot(k_ref[places[n], :], both, preferred_element_type=f32)
+            terms.append(jnp.where(allowed, st, mask_fill))
         if bounded:
             probs = [jnp.exp2(term).astype(bf16) for term in terms]
         else:
+            old = top[qb]
             peak = jnp.maximum(
                 jnp.max(terms[0], axis=0, keepdims=True), jnp.max(terms[1], axis=0, keepdims=True)
             )
-            if not first:
-                old = top[...]
-                peak = jnp.maximum(old, peak)
-                shrink = jnp.exp2(old - peak)
-            top[...] = peak
+            peak = jnp.maximum(old, peak)
+            shrink = jnp.exp2(old - peak)
+            top[qb] = peak
             probs = [jnp.exp2(term - peak).astype(bf16) for term in terms]
         probs = jnp.concatenate(probs, axis=0)
         vt = jnp.concatenate([vt_ref[:, places[0]], vt_ref[:, places[1]]], axis=1)
@@ -89,59 +93,78 @@
             cols = slice(head * BLK, (head + 1) * BLK)
             left = jnp.concatenate([vt[head * HD : (head + 1) * HD], ones], axis=0)
             part = jnp.dot(left, probs[:, cols], preferred_element_type=f32)
-            if first:
-                acc[head] = part
-            elif bounded:
-                acc[head] += part
-            else:
-                acc[head] = acc[head] * shrink[:, cols] + part
+            acc[qb, head] = part + (acc[qb, head] if bounded else acc[qb, head] * shrink[:, cols])
 
     def all_visits(bounded):
-        visit(qb, True, bounded)
-
-        def more(i, carry):
-            visit(qb - 2 * i, False, bounded)
-            return carry
-
-        lax.fori_loop(1, (qb - tab_ref[0, qb]) // 2 + 1, more, 0)
+        count = lax.fori_loop(0, blocks, lambda b, n: n + visits_of(b), 0)
+
+        def step(n, state):
+            qb, i = state
+            visit(qb, i, bounded)
+            more = i + 1 < visits_of(qb)
+            return jnp.where(more, qb, jnp.minimum(qb + 1, blocks - 1)), jnp.where(more, i + 1, 0)
+
+        lax.fori_loop(0, count, step, (jnp.int32(0), jnp.int32(0)))
 
     small = tab_ref[3, 0] > 0
+    acc[...] = jnp.zeros_like(acc)
 
     @pl.when(small)
     def _():
         top[...] = jnp.zeros_like(top)
         all_visits(True)
 
-    pl.when(jnp.logical_not(small))(lambda: all_visits(False))
-    total = jnp.concatenate([acc[0, HD : HD + 1], acc[1, HD : HD + 1]], axis=1)
-    lse_ref[0] = top[...] + jnp.log2(total)
-    heads = jnp.concatenate([acc[h, :HD] / acc[h, HD : HD + 1] for h in range(2)], axis=0)
-    ot_ref[0] = heads
-    o_ref[...] = heads.T.astype(bf16)
+    @pl.when(jnp.logical_not(small))
+    def _():
+        top[...] = jnp.full_like(top, mask_fill)
+        all_visits(False)
+
+    def outgoing(b):
+        at = place_of(b)
+        return (
+            pltpu.make_async_copy(o_buf.at[b], o_hbm.at[at], out_sem.at[0]),
+            pltpu.make_async_copy(ot_buf.at[b], ot_hbm.at[b], out_sem.at[1]),
+        )
+
+    def close(b):
+        total = jnp.concatenate([acc[b, 0, HD : HD + 1], acc[b, 1, HD : HD + 1]], axis=1)
+        lse_ref[b] = top[b] + jnp.log2(total)
+        heads = jnp.concatenate([acc[b, h, :HD] / acc[b, h, HD : HD + 1] for h in range(2)], axis=0)
+        ot_buf[b] = heads
+        o_buf[b] = heads.T.astype(bf16)
+        for copy in outgoing(b):
+            copy.start()
+
+    def close_two(n, carry):
+        close(2 * n)
+        close(2 * n + 1)
+        return carry
+
+    lax.fori_loop(0, blocks // 2, close_two, 0)
+    for whole_copy in (
+        pltpu.make_async_copy(ot_buf, ot_hbm, out_sem.at[1]),
+        pltpu.make_async_copy(o_hbm, o_hbm, out_sem.at[0]),
+    ):
+        whole_copy.wait()
 
 
 def attend(tab, qt, start, k, vt):
     count = k.shape[0]
     blocks = count // BLK
+    vmem, any_ = pl.BlockSpec(memory_space=pltpu.VMEM), pl.BlockSpec(memory_space=pl.ANY)
     return pl.pallas_call(
         attend_kernel,
         grid_spec=pltpu.PrefetchScalarGridSpec(
             num_scalar_prefetch=1,
-            grid=(blocks,),
-            in_specs=[
-                pl.BlockSpec((PAIR, BLK), lambda b, t: (0, t[2, b])),
-                pl.BlockSpec((1, 1, BLK), lambda b, t: (b, 0, 0)),
-                whole(k.shape),
-                whole(vt.shape),
-            ],
-            out_specs=[
-                pl.BlockSpec((BLK, PAIR), lambda b, t: (t[2, b], 0)),
-                pl.BlockSpec((1, PAIR, BLK), lambda b, t: (b, 0, 0)),
-                pl.BlockSpec((1, 1, 2 * BLK), lambda b, t: (b, 0, 0)),
-            ],
+            grid=(),
+            in_specs=[vmem] * 4,
+            out_specs=[any_, any_, vmem],
             scratch_shapes=[
-                pltpu.VMEM((2, HD + EXTRA, BLK), f32),
-                pltpu.VMEM((1, 2 * BLK), f32),
+                pltpu.VMEM((blocks, 2, HD + EXTRA, BLK), f32),
+                pltpu.VMEM((blocks, 1, 2 * BLK), f32),
+                pltpu.VMEM((blocks, BLK, PAIR), bf16),
+                pltpu.VMEM((blocks, PAIR, BLK), f32),
+                pltpu.SemaphoreType.DMA((2,)),
             ],
         ),
         out_shape=[
@@ -161,163 +184,126 @@
 
 
 def attend_back_kernel(
-    tab_ref, k_ref, kt_ref, v_ref, ut_ref, w_ref, qt_ref, start_ref, do_ref, ot_ref, lse_ref,
-    gain_ref, bias_ref, dh_ref, gw_ref, gn_ref, dqt, dk_acc, dv_acc, dot, dom, qm, delta, total, sums,
+    tab_ref, k_hbm, kt_hbm, v_hbm, qt_ref, start_ref, do_ref, ot_ref, lse_ref, out_hbm,
+    k_ref, kt_ref, v_ref, out_buf, dqt, dk, dv, dot, dom, qm, delta, in_sem, out_sem,
 ):
-    kb = pl.program_id(0)
-    blocks = pl.num_programs(0) - 1
-    now, before = kb % 2, (kb + 1) % 2
+    blocks = start_ref.shape[0]
     row = lax.broadcasted_iota(jnp.int32, (BLK, 2 * BLK), 0)
-
-    def at(qb):
-        return pl.ds(pl.multiple_of(tab_ref[2, qb] * BLK, BLK), BLK)
-
-    @pl.when(kb == 0)
-    def _():
-        total[...] = jnp.zeros_like(total)
-        sums[...] = jnp.zeros_like(sums)
-        dk_acc[1] = jnp.zeros(dk_acc.shape[1:], f32)
-        dv_acc[1] = jnp.zeros(dv_acc.shape[1:], f32)
-
-        def prepare(qb, carry):
-            dqt[qb] = jnp.zeros((PAIR, BLK), f32)
-            d_out = do_ref[at(qb), :]
-            dom[qb] = split_heads(d_out)
-            qm[qb] = split_heads(qt_ref[:, at(qb)].T)
-            turned = d_out.astype(f32).T
-            dot[qb] = turned.astype(bf16)
-            both = turned * ot_ref[qb]
-            delta[qb] = jnp.concatenate(
-                [
-                    jnp.sum(both[:HD], axis=0, keepdims=True),
-                    jnp.sum(both[HD:], axis=0, keepdims=True),
-                ],
-                axis=1,
-            )
-            return carry
-
-        lax.fori_loop(0, blocks, prepare, 0)
-
-    k = k_ref[...]
-    v = v_ref[...]
-    kt = kt_ref[...]
-
-    def tile(qb, diagonal):
-        qt = qt_ref[:, at(qb)]
-        d_out = dot[qb]
+    reach = row - jnp.bitwise_and(lax.broadcasted_iota(jnp.int32, (BLK, 2 * BLK), 1), BLK - 1)
+    loads = [
+        pltpu.make_async_copy(src, dst, in_sem.at[i])
+        for i, (src, dst) in enumerate(((k_hbm, k_ref), (kt_hbm, kt_ref), (v_hbm, v_ref)))
+    ]
+    for copy in loads:
+        copy.start()
+
+    def at(b):
+        return pl.ds(pl.multiple_of(tab_ref[2, b] * BLK, BLK), BLK)
+
+    def prepare(qb):
+        dqt[qb] = jnp.zeros((PAIR, BLK), f32)
+        dk[qb] = jnp.zeros((BLK, PAIR), f32)
+        dv[qb] = jnp.zeros((BLK, PAIR), f32)
+        d_out = do_ref[at(qb), :]
+        dom[qb] = split_heads(d_out)
+        qm[qb] = split_heads(qt_ref[:, at(qb)].T)
+        turned = d_out.astype(f32).T
+        dot[qb] = turned.astype(bf16)
+        both = turned * ot_ref[qb]
+        delta[qb] = jnp.concatenate(
+            [jnp.sum(both[:HD], axis=0, keepdims=True), jnp.sum(both[HD:], axis=0, keepdims=True)], axis=1
+        )
+
+    def prepare_two(n, carry):
+        prepare(2 * n)
+        prepare(2 * n + 1)
+        return carry
+
+    lax.fori_loop(0, blocks // 2, prepare_two, 0)
+    for copy in loads:
+        copy.wait()
+
+    def tile(kb, qb, live):
+        kt = kt_ref[:, at(kb)]
         start = jnp.concatenate([start_ref[qb], start_ref[qb]], axis=1)
-        st = jnp.dot(k, two_heads(qt), preferred_element_type=f32)
-        dpt = jnp.dot(v, two_heads(d_out), preferred_element_type=f32)
-        allowed = row >= start - kb * BLK
-        if diagonal:
-            col = lax.broadcasted_iota(jnp.int32, (BLK, 2 * BLK), 1)
-            allowed = allowed & (row <= jnp.bitwise_and(col, BLK - 1))
+        st = jnp.dot(k_ref[at(kb), :], two_heads(qt_ref[:, at(qb)]), preferred_element_type=f32)
+        dpt = jnp.dot(v_ref[at(kb), :], two_heads(dot[qb]), preferred_element_type=f32)
+        allowed = (row >= start - kb * BLK) & (reach <= jnp.where(live, (qb - kb) * BLK, -2 * BLK))
         pt = jnp.exp2(jnp.where(allowed, st - lse_ref[qb], mask_fill))
         dst = (pt * (dpt - delta[qb])).astype(bf16)
         part_v = jnp.dot(pt.astype(bf16), dom[qb], preferred_element_type=f32)
         part_k = jnp.dot(dst, qm[qb], preferred_element_type=f32)
-        if diagonal:
-            dv_acc[now] = part_v
-            dk_acc[now] = part_k
-        else:
-            dv_acc[now] += part_v
-            dk_acc[now] += part_k
-        for head in range(2):
-            mine = slice(head * HD, (head + 1) * HD)
-            cols = slice(head * BLK, (head + 1) * BLK)
-            dqt[qb, mine] += jnp.dot(kt[mine], dst[:, cols], preferred_element_type=f32)
-
-    def close():
-        block = jnp.maximum(kb - 1, 0)
-        dq = (dqt[block] * SCORE_SCALE).T
-        joined = jnp.concatenate([dq, dk_acc[before] * LN2, dv_acc[before]], axis=1)
-        if_any = jnp.where(kb == 0, 0.0, 1.0)
-        joined = (joined * if_any).astype(bf16)
-        dh_ref[...] = contract(joined, w_ref[...], 1, 1).astype(bf16)
-        total[...] += jnp.dot(ut_ref[...], joined, preferred_element_type=f32)
-        sums[...] += jnp.sum(joined.astype(f32), axis=0, keepdims=True)
-
-    @pl.when(kb < blocks)
-    def _():
-        close()
-        tile(kb, True)
-        last = tab_ref[1, kb]
-
-        def visit(i, carry):
-            tile(kb + 1 + 2 * i, False)
-            tile(kb + 2 + 2 * i, False)
-            return carry
-
-        lax.fori_loop(0, (last - kb) // 2, visit, 0)
-
-        @pl.when((last - kb) % 2 == 1)
-        def _():
-            tile(last, False)
-
-    @pl.when(kb == blocks)
-    def _():
-        close()
-        shard = gw_ref.shape[1]
-        for j in range(gw_ref.shape[0]):
-            part = pl.ds(j * shard, shard)
-            gain, bias = (
-                jnp.broadcast_to(ref[:, part], (shard, shard)).T[:, :1] for ref in (gain_ref, bias_ref)
-            )
-            gw_ref[j] = (total[part] * gain + bias * sums[...]).astype(bf16)
-            w = w_ref[part].astype(f32)
-            for i, term in enumerate((w * total[part], w * sums[...])):
-                column = jnp.sum(term, axis=1, keepdims=True)
-                gn_ref[i : i + 1, part] = jnp.broadcast_to(column, (shard, shard)).T[:1]
-
-
-def attend_back(tab, k, kt, v, unit_t, weight, qt, start, d_out, ot, lse, gain, bias, shards):
+        part_q = [
+            jnp.dot(kt[head * HD : (head + 1) * HD], dst[:, head * BLK : (head + 1) * BLK], preferred_element_type=f32)
+            for head in range(2)
+        ]
+        return kb, qb, part_v, part_k, jnp.concatenate(part_q, axis=0)
+
+    def add(kb, qb, part_v, part_k, part_q):
+        dv[kb] += part_v
+        dk[kb] += part_k
+        dqt[qb] += part_q
+
+    def following(kb, qb):
+        more = qb < tab_ref[1, kb]
+        beyond = jnp.minimum(kb + 1, blocks - 1)
+        return jnp.where(more, kb, beyond), jnp.where(more, qb + 1, beyond)
+
+    tiles = lax.fori_loop(0, blocks, lambda b, n: n + tab_ref[1, b] - b + 1, 0)
+
+    def step(n, state):
+        second = following(*state)
+        terms = [tile(*state, True), tile(*second, 2 * n + 1 < tiles)]
+        for term in terms:
+            add(*term)
+        return following(*second)
+
+    lax.fori_loop(0, (tiles + 1) // 2, step, (jnp.int32(0), jnp.int32(0)))
+    def close(b):
+        out_buf[b] = jnp.concatenate([(dqt[b] * SCORE_SCALE).T, dk[b] * LN2, dv[b]], axis=1).astype(bf16)
+        pltpu.make_async_copy(out_buf.at[b], out_hbm.at[at(b)], out_sem.at[0]).start()
+
+    def close_four(n, carry):
+        for i in range(4):
+            close(4 * n + i)
+        return carry
+
+    lax.fori_loop(0, blocks // 4, close_four, 0)
+    pltpu.make_async_copy(out_hbm, out_hbm, out_sem.at[0]).wait()
+
+
+def attend_back(tab, k, kt, v, qt, start, d_out, ot, lse):
     count = k.shape[0]
-    width = unit_t.shape[0]
-    shard = width // shards
     blocks = count // BLK
+    vmem, any_ = pl.BlockSpec(memory_space=pltpu.VMEM), pl.BlockSpec(memory_space=pl.ANY)
+    buf = pltpu.VMEM
     return pl.pallas_call(
         attend_back_kernel,
         grid_spec=pltpu.PrefetchScalarGridSpec(
             num_scalar_prefetch=1,
-            grid=(blocks + 1,),
-            in_specs=[
-                pl.BlockSpec((BLK, PAIR), lambda b, t: (t[2, jnp.minimum(b, blocks - 1)], 0)),
-                pl.BlockSpec((PAIR, BLK), lambda b, t: (0, t[2, jnp.minimum(b, blocks - 1)])),
-                pl.BlockSpec((BLK, PAIR), lambda b, t: (t[2, jnp.minimum(b, blocks - 1)], 0)),
-                pl.BlockSpec((width, BLK), lambda b, t: (0, t[2, jnp.maximum(b - 1, 0)])),
-                whole(weight.shape),
-                whole(qt.shape),
-                whole(start.shape),
-                whole(d_out.shape),
-                whole(ot.shape),
-                whole(lse.shape),
-                whole(gain.shape),
-                whole(bias.shape),
-            ],
-            out_specs=[
-                pl.BlockSpec((BLK, width), lambda b, t: (t[2, jnp.maximum(b - 1, 0)], 0)),
-                whole((shards, shard, 3 * PAIR)),
-                whole((2, width)),
-            ],
+            grid=(),
+            in_specs=[any_] * 3 + [vmem] * 5,
+            out_specs=any_,
             scratch_shapes=[
-                pltpu.VMEM((blocks, PAIR, BLK), f32),
-                pltpu.VMEM((2, BLK, PAIR), f32),
-                pltpu.VMEM((2, BLK, PAIR), f32),
-                pltpu.VMEM((blocks, PAIR, BLK), bf16),
-                pltpu.VMEM((blocks, 2 * BLK, PAIR), bf16),
-                pltpu.VMEM((blocks, 2 * BLK, PAIR), bf16),
-                pltpu.VMEM((blocks, 1, 2 * BLK), f32),
-                pltpu.VMEM(weight.shape, f32),
-                pltpu.VMEM((1, 3 * PAIR), f32),
+                buf(k.shape, bf16),
+                buf(kt.shape, bf16),
+                buf(v.shape, bf16),
+                buf((blocks, BLK, 3 * PAIR), bf16),
+                buf((blocks, PAIR, BLK), f32),
+                buf((blocks, BLK, PAIR), f32),
+                buf((blocks, BLK, PAIR), f32),
+                buf((blocks, PAIR, BLK), bf16),
+                buf((blocks, 2 * BLK, PAIR), bf16),
+                buf((blocks, 2 * BLK, PAIR), bf16),
+                buf((blocks, 1, 2 * BLK), f32),
+                pltpu.SemaphoreType.DMA((3,)),
+                pltpu.SemaphoreType.DMA((1,)),
             ],
         ),
-        out_shape=[
-            jax.ShapeDtypeStruct((count, width), bf16),
-            jax.ShapeDtypeStruct((shards, shard, 3 * PAIR), bf16),
-            jax.ShapeDtypeStruct((2, width), f32),
-        ],
+        out_shape=jax.ShapeDtypeStruct((count, 3 * PAIR), bf16),
+        compiler_params=pltpu.CompilerParams(vmem_limit_bytes=60 * 1024 * 1024),
         name="attend_back",
-    )(tab, k, kt, v, unit_t, weight, qt, start, d_out, ot, lse, gain, bias)
+    )(tab, k, kt, v, qt, start, d_out, ot, lse)
 
 
 def layer_norm(values, gain_vec, offset):
@@ -1310,13 +1296,14 @@
 
 
 def tail_kernel(
-    dh_ref, x_hbm, dmid_hbm, gain_ref, keep_ref, from_y_ref, from_x_ref, from_xy_ref, gw_ref, gn_ref, gvecs_ref, gub_ref,
+    d_qkv_hbm, ut_hbm, x_hbm, dmid_hbm, w_ref, gain_ref, bias_ref, keep_ref, from_y_ref, from_x_ref, from_xy_ref,
+    gvecs_ref, gub_ref,
     home_buf, gfull, wall, sum_ref,
-    x_ref, dmid_ref, core_buf, own_dh, x_out, x_buf, dx_out,
+    d_qkv, ut_ref, total, sums, gw_ref, core_out, x_ref, dmid_ref, core_buf, own_dh, x_out, x_buf, dx_out,
     gsum, gz1s, gz1r, gz2s, gz2r,
     wy, ws, wz1s, wz1r, wz2s, wz2r, wfull,
     small_ref, small_out, small_in,
-    local_sem, self_sem, core_s, core_r, x_s, x_r, home_s, home_r, g_s, g_r, w_s, w_r, s_s, s_r, in_sem,
+    load_sem, self_sem, core_s, core_r, x_s, x_r, home_s, home_r, g_s, g_r, w_s, w_r, s_s, s_r, in_sem,
 ):
     z, x, y, c = (lax.axis_index(name) for name in AXES)
     odd, upper = lax.rem(z, 2), lax.div(z, 2)
@@ -1328,13 +1315,17 @@
     home = [{"z": 2 * c + upper, "c": odd}, {"z": 2 * c + 1 - upper, "c": odd}]
     origin = [{"z": 2 * odd + c, "c": upper}, {"z": 2 * (1 - odd) + c, "c": upper}]
     stay = (c == upper) & (odd == c)
+    loads = []
+    for i in range(chunks):
+        part = pl.ds(i * TAIL_CHUNK, TAIL_CHUNK)
+        loads.append(pltpu.make_async_copy(d_qkv_hbm.at[:, part], d_qkv.at[:, part], load_sem.at[i]))
     inputs = [
-        pltpu.make_async_copy(x_hbm, x_ref, in_sem.at[0]), pltpu.make_async_copy(dmid_hbm, dmid_ref, in_sem.at[1])
+        pltpu.make_async_copy(src, dst, in_sem.at[i])
+        for i, (src, dst) in enumerate(((ut_hbm, ut_ref), (x_hbm, x_ref), (dmid_hbm, dmid_ref)))
     ]
-    for copy in inputs:
+    for copy in loads + inputs:
         copy.start()
     small_ref[...] = jnp.zeros_like(small_ref)
-    small_ref[0:2] = gn_ref[...]
     small_ref[2:4] = gvecs_ref[1:3]
     small_ref[4:5] = gvecs_ref[0:1]
     small_ref[5:6] = gvecs_ref[3:4]
@@ -1345,19 +1336,45 @@
         [home[0], origin[0]],
         jnp.logical_not(stay),
     )
-    small_peers = [by_x, by_core, by_y, by_z1, by_z2]
-    s_copy = [send(small_ref, small_in.at[0], s_s, s_r, 0, small_peers[0])]
-    to_core, locals_ = [], []
-    for i in range(chunks):
+    small_peers = [by_core, by_y, by_z1, by_z2, by_x]
+    to_core, w_copy, s_copy = [], {}, []
+
+    def share(i):
         part = pl.ds(i * TAIL_CHUNK, TAIL_CHUNK)
-        to_core.append(
-            send(dh_ref.at[pl.ds(2, 2), part], core_buf.at[:, part], core_s, core_r, i, by_core)
-        )
-        copy = pltpu.make_async_copy(dh_ref.at[pl.ds(0, 2), part], own_dh.at[:, part], local_sem.at[i])
-        copy.start()
-        locals_.append(copy)
-    w_copy = {}
-    w_copy["y"] = send(gw_ref.at[pl.ds(2 * (1 - y), 2)], wy, w_s, w_r, 0, by_y)
+        loads[i].wait()
+        for g in (3, 2, 1, 0):
+            value = contract(d_qkv[g, part], w_ref[...], 1, 1)
+            if g >= 2:
+                core_out[g - 2, part] = value.astype(bf16)
+            else:
+                own_dh[g, part] = value
+            if g == 2:
+                to_core.append(
+                    send(core_out.at[:, part], core_buf.at[:, part], core_s, core_r, i, by_core)
+                )
+
+    def weight(g):
+        if g == 0:
+            inputs[0].wait()
+        rows = d_qkv[g]
+        part = jnp.dot(ut_ref[:, g * rows.shape[0] : (g + 1) * rows.shape[0]], rows, preferred_element_type=f32)
+        line = jnp.sum(rows.astype(f32), axis=0, keepdims=True)
+        total[...] = part if g == 0 else total[...] + part
+        sums[...] = line if g == 0 else sums[...] + line
+
+    def weight_close():
+        shard = gw_ref.shape[1]
+        for j in range(gw_ref.shape[0]):
+            part = pl.ds(j * shard, shard)
+            gain, bias = (jnp.broadcast_to(ref[:, part], (shard, shard)).T[:, :1] for ref in (gain_ref, bias_ref))
+            gw_ref[j] = (total[part] * gain + bias * sums[...]).astype(bf16)
+            w = w_ref[part].astype(f32)
+            for i, term in enumerate((w * total[part], w * sums[...])):
+                column = jnp.sum(term, axis=1, keepdims=True)
+                small_ref[i : i + 1, part] = jnp.broadcast_to(column, (shard, shard)).T[:1]
+        s_copy.append(send(small_ref, small_in.at[0], s_s, s_r, 0, small_peers[0]))
+        w_copy["y"] = send(gw_ref.at[pl.ds(2 * (1 - y), 2)], wy, w_s, w_r, 0, by_y)
+
     g_copy = {}
 
     def g_start(p):
@@ -1443,17 +1460,16 @@
     def add_core(i):
         part = pl.ds(i * TAIL_CHUNK, TAIL_CHUNK)
         to_core[i].wait()
-        locals_[i].wait()
-        x_out[part] = (own_dh[1, part].astype(f32) + core_buf[1, part].astype(f32)).astype(bf16)
+        x_out[part] = (own_dh[1, part] + core_buf[1, part].astype(f32)).astype(bf16)
         x_copy.append(send(x_out.at[part], x_buf.at[part], x_s, x_r, i, by_x))
 
     def finish(i):
         part = pl.ds(i * TAIL_CHUNK, TAIL_CHUNK)
         if i == 0:
-            for copy in inputs:
+            for copy in inputs[1:]:
                 copy.wait()
         x_copy[i].wait()
-        d_low = own_dh[0, part].astype(f32) + core_buf[0, part].astype(f32) + x_buf[part].astype(f32)
+        d_low = own_dh[0, part] + core_buf[0, part].astype(f32) + x_buf[part].astype(f32)
         unit, inv = norm_parts(x_ref[part].astype(f32))
         scaled = d_low * gain_ref[...]
         dx = dmid_ref[part] + inv * (
@@ -1498,46 +1514,59 @@
         else:
             remote()
 
+    share(0)
+    share(1)
+    add_core(0)
+    share(2)
     g_start(0)
-    add_core(0)
+    add_core(1)
+    share(3)
     g_start(1)
-    add_core(1)
+    add_core(2)
+    share(4)
     g_start(2)
-    add_core(2)
-    s_next(0)
-    s_next(1)
+    add_core(3)
+    share(5)
+    share(6)
+    add_core(4)
+    share(7)
+    add_core(5)
+    weight(0)
+    weight(1)
+    weight(2)
+    weight(3)
+    weight_close()
     g_second(0)
-    w_second()
     g_second(1)
     g_second(2)
+    add_core(6)
+    add_core(7)
+    s_next(0)
+    w_second()
     finish(0)
-    add_core(3)
-    s_next(2)
     g_third(0)
-    finish(1)
-    add_core(4)
-    w_third()
     g_third(1)
     g_third(2)
-    s_next(3)
-    finish(2)
-    add_core(5)
+    s_next(1)
+    w_third()
+    finish(1)
     g_fourth(0)
-    w_fourth()
-    finish(3)
-    add_core(6)
-    s_next(4)
     g_fourth(1)
     g_fourth(2)
+    s_next(2)
+    w_fourth()
+    finish(2)
+    g_fifth(0)
+    g_fifth(1)
+    g_fifth(2)
     w_fifth()
+    s_next(3)
+    finish(3)
+    w_sixth()
     finish(4)
-    add_core(7)
-    g_fifth(0)
+    s_next(4)
     finish(5)
-    w_sixth()
-    g_fifth(1)
     finish(6)
-    g_fifth(2)
     finish(7)
     w_copy["core"].wait()
     w_copy["x"].wait()
@@ -1550,9 +1579,9 @@
         g_copy["x", p].wait()
 
 
-def tail(dh, x, dmid, gain, keep, from_y, from_x, from_xy, gw, gn, gvecs, gub):
+def tail(d_qkv, unit_t, x, dmid, weight, gain, bias, keep, from_y, from_x, from_xy, gvecs, gub):
     count, width = x.shape
-    shard = gw.shape[1]
+    shard = width // 4
     half = count // 2
     chunks = count // TAIL_CHUNK
     sixth = keep.shape[1]
@@ -1561,7 +1590,7 @@
     buf = pltpu.VMEM
     return pl.pallas_call(
         tail_kernel,
-        in_specs=[pl.BlockSpec(memory_space=pl.ANY)] * 3 + [vmem] * 9,
+        in_specs=[pl.BlockSpec(memory_space=pl.ANY)] * 4 + [vmem] * 9,
         out_specs=[vmem] * 4,
         out_shape=[
             jax.ShapeDtypeStruct((2, half, width), bf16),
@@ -1570,10 +1599,16 @@
             jax.ShapeDtypeStruct((16, width), f32),
         ],
         scratch_shapes=[
+            buf(d_qkv.shape, bf16),
+            buf(unit_t.shape, bf16),
+            buf(weight.shape, f32),
+            buf((1, 3 * PAIR), f32),
+            buf((4, shard, 3 * PAIR), bf16),
+            buf((2, count, width), bf16),
             buf((count, width), bf16),
             buf((count, width), f32),
             buf((2, count, width), bf16),
-            buf((2, count, width), bf16),
+            buf((2, count, width), f32),
             buf((count, width), bf16),
             buf((count, width), bf16),
             buf((count, width), bf16),
@@ -1606,13 +1641,13 @@
             dma((8,)),
             dma((5,)),
             dma((5,)),
-            dma((2,)),
+            dma((3,)),
         ],
         compiler_params=pltpu.CompilerParams(
             collective_id=5, has_side_effects=True, vmem_limit_bytes=56 * 1024 * 1024
         ),
         name="tail",
-    )(dh, x, dmid, gain, keep, from_y, from_x, from_xy, gw, gn, gvecs, gub)
+    )(d_qkv, unit_t, x, dmid, weight, gain, bias, keep, from_y, from_x, from_xy, gvecs, gub)
 
 def results_kernel(
     y_ref, dx_ref, down_ref, up_ref, out_ref, wall_ref, sum_ref,
@@ -1721,12 +1756,10 @@
         o.reshape(4, -1, PAIR), own_x, near_dy, out_grad, full_out, full_up, full_down, vecs, full_ubias, 4
     )
     from_y, from_x, from_xy = swap(to_y, dy=1), swap(to_x, dx=1), swap(to_xy, dy=1, dx=1)
-    dh, g_heads, g_norm = attend_back(
-        tab, k, kt, v, unit, w_heads, qt, start, d_o.reshape(-1, PAIR), ot, lse, gain_one, bias_one, 4
-    )
+    d_qkv = attend_back(tab, k, kt, v, qt, start, d_o.reshape(-1, PAIR), ot, lse)
     dx, flat, heads, sums = tail(
-        dh.reshape(4, -1, dh.shape[1]), own_x, d_middle, gain_one, keep, from_y, from_x, from_xy,
-        g_heads, g_norm, g_vecs, g_ubias,
+        d_qkv.reshape(4, -1, 3 * PAIR), unit, own_x, d_middle, w_heads, gain_one, bias_one,
+        keep, from_y, from_x, from_xy, g_vecs, g_ubias,
     )
     outputs, input_grad, grad_down, grad_up, grad_out, grad_qkv, *vec = results(outputs, dx, flat, heads, sums)
     vec = [member.reshape(-1) for member in vec]

time: 233 us -> 224 us (0.961)
  Pallas kernels: 225 us -> 217 us
    pallas_call x1, Pallas kernels: 36.2 us -> 31.3 us  [attend_back(): pl.pallas_call(attend_back_kernel, grid_spec=pltpu.PrefetchScalarGridSpec...]
    pallas_call x1, Pallas kernels: 69.6 us -> 66.7 us  [tail(): pl.pallas_call(tail_kernel, in_specs=[pl.BlockSpec(memory_space=pl.ANY)]...]
  transfers between devices with their start and end apart: 3 -> 3, of which waited for: 0 -> 0; matrix products, arithmetic and copies ran while one was open for 1% -> 1% of each run, Pallas kernels for 16% -> 14%
where the time goes in v5:
time: 224 us
  Pallas kernels  217 us (97%)
  starting transfers between devices  3.59 us (2%)
  local copies, waits for them, and re-layouts  2.55 us (1%)
    pallas_call x1, Pallas kernels, tail(): pl.pallas_call(tail_kernel, in_specs=[pl.BlockSpec(memory_space=pl.ANY)]...  66.7 us
    pallas_call x1, Pallas kernels, head(): pl.pallas_call(head_kernel, in_specs=[any_, any_, vmem, smem] + [vmem] *...  47.1 us
    pallas_call x1, Pallas kernels, feed(): pl.pallas_call(feed_kernel, grid=(feed_steps,), in_specs=[any_, rows, pl....  45.1 us
    pallas_call x1, Pallas kernels, attend_back(): pl.pallas_call(attend_back_kernel, grid_spec=pltpu.PrefetchScalarGridSpec...  31.3 us
    pallas_call x1, Pallas kernels, attend(): pl.pallas_call(attend_kernel, grid_spec=pltpu.PrefetchScalarGridSpec(num_...  21.2 us
    pallas_call x1, Pallas kernels, results(): pl.pallas_call(results_kernel, grid=(steps,), in_specs=[tokens, tokens, p...  5.37 us
  transfers between devices with their start and end apart: 3, of which 0 were waited for; matrix products, arithmetic and copies ran while one was open for 1% of the time, Pallas kernels for 14%

profile of v5, /device:TPU:0, one launch (start us, length us, event | category | flops | bytes accessed | tf_op | source)
XLA Modules:
  0.0 223.8 jit_solution(14460515348681062472)
XLA Ops:
  0.7 47.1 %head.1 = (bf16[128,4096]{1,0:T(8,128)(2,1)}, bf16[4096,128]{1,0:T(8,128)(2,1)}, bf16[128,4096]{1,0:T(8,128)(2,1)}, bf16[4096,128]{1,0:T(8,128)(2,1)}, bf16[128,...) custom-call(bf16[2,1,512,512]{3,2,1,0:T(8,128)(2,1)} %x_in_ref.1, ...), custom_call_target="tpu_custom_call" | custom-call | tf_op jit(solution)/shard_map/head/pallas_call | solution.py:981
  47.8 21.2 %attend.1 = (bf16[4096,128]{1,0:T(8,128)(2,1)}, f32[16,128,256]{2,1,0:T(8,128)}, f32[16,1,512]{2,1,0:T(1,128)}) custom-call(s32[8,128]{1,0:T(8,128)} %get-tuple-element.58.tab_ref, bf16[128,4096]{1,0:T(8,128)(2,1)} %get-tuple-element.59.qt_ref, s32[16,1,256]{2,1,0:T(1,128)} %get-tuple-element.60.start_ref, bf16[4096,128]{1,0:T(8,128)(2,1)} %get-tuple-element.61.k_ref.k_hbm, ...), custom_call_target="tpu_custom_call" | custom-call | tf_op jit(solution)/shard_map/attend/pallas_call | solution.py:155
  68.9 45.1 %feed.1 = (bf16[4,1024,128]{2,1,0:T(8,128)(2,1)}, bf16[2,512,512]{2,1,0:T(8,128)(2,1)}, f32[1024,512]{1,0:T(8,128)}, bf16[3,192,512]{2,1,0:T(8,128)(2,1)}, bf16[...) custom-call(bf16[4,1024,128]{2,1,0:T(8,128)(2,1)} %bitcast.24, ...), custom_call_target="tpu_custom_call" | custom-call | tf_op jit(solution)/shard_map/feed/pallas_call | solution.py:1243
  114.1 2.0 collective-permute-start
  116.1 1.5 collective-permute-start.1
  117.6 0.0 collective-permute-start.2
  117.7 31.3 %attend_back.1 = bf16[4096,384]{1,0:T(8,128)(2,1)} custom-call(s32[8,128]{1,0:T(8,128)} %get-tuple-element.58.tab_ref, bf16[4096,128]{1,0:T(8,128)(2,1)} %get-tuple-element.61.k_ref.k_hbm, bf16[128,4096]{1,0:T(8,128)(2,1)} %get-tuple-element.72.kt_hbm, bf16[4096,128]{1,0:T(8,128)(2,1)} %get-tuple-element.73.v_hbm, ...), custom_call_target="tpu_custom_call" | custom-call | tf_op jit(solution)/shard_map/attend_back/pallas_call | solution.py:280
  149.0 1.4 fusion
  150.3 0.0 collective-permute-done.from_y_ref
  150.3 0.0 copy-start
  150.3 0.0 collective-permute-done.1.from_x_ref
  150.4 0.0 copy-start.1
  150.4 0.0 collective-permute-done.2.from_xy_ref
  150.4 0.0 copy-start.2
  150.4 0.8 copy-done
  151.2 0.2 copy-done.1
  151.4 0.2 copy-done.2
  151.5 66.7 %tail.1 = (bf16[2,512,512]{2,1,0:T(8,128)(2,1)}, bf16[3,2,192,512]{3,2,1,0:T(8,128)(2,1)}, bf16[4,128,384]{2,1,0:T(8,128)(2,1)}, f32[16,512]{1,0:T(8,128)}) custom-call(bf16[4,1024,384]{2,1,0:T(8,128)(2,1)} %bitcast.19, bf16[512,4096]{1,0:T(8,128)(2,1)} %get-tuple-element.77.ut_hbm, bf16[1024,512]{1,0:T(8,128)(2,1)} %get-tuple-element.64.x_ref.x_hbm, ...), custom_call_target="tpu_custom_call" | custom-call | tf_op jit(solution)/shard_map/tail/pallas_call | solution.py:1591
  218.3 5.4 %results.1 = (bf16[2,1,512,512]{3,2,1,0:T(8,128)(2,1)}, f32[2,1,512,512]{3,2,1,0:T(8,128)}, f32[512,512]{1,0:T(8,128)}, f32[128,2048]{1,0:T(8,128)}, f32[128,512...) custom-call(bf16[2,512,512]{2,1,0:T(8,128)(2,1)} %get-tuple-element., ...), custom_call_target="tpu_custom_call" | custom-call | tf_op jit(solution)/shard_map/results/pallas_call | solution.py:1681
Async XLA Ops:
  114.1 36.3 %collective-permute-start = (bf16[3,192,512]{2,1,0:T(8,128)(2,1)}, bf16[3,192,512]{2,1,0:T(8,128)(2,1)S(1)}, u32[]{:S(2)}, u32[]{:S(2)}) collective-permute-start(bf16[3,192,512]{2,1,0:T(8,128)(2,1)} %get-tuple-element.81), channel_id=1, source_target_pairs={{0,2},{1,3},{2,0},{3,1},{4,6},{5,7},{6,4},{7,5},{8,10},{9,11},{10,... | collective-permute-start | bytes 1769480 | tf_op jit(solution)/shard_map/ppermute | solution.py:1736
  116.1 34.2 %collective-permute-start.1 = (bf16[3,192,512]{2,1,0:T(8,128)(2,1)}, bf16[3,192,512]{2,1,0:T(8,128)(2,1)S(1)}, u32[]{:S(2)}, u32[]{:S(2)}) collective-permute-start(bf16[3,192,512]{2,1,0:T(8,128)(2,1)} %get-tuple-element.82), channel_id=1, source_target_pairs={{0,4},{1,5},{2,6},{3,7},{4,0},{5,1},{6,2},{7,3},{8,12},{9,13},{10,... | collective-permute-start | bytes 1769480 | tf_op jit(solution)/shard_map/ppermute | solution.py:1736
  117.6 32.7 %collective-permute-start.2 = (bf16[3,192,512]{2,1,0:T(8,128)(2,1)}, bf16[3,192,512]{2,1,0:T(8,128)(2,1)S(1)}, u32[]{:S(2)}, u32[]{:S(2)}) collective-permute-start(bf16[3,192,512]{2,1,0:T(8,128)(2,1)} %get-tuple-element.83), channel_id=1, source_target_pairs={{0,6},{1,7},{2,4},{3,5},{4,2},{5,3},{6,0},{7,1},{8,14},{9,15},{10,... | collective-permute-start | bytes 1769480 | tf_op jit(solution)/shard_map/ppermute | solution.py:1736
  150.3 0.8 copy-start
  150.4 1.0 copy-start.1
  150.4 1.2 copy-start.2

commit v6 on v5

--- a/solution.py
+++ b/solution.py
@@ -64,14 +64,15 @@
     def visits_of(qb):
         return (qb - tab_ref[0, qb]) // 2 + 1
 
-    def visit(qb, i, bounded):
+    def visit(qb, i, bounded, live=True):
         kb = qb - 2 * i
         both = two_heads(qt_ref[:, place_of(qb)])
         start = jnp.concatenate([start_ref[qb], start_ref[qb]], axis=1)
         places = [place_of(kb), place_of(kb - 1)]
         terms = []
         for n in range(2):
-            allowed = row >= start - (kb - n) * BLK
+            first_row = start - (kb - n) * BLK
+            allowed = row >= (first_row if live is True else jnp.where(live, first_row, BLK))
             if n == 0:
                 allowed = allowed & (reach <= (qb - kb) * BLK)
             st = jnp.dot(k_ref[places[n], :], both, preferred_element_type=f32)
@@ -89,22 +90,35 @@
             probs = [jnp.exp2(term - peak).astype(bf16) for term in terms]
         probs = jnp.concatenate(probs, axis=0)
         vt = jnp.concatenate([vt_ref[:, places[0]], vt_ref[:, places[1]]], axis=1)
+        parts = []
         for head in range(2):
             cols = slice(head * BLK, (head + 1) * BLK)
             left = jnp.concatenate([vt[head * HD : (head + 1) * HD], ones], axis=0)
             part = jnp.dot(left, probs[:, cols], preferred_element_type=f32)
-            acc[qb, head] = part + (acc[qb, head] if bounded else acc[qb, head] * shrink[:, cols])
+            parts.append(part)
+            if not bounded:
+                acc[qb, head] = part + acc[qb, head] * shrink[:, cols]
+        return parts
 
     def all_visits(bounded):
         count = lax.fori_loop(0, blocks, lambda b, n: n + visits_of(b), 0)
 
-        def step(n, state):
-            qb, i = state
-            visit(qb, i, bounded)
+        def following(qb, i):
             more = i + 1 < visits_of(qb)
             return jnp.where(more, qb, jnp.minimum(qb + 1, blocks - 1)), jnp.where(more, i + 1, 0)
 
-        lax.fori_loop(0, count, step, (jnp.int32(0), jnp.int32(0)))
+        def step(n, state):
+            if not bounded:
+                visit(*state, False)
+                return following(*state)
+            second = following(*state)
+            members = [visit(*state, True), visit(*second, True, 2 * n + 1 < count)]
+            for (qb, _), parts in zip((state, second), members):
+                for head in range(2):
+                    acc[qb, head] += parts[head]
+            return following(*second)
+
+        lax.fori_loop(0, (count + 1) // 2 if bounded else count, step, (jnp.int32(0), jnp.int32(0)))
 
     small = tab_ref[3, 0] > 0
     acc[...] = jnp.zeros_like(acc)
@@ -184,15 +198,15 @@
 
 
 def attend_back_kernel(
-    tab_ref, k_hbm, kt_hbm, v_hbm, qt_ref, start_ref, do_ref, ot_ref, lse_ref, out_hbm,
-    k_ref, kt_ref, v_ref, out_buf, dqt, dk, dv, dot, dom, qm, delta, in_sem, out_sem,
+    tab_ref, k_hbm, kt_hbm, v_hbm, y_hbm, qt_ref, start_ref, do_ref, ot_ref, lse_ref, out_hbm, y_out,
+    k_ref, kt_ref, v_ref, y_buf, out_buf, dqt, dk, dv, dot, dom, qm, delta, in_sem, out_sem,
 ):
     blocks = start_ref.shape[0]
     row = lax.broadcasted_iota(jnp.int32, (BLK, 2 * BLK), 0)
     reach = row - jnp.bitwise_and(lax.broadcasted_iota(jnp.int32, (BLK, 2 * BLK), 1), BLK - 1)
     loads = [
         pltpu.make_async_copy(src, dst, in_sem.at[i])
-        for i, (src, dst) in enumerate(((k_hbm, k_ref), (kt_hbm, kt_ref), (v_hbm, v_ref)))
+        for i, (src, dst) in enumerate(((k_hbm, k_ref), (kt_hbm, kt_ref), (v_hbm, v_ref), (y_hbm, y_buf)))
     ]
     for copy in loads:
         copy.start()
@@ -222,6 +236,8 @@
     lax.fori_loop(0, blocks // 2, prepare_two, 0)
     for copy in loads:
         copy.wait()
+    y_copy = pltpu.make_async_copy(y_buf, y_out.at[:, 0], out_sem.at[1])
+    y_copy.start()
 
     def tile(kb, qb, live):
         kt = kt_ref[:, at(kb)]
@@ -270,9 +286,10 @@
 
     lax.fori_loop(0, blocks // 4, close_four, 0)
     pltpu.make_async_copy(out_hbm, out_hbm, out_sem.at[0]).wait()
-
-
-def attend_back(tab, k, kt, v, qt, start, d_out, ot, lse):
+    y_copy.wait()
+
+
+def attend_back(tab, k, kt, v, y, qt, start, d_out, ot, lse):
     count = k.shape[0]
     blocks = count // BLK
     vmem, any_ = pl.BlockSpec(memory_space=pltpu.VMEM), pl.BlockSpec(memory_space=pl.ANY)
@@ -282,12 +299,13 @@
         grid_spec=pltpu.PrefetchScalarGridSpec(
             num_scalar_prefetch=1,
             grid=(),
-            in_specs=[any_] * 3 + [vmem] * 5,
-            out_specs=any_,
+            in_specs=[any_] * 4 + [vmem] * 5,
+            out_specs=[any_, any_],
             scratch_shapes=[
                 buf(k.shape, bf16),
                 buf(kt.shape, bf16),
                 buf(v.shape, bf16),
+                buf(y.shape, bf16),
                 buf((blocks, BLK, 3 * PAIR), bf16),
                 buf((blocks, PAIR, BLK), f32),
                 buf((blocks, BLK, PAIR), f32),
@@ -296,14 +314,17 @@
                 buf((blocks, 2 * BLK, PAIR), bf16),
                 buf((blocks, 2 * BLK, PAIR), bf16),
                 buf((blocks, 1, 2 * BLK), f32),
-                pltpu.SemaphoreType.DMA((3,)),
-                pltpu.SemaphoreType.DMA((1,)),
+                pltpu.SemaphoreType.DMA((4,)),
+                pltpu.SemaphoreType.DMA((2,)),
             ],
         ),
-        out_shape=jax.ShapeDtypeStruct((count, 3 * PAIR), bf16),
+        out_shape=[
+            jax.ShapeDtypeStruct((count, 3 * PAIR), bf16),
+            jax.ShapeDtypeStruct((y.shape[0], 1) + y.shape[1:], bf16),
+        ],
         compiler_params=pltpu.CompilerParams(vmem_limit_bytes=60 * 1024 * 1024),
         name="attend_back",
-    )(tab, k, kt, v, qt, start, d_out, ot, lse)
+    )(tab, k, kt, v, y, qt, start, d_out, ot, lse)
 
 
 def layer_norm(values, gain_vec, offset):
@@ -1032,10 +1053,10 @@
 
 
 def feed_kernel(
-    o_ref, x_ref, dy_near_ref, dy_in_ref, wo_ref, wu_ref, wd_ref, vec_ref, ub_ref,
+    o_ref, x_ref, dy_near_ref, dy_in_ref, wo_hbm, wu_hbm, wd_hbm, vec_ref, ub_ref,
     do_ref, y_home, dmid_ref, keep_ref, to_y_ref, to_x_ref, to_xy_ref, gvec_ref, gub_ref,
     attn_all, gd_ref, gu_ref, go_ref, attn_in, do_out, y_out, grad_ref, grad_in,
-    dy_ref, dy_far, a_s, a_r, a_l, d_s, d_r, d_l, y_s, y_r, y_l, g_s, g_r, c_s, c_r,
+    wo_ref, wu_ref, wd_ref, dy_ref, dy_far, w_sem, a_s, a_r, a_l, d_s, d_r, d_l, y_s, y_r, y_l, g_s, g_r, c_s, c_r,
 ):
     step = pl.program_id(0)
     steps = pl.num_programs(0)
@@ -1096,8 +1117,15 @@
             send_sem=c_s.at[i], recv_sem=c_r.at[i], device_id=origin[1], device_id_type=MESH,
         )
 
+    w_loads = [
+        pltpu.make_async_copy(src, dst, w_sem.at[i])
+        for i, (src, dst) in enumerate(((wo_hbm, wo_ref), (wu_hbm, wu_ref), (wd_hbm, wd_ref)))
+    ]
+
     @pl.when(step == 0)
     def _():
+        for copy in w_loads:
+            copy.start()
         greet(mates[1:] + [home[1], origin[1]], [home[0], origin[0]], leave)
         for i in range(feed_steps):
             for g in (1, 3, 2):
@@ -1119,6 +1147,11 @@
     def _():
         dy_copy(step - half).wait()
         dy_ref[...] = dy_far[pl.ds(pl.multiple_of((step - half) * tile, tile), tile)]
+
+    @pl.when(step == 0)
+    def _():
+        for copy in w_loads:
+            copy.wait()
 
     attn_own(step).wait()
     for g in range(1, groups):
@@ -1244,7 +1277,7 @@
         feed_kernel,
         grid=(feed_steps,),
         in_specs=[
-            any_, rows, pl.BlockSpec((tile, width), lambda i: (jnp.minimum(i, feed_steps // 2 - 1), 0)), any_, whole(w_out.shape), whole(w_up.shape), whole(w_down.shape),
+            any_, rows, pl.BlockSpec((tile, width), lambda i: (jnp.minimum(i, feed_steps // 2 - 1), 0)), any_, any_, any_, any_,
             whole(vecs.shape), whole(up_bias.shape),
         ],
         out_specs=[any_, any_, rows] + [whole(piece)] * 4 + [whole(vecs.shape), whole(up_bias.shape)],
@@ -1269,8 +1302,12 @@
             buf((feed_steps, tile, width), bf16),
             buf((shards, flat, width), bf16),
             buf((2, flat, width), bf16),
+            buf(w_out.shape, bf16),
+            buf(w_up.shape, bf16),
+            buf(w_down.shape, bf16),
             buf((tile, width), bf16),
             buf((count // 2, width), bf16),
+            dma((3,)),
             dma((3, feed_steps)),
             dma((3, feed_steps)),
             dma((feed_steps,)),
@@ -1296,10 +1333,10 @@
 
 
 def tail_kernel(
-    d_qkv_hbm, ut_hbm, x_hbm, dmid_hbm, w_ref, gain_ref, bias_ref, keep_ref, from_y_ref, from_x_ref, from_xy_ref,
+    d_qkv_hbm, ut_hbm, x_hbm, dmid_hbm, keep_hbm, from_y_hbm, from_x_hbm, from_xy_hbm, w_ref, vec_ref,
     gvecs_ref, gub_ref,
     home_buf, gfull, wall, sum_ref,
-    d_qkv, ut_ref, total, sums, gw_ref, core_out, x_ref, dmid_ref, core_buf, own_dh, x_out, x_buf, dx_out,
+    keep_ref, from_y_ref, from_x_ref, from_xy_ref, d_qkv, ut_ref, total, sums, gw_ref, core_out, x_ref, dmid_ref, core_buf, own_dh, x_out, x_buf, dx_out,
     gsum, gz1s, gz1r, gz2s, gz2r,
     wy, ws, wz1s, wz1r, wz2s, wz2r, wfull,
     small_ref, small_out, small_in,
@@ -1323,7 +1360,13 @@
         pltpu.make_async_copy(src, dst, in_sem.at[i])
         for i, (src, dst) in enumerate(((ut_hbm, ut_ref), (x_hbm, x_ref), (dmid_hbm, dmid_ref)))
     ]
-    for copy in loads + inputs:
+    g_loads = [
+        pltpu.make_async_copy(src, dst, in_sem.at[3 + i])
+        for i, (src, dst) in enumerate((
+            (keep_hbm, keep_ref), (from_y_hbm, from_y_ref), (from_x_hbm, from_x_ref), (from_xy_hbm, from_xy_ref)
+        ))
+    ]
+    for copy in loads[:2] + g_loads + loads[2:] + inputs:
         copy.start()
     small_ref[...] = jnp.zeros_like(small_ref)
     small_ref[2:4] = gvecs_ref[1:3]
@@ -1366,7 +1409,7 @@
         shard = gw_ref.shape[1]
         for j in range(gw_ref.shape[0]):
             part = pl.ds(j * shard, shard)
-            gain, bias = (jnp.broadcast_to(ref[:, part], (shard, shard)).T[:, :1] for ref in (gain_ref, bias_ref))
+            gain, bias = (jnp.broadcast_to(ref[:, part], (shard, shard)).T[:, :1] for ref in (vec_ref.at[0:1], vec_ref.at[1:2]))
             gw_ref[j] = (total[part] * gain + bias * sums[...]).astype(bf16)
             w = w_ref[part].astype(f32)
             for i, term in enumerate((w * total[part], w * sums[...])):
@@ -1378,6 +1421,9 @@
     g_copy = {}
 
     def g_start(p):
+        if p == 0:
+            for copy in g_loads:
+                copy.wait()
         for half in range(2):
             part = pl.ds(96 * half, 96)
             gsum[p, part] = (
@@ -1471,7 +1517,7 @@
         x_copy[i].wait()
         d_low = own_dh[0, part] + core_buf[0, part].astype(f32) + x_buf[part].astype(f32)
         unit, inv = norm_parts(x_ref[part].astype(f32))
-        scaled = d_low * gain_ref[...]
+        scaled = d_low * vec_ref[0:1]
         dx = dmid_ref[part] + inv * (
             scaled
             - jnp.mean(scaled, axis=-1, keepdims=True)
@@ -1579,7 +1625,7 @@
         g_copy["x", p].wait()
 
 
-def tail(d_qkv, unit_t, x, dmid, weight, gain, bias, keep, from_y, from_x, from_xy, gvecs, gub):
+def tail(d_qkv, unit_t, x, dmid, keep, from_y, from_x, from_xy, weight, vecs, gvecs, gub):
     count, width = x.shape
     shard = width // 4
     half = count // 2
@@ -1590,7 +1636,7 @@
     buf = pltpu.VMEM
     return pl.pallas_call(
         tail_kernel,
-        in_specs=[pl.BlockSpec(memory_space=pl.ANY)] * 4 + [vmem] * 9,
+        in_specs=[pl.BlockSpec(memory_space=pl.ANY)] * 8 + [vmem] * 4,
         out_specs=[vmem] * 4,
         out_shape=[
             jax.ShapeDtypeStruct((2, half, width), bf16),
@@ -1599,6 +1645,10 @@
             jax.ShapeDtypeStruct((16, width), f32),
         ],
         scratch_shapes=[
+            buf(keep.shape, bf16),
+            buf(keep.shape, bf16),
+            buf(keep.shape, bf16),
+            buf(keep.shape, bf16),
             buf(d_qkv.shape, bf16),
             buf(unit_t.shape, bf16),
             buf(weight.shape, f32),
@@ -1641,21 +1691,20 @@
             dma((8,)),
             dma((5,)),
             dma((5,)),
-            dma((3,)),
+            dma((7,)),
         ],
         compiler_params=pltpu.CompilerParams(
-            collective_id=5, has_side_effects=True, vmem_limit_bytes=56 * 1024 * 1024
+            collective_id=5, has_side_effects=True, vmem_limit_bytes=60 * 1024 * 1024
         ),
         name="tail",
-    )(d_qkv, unit_t, x, dmid, weight, gain, bias, keep, from_y, from_x, from_xy, gvecs, gub)
+    )(d_qkv, unit_t, x, dmid, keep, from_y, from_x, from_xy, weight, vecs, gvecs, gub)
 
 def results_kernel(
-    y_ref, dx_ref, down_ref, up_ref, out_ref, wall_ref, sum_ref,
-    y_out, dx_out, gd_ref, gu_ref, go_ref, gq_ref, *vectors,
+    dx_ref, down_ref, up_ref, out_ref, wall_ref, sum_ref,
+    dx_out, gd_ref, gu_ref, go_ref, gq_ref, *vectors,
 ):
     step = pl.program_id(0)
     width = dx_ref.shape[-1]
-    y_out[:, 0] = y_ref[...]
     dx_out[:, 0] = dx_ref[...].astype(f32)
     gd_ref[...] = down_ref[...].astype(f32)
     gu_ref[...] = up_ref[...].astype(f32)
@@ -1670,7 +1719,7 @@
     vectors[6][...] = sum_ref[pl.ds(6 + mine, 1), :]
 
 
-def results(y, dx, flat, wall, sums):
+def results(dx, flat, wall, sums):
     half, width = dx.shape[1:]
     shard = wall.shape[1]
     steps = 4
@@ -1683,7 +1732,6 @@
         grid=(steps,),
         in_specs=[
             tokens,
-            tokens,
             pl.BlockSpec((shard, width), lambda i: (i, 0)),
             pl.BlockSpec((shard, width), lambda i: (steps + i, 0)),
             pl.BlockSpec((shard, width), lambda i: (2 * steps, 0)),
@@ -1691,7 +1739,6 @@
             whole(sums.shape),
         ],
         out_specs=[
-            tokens_out,
             tokens_out,
             pl.BlockSpec((shard, width), lambda i: (i, 0)),
             pl.BlockSpec((shard, width), lambda i: (0, i)),
@@ -1701,7 +1748,6 @@
         + [whole((1, shard))] * 6
         + [whole((1, width))],
         out_shape=[
-            shape((2, 1, half, width), bf16),
             shape((2, 1, half, width), f32),
             shape((width, width), f32),
             shape((shard, 4 * width), f32),
@@ -1710,8 +1756,9 @@
         ]
         + [shape((1, shard), f32)] * 6
         + [shape((1, width), f32)],
+        compiler_params=pltpu.CompilerParams(vmem_limit_bytes=60 * 1024 * 1024),
         name="results",
-    )(y, dx, flat, flat, flat, wall, sums)
+    )(dx, flat, flat, flat, wall, sums)
 
 
 def place(z, x, y, c):
@@ -1750,18 +1797,17 @@
     ) = head(
         inputs, out_grad, segment_ids.reshape(2, -1, 128), block_order, vectors, w_qkv, w_out, w_up, w_down
     )
-    gain_one, bias_one = vecs[0:1], vecs[1:2]
     o, ot, lse = attend(tab, qt, start, k, vt)
     d_o, outputs, d_middle, keep, to_y, to_x, to_xy, g_vecs, g_ubias = feed(
         o.reshape(4, -1, PAIR), own_x, near_dy, out_grad, full_out, full_up, full_down, vecs, full_ubias, 4
     )
     from_y, from_x, from_xy = swap(to_y, dy=1), swap(to_x, dx=1), swap(to_xy, dy=1, dx=1)
-    d_qkv = attend_back(tab, k, kt, v, qt, start, d_o.reshape(-1, PAIR), ot, lse)
+    d_qkv, outputs = attend_back(tab, k, kt, v, outputs, qt, start, d_o.reshape(-1, PAIR), ot, lse)
     dx, flat, heads, sums = tail(
-        d_qkv.reshape(4, -1, 3 * PAIR), unit, own_x, d_middle, w_heads, gain_one, bias_one,
-        keep, from_y, from_x, from_xy, g_vecs, g_ubias,
-    )
-    outputs, input_grad, grad_down, grad_up, grad_out, grad_qkv, *vec = results(outputs, dx, flat, heads, sums)
+        d_qkv.reshape(4, -1, 3 * PAIR), unit, own_x, d_middle, keep, from_y, from_x, from_xy,
+        w_heads, vecs, g_vecs, g_ubias,
+    )
+    input_grad, grad_down, grad_up, grad_out, grad_qkv, *vec = results(dx, flat, heads, sums)
     vec = [member.reshape(-1) for member in vec]
     return (
         outputs, input_grad, grad_qkv, grad_out, grad_up, grad_down,

time: 224 us -> 218 us (0.973)
  Pallas kernels: 217 us -> 212 us
    pallas_call x1, Pallas kernels: 21.2 us -> 18.5 us  [attend(): pl.pallas_call(attend_kernel, grid_spec=pltpu.PrefetchScalarGridSpec(num_...]
  transfers between devices with their start and end apart: 3 -> 3, of which waited for: 0 -> 0; matrix products, arithmetic and copies ran while one was open for 1% -> 0% of each run, Pallas kernels for 14% -> 15%
where the time goes in v6:
time: 218 us; the launch traced here: 217 us
  Pallas kernels  212 us (97%)
  starting transfers between devices  3.55 us (2%)
    pallas_call x1, Pallas kernels, tail(): pl.pallas_call(tail_kernel, in_specs=[pl.BlockSpec(memory_space=pl.ANY)]...  65.1 us
    pallas_call x1, Pallas kernels, head(): pl.pallas_call(head_kernel, in_specs=[any_, any_, vmem, smem] + [vmem] *...  47.1 us
    pallas_call x1, Pallas kernels, feed(): pl.pallas_call(feed_kernel, grid=(feed_steps,), in_specs=[any_, rows, pl....  44.3 us
    pallas_call x1, Pallas kernels, attend_back(): pl.pallas_call(attend_back_kernel, grid_spec=pltpu.PrefetchScalarGridSpec...  31.6 us
    pallas_call x1, Pallas kernels, attend(): pl.pallas_call(attend_kernel, grid_spec=pltpu.PrefetchScalarGridSpec(num_...  18.5 us
    pallas_call x1, Pallas kernels, results(): pl.pallas_call(results_kernel, grid=(steps,), in_specs=[tokens, pl.BlockS...  4.9 us
  transfers between devices with their start and end apart: 3, of which 0 were waited for; matrix products, arithmetic and copies ran while one was open for 0% of the time, Pallas kernels for 15%

profile of v6, /device:TPU:0, one launch (start us, length us, event | category | flops | bytes accessed | tf_op | source)
XLA Modules:
  0.0 217.3 jit_solution(7028039819259291139)
XLA Ops:
  0.7 47.1 %head.1 = (bf16[128,4096]{1,0:T(8,128)(2,1)}, bf16[4096,128]{1,0:T(8,128)(2,1)}, bf16[128,4096]{1,0:T(8,128)(2,1)}, bf16[4096,128]{1,0:T(8,128)(2,1)}, bf16[128,...) custom-call(bf16[2,1,512,512]{3,2,1,0:T(8,128)(2,1)} %x_in_ref.1, ...), custom_call_target="tpu_custom_call" | custom-call | tf_op jit(solution)/shard_map/head/pallas_call | solution.py:1002
  47.8 18.5 %attend.1 = (bf16[4096,128]{1,0:T(8,128)(2,1)}, f32[16,128,256]{2,1,0:T(8,128)}, f32[16,1,512]{2,1,0:T(1,128)}) custom-call(s32[8,128]{1,0:T(8,128)} %get-tuple-element.59.tab_ref, bf16[128,4096]{1,0:T(8,128)(2,1)} %get-tuple-element.63.qt_ref, s32[16,1,256]{2,1,0:T(1,128)} %get-tuple-element.64.start_ref, bf16[4096,128]{1,0:T(8,128)(2,1)} %get-tuple-element.60.k_ref.k_hbm, ...), custom_call_target="tpu_custom_call" | custom-call | tf_op jit(solution)/shard_map/attend/pallas_call | solution.py:169
  66.3 44.3 %feed.1 = (bf16[4,1024,128]{2,1,0:T(8,128)(2,1)}, bf16[2,512,512]{2,1,0:T(8,128)(2,1)}, f32[1024,512]{1,0:T(8,128)}, bf16[3,192,512]{2,1,0:T(8,128)(2,1)}, bf16[...) custom-call(bf16[4,1024,128]{2,1,0:T(8,128)(2,1)} %bitcast.23, ...), custom_call_target="tpu_custom_call" | custom-call | tf_op jit(solution)/shard_map/feed/pallas_call | solution.py:1276
  110.7 1.6 collective-permute-start
  112.3 1.5 collective-permute-start.1
  113.8 0.5 collective-permute-start.2
  114.2 31.6 %attend_back.1 = (bf16[4096,384]{1,0:T(8,128)(2,1)}, bf16[2,1,512,512]{3,2,1,0:T(8,128)(2,1)}) custom-call(s32[8,128]{1,0:T(8,128)} %get-tuple-element.59.tab_ref, bf16[4096,128]{1,0:T(8,128)(2,1)} %get-tuple-element.60.k_ref.k_hbm, bf16[128,4096]{1,0:T(8,128)(2,1)} %get-tuple-element.61.kt_hbm, bf16[4096,128]{1,0:T(8,128)(2,1)} %get-tuple-element.62.v_hbm, ...), custom_call_target="tpu_custom_call" | custom-call | tf_op jit(solution)/shard_map/attend_back/pallas_call | solution.py:297
  145.8 0.0 collective-permute-done.from_y_hbm
  145.8 0.0 copy-start
  145.8 0.0 collective-permute-done.1.from_x_hbm
  145.9 0.0 copy-start.1
  145.9 0.0 collective-permute-done.2.from_xy_hbm
  145.9 0.0 copy-start.2
  145.9 0.8 copy-done
  146.6 0.2 copy-done.1
  146.8 0.2 copy-done.2
  147.0 65.1 %tail.1 = (bf16[2,512,512]{2,1,0:T(8,128)(2,1)}, bf16[3,2,192,512]{3,2,1,0:T(8,128)(2,1)}, bf16[4,128,384]{2,1,0:T(8,128)(2,1)}, f32[16,512]{1,0:T(8,128)}) custom-call(bf16[4,1024,384]{2,1,0:T(8,128)(2,1)} %bitcast.22, bf16[512,4096]{1,0:T(8,128)(2,1)} %get-tuple-element.80.ut_hbm, bf16[1024,512]{1,0:T(8,128)(2,1)} %get-tuple-element.67.x_ref.x_hbm, ...), custom_call_target="tpu_custom_call" | custom-call | tf_op jit(solution)/shard_map/tail/pallas_call | solution.py:1637
  212.2 4.9 %results.1 = (f32[2,1,512,512]{3,2,1,0:T(8,128)}, f32[512,512]{1,0:T(8,128)}, f32[128,2048]{1,0:T(8,128)}, f32[128,512]{1,0:T(8,128)}, f32[128,1536]{1,0:T(8,128...) custom-call(bf16[2,512,512]{2,1,0:T(8,128)(2,1)} %get-tuple-element., ...), custom_call_target="tpu_custom_call" | custom-call | tf_op jit(solution)/shard_map/results/pallas_call | solution.py:1730
Async XLA Ops:
  110.7 35.2 %collective-permute-start = (bf16[3,192,512]{2,1,0:T(8,128)(2,1)}, bf16[3,192,512]{2,1,0:T(8,128)(2,1)S(1)}, u32[]{:S(2)}, u32[]{:S(2)}) collective-permute-start(bf16[3,192,512]{2,1,0:T(8,128)(2,1)} %get-tuple-element.83), channel_id=1, source_target_pairs={{0,2},{1,3},{2,0},{3,1},{4,6},{5,7},{6,4},{7,5},{8,10},{9,11},{10,... | collective-permute-start | bytes 1769480 | tf_op jit(solution)/shard_map/ppermute | solution.py:1783
  112.3 33.6 %collective-permute-start.1 = (bf16[3,192,512]{2,1,0:T(8,128)(2,1)}, bf16[3,192,512]{2,1,0:T(8,128)(2,1)S(1)}, u32[]{:S(2)}, u32[]{:S(2)}) collective-permute-start(bf16[3,192,512]{2,1,0:T(8,128)(2,1)} %get-tuple-element.84), channel_id=1, source_target_pairs={{0,4},{1,5},{2,6},{3,7},{4,0},{5,1},{6,2},{7,3},{8,12},{9,13},{10,... | collective-permute-start | bytes 1769480 | tf_op jit(solution)/shard_map/ppermute | solution.py:1783
  113.8 32.1 %collective-permute-start.2 = (bf16[3,192,512]{2,1,0:T(8,128)(2,1)}, bf16[3,192,512]{2,1,0:T(8,128)(2,1)S(1)}, u32[]{:S(2)}, u32[]{:S(2)}) collective-permute-start(bf16[3,192,512]{2,1,0:T(8,128)(2,1)} %get-tuple-element.85), channel_id=1, source_target_pairs={{0,6},{1,7},{2,4},{3,5},{4,2},{5,3},{6,0},{7,1},{8,14},{9,15},{10,... | collective-permute-start | bytes 1769480 | tf_op jit(solution)/shard_map/ppermute | solution.py:1783
  145.8 0.8 copy-start
  145.9 1.0 copy-start.1
  145.9 1.2 copy-start.2

commit v7 on v6

--- a/solution.py
+++ b/solution.py
@@ -198,15 +198,15 @@
 
 
 def attend_back_kernel(
-    tab_ref, k_hbm, kt_hbm, v_hbm, y_hbm, qt_ref, start_ref, do_ref, ot_ref, lse_ref, out_hbm, y_out,
-    k_ref, kt_ref, v_ref, y_buf, out_buf, dqt, dk, dv, dot, dom, qm, delta, in_sem, out_sem,
+    tab_ref, k_hbm, kt_hbm, v_hbm, qt_ref, start_ref, do_ref, ot_ref, lse_ref, out_hbm,
+    k_ref, kt_ref, v_ref, out_buf, dqt, dk, dv, dot, dom, qm, delta, in_sem, out_sem,
 ):
     blocks = start_ref.shape[0]
     row = lax.broadcasted_iota(jnp.int32, (BLK, 2 * BLK), 0)
     reach = row - jnp.bitwise_and(lax.broadcasted_iota(jnp.int32, (BLK, 2 * BLK), 1), BLK - 1)
     loads = [
         pltpu.make_async_copy(src, dst, in_sem.at[i])
-        for i, (src, dst) in enumerate(((k_hbm, k_ref), (kt_hbm, kt_ref), (v_hbm, v_ref), (y_hbm, y_buf)))
+        for i, (src, dst) in enumerate(((k_hbm, k_ref), (kt_hbm, kt_ref), (v_hbm, v_ref)))
     ]
     for copy in loads:
         copy.start()
@@ -236,8 +236,6 @@
     lax.fori_loop(0, blocks // 2, prepare_two, 0)
     for copy in loads:
         copy.wait()
-    y_copy = pltpu.make_async_copy(y_buf, y_out.at[:, 0], out_sem.at[1])
-    y_copy.start()
 
     def tile(kb, qb, live):
         kt = kt_ref[:, at(kb)]
@@ -286,10 +284,9 @@
 
     lax.fori_loop(0, blocks // 4, close_four, 0)
     pltpu.make_async_copy(out_hbm, out_hbm, out_sem.at[0]).wait()
-    y_copy.wait()
-
-
-def attend_back(tab, k, kt, v, y, qt, start, d_out, ot, lse):
+
+
+def attend_back(tab, k, kt, v, qt, start, d_out, ot, lse):
     count = k.shape[0]
     blocks = count // BLK
     vmem, any_ = pl.BlockSpec(memory_space=pltpu.VMEM), pl.BlockSpec(memory_space=pl.ANY)
@@ -299,13 +296,12 @@
         grid_spec=pltpu.PrefetchScalarGridSpec(
             num_scalar_prefetch=1,
             grid=(),
-            in_specs=[any_] * 4 + [vmem] * 5,
-            out_specs=[any_, any_],
+            in_specs=[any_] * 3 + [vmem] * 5,
+            out_specs=any_,
             scratch_shapes=[
                 buf(k.shape, bf16),
                 buf(kt.shape, bf16),
                 buf(v.shape, bf16),
-                buf(y.shape, bf16),
                 buf((blocks, BLK, 3 * PAIR), bf16),
                 buf((blocks, PAIR, BLK), f32),
                 buf((blocks, BLK, PAIR), f32),
@@ -314,17 +310,14 @@
                 buf((blocks, 2 * BLK, PAIR), bf16),
                 buf((blocks, 2 * BLK, PAIR), bf16),
                 buf((blocks, 1, 2 * BLK), f32),
-                pltpu.SemaphoreType.DMA((4,)),
-                pltpu.SemaphoreType.DMA((2,)),
+                pltpu.SemaphoreType.DMA((3,)),
+                pltpu.SemaphoreType.DMA((1,)),
             ],
         ),
-        out_shape=[
-            jax.ShapeDtypeStruct((count, 3 * PAIR), bf16),
-            jax.ShapeDtypeStruct((y.shape[0], 1) + y.shape[1:], bf16),
-        ],
+        out_shape=jax.ShapeDtypeStruct((count, 3 * PAIR), bf16),
         compiler_params=pltpu.CompilerParams(vmem_limit_bytes=60 * 1024 * 1024),
         name="attend_back",
-    )(tab, k, kt, v, y, qt, start, d_out, ot, lse)
+    )(tab, k, kt, v, qt, start, d_out, ot, lse)
 
 
 def layer_norm(values, gain_vec, offset):
@@ -1047,14 +1040,14 @@
         ),
         name="head",
     )(x_in, dy_in, docs_in, order, *[v.reshape(-1, shard) for v in vectors], w_qkv, w_out, w_up, w_down)
-FF_TILE = 512
+FF_TILE = 1024
 PIECES = 3
 feed_steps = 4
 
 
 def feed_kernel(
     o_ref, x_ref, dy_near_ref, dy_in_ref, wo_hbm, wu_hbm, wd_hbm, vec_ref, ub_ref,
-    do_ref, y_home, dmid_ref, keep_ref, to_y_ref, to_x_ref, to_xy_ref, gvec_ref, gub_ref,
+    do_ref, y_home, y_far_ref, dmid_ref, keep_ref, to_y_ref, to_x_ref, to_xy_ref, gvec_ref, gub_ref,
     attn_all, gd_ref, gu_ref, go_ref, attn_in, do_out, y_out, grad_ref, grad_in,
     wo_ref, wu_ref, wd_ref, dy_ref, dy_far, w_sem, a_s, a_r, a_l, d_s, d_r, d_l, y_s, y_r, y_l, g_s, g_r, c_s, c_r,
 ):
@@ -1092,17 +1085,17 @@
     def do_own(i):
         return pltpu.make_async_copy(do_out.at[i, 0], do_ref.at[0, pl.ds(i * tile, tile)], d_l.at[i])
 
-    def y_rows(i, block):
-        return y_home.at[block, pl.ds(lax.rem(i, half) * tile, tile)]
-
-    def y_copy(i, turn, block):
+    def y_rows(i):
+        return y_home.at[pl.ds(i * tile, tile)]
+
+    def y_copy(i):
         return pltpu.make_async_remote_copy(
-            src_ref=y_out.at[i], dst_ref=y_rows(i, block),
-            send_sem=y_s.at[i], recv_sem=y_r.at[i], device_id=home[turn], device_id_type=MESH,
-        )
-
-    def y_own(i, block):
-        return pltpu.make_async_copy(y_out.at[i], y_rows(i, block), y_l.at[i])
+            src_ref=y_out.at[i], dst_ref=y_rows(i),
+            send_sem=y_s.at[i], recv_sem=y_r.at[i], device_id=home[0], device_id_type=MESH,
+        )
+
+    def y_own(i):
+        return pltpu.make_async_copy(y_out.at[i], y_rows(i), y_l.at[i])
 
     def grad_copy(i):
         return pltpu.make_async_remote_copy(
@@ -1187,19 +1180,21 @@
         d_low = d_low + contract(d_hidden_low, up, 1, 1)
         gd_ref[part, :] += contract(active, dy, 0, 0)
         gu_ref[:, part] += contract(low, d_hidden_low, 0, 0)
-    y_out[step] = total.astype(bf16)
-
-    @pl.when((step < half) & stay)
+    @pl.when(step < half)
     def _():
-        y_own(step, upper).start()
-
-    @pl.when((step < half) & leave)
-    def _():
-        y_copy(step, 0, upper).start()
+        y_out[step] = total.astype(bf16)
+
+        @pl.when(stay)
+        def _():
+            y_own(step).start()
+
+        @pl.when(leave)
+        def _():
+            y_copy(step).start()
 
     @pl.when(step >= half)
     def _():
-        y_copy(step, 1, upper).start()
+        y_far_ref[...] = total.astype(bf16)
 
     scaled = d_low * gain
     d_middle = dy32 + inv * (
@@ -1244,13 +1239,11 @@
             if j < half:
                 @pl.when(stay)
                 def _():
-                    y_own(j, odd).wait()
+                    y_own(j).wait()
 
                 @pl.when(leave)
                 def _():
-                    y_copy(j, 0, odd).wait()
-            else:
-                y_copy(j, 1, 1 - odd).wait()
+                    y_copy(j).wait()
         sixth = keep_ref.shape[1]
         for j in range(2):
             grad_copy(j).wait()
@@ -1280,10 +1273,12 @@
             any_, rows, pl.BlockSpec((tile, width), lambda i: (jnp.minimum(i, feed_steps // 2 - 1), 0)), any_, any_, any_, any_,
             whole(vecs.shape), whole(up_bias.shape),
         ],
-        out_specs=[any_, any_, rows] + [whole(piece)] * 4 + [whole(vecs.shape), whole(up_bias.shape)],
+        out_specs=[any_, any_, pl.BlockSpec((tile, width), lambda i: (jnp.maximum(i - feed_steps // 2, 0), 0)), rows]
+        + [whole(piece)] * 4 + [whole(vecs.shape), whole(up_bias.shape)],
         out_shape=[
             shape((groups, count, PAIR), bf16),
-            shape((2, count // 2, width), bf16),
+            shape((count // 2, width), bf16),
+            shape((count // 2, width), bf16),
             shape((count, width), f32),
             shape(piece, bf16),
             shape(piece, bf16),
@@ -1299,7 +1294,7 @@
             buf(w_out.shape, f32),
             buf((groups, count, PAIR), bf16),
             buf((feed_steps, groups, tile, PAIR), bf16),
-            buf((feed_steps, tile, width), bf16),
+            buf((feed_steps // 2, tile, width), bf16),
             buf((shards, flat, width), bf16),
             buf((2, flat, width), bf16),
             buf(w_out.shape, bf16),
@@ -1314,9 +1309,9 @@
             dma((3, feed_steps)),
             dma((3, feed_steps)),
             dma((feed_steps,)),
-            dma((feed_steps,)),
-            dma((feed_steps,)),
-            dma((feed_steps,)),
+            dma((feed_steps // 2,)),
+            dma((feed_steps // 2,)),
+            dma((feed_steps // 2,)),
             dma((2,)),
             dma((2,)),
             dma((feed_steps // 2,)),
@@ -1700,11 +1695,14 @@
     )(d_qkv, unit_t, x, dmid, keep, from_y, from_x, from_xy, weight, vecs, gvecs, gub)
 
 def results_kernel(
-    dx_ref, down_ref, up_ref, out_ref, wall_ref, sum_ref,
-    dx_out, gd_ref, gu_ref, go_ref, gq_ref, *vectors,
+    y_near_ref, y_far_ref, dx_ref, down_ref, up_ref, out_ref, wall_ref, sum_ref,
+    y_out, dx_out, gd_ref, gu_ref, go_ref, gq_ref, *vectors,
 ):
     step = pl.program_id(0)
     width = dx_ref.shape[-1]
+    odd = lax.rem(lax.axis_index("z"), 2)
+    y_out[odd, 0] = y_near_ref[...]
+    y_out[1 - odd, 0] = y_far_ref[...]
     dx_out[:, 0] = dx_ref[...].astype(f32)
     gd_ref[...] = down_ref[...].astype(f32)
     gu_ref[...] = up_ref[...].astype(f32)
@@ -1719,7 +1717,7 @@
     vectors[6][...] = sum_ref[pl.ds(6 + mine, 1), :]
 
 
-def results(dx, flat, wall, sums):
+def results(y_near, y_far, dx, flat, wall, sums):
     half, width = dx.shape[1:]
     shard = wall.shape[1]
     steps = 4
@@ -1731,6 +1729,8 @@
         results_kernel,
         grid=(steps,),
         in_specs=[
+            pl.BlockSpec((half // steps, width), lambda i: (i, 0)),
+            pl.BlockSpec((half // steps, width), lambda i: (i, 0)),
             tokens,
             pl.BlockSpec((shard, width), lambda i: (i, 0)),
             pl.BlockSpec((shard, width), lambda i: (steps + i, 0)),
@@ -1740,6 +1740,7 @@
         ],
         out_specs=[
             tokens_out,
+            tokens_out,
             pl.BlockSpec((shard, width), lambda i: (i, 0)),
             pl.BlockSpec((shard, width), lambda i: (0, i)),
             whole((shard, width)),
@@ -1748,6 +1749,7 @@
         + [whole((1, shard))] * 6
         + [whole((1, width))],
         out_shape=[
+            shape((2, 1, half, width), bf16),
             shape((2, 1, half, width), f32),
             shape((width, width), f32),
             shape((shard, 4 * width), f32),
@@ -1758,7 +1760,7 @@
         + [shape((1, width), f32)],
         compiler_params=pltpu.CompilerParams(vmem_limit_bytes=60 * 1024 * 1024),
         name="results",
-    )(dx, flat, flat, flat, wall, sums)
+    )(y_near, y_far, dx, flat, flat, flat, wall, sums)
 
 
 def place(z, x, y, c):
@@ -1798,16 +1800,19 @@
         inputs, out_grad, segment_ids.reshape(2, -1, 128), block_order, vectors, w_qkv, w_out, w_up, w_down
     )
     o, ot, lse = attend(tab, qt, start, k, vt)
-    d_o, outputs, d_middle, keep, to_y, to_x, to_xy, g_vecs, g_ubias = feed(
+    d_o, y_near, y_far, d_middle, keep, to_y, to_x, to_xy, g_vecs, g_ubias = feed(
         o.reshape(4, -1, PAIR), own_x, near_dy, out_grad, full_out, full_up, full_down, vecs, full_ubias, 4
     )
+    y_far = move(y_far, [(place(z, x, y, c), place(2 * c + 1 - z // 2, x, y, z % 2)) for z, x, y, c in everyone()])
     from_y, from_x, from_xy = swap(to_y, dy=1), swap(to_x, dx=1), swap(to_xy, dy=1, dx=1)
-    d_qkv, outputs = attend_back(tab, k, kt, v, outputs, qt, start, d_o.reshape(-1, PAIR), ot, lse)
+    d_qkv = attend_back(tab, k, kt, v, qt, start, d_o.reshape(-1, PAIR), ot, lse)
     dx, flat, heads, sums = tail(
         d_qkv.reshape(4, -1, 3 * PAIR), unit, own_x, d_middle, keep, from_y, from_x, from_xy,
         w_heads, vecs, g_vecs, g_ubias,
     )
-    input_grad, grad_down, grad_up, grad_out, grad_qkv, *vec = results(dx, flat, heads, sums)
+    outputs, input_grad, grad_down, grad_up, grad_out, grad_qkv, *vec = results(
+        y_near, y_far, dx, flat, heads, sums
+    )
     vec = [member.reshape(-1) for member in vec]
     return (
         outputs, input_grad, grad_qkv, grad_out, grad_up, grad_down,

time: 218 us -> 213 us (0.977)
  Pallas kernels: 212 us -> 205 us
    pallas_call x1, Pallas kernels: 44.3 us -> 37 us  [feed(): pl.pallas_call(feed_kernel, grid=(feed_steps,), in_specs=[any_, rows, pl....]
    ppermute x3 -> x4, starting transfers between devices: 3.55 us -> 4.59 us  [move(): return lax.ppermute(value, AXES, pairs)]
  transfers between devices with their start and end apart: 3 -> 4, of which waited for: 0 -> 0; matrix products, arithmetic and copies ran while one was open for 0% -> 0% of each run, Pallas kernels for 15% -> 46%
where the time goes in v7:
time: 213 us
  Pallas kernels  205 us (96%)
  starting transfers between devices  4.59 us (2%)
    pallas_call x1, Pallas kernels, tail(): pl.pallas_call(tail_kernel, in_specs=[pl.BlockSpec(memory_space=pl.ANY)]...  65.8 us
    pallas_call x1, Pallas kernels, head(): pl.pallas_call(head_kernel, in_specs=[any_, any_, vmem, smem] + [vmem] *...  47.1 us
    pallas_call x1, Pallas kernels, feed(): pl.pallas_call(feed_kernel, grid=(feed_steps,), in_specs=[any_, rows, pl....  37 us
    pallas_call x1, Pallas kernels, attend_back(): pl.pallas_call(attend_back_kernel, grid_spec=pltpu.PrefetchScalarGridSpec...  31.2 us
    pallas_call x1, Pallas kernels, attend(): pl.pallas_call(attend_kernel, grid_spec=pltpu.PrefetchScalarGridSpec(num_...  18.5 us
    pallas_call x1, Pallas kernels, results(): pl.pallas_call(results_kernel, grid=(steps,), in_specs=[pl.BlockSpec((hal...  5.46 us
    ppermute x4, starting transfers between devices, move(): return lax.ppermute(value, AXES, pairs)  4.59 us
  transfers between devices with their start and end apart: 4, of which 0 were waited for; matrix products, arithmetic and copies ran while one was open for 0% of the time, Pallas kernels for 46%

profile of v7, /device:TPU:0, one launch (start us, length us, event | category | flops | bytes accessed | tf_op | source)
XLA Modules:
  0.0 212.7 jit_solution(6571547843136771436)
XLA Ops:
  0.7 47.1 %head.1 = (bf16[128,4096]{1,0:T(8,128)(2,1)}, bf16[4096,128]{1,0:T(8,128)(2,1)}, bf16[128,4096]{1,0:T(8,128)(2,1)}, bf16[4096,128]{1,0:T(8,128)(2,1)}, bf16[128,...) custom-call(bf16[2,1,512,512]{3,2,1,0:T(8,128)(2,1)} %x_in_ref.1, ...), custom_call_target="tpu_custom_call" | custom-call | tf_op jit(solution)/shard_map/head/pallas_call | solution.py:995
  47.8 18.5 %attend.1 = (bf16[4096,128]{1,0:T(8,128)(2,1)}, f32[16,128,256]{2,1,0:T(8,128)}, f32[16,1,512]{2,1,0:T(1,128)}) custom-call(s32[8,128]{1,0:T(8,128)} %get-tuple-element.59.tab_ref, bf16[128,4096]{1,0:T(8,128)(2,1)} %get-tuple-element.60.qt_ref, s32[16,1,256]{2,1,0:T(1,128)} %get-tuple-element.61.start_ref, bf16[4096,128]{1,0:T(8,128)(2,1)} %get-tuple-element.62.k_ref.k_hbm, ...), custom_call_target="tpu_custom_call" | custom-call | tf_op jit(solution)/shard_map/attend/pallas_call | solution.py:169
  66.3 37.0 %feed.1 = (bf16[4,1024,128]{2,1,0:T(8,128)(2,1)}, bf16[512,512]{1,0:T(8,128)(2,1)}, bf16[512,512]{1,0:T(8,128)(2,1)}, f32[1024,512]{1,0:T(8,128)}, bf16[3,192,51...) custom-call(bf16[4,1024,128]{2,1,0:T(8,128)(2,1)} %bitcast.24, ...), custom_call_target="tpu_custom_call" | custom-call | tf_op jit(solution)/shard_map/feed/pallas_call | solution.py:1269
  103.3 2.6 %collective-permute-start.1 = (bf16[3,192,512]{2,1,0:T(8,128)(2,1)}, bf16[3,192,512]{2,1,0:T(8,128)(2,1)S(1)}, u32[]{:S(2)}, u32[]{:S(2)}) collective-permute-start(bf16[3,192,512]{2,1,0:T(8,128)(2,1)} %get-tuple-element.82), channel_id=1, source_target_pairs={{0,2},{1,3},{2,0},{3,1},{4,6},{5,7},{6,4},{7,5},{8,10},{9,11},{10,... | collective-permute-start | bytes 1769480 | tf_op jit(solution)/shard_map/ppermute | solution.py:1785
  105.9 1.2 collective-permute-start.2
  107.2 0.3 collective-permute-start.3
  107.5 0.4 collective-permute-start
  107.9 31.2 %attend_back.1 = bf16[4096,384]{1,0:T(8,128)(2,1)} custom-call(s32[8,128]{1,0:T(8,128)} %get-tuple-element.59.tab_ref, bf16[4096,128]{1,0:T(8,128)(2,1)} %get-tuple-element.62.k_ref.k_hbm, bf16[128,4096]{1,0:T(8,128)(2,1)} %get-tuple-element.74.kt_hbm, bf16[4096,128]{1,0:T(8,128)(2,1)} %get-tuple-element.75.v_hbm, ...), custom_call_target="tpu_custom_call" | custom-call | tf_op jit(solution)/shard_map/attend_back/pallas_call | solution.py:294
  139.2 0.0 collective-permute-done.1.from_y_hbm
  139.2 0.0 copy-start
  139.2 0.0 collective-permute-done.2.from_x_hbm
  139.2 0.0 copy-start.1
  139.2 0.0 collective-permute-done.3.from_xy_hbm
  139.2 0.0 copy-start.2
  139.2 0.8 copy-done
  140.0 0.2 copy-done.1
  140.2 0.2 copy-done.2
  140.4 65.8 %tail.1 = (bf16[2,512,512]{2,1,0:T(8,128)(2,1)}, bf16[3,2,192,512]{3,2,1,0:T(8,128)(2,1)}, bf16[4,128,384]{2,1,0:T(8,128)(2,1)}, f32[16,512]{1,0:T(8,128)}) custom-call(bf16[4,1024,384]{2,1,0:T(8,128)(2,1)} %bitcast.19, bf16[512,4096]{1,0:T(8,128)(2,1)} %get-tuple-element.79.ut_hbm, bf16[1024,512]{1,0:T(8,128)(2,1)} %get-tuple-element.65.x_ref.x_hbm, ...), custom_call_target="tpu_custom_call" | custom-call | tf_op jit(solution)/shard_map/tail/pallas_call | solution.py:1632
  206.2 0.0 collective-permute-done.y_far_ref
  206.2 0.0 copy-start.3
  206.2 0.8 copy-done.3
  207.0 5.5 %results.1 = (bf16[2,1,512,512]{3,2,1,0:T(8,128)(2,1)}, f32[2,1,512,512]{3,2,1,0:T(8,128)}, f32[512,512]{1,0:T(8,128)}, f32[128,2048]{1,0:T(8,128)}, f32[128,512...) custom-call(bf16[512,512]{1,0:T(8,128)(2,1)} %get-tuple-element.72.y, ...), custom_call_target="tpu_custom_call" | custom-call | tf_op jit(solution)/shard_map/results/pallas_call | solution.py:1728
Async XLA Ops:
  103.3 35.8 %collective-permute-start.1 = (bf16[3,192,512]{2,1,0:T(8,128)(2,1)}, bf16[3,192,512]{2,1,0:T(8,128)(2,1)S(1)}, u32[]{:S(2)}, u32[]{:S(2)}) collective-permute-start(bf16[3,192,512]{2,1,0:T(8,128)(2,1)} %get-tuple-element.82), channel_id=1, source_target_pairs={{0,2},{1,3},{2,0},{3,1},{4,6},{5,7},{6,4},{7,5},{8,10},{9,11},{10,... | collective-permute-start | bytes 1769480 | tf_op jit(solution)/shard_map/ppermute | solution.py:1785
  105.9 33.2 %collective-permute-start.2 = (bf16[3,192,512]{2,1,0:T(8,128)(2,1)}, bf16[3,192,512]{2,1,0:T(8,128)(2,1)S(1)}, u32[]{:S(2)}, u32[]{:S(2)}) collective-permute-start(bf16[3,192,512]{2,1,0:T(8,128)(2,1)} %get-tuple-element.83), channel_id=1, source_target_pairs={{0,4},{1,5},{2,6},{3,7},{4,0},{5,1},{6,2},{7,3},{8,12},{9,13},{10,... | collective-permute-start | bytes 1769480 | tf_op jit(solution)/shard_map/ppermute | solution.py:1785
  107.2 32.0 %collective-permute-start.3 = (bf16[3,192,512]{2,1,0:T(8,128)(2,1)}, bf16[3,192,512]{2,1,0:T(8,128)(2,1)S(1)}, u32[]{:S(2)}, u32[]{:S(2)}) collective-permute-start(bf16[3,192,512]{2,1,0:T(8,128)(2,1)} %get-tuple-element.84), channel_id=1, source_target_pairs={{0,6},{1,7},{2,4},{3,5},{4,2},{5,3},{6,0},{7,1},{8,14},{9,15},{10,... | collective-permute-start | bytes 1769480 | tf_op jit(solution)/shard_map/ppermute | solution.py:1785
  107.5 98.7 %collective-permute-start = (bf16[512,512]{1,0:T(8,128)(2,1)}, bf16[512,512]{1,0:T(8,128)(2,1)S(1)}, u32[]{:S(2)}, u32[]{:S(2)}) collective-permute-start(bf16[512,512]{1,0:T(8,128)(2,1)} %get-tuple-element.73), channel_id=1, source_target_pairs={{0,8},{1,24},{2,10},{3,26},{4,12},{5,28},{6,14},{7,30},{8,9},{9,25... | collective-permute-start | bytes 1572872 | tf_op jit(solution)/shard_map/ppermute | solution.py:1785
  139.2 0.8 copy-start
  139.2 1.0 copy-start.1
  139.2 1.2 copy-start.2
  206.2 0.8 copy-start.3

commit v8 on v7

--- a/solution.py
+++ b/solution.py
@@ -1571,42 +1571,42 @@
     share(6)
     add_core(4)
     share(7)
-    add_core(5)
     weight(0)
+    finish(0)
     weight(1)
-    weight(2)
-    weight(3)
-    weight_close()
     g_second(0)
     g_second(1)
     g_second(2)
+    weight(2)
+    finish(1)
+    add_core(5)
+    weight(3)
+    weight_close()
     add_core(6)
-    add_core(7)
     s_next(0)
     w_second()
-    finish(0)
     g_third(0)
     g_third(1)
     g_third(2)
+    finish(2)
+    add_core(7)
     s_next(1)
     w_third()
-    finish(1)
     g_fourth(0)
     g_fourth(1)
     g_fourth(2)
+    finish(3)
     s_next(2)
     w_fourth()
-    finish(2)
     g_fifth(0)
     g_fifth(1)
     g_fifth(2)
+    finish(4)
     w_fifth()
     s_next(3)
-    finish(3)
     w_sixth()
-    finish(4)
+    finish(5)
     s_next(4)
-    finish(5)
     finish(6)
     finish(7)
     w_copy["core"].wait()

time: 213 us -> 212 us (level)
  transfers between devices with their start and end apart: 4 -> 4, of which waited for: 0 -> 0; matrix products, arithmetic and copies ran while one was open for 0% -> 0% of each run, Pallas kernels for 46% -> 45%
where the time goes in v8:
time: 212 us
  Pallas kernels  205 us (97%)
  starting transfers between devices  4.1 us (2%)
    pallas_call x1, Pallas kernels, tail(): pl.pallas_call(tail_kernel, in_specs=[pl.BlockSpec(memory_space=pl.ANY)]...  64.6 us
    pallas_call x1, Pallas kernels, head(): pl.pallas_call(head_kernel, in_specs=[any_, any_, vmem, smem] + [vmem] *...  47.1 us
    pallas_call x1, Pallas kernels, feed(): pl.pallas_call(feed_kernel, grid=(feed_steps,), in_specs=[any_, rows, pl....  37 us
    pallas_call x1, Pallas kernels, attend_back(): pl.pallas_call(attend_back_kernel, grid_spec=pltpu.PrefetchScalarGridSpec...  31.3 us
    pallas_call x1, Pallas kernels, attend(): pl.pallas_call(attend_kernel, grid_spec=pltpu.PrefetchScalarGridSpec(num_...  19.3 us
    pallas_call x1, Pallas kernels, results(): pl.pallas_call(results_kernel, grid=(steps,), in_specs=[pl.BlockSpec((hal...  5.46 us
  transfers between devices with their start and end apart: 4, of which 0 were waited for; matrix products, arithmetic and copies ran while one was open for 0% of the time, Pallas kernels for 45%

profile of v8, /device:TPU:0, one launch (start us, length us, event | category | flops | bytes accessed | tf_op | source)
XLA Modules:
  0.0 211.8 jit_solution(11000662825710751385)
XLA Ops:
  0.7 47.1 %head.1 = (bf16[128,4096]{1,0:T(8,128)(2,1)}, bf16[4096,128]{1,0:T(8,128)(2,1)}, bf16[128,4096]{1,0:T(8,128)(2,1)}, bf16[4096,128]{1,0:T(8,128)(2,1)}, bf16[128,...) custom-call(bf16[2,1,512,512]{3,2,1,0:T(8,128)(2,1)} %x_in_ref.1, ...), custom_call_target="tpu_custom_call" | custom-call | tf_op jit(solution)/shard_map/head/pallas_call | solution.py:995
  47.8 19.3 %attend.1 = (bf16[4096,128]{1,0:T(8,128)(2,1)}, f32[16,128,256]{2,1,0:T(8,128)}, f32[16,1,512]{2,1,0:T(1,128)}) custom-call(s32[8,128]{1,0:T(8,128)} %get-tuple-element.59.tab_ref, bf16[128,4096]{1,0:T(8,128)(2,1)} %get-tuple-element.60.qt_ref, s32[16,1,256]{2,1,0:T(1,128)} %get-tuple-element.61.start_ref, bf16[4096,128]{1,0:T(8,128)(2,1)} %get-tuple-element.62.k_ref.k_hbm, ...), custom_call_target="tpu_custom_call" | custom-call | tf_op jit(solution)/shard_map/attend/pallas_call | solution.py:169
  67.1 37.0 %feed.1 = (bf16[4,1024,128]{2,1,0:T(8,128)(2,1)}, bf16[512,512]{1,0:T(8,128)(2,1)}, bf16[512,512]{1,0:T(8,128)(2,1)}, f32[1024,512]{1,0:T(8,128)}, bf16[3,192,51...) custom-call(bf16[4,1024,128]{2,1,0:T(8,128)(2,1)} %bitcast.24, ...), custom_call_target="tpu_custom_call" | custom-call | tf_op jit(solution)/shard_map/feed/pallas_call | solution.py:1269
  104.1 1.8 collective-permute-start.1
  105.9 1.3 collective-permute-start.2
  107.2 0.5 collective-permute-start.3
  107.7 0.5 collective-permute-start
  108.2 31.3 %attend_back.1 = bf16[4096,384]{1,0:T(8,128)(2,1)} custom-call(s32[8,128]{1,0:T(8,128)} %get-tuple-element.59.tab_ref, bf16[4096,128]{1,0:T(8,128)(2,1)} %get-tuple-element.62.k_ref.k_hbm, bf16[128,4096]{1,0:T(8,128)(2,1)} %get-tuple-element.74.kt_hbm, bf16[4096,128]{1,0:T(8,128)(2,1)} %get-tuple-element.75.v_hbm, ...), custom_call_target="tpu_custom_call" | custom-call | tf_op jit(solution)/shard_map/attend_back/pallas_call | solution.py:294
  139.5 0.0 collective-permute-done.1.from_y_hbm
  139.5 0.0 copy-start
  139.5 0.0 collective-permute-done.2.from_x_hbm
  139.5 0.0 copy-start.1
  139.5 0.0 collective-permute-done.3.from_xy_hbm
  139.6 0.0 copy-start.2
  139.6 0.8 copy-done
  140.3 0.2 copy-done.1
  140.5 0.2 copy-done.2
  140.7 64.6 %tail.1 = (bf16[2,512,512]{2,1,0:T(8,128)(2,1)}, bf16[3,2,192,512]{3,2,1,0:T(8,128)(2,1)}, bf16[4,128,384]{2,1,0:T(8,128)(2,1)}, f32[16,512]{1,0:T(8,128)}) custom-call(bf16[4,1024,384]{2,1,0:T(8,128)(2,1)} %bitcast.19, bf16[512,4096]{1,0:T(8,128)(2,1)} %get-tuple-element.79.ut_hbm, bf16[1024,512]{1,0:T(8,128)(2,1)} %get-tuple-element.65.x_ref.x_hbm, ...), custom_call_target="tpu_custom_call" | custom-call | tf_op jit(solution)/shard_map/tail/pallas_call | solution.py:1632
  205.3 0.0 collective-permute-done.y_far_ref
  205.4 0.0 copy-start.3
  205.4 0.8 copy-done.3
  206.2 5.5 %results.1 = (bf16[2,1,512,512]{3,2,1,0:T(8,128)(2,1)}, f32[2,1,512,512]{3,2,1,0:T(8,128)}, f32[512,512]{1,0:T(8,128)}, f32[128,2048]{1,0:T(8,128)}, f32[128,512...) custom-call(bf16[512,512]{1,0:T(8,128)(2,1)} %get-tuple-element.72.y, ...), custom_call_target="tpu_custom_call" | custom-call | tf_op jit(solution)/shard_map/results/pallas_call | solution.py:1728
Async XLA Ops:
  104.1 35.4 %collective-permute-start.1 = (bf16[3,192,512]{2,1,0:T(8,128)(2,1)}, bf16[3,192,512]{2,1,0:T(8,128)(2,1)S(1)}, u32[]{:S(2)}, u32[]{:S(2)}) collective-permute-start(bf16[3,192,512]{2,1,0:T(8,128)(2,1)} %get-tuple-element.82), channel_id=1, source_target_pairs={{0,2},{1,3},{2,0},{3,1},{4,6},{5,7},{6,4},{7,5},{8,10},{9,11},{10,... | collective-permute-start | bytes 1769480 | tf_op jit(solution)/shard_map/ppermute | solution.py:1785
  105.9 33.6 %collective-permute-start.2 = (bf16[3,192,512]{2,1,0:T(8,128)(2,1)}, bf16[3,192,512]{2,1,0:T(8,128)(2,1)S(1)}, u32[]{:S(2)}, u32[]{:S(2)}) collective-permute-start(bf16[3,192,512]{2,1,0:T(8,128)(2,1)} %get-tuple-element.83), channel_id=1, source_target_pairs={{0,4},{1,5},{2,6},{3,7},{4,0},{5,1},{6,2},{7,3},{8,12},{9,13},{10,... | collective-permute-start | bytes 1769480 | tf_op jit(solution)/shard_map/ppermute | solution.py:1785
  107.2 32.4 %collective-permute-start.3 = (bf16[3,192,512]{2,1,0:T(8,128)(2,1)}, bf16[3,192,512]{2,1,0:T(8,128)(2,1)S(1)}, u32[]{:S(2)}, u32[]{:S(2)}) collective-permute-start(bf16[3,192,512]{2,1,0:T(8,128)(2,1)} %get-tuple-element.84), channel_id=1, source_target_pairs={{0,6},{1,7},{2,4},{3,5},{4,2},{5,3},{6,0},{7,1},{8,14},{9,15},{10,... | collective-permute-start | bytes 1769480 | tf_op jit(solution)/shard_map/ppermute | solution.py:1785
  107.7 97.6 %collective-permute-start = (bf16[512,512]{1,0:T(8,128)(2,1)}, bf16[512,512]{1,0:T(8,128)(2,1)S(1)}, u32[]{:S(2)}, u32[]{:S(2)}) collective-permute-start(bf16[512,512]{1,0:T(8,128)(2,1)} %get-tuple-element.73), channel_id=1, source_target_pairs={{0,8},{1,24},{2,10},{3,26},{4,12},{5,28},{6,14},{7,30},{8,9},{9,25... | collective-permute-start | bytes 1572872 | tf_op jit(solution)/shard_map/ppermute | solution.py:1785
  139.5 0.8 copy-start
  139.5 1.0 copy-start.1
  139.6 1.2 copy-start.2
  205.4 0.8 copy-start.3

commit v9 on v8

--- a/solution.py
+++ b/solution.py
@@ -228,12 +228,12 @@
             [jnp.sum(both[:HD], axis=0, keepdims=True), jnp.sum(both[HD:], axis=0, keepdims=True)], axis=1
         )
 
-    def prepare_two(n, carry):
-        prepare(2 * n)
-        prepare(2 * n + 1)
+    def prepare_four(n, carry):
+        for i in range(4):
+            prepare(4 * n + i)
         return carry
 
-    lax.fori_loop(0, blocks // 2, prepare_two, 0)
+    lax.fori_loop(0, blocks // 4, prepare_four, 0)
     for copy in loads:
         copy.wait()
 

time: 212 us -> 210 us (level)
    pallas_call x1, Pallas kernels: 64.6 us -> 62.5 us  [tail(): pl.pallas_call(tail_kernel, in_specs=[pl.BlockSpec(memory_space=pl.ANY)]...]
where the time goes in v9:
time: 210 us
  Pallas kernels  203 us (97%)
  starting transfers between devices  4.12 us (2%)
    pallas_call x1, Pallas kernels, tail(): pl.pallas_call(tail_kernel, in_specs=[pl.BlockSpec(memory_space=pl.ANY)]...  62.5 us
    pallas_call x1, Pallas kernels, head(): pl.pallas_call(head_kernel, in_specs=[any_, any_, vmem, smem] + [vmem] *...  47.1 us
    pallas_call x1, Pallas kernels, feed(): pl.pallas_call(feed_kernel, grid=(feed_steps,), in_specs=[any_, rows, pl....  37.1 us
    pallas_call x1, Pallas kernels, attend_back(): pl.pallas_call(attend_back_kernel, grid_spec=pltpu.PrefetchScalarGridSpec...  31.3 us
    pallas_call x1, Pallas kernels, attend(): pl.pallas_call(attend_kernel, grid_spec=pltpu.PrefetchScalarGridSpec(num_...  19.3 us
    pallas_call x1, Pallas kernels, results(): pl.pallas_call(results_kernel, grid=(steps,), in_specs=[pl.BlockSpec((hal...  5.46 us
  transfers between devices with their start and end apart: 4, of which 0 were waited for; matrix products, arithmetic and copies ran while one was open for 0% of the time, Pallas kernels for 45%

profile of v9, /device:TPU:0, one launch (start us, length us, event | category | flops | bytes accessed | tf_op | source)
XLA Modules:
  0.0 209.8 jit_solution(9658492343409587553)
XLA Ops:
  0.7 47.1 %head.1 = (bf16[128,4096]{1,0:T(8,128)(2,1)}, bf16[4096,128]{1,0:T(8,128)(2,1)}, bf16[128,4096]{1,0:T(8,128)(2,1)}, bf16[4096,128]{1,0:T(8,128)(2,1)}, bf16[128,...) custom-call(bf16[2,1,512,512]{3,2,1,0:T(8,128)(2,1)} %x_in_ref.1, ...), custom_call_target="tpu_custom_call" | custom-call | tf_op jit(solution)/shard_map/head/pallas_call | solution.py:995
  47.8 19.3 %attend.1 = (bf16[4096,128]{1,0:T(8,128)(2,1)}, f32[16,128,256]{2,1,0:T(8,128)}, f32[16,1,512]{2,1,0:T(1,128)}) custom-call(s32[8,128]{1,0:T(8,128)} %get-tuple-element.59.tab_ref, bf16[128,4096]{1,0:T(8,128)(2,1)} %get-tuple-element.60.qt_ref, s32[16,1,256]{2,1,0:T(1,128)} %get-tuple-element.61.start_ref, bf16[4096,128]{1,0:T(8,128)(2,1)} %get-tuple-element.62.k_ref.k_hbm, ...), custom_call_target="tpu_custom_call" | custom-call | tf_op jit(solution)/shard_map/attend/pallas_call | solution.py:169
  67.1 37.1 %feed.1 = (bf16[4,1024,128]{2,1,0:T(8,128)(2,1)}, bf16[512,512]{1,0:T(8,128)(2,1)}, bf16[512,512]{1,0:T(8,128)(2,1)}, f32[1024,512]{1,0:T(8,128)}, bf16[3,192,51...) custom-call(bf16[4,1024,128]{2,1,0:T(8,128)(2,1)} %bitcast.24, ...), custom_call_target="tpu_custom_call" | custom-call | tf_op jit(solution)/shard_map/feed/pallas_call | solution.py:1269
  104.2 1.7 collective-permute-start.1
  105.9 1.3 collective-permute-start.2
  107.2 0.6 collective-permute-start.3
  107.8 0.6 collective-permute-start
  108.3 31.3 %attend_back.1 = bf16[4096,384]{1,0:T(8,128)(2,1)} custom-call(s32[8,128]{1,0:T(8,128)} %get-tuple-element.59.tab_ref, bf16[4096,128]{1,0:T(8,128)(2,1)} %get-tuple-element.62.k_ref.k_hbm, bf16[128,4096]{1,0:T(8,128)(2,1)} %get-tuple-element.74.kt_hbm, bf16[4096,128]{1,0:T(8,128)(2,1)} %get-tuple-element.75.v_hbm, ...), custom_call_target="tpu_custom_call" | custom-call | tf_op jit(solution)/shard_map/attend_back/pallas_call | solution.py:294
  139.6 0.0 collective-permute-done.1.from_y_hbm
  139.6 0.0 copy-start
  139.6 0.0 collective-permute-done.2.from_x_hbm
  139.6 0.0 copy-start.1
  139.6 0.0 collective-permute-done.3.from_xy_hbm
  139.6 0.0 copy-start.2
  139.6 0.8 copy-done
  140.4 0.2 copy-done.1
  140.6 0.2 copy-done.2
  140.8 62.5 %tail.1 = (bf16[2,512,512]{2,1,0:T(8,128)(2,1)}, bf16[3,2,192,512]{3,2,1,0:T(8,128)(2,1)}, bf16[4,128,384]{2,1,0:T(8,128)(2,1)}, f32[16,512]{1,0:T(8,128)}) custom-call(bf16[4,1024,384]{2,1,0:T(8,128)(2,1)} %bitcast.19, bf16[512,4096]{1,0:T(8,128)(2,1)} %get-tuple-element.79.ut_hbm, bf16[1024,512]{1,0:T(8,128)(2,1)} %get-tuple-element.65.x_ref.x_hbm, ...), custom_call_target="tpu_custom_call" | custom-call | tf_op jit(solution)/shard_map/tail/pallas_call | solution.py:1632
  203.3 0.0 collective-permute-done.y_far_ref
  203.3 0.0 copy-start.3
  203.3 0.8 copy-done.3
  204.1 5.5 %results.1 = (bf16[2,1,512,512]{3,2,1,0:T(8,128)(2,1)}, f32[2,1,512,512]{3,2,1,0:T(8,128)}, f32[512,512]{1,0:T(8,128)}, f32[128,2048]{1,0:T(8,128)}, f32[128,512...) custom-call(bf16[512,512]{1,0:T(8,128)(2,1)} %get-tuple-element.72.y, ...), custom_call_target="tpu_custom_call" | custom-call | tf_op jit(solution)/shard_map/results/pallas_call | solution.py:1728
Async XLA Ops:
  104.2 35.4 %collective-permute-start.1 = (bf16[3,192,512]{2,1,0:T(8,128)(2,1)}, bf16[3,192,512]{2,1,0:T(8,128)(2,1)S(1)}, u32[]{:S(2)}, u32[]{:S(2)}) collective-permute-start(bf16[3,192,512]{2,1,0:T(8,128)(2,1)} %get-tuple-element.82), channel_id=1, source_target_pairs={{0,2},{1,3},{2,0},{3,1},{4,6},{5,7},{6,4},{7,5},{8,10},{9,11},{10,... | collective-permute-start | bytes 1769480 | tf_op jit(solution)/shard_map/ppermute | solution.py:1785
  105.9 33.7 %collective-permute-start.2 = (bf16[3,192,512]{2,1,0:T(8,128)(2,1)}, bf16[3,192,512]{2,1,0:T(8,128)(2,1)S(1)}, u32[]{:S(2)}, u32[]{:S(2)}) collective-permute-start(bf16[3,192,512]{2,1,0:T(8,128)(2,1)} %get-tuple-element.83), channel_id=1, source_target_pairs={{0,4},{1,5},{2,6},{3,7},{4,0},{5,1},{6,2},{7,3},{8,12},{9,13},{10,... | collective-permute-start | bytes 1769480 | tf_op jit(solution)/shard_map/ppermute | solution.py:1785
  107.2 32.4 %collective-permute-start.3 = (bf16[3,192,512]{2,1,0:T(8,128)(2,1)}, bf16[3,192,512]{2,1,0:T(8,128)(2,1)S(1)}, u32[]{:S(2)}, u32[]{:S(2)}) collective-permute-start(bf16[3,192,512]{2,1,0:T(8,128)(2,1)} %get-tuple-element.84), channel_id=1, source_target_pairs={{0,6},{1,7},{2,4},{3,5},{4,2},{5,3},{6,0},{7,1},{8,14},{9,15},{10,... | collective-permute-start | bytes 1769480 | tf_op jit(solution)/shard_map/ppermute | solution.py:1785
  107.8 95.6 %collective-permute-start = (bf16[512,512]{1,0:T(8,128)(2,1)}, bf16[512,512]{1,0:T(8,128)(2,1)S(1)}, u32[]{:S(2)}, u32[]{:S(2)}) collective-permute-start(bf16[512,512]{1,0:T(8,128)(2,1)} %get-tuple-element.73), channel_id=1, source_target_pairs={{0,8},{1,24},{2,10},{3,26},{4,12},{5,28},{6,14},{7,30},{8,9},{9,25... | collective-permute-start | bytes 1572872 | tf_op jit(solution)/shard_map/ppermute | solution.py:1785
  139.6 0.8 copy-start
  139.6 1.0 copy-start.1
  139.6 1.2 copy-start.2
  203.3 0.8 copy-start.3
